TPU v7x, 512 devices: a whole 4x4x16 slice. The times are simulated.
512 devices in a mesh: seq: 32 (over z_hi, x, core), sub: 16 (over z_lo, y).
Axes of the slice: x: 4, y: 4, z: 16 (z_hi: 4, z_lo: 4; z = z_hi * 4 + z_lo), core: 2. Of those that a mesh axis runs over, the one named last changes fastest.
Arguments:
- activations: bfloat16 [65536, 1024], P(('seq', 'sub')), may hold values from -6 to 6
- conv_weight: bfloat16 [5, 1152, 1024], P(None, 'sub'), may hold values from -1 to 1
- cotangent: bfloat16 [16384, 1152], P('seq', 'sub'), may hold values from -6 to 6
Outputs:
- features: bfloat16 [16384, 1152], P('seq', 'sub')
- input_grad: bfloat16 [65536, 1024], P(('seq', 'sub'))
- weight_grad: float32 [1024, 5, 1152], P('seq', None, 'sub')
All inputs are finite; a program needn't handle non-finite values.
Results may differ from a plain program's by a relative error of at most 0.02.
Values may be sent and summed in bfloat16 or wider, within the bound.
No kernel may reach another device: no remote copies, remote signals or barrier semaphores. Data moves between devices by JAX's collectives and lax.ppermute only.
A program may use at most 64 MiB of HBM per device.

v0:
```python
import jax
import jax.numpy as jnp
from jax import lax
from jax.sharding import PartitionSpec as P

EPSILON = 1e-06


def padded_2(block, sides, width):
    for axis, dim in sides:
        count = lax.axis_size(axis)
        forward = [(i, i + 1) for i in range(count - 1)]
        backward = [(target, source) for source, target in forward]
        low = lax.ppermute(
            lax.slice_in_dim(block, block.shape[dim] - width, None, axis=dim), axis, forward
        )
        high = lax.ppermute(lax.slice_in_dim(block, 0, width, axis=dim), axis, backward)
        block = jnp.concatenate([low, block, high], axis=dim)
    return block


def gelu_slope(tensor):
    return (
        0.5 * (1.0 + jax.scipy.special.erf(tensor * 0.7071067811865476))
        + tensor * jnp.exp(-0.5 * tensor * tensor) * 0.3989422804014327
    )


def pool_pairs(tensor):
    half_rows = tensor.shape[0] // 2
    return 0.5 * jnp.sum(tensor.reshape(half_rows, 2, tensor.shape[1]), axis=1)


def per_device(activations, conv_weight, cotangent):
    tap_count = conv_weight.shape[0]
    in_width = activations.shape[1]
    out_width = conv_weight.shape[1]
    full_out = out_width * lax.axis_size("sub")
    x_float = activations.astype(jnp.float32)
    inv_first = lax.rsqrt(jnp.mean(x_float * x_float, axis=1, keepdims=True) + EPSILON)
    normed_first = x_float * inv_first
    pooled = pool_pairs(jax.nn.gelu(normed_first, approximate=False)).astype(jnp.bfloat16)
    gathered = lax.all_gather(pooled, "sub", axis=0, tiled=True)
    block_rows = gathered.shape[0]
    padded = padded_2(gathered, (("seq", 0),), 2)
    conv_acc = jnp.zeros((block_rows, out_width), jnp.float32)
    for offset in range(tap_count):
        conv_acc = conv_acc + lax.dot_general(
            padded[offset : offset + block_rows],
            conv_weight[offset],
            (((1,), (1,)), ((), ())),
            preferred_element_type=jnp.float32,
        )
    conv_out = conv_acc.astype(jnp.bfloat16)
    y_float = conv_out.astype(jnp.float32)
    square_sum = lax.psum(jnp.sum(y_float * y_float, axis=1), "sub")
    inv_second = lax.rsqrt(square_sum / full_out + EPSILON)[:, None]
    normed_second = y_float * inv_second
    features = pool_pairs(jax.nn.gelu(normed_second, approximate=False)).astype(jnp.bfloat16)
    upstream = 0.5 * jnp.repeat(cotangent.astype(jnp.float32), 2, axis=0)
    slope_second = upstream * gelu_slope(normed_second)
    inner_second = lax.psum(jnp.sum(slope_second * normed_second, axis=1), "sub")
    conv_grad = (
        inv_second * (slope_second - normed_second * (inner_second / full_out)[:, None])
    ).astype(jnp.bfloat16)
    grad_padded = padded_2(conv_grad, (("seq", 0),), 2)
    running = jnp.zeros((block_rows, in_width), jnp.float32)
    for offset in range(tap_count):
        window = lax.dynamic_slice_in_dim(grad_padded, 0 + 4 - offset, block_rows, 0)
        running = running + jnp.dot(window, conv_weight[offset], preferred_element_type=jnp.float32)
    owned = lax.psum_scatter(
        running.astype(jnp.bfloat16), "sub", scatter_dimension=1, tiled=True
    ).astype(jnp.float32)
    pooled_grad = lax.all_to_all(
        owned.astype(jnp.bfloat16), "sub", split_axis=0, concat_axis=1, tiled=True
    ).astype(owned.dtype)
    slope_first = 0.5 * jnp.repeat(pooled_grad, 2, axis=0) * gelu_slope(normed_first)
    inner_first = jnp.mean(slope_first * normed_first, axis=1, keepdims=True)
    input_grad = (inv_first * (slope_first - normed_first * inner_first)).astype(jnp.bfloat16)
    pieces = [
        lax.dot_general(
            padded[offset : offset + block_rows],
            conv_grad,
            (((0,), (0,)), ((), ())),
            preferred_element_type=jnp.float32,
        )
        for offset in range(tap_count)
    ]
    weight_grad = lax.psum_scatter(
        jnp.stack(pieces, axis=1).astype(jnp.bfloat16), "seq", scatter_dimension=0, tiled=True
    ).astype(jnp.float32)
    return (features, input_grad, weight_grad)


def solution(mesh):
    return jax.shard_map(
        per_device,
        mesh=mesh,
        in_specs=(P(("seq", "sub"), None), P(None, "sub", None), P("seq", "sub")),
        out_specs=(P("seq", "sub"), P(("seq", "sub"), None), P("seq", None, "sub")),
        check_vma=False,
    )
```

profile of v0, /device:TPU:8, one launch (start us, length us, event | category | flops | bytes accessed | tf_op | source)
XLA Modules:
  0.0 446.3 jit_solution(8332122157335202841)
XLA Ops:
  7.2 1.1 fusion.93
  8.3 2.2 fusion.55
  12.7 91.6 %all-gather.2.cloned.1.call-done = bf16[1024,1024]{1,0:T(8,128)(2,1)} async-done(((bf16[64,1024]{1,0:T(8,128)(2,1)}), bf16[1024,1024]{1,0:T(8,128)(2,1)}) %all-gather.2.cloned.1.call-update) | async-done | bytes 2097168 | tf_op jit(solution)/shard_map/all_gather | solution.py:43
  104.3 0.9 fusion.151
  105.2 1.3 collective-permute-start
  106.5 1.3 collective-permute-start.1
  107.8 2.4 fusion.125
  110.3 0.9 collective-permute-done.1
  111.3 0.8 fusion.3
  112.1 0.7 fusion.9
  112.8 0.8 fusion.17
  113.6 1.7 multiply_reduce_fusion.1
  115.3 38.7 %psum.14 = f32[1024]{0:T(1024)S(1)} all-reduce(f32[1024]{0:T(1024)S(1)} %get-tuple-element.22), channel_id=1, replica_groups=mesh['seq'=32,'sub'=16] {'sub'}, use_global_device_ids=true, to_apply=%region_3.0 | all-reduce | flops 1024 | bytes 8192 | tf_op jit(solution)/shard_map/psum | solution.py:56
  154.2 42.8 %psum.15 = f32[1024]{0:T(1024)S(1)} all-reduce(f32[1024]{0:T(1024)S(1)} %get-tuple-element.14), channel_id=1, replica_groups=mesh['seq'=32,'sub'=16] {'sub'}, use_global_device_ids=true, to_apply=%region_6.0 | all-reduce | flops 1024 | bytes 8192 | tf_op jit(solution)/shard_map/psum | solution.py:62
  197.0 0.7 multiply_convert_fusion
  197.8 1.4 collective-permute-start.2
  199.2 1.7 fusion.123
  200.8 3.0 collective-permute-start.3
  203.9 0.8 fusion.117
  204.7 0.8 fusion.113
  205.5 0.8 fusion.110
  206.3 2.8 add_convert_fusion
  211.2 1.1 copy-done.3
  213.6 2.5 copy.17
  216.2 92.8 %reduce-scatter.3.cloned.1.call-done = bf16[1024,64]{0,1:T(8,128)(2,1)} async-done(((bf16[1024,1024]{0,1:T(8,128)(2,1)}), bf16[1024,64]{0,1:T(8,128)(2,1)}) %reduce-scatter.3.cloned.1.call-update) | async-done | bytes 131088 | tf_op jit(solution)/shard_map/reduce_scatter | solution.py:71
  308.9 1.1 copy.20
  310.0 0.9 reshape.40
  310.9 8.1 %all-to-all-start = ((bf16[16,2,2048]{2,1,0:T(2,128)(2,1)}), bf16[16,2,2048]{2,1,0:T(2,128)(2,1)S(1)}, u32[]{:S(2)}, u32[]{:S(2)}) async-start(bf16[16,2,2048]{2,1,0:T(2,128)(2,1)} %reshape.40), calls=%async_computation.1 | async-start | bytes 262144 | tf_op jit(solution)/shard_map/all_to_all | solution.py:74
  319.9 0.7 copy.18
  320.6 114.9 %reduce-scatter.5.cloned.1.call-done = bf16[32,5,72]{2,1,0:T(8,128)(2,1)} async-done(((bf16[1024,5,72]{2,1,0:T(8,128)(2,1)}), bf16[32,5,72]{2,1,0:T(8,128)(2,1)}) %reduce-scatter.5.cloned.1.call-update) | async-done | bytes 23056 | tf_op jit(solution)/shard_map/reduce_scatter | solution.py:89
  435.5 1.5 copy.19
  438.8 1.0 fusion.90
  (53 shorter events, 8.7 us)
Async XLA Ops:
  7.2 5.0 %copy-start.6 = (bf16[512,72]{0,1:T(8,128)(2,1)S(1)}, bf16[512,72]{0,1:T(8,128)(2,1)}, u32[]{:S(2)}) copy-start(bf16[512,72]{0,1:T(8,128)(2,1)} %param.5) | copy-start | bytes 221188
  7.2 97.1 %all-gather.2.cloned.1.call-start = ((), (), s32[]{:S(2)}) async-start(), calls=%async_computation.3 | async-start | bytes 2228224 | tf_op jit(solution)/shard_map/all_gather | solution.py:43
  10.5 97.3 %copy-start.4 = (bf16[5,72,1024]{2,1,0:T(8,128)(2,1)S(1)}, bf16[5,72,1024]{2,1,0:T(8,128)(2,1)}, u32[]{:S(2)}) copy-start(bf16[5,72,1024]{2,1,0:T(8,128)(2,1)} %param.4) | copy-start | bytes 2211844
  12.1 296.8 %reduce-scatter.3.cloned.1.call-start = ((), (), s32[]{:S(2)}) async-start(), calls=%async_computation.4 | async-start | bytes 2228224 | tf_op jit(solution)/shard_map/reduce_scatter | solution.py:71
  104.3 5.9 %copy-start = (bf16[1024,1024]{1,0:T(8,128)(2,1)S(1)}, bf16[1024,1024]{1,0:T(8,128)(2,1)}, u32[]{:S(2)}) copy-start(bf16[1024,1024]{1,0:T(8,128)(2,1)} %all-gather.2.cloned.1.call-done) | copy-start | bytes 6291460
  105.2 6.8 %collective-permute-start = (bf16[2,1024]{1,0:T(2,128)(2,1)S(1)}, bf16[2,1024]{1,0:T(2,128)(2,1)S(1)}, u32[]{:S(2)}, u32[]{:S(2)}) collective-permute-start(bf16[2,1024]{1,0:T(2,128)(2,1)S(1)} %get-tuple-element.16), channel_id=1, source_target_pairs={{0,16},{16,32},{32,48},{48,64},{64,80},{80,96},{96,112},{112,128},... | collective-permute-start | bytes 12296 | tf_op jit(solution)/shard_map/ppermute | solution.py:14
  106.5 4.8 %collective-permute-start.1 = (bf16[2,1024]{1,0:T(2,128)(2,1)S(1)}, bf16[2,1024]{1,0:T(2,128)(2,1)S(1)}, u32[]{:S(2)}, u32[]{:S(2)}) collective-permute-start(bf16[2,1024]{1,0:T(2,128)(2,1)S(1)} %get-tuple-element.17), channel_id=1, source_target_pairs={{16,0},{32,16},{48,32},{64,48},{80,64},{96,80},{112,96},{128,112},... | collective-permute-start | bytes 12296 | tf_op jit(solution)/shard_map/ppermute | solution.py:17
  111.3 2.3 copy-start.2
  197.8 6.1 %copy-start.5 = (bf16[5,72,1024]{2,1,0:T(8,128)(2,1)S(1)}, bf16[5,72,1024]{2,1,0:T(8,128)(2,1)}, u32[]{:S(2)}) copy-start(bf16[5,72,1024]{2,1,0:T(8,128)(2,1)} %param.4) | copy-start | bytes 2211844
  197.8 6.1 %collective-permute-start.2 = (bf16[2,72]{0,1:T(8,128)(2,1)S(1)}, bf16[2,72]{0,1:T(8,128)(2,1)S(1)}, u32[]{:S(2)}, u32[]{:S(2)}) collective-permute-start(bf16[2,72]{0,1:T(8,128)(2,1)S(1)} %get-tuple-element.20), channel_id=1, source_target_pairs={{16,0},{32,16},{48,32},{64,48},{80,64},{96,80},{112,96},{128,112},... | collective-permute-start | bytes 872 | tf_op jit(solution)/shard_map/ppermute | solution.py:17
  200.8 4.7 %collective-permute-start.3 = (bf16[2,72]{0,1:T(8,128)(2,1)S(1)}, bf16[2,72]{0,1:T(8,128)(2,1)S(1)}, u32[]{:S(2)}, u32[]{:S(2)}) collective-permute-start(bf16[2,72]{0,1:T(8,128)(2,1)S(1)} %get-tuple-element.21), channel_id=1, source_target_pairs={{0,16},{16,32},{32,48},{48,64},{64,80},{80,96},{96,112},{112,128},... | collective-permute-start | bytes 872 | tf_op jit(solution)/shard_map/ppermute | solution.py:14
  209.1 226.4 %reduce-scatter.5.cloned.1.call-start = ((), (), s32[]{:S(2)}) async-start(), calls=%async_computation.5 | async-start | bytes 2162688 | tf_op jit(solution)/shard_map/reduce_scatter | solution.py:89
  210.7 1.6 copy-start.3
  310.9 126.1 %all-to-all-start = ((bf16[16,2,2048]{2,1,0:T(2,128)(2,1)}), bf16[16,2,2048]{2,1,0:T(2,128)(2,1)S(1)}, u32[]{:S(2)}, u32[]{:S(2)}) async-start(bf16[16,2,2048]{2,1,0:T(2,128)(2,1)} %reshape.40), calls=%async_computation.1 | async-start | bytes 262144 | tf_op jit(solution)/shard_map/all_to_all | solution.py:74
  437.2 1.1 copy-start.1
Sparse Core Ops, SparseCore 0:
  12.2 92.0 all-gather.1
  209.3 99.6 reduce-scatter.2
  313.3 122.1 reduce-scatter.4
where the time goes:
time: 447 us; the launch traced here: 446 us
  waiting for transfers between devices  300 us (67%)
  blocking collectives  81.5 us (18%)
  matrix products  16.3 us (4%)
  starting transfers between devices  15.5 us (3%)
  between operations  14 us (3%)
  local copies, waits for them, and re-layouts  11.2 us (3%)
  other arithmetic  7.52 us (2%)
    reduce_scatter x1, waiting for transfers between devices, per_device(): lax.psum_scatter(jnp.stack(pieces, axis=1).astype(jnp.bfloat16), 'seq', s...  115 us
    reduce_scatter x1, waiting for transfers between devices, per_device(): lax.psum_scatter(running.astype(jnp.bfloat16), 'sub', scatter_dimension=1...  92.8 us
    all_gather x1, waiting for transfers between devices, per_device(): gathered = lax.all_gather(pooled, 'sub', axis=0, tiled=True)  91.6 us
    psum x1, blocking collectives, per_device(): lax.psum(jnp.sum(slope_second * normed_second, axis=1), 'sub')  42.8 us
    psum x1, blocking collectives, per_device(): square_sum = lax.psum(jnp.sum(y_float * y_float, axis=1), 'sub')  38.7 us
  transfers between devices with their start and end apart: 8, of which 4 were waited for; matrix products, arithmetic and copies ran while one was open for 4% of the time, Pallas kernels for 0%

commit v1 on v0

v1 whole, which is shorter than its diff:
```python
import jax
import jax.numpy as jnp
from jax import lax
from jax.sharding import Mesh, PartitionSpec as P

EPSILON = 1e-06
AXES = ("zh", "x", "core", "zl", "y")
SEQ = ("zh", "x", "core")
SUB = ("zl", "y")
bf16 = jnp.bfloat16
f32 = jnp.float32


def gelu_slope(tensor):
    return (
        0.5 * (1.0 + jax.scipy.special.erf(tensor * 0.7071067811865476))
        + tensor * jnp.exp(-0.5 * tensor * tensor) * 0.3989422804014327
    )


def pool_pairs(tensor):
    half_rows = tensor.shape[0] // 2
    return 0.5 * jnp.sum(tensor.reshape(half_rows, 2, tensor.shape[1]), axis=1)


def shift(block, axis, step):
    count = lax.axis_size(axis)
    pairs = [(i, i + step) for i in range(count) if 0 <= i + step < count]
    return lax.ppermute(block, axis, pairs)


def padded_2(block):
    low = shift(block[-2:], SEQ, 1)
    high = shift(block[:2], SEQ, -1)
    return jnp.concatenate([low, block, high], axis=0)


def gather_all(block, axis):
    count = lax.axis_size(axis)
    return lax.all_to_all(jnp.broadcast_to(block, (count, *block.shape)), axis, 0, 0)


def small_sum(vector):
    return jnp.sum(gather_all(vector.reshape(8, 128), SUB), axis=0).reshape(-1)


def per_device(activations, conv_weight, cotangent):
    tap_count, out_width, in_width = conv_weight.shape
    full_out = out_width * lax.axis_size(SUB)
    x_float = activations.astype(f32)
    inv_first = lax.rsqrt(jnp.mean(x_float * x_float, axis=1, keepdims=True) + EPSILON)
    normed_first = x_float * inv_first
    pooled = pool_pairs(jax.nn.gelu(normed_first, approximate=False)).astype(bf16)
    gathered = gather_all(pooled, SUB).reshape(-1, in_width)
    rows = gathered.shape[0]
    padded = padded_2(gathered)
    conv_acc = jnp.zeros((rows, out_width), f32)
    for k in range(tap_count):
        conv_acc = conv_acc + lax.dot_general(
            padded[k : k + rows], conv_weight[k], (((1,), (1,)), ((), ())),
            preferred_element_type=f32,
        )
    conv_out = conv_acc.astype(bf16)
    y_float = conv_out.astype(f32)
    square_sum = small_sum(jnp.sum(y_float * y_float, axis=1))
    inv_second = lax.rsqrt(square_sum / full_out + EPSILON)[:, None]
    normed_second = y_float * inv_second
    features = pool_pairs(jax.nn.gelu(normed_second, approximate=False)).astype(bf16)
    upstream = 0.5 * jnp.repeat(cotangent.astype(f32), 2, axis=0)
    slope_second = upstream * gelu_slope(normed_second)
    inner_second = small_sum(jnp.sum(slope_second * normed_second, axis=1))
    conv_grad = (
        inv_second * (slope_second - normed_second * (inner_second / full_out)[:, None])
    ).astype(bf16)
    grad_padded = padded_2(conv_grad)
    windows = [grad_padded[4 - k : 4 - k + rows] for k in range(tap_count)]
    running = jnp.zeros((rows, in_width), f32)
    for k in range(tap_count):
        running = running + jnp.dot(windows[k], conv_weight[k], preferred_element_type=f32)
    parts = lax.all_to_all(running.astype(bf16).reshape(16, -1, in_width), SUB, 0, 0)
    pooled_grad = jnp.sum(parts.astype(f32), axis=0)
    slope_first = 0.5 * jnp.repeat(pooled_grad, 2, axis=0) * gelu_slope(normed_first)
    inner_first = jnp.mean(slope_first * normed_first, axis=1, keepdims=True)
    input_grad = (inv_first * (slope_first - normed_first * inner_first)).astype(bf16)

    wide = jnp.concatenate(windows, axis=1)
    weight_part = lax.dot_general(
        gathered, wide, (((0,), (0,)), ((), ())), preferred_element_type=f32
    )
    core = lax.axis_index("core")
    halves = weight_part.reshape(16, 2, 32, tap_count * out_width)
    mine = jnp.where(core == 0, halves[:, 0], halves[:, 1])
    other = jnp.where(core == 0, halves[:, 1], halves[:, 0]).astype(bf16)
    total = mine + lax.ppermute(other, "core", [(0, 1), (1, 0)]).astype(f32)
    total = total.reshape(4, 4, 32, -1).transpose(1, 0, 2, 3).astype(bf16)
    total = jnp.sum(lax.all_to_all(total, "x", 0, 0).astype(f32), axis=0)
    total = jnp.sum(lax.all_to_all(total.astype(bf16), "zh", 0, 0).astype(f32), axis=0)
    weight_grad = total.reshape(32, tap_count, out_width)
    return (features, input_grad, weight_grad)


def solution(mesh):
    split = Mesh(mesh.devices.reshape(4, 4, 2, 4, 4), AXES)
    return jax.shard_map(
        per_device,
        mesh=split,
        in_specs=(P(AXES, None), P(None, SUB, None), P(SEQ, SUB)),
        out_specs=(P(SEQ, SUB), P(AXES, None), P(SEQ, None, SUB)),
        check_vma=False,
    )
```

time: 447 us -> 232 us (0.52)
  the two profiles are of different devices: /device:TPU:8 before, /device:TPU:64 now
where the time goes in v1:
time: 232 us; the launch traced here: 231 us
  waiting for transfers between devices  66.6 us (29%)
  starting transfers between devices  62.5 us (27%)
  blocking collectives  56.4 us (24%)
  matrix products  28.1 us (12%)
  other arithmetic  8.67 us (4%)
  local copies, waits for them, and re-layouts  8 us (3%)
    all_to_all x1, blocking collectives, gather_all(): lax.all_to_all(jnp.broadcast_to(block, (count, *block.shape)), axis, 0, 0)  56.4 us
    all_to_all x1, waiting for transfers between devices, per_device(): lax.all_to_all(running.astype(bf16).reshape(16, -1, in_width), SUB, 0, 0)  43.8 us
    dot_general x5, matrix products, per_device(): jnp.dot(windows[k], conv_weight[k], preferred_element_type=f32)  23 us
    all_to_all x1, starting transfers between devices, per_device(): total = jnp.sum(lax.all_to_all(total, 'x', 0, 0).astype(f32), axis=0)  20.6 us
    all_to_all x1, starting transfers between devices, per_device(): lax.all_to_all(total.astype(bf16), 'zh', 0, 0).astype(f32)  13.9 us
    all_to_all x2, starting transfers between devices, gather_all(): lax.all_to_all(jnp.broadcast_to(block, (count, *block.shape)), axis, 0, 0)  11.5 us
    all_to_all x2, waiting for transfers between devices, gather_all(): lax.all_to_all(jnp.broadcast_to(block, (count, *block.shape)), axis, 0, 0)  8.91 us
    ppermute x4, starting transfers between devices, shift(): return lax.ppermute(block, axis, pairs)  7.01 us
  transfers between devices with their start and end apart: 10, of which 7 were waited for; matrix products, arithmetic and copies ran while one was open for 13% of the time, Pallas kernels for 0%

profile of v1, /device:TPU:64, one launch (start us, length us, event | category | flops | bytes accessed | tf_op | source)
XLA Modules:
  0.0 231.2 jit_solution(2087620436080150799)
XLA Ops:
  0.6 1.1 fusion.77
  1.7 2.2 fusion.39
  5.1 56.4 %all_to_all.30 = bf16[16,64,1024]{2,1,0:T(8,128)(2,1)S(1)} all-to-all(bf16[16,64,1024]{2,1,0:T(8,128)(2,1)S(1)} %broadcast_in_dim.19), channel_id=1, replica_groups=mesh['zh'=4,'x'=4,'core'=2,'zl'=4,'y'=4] {'zl','y'}, dimensions={0} | all-to-all | bytes 4194304 | tf_op jit(solution)/shard_map/all_to_all | solution.py:40
  61.5 1.3 collective-permute-start
  62.8 1.3 collective-permute-start.1
  64.1 0.8 fusion.106
  64.9 2.7 %collective-permute-done.1 = bf16[2,1024]{1,0:T(2,128)(2,1)S(1)} collective-permute-done((bf16[2,1024]{1,0:T(2,128)(2,1)S(1)}, bf16[2,1024]{1,0:T(2,128)(2,1)S(1)}, u32[]{:S(2)}, u32[]{:S(2)}) %collective-permute-start.1) | collective-permute-done | bytes 4128 | tf_op jit(solution)/shard_map/ppermute | solution.py:29
  67.6 0.8 fusion.2
  69.1 0.8 fusion.19
  69.9 0.8 multiply_reduce_fusion.1
  71.3 5.4 %all-to-all-start.1 = ((f32[16,8,128]{2,1,0:T(8,128)}), f32[16,8,128]{2,1,0:T(8,128)S(1)}, u32[]{:S(2)}, u32[]{:S(2)}) async-start(f32[16,8,128]{2,1,0:T(8,128)} %broadcast_in_dim.20), calls=%async_computation.1 | async-start | bytes 131072 | tf_op jit(solution)/shard_map/all_to_all | solution.py:40
  77.2 5.3 %all-to-all-done.1 = f32[16,8,128]{2,1,0:T(8,128)S(1)} async-done(((f32[16,8,128]{2,1,0:T(8,128)}), f32[16,8,128]{2,1,0:T(8,128)S(1)}, u32[]{:S(2)}, u32[]{:S(2)}) %all-to-all-start.1) | async-done | bytes 65568 | tf_op jit(solution)/shard_map/all_to_all | solution.py:40
  83.3 6.1 %all-to-all-start.2 = ((f32[16,8,128]{2,1,0:T(8,128)}), f32[16,8,128]{2,1,0:T(8,128)S(1)}, u32[]{:S(2)}, u32[]{:S(2)}) async-start(f32[16,8,128]{2,1,0:T(8,128)} %broadcast_in_dim.22), calls=%async_computation.2 | async-start | bytes 131072 | tf_op jit(solution)/shard_map/all_to_all | solution.py:40
  89.4 2.6 %copy.34 = bf16[1024,1024]{1,0:T(8,128)(2,1)} copy(bf16[1024,1024]{0,1:T(8,128)(2,1)S(1)} %bitcast.84) | data formatting | bytes 4194304 | tf_op jit(solution)/shard_map/dot_general | solution.py:87
  92.0 3.7 %all-to-all-done.2 = f32[16,8,128]{2,1,0:T(8,128)S(1)} async-done(((f32[16,8,128]{2,1,0:T(8,128)}), f32[16,8,128]{2,1,0:T(8,128)S(1)}, u32[]{:S(2)}, u32[]{:S(2)}) %all-to-all-start.2) | async-done | bytes 65568 | tf_op jit(solution)/shard_map/all_to_all | solution.py:40
  96.4 1.4 collective-permute-start.2
  97.8 3.6 %fusion.104 = f32[1024,1024]{1,0:T(8,128)} fusion(bf16[1024,72]{0,1:T(8,128)(2,1)S(1)} %get-tuple-element.18, bf16[5,72,1024]{2,1,0:T(8,128)(2,1)} %param.4), kind=kOutput, calls=%fused_computation.126 | convolution fusion | flops 150994944 | bytes 4489216 | tf_op jit(solution)/shard_map/dot_general | solution.py:79
  101.4 3.0 %collective-permute-start.3 = (bf16[2,72]{0,1:T(8,128)(2,1)S(1)}, bf16[2,72]{0,1:T(8,128)(2,1)S(1)}, u32[]{:S(2)}, u32[]{:S(2)}) collective-permute-start(bf16[2,72]{0,1:T(8,128)(2,1)S(1)} %get-tuple-element.21), channel_id=1, source_target_pairs={{0,16},{16,32},{32,48},{48,64},{64,80},{80,96},{96,112},{112,128},... | collective-permute-start | bytes 872 | tf_op jit(solution)/shard_map/ppermute | solution.py:29
  105.5 1.3 fusion.31
  106.9 3.8 %collective-permute-start.4 = (bf16[16,32,360]{2,1,0:T(8,128)(2,1)S(1)}, bf16[16,32,360]{2,1,0:T(8,128)(2,1)S(1)}, u32[]{:S(2)}, u32[]{:S(2)}) collective-permute-start(bf16[16,32,360]{2,1,0:T(8,128)(2,1)S(1)} %fusion.79), channel_id=1, source_target_pairs={{0,16},{16,0},{1,17},{17,1},{2,18},{18,2},{3,19},{19,3},{4,20},{20... | collective-permute-start | bytes 1105928 | tf_op jit(solution)/shard_map/ppermute | solution.py:94
  110.7 3.7 %fusion.101 = f32[1024,1024]{1,0:T(8,128)} fusion(bf16[5,72,1024]{2,1,0:T(8,128)(2,1)} %param.4, bf16[2,72]{0,1:T(8,128)(2,1)S(1)} %collective-permute-done.3, bf16[1024,72]{0,1:T(8,128)(2,1)S(1)} %get-tuple-element.18), kind=kOutput, calls=%fused_computation.123 | convolution fusion | flops 151289856 | bytes 4489504 | tf_op jit(solution)/shard_map/dot_general | solution.py:79
  114.4 3.7 %fusion.108 = f32[1024,1024]{1,0:T(8,128)} fusion(bf16[5,72,1024]{2,1,0:T(8,128)(2,1)} %param.4, bf16[2,72]{0,1:T(8,128)(2,1)S(1)} %collective-permute-done.2, bf16[1024,72]{0,1:T(8,128)(2,1)S(1)} %get-tuple-element.18), kind=kOutput, calls=%fused_computation.130 | convolution fusion | flops 151289856 | bytes 4489504 | tf_op jit(solution)/shard_map/dot_general | solution.py:79
  118.3 0.8 copy.45
  119.1 20.6 %all-to-all-start.4 = ((bf16[4,4,32,360]{3,2,1,0:T(8,128)(2,1)}), bf16[4,4,32,360]{3,2,1,0:T(8,128)(2,1)S(1)}, u32[]{:S(2)}, u32[]{:S(2)}) async-start(bf16[4,4,32,360]{3,2,1,0:T(8,128)(2,1)} %bitcast.77), calls=%async_computation.4 | async-start | bytes 786432 | tf_op jit(solution)/shard_map/all_to_all | solution.py:96
  139.6 3.7 %fusion.111 = f32[1024,1024]{1,0:T(8,128)} fusion(bf16[5,72,1024]{2,1,0:T(8,128)(2,1)} %param.4, bf16[1024,72]{0,1:T(8,128)(2,1)S(1)} %get-tuple-element.18, bf16[2,72]{0,1:T(8,128)(2,1)S(1)} %collective-permute-done.2), kind=kOutput, calls=%fused_computation.133 | convolution fusion | flops 151289856 | bytes 4489504 | tf_op jit(solution)/shard_map/dot_general | solution.py:79
  143.3 4.6 %all-to-all-done.4 = bf16[4,4,32,360]{3,2,1,0:T(8,128)(2,1)S(1)} async-done(((bf16[4,4,32,360]{3,2,1,0:T(8,128)(2,1)}), bf16[4,4,32,360]{3,2,1,0:T(8,128)(2,1)S(1)}, u32[]{:S(2)}, u32[]{:S(2)}) %all-to-all-start.4) | async-done | bytes 368672 | tf_op jit(solution)/shard_map/all_to_all | solution.py:96
  148.6 13.9 %all-to-all-start.5 = ((bf16[4,32,360]{2,1,0:T(8,128)(2,1)}), bf16[4,32,360]{2,1,0:T(8,128)(2,1)S(1)}, u32[]{:S(2)}, u32[]{:S(2)}) async-start(bf16[4,32,360]{2,1,0:T(8,128)(2,1)} %reduce_sum.111), calls=%async_computation.5 | async-start | bytes 196608 | tf_op jit(solution)/shard_map/all_to_all | solution.py:97
  162.5 8.3 %add_convert_fusion = bf16[1024,1024]{1,0:T(8,128)(2,1)} fusion(f32[1024,1024]{1,0:T(8,128)} %fusion.101, f32[1024,1024]{1,0:T(8,128)} %fusion.104, f32[1024,1024]{1,0:T(8,128)} %fusion.111, f32[1024,1024]{1,0:T(8,128)} %fusion.108, bf16[5,72,1024]{2,1,0:T(8,128)(2,1)} %param.4, bf16[1024,72]{0,1:T(8,128)(2,1)S(1)} %get-tuple-element.18, ...), kind=kOutput, calls=%fused_computation.1 | convolution fusion | flops 156532736 | bytes 19169568 | tf_op jit(solution)/shard_map/dot_general | solution.py:79
  170.8 6.0 %all-to-all-done.5 = bf16[4,32,360]{2,1,0:T(8,128)(2,1)S(1)} async-done(((bf16[4,32,360]{2,1,0:T(8,128)(2,1)}), bf16[4,32,360]{2,1,0:T(8,128)(2,1)S(1)}, u32[]{:S(2)}, u32[]{:S(2)}) %all-to-all-start.5) | async-done | bytes 92192 | tf_op jit(solution)/shard_map/all_to_all | solution.py:97
  176.8 5.8 %all-to-all-start.3 = ((bf16[16,64,1024]{2,1,0:T(8,128)(2,1)}), bf16[16,64,1024]{2,1,0:T(8,128)(2,1)S(1)}, u32[]{:S(2)}, u32[]{:S(2)}) async-start(bf16[16,64,1024]{2,1,0:T(8,128)(2,1)} %bitcast.85), calls=%async_computation.3 | async-start | bytes 4194304 | tf_op jit(solution)/shard_map/all_to_all | solution.py:80
  185.0 43.8 %all-to-all-done.3 = bf16[16,64,1024]{2,1,0:T(8,128)(2,1)S(1)} async-done(((bf16[16,64,1024]{2,1,0:T(8,128)(2,1)}), bf16[16,64,1024]{2,1,0:T(8,128)(2,1)S(1)}, u32[]{:S(2)}, u32[]{:S(2)}) %all-to-all-start.3) | async-done | bytes 2097184 | tf_op jit(solution)/shard_map/all_to_all | solution.py:80
  230.2 0.9 fusion.74
  (53 shorter events, 10.4 us)
Async XLA Ops:
  5.1 59.0 %copy-start.2 = (bf16[5,72,1024]{2,1,0:T(8,128)(2,1)S(1)}, bf16[5,72,1024]{2,1,0:T(8,128)(2,1)}, u32[]{:S(2)}) copy-start(bf16[5,72,1024]{2,1,0:T(8,128)(2,1)} %param.4) | copy-start | bytes 2211844
  61.5 6.8 %collective-permute-start = (bf16[2,1024]{1,0:T(2,128)(2,1)S(1)}, bf16[2,1024]{1,0:T(2,128)(2,1)S(1)}, u32[]{:S(2)}, u32[]{:S(2)}) collective-permute-start(bf16[2,1024]{1,0:T(2,128)(2,1)S(1)} %get-tuple-element.16), channel_id=1, source_target_pairs={{0,16},{16,32},{32,48},{48,64},{64,80},{80,96},{96,112},{112,128},... | collective-permute-start | bytes 12296 | tf_op jit(solution)/shard_map/ppermute | solution.py:29
  62.8 4.8 %collective-permute-start.1 = (bf16[2,1024]{1,0:T(2,128)(2,1)S(1)}, bf16[2,1024]{1,0:T(2,128)(2,1)S(1)}, u32[]{:S(2)}, u32[]{:S(2)}) collective-permute-start(bf16[2,1024]{1,0:T(2,128)(2,1)S(1)} %get-tuple-element.17), channel_id=1, source_target_pairs={{16,0},{32,16},{48,32},{64,48},{80,64},{96,80},{112,96},{128,112},... | collective-permute-start | bytes 12296 | tf_op jit(solution)/shard_map/ppermute | solution.py:29
  69.9 6.8 %copy-start.3 = (bf16[512,72]{0,1:T(8,128)(2,1)S(1)}, bf16[512,72]{0,1:T(8,128)(2,1)}, u32[]{:S(2)}) copy-start(bf16[512,72]{0,1:T(8,128)(2,1)} %param.5) | copy-start | bytes 221188
  71.3 11.2 %all-to-all-start.1 = ((f32[16,8,128]{2,1,0:T(8,128)}), f32[16,8,128]{2,1,0:T(8,128)S(1)}, u32[]{:S(2)}, u32[]{:S(2)}) async-start(f32[16,8,128]{2,1,0:T(8,128)} %broadcast_in_dim.20), calls=%async_computation.1 | async-start | bytes 131072 | tf_op jit(solution)/shard_map/all_to_all | solution.py:40
  83.3 12.3 %all-to-all-start.2 = ((f32[16,8,128]{2,1,0:T(8,128)}), f32[16,8,128]{2,1,0:T(8,128)S(1)}, u32[]{:S(2)}, u32[]{:S(2)}) async-start(f32[16,8,128]{2,1,0:T(8,128)} %broadcast_in_dim.22), calls=%async_computation.2 | async-start | bytes 131072 | tf_op jit(solution)/shard_map/all_to_all | solution.py:40
  96.4 9.1 %copy-start.1 = (bf16[1024,1024]{1,0:T(8,128)(2,1)S(1)}, bf16[1024,1024]{1,0:T(8,128)(2,1)}, u32[]{:S(2)}) copy-start(bf16[1024,1024]{1,0:T(8,128)(2,1)} %copy.34) | copy-start | bytes 6291460
  96.4 8.0 %collective-permute-start.2 = (bf16[2,72]{0,1:T(8,128)(2,1)S(1)}, bf16[2,72]{0,1:T(8,128)(2,1)S(1)}, u32[]{:S(2)}, u32[]{:S(2)}) collective-permute-start(bf16[2,72]{0,1:T(8,128)(2,1)S(1)} %get-tuple-element.20), channel_id=1, source_target_pairs={{16,0},{32,16},{48,32},{64,48},{80,64},{96,80},{112,96},{128,112},... | collective-permute-start | bytes 872 | tf_op jit(solution)/shard_map/ppermute | solution.py:29
  101.4 3.8 %collective-permute-start.3 = (bf16[2,72]{0,1:T(8,128)(2,1)S(1)}, bf16[2,72]{0,1:T(8,128)(2,1)S(1)}, u32[]{:S(2)}, u32[]{:S(2)}) collective-permute-start(bf16[2,72]{0,1:T(8,128)(2,1)S(1)} %get-tuple-element.21), channel_id=1, source_target_pairs={{0,16},{16,32},{32,48},{48,64},{64,80},{80,96},{96,112},{112,128},... | collective-permute-start | bytes 872 | tf_op jit(solution)/shard_map/ppermute | solution.py:29
  106.9 11.2 %collective-permute-start.4 = (bf16[16,32,360]{2,1,0:T(8,128)(2,1)S(1)}, bf16[16,32,360]{2,1,0:T(8,128)(2,1)S(1)}, u32[]{:S(2)}, u32[]{:S(2)}) collective-permute-start(bf16[16,32,360]{2,1,0:T(8,128)(2,1)S(1)} %fusion.79), channel_id=1, source_target_pairs={{0,16},{16,0},{1,17},{17,1},{2,18},{18,2},{3,19},{19,3},{4,20},{20... | collective-permute-start | bytes 1105928 | tf_op jit(solution)/shard_map/ppermute | solution.py:94
  119.1 28.8 %all-to-all-start.4 = ((bf16[4,4,32,360]{3,2,1,0:T(8,128)(2,1)}), bf16[4,4,32,360]{3,2,1,0:T(8,128)(2,1)S(1)}, u32[]{:S(2)}, u32[]{:S(2)}) async-start(bf16[4,4,32,360]{3,2,1,0:T(8,128)(2,1)} %bitcast.77), calls=%async_computation.4 | async-start | bytes 786432 | tf_op jit(solution)/shard_map/all_to_all | solution.py:96
  148.6 28.2 %all-to-all-start.5 = ((bf16[4,32,360]{2,1,0:T(8,128)(2,1)}), bf16[4,32,360]{2,1,0:T(8,128)(2,1)S(1)}, u32[]{:S(2)}, u32[]{:S(2)}) async-start(bf16[4,32,360]{2,1,0:T(8,128)(2,1)} %reduce_sum.111), calls=%async_computation.5 | async-start | bytes 196608 | tf_op jit(solution)/shard_map/all_to_all | solution.py:97
  176.8 52.0 %all-to-all-start.3 = ((bf16[16,64,1024]{2,1,0:T(8,128)(2,1)}), bf16[16,64,1024]{2,1,0:T(8,128)(2,1)S(1)}, u32[]{:S(2)}, u32[]{:S(2)}) async-start(bf16[16,64,1024]{2,1,0:T(8,128)(2,1)} %bitcast.85), calls=%async_computation.3 | async-start | bytes 4194304 | tf_op jit(solution)/shard_map/all_to_all | solution.py:80
  185.0 44.8 %copy-start = (bf16[128,1024]{1,0:T(8,128)(2,1)S(1)}, bf16[128,1024]{1,0:T(8,128)(2,1)}, u32[]{:S(2)}) copy-start(bf16[128,1024]{1,0:T(8,128)(2,1)} %param.3) | copy-start | bytes 786436

commit v2 on v1

v2 whole, which is shorter than its diff:
```python
import jax
import jax.numpy as jnp
from jax import lax
from jax.sharding import Mesh, PartitionSpec as P

EPSILON = 1e-06
AXES = ("zh", "x", "core", "zl", "y")
SEQ = ("zh", "x", "core")
SUB = ("zl", "y")
bf16 = jnp.bfloat16
f32 = jnp.float32


def gelu_slope(tensor):
    return (
        0.5 * (1.0 + jax.scipy.special.erf(tensor * 0.7071067811865476))
        + tensor * jnp.exp(-0.5 * tensor * tensor) * 0.3989422804014327
    )


def pool_pairs(tensor):
    half_rows = tensor.shape[0] // 2
    return 0.5 * jnp.sum(tensor.reshape(half_rows, 2, tensor.shape[1]), axis=1)


def shift(block, axis, step):
    count = lax.axis_size(axis)
    pairs = [(i, i + step) for i in range(count) if 0 <= i + step < count]
    return lax.ppermute(block, axis, pairs)


def gather_all(block, axis):
    count = lax.axis_size(axis)
    return lax.all_to_all(jnp.broadcast_to(block, (count, *block.shape)), axis, 0, 0)


def rms_normed(rows):
    wide = rows.astype(f32)
    inv = lax.rsqrt(jnp.mean(wide * wide, axis=1, keepdims=True) + EPSILON)
    return wide * inv, inv


def pooled_of(normed):
    return pool_pairs(jax.nn.gelu(normed, approximate=False)).astype(bf16)


def per_device(activations, conv_weight, cotangent):
    tap_count, out_width, in_width = conv_weight.shape
    full_out = out_width * lax.axis_size(SUB)
    core = lax.axis_index("core")
    half = in_width // 2
    rows = activations.shape[0] // 2
    span = rows + 8
    group = 4 * out_width

    own_half = jnp.where(core == 0, conv_weight[:, :, :half], conv_weight[:, :, half:])
    first = gather_all(own_half, "y")
    second = lax.ppermute(first, "core", [(0, 1), (1, 0)])
    weights = jnp.where(
        core == 0,
        jnp.concatenate([first, second], axis=3),
        jnp.concatenate([second, first], axis=3),
    )
    weights = weights.transpose(1, 0, 2, 3).reshape(tap_count, group, in_width)

    low = shift(activations[-8:], AXES, 1)
    high = shift(activations[:8], AXES, -1)
    normed_first, inv_first = rms_normed(activations)
    pooled = pooled_of(normed_first)
    edges = pooled_of(rms_normed(jnp.concatenate([low, high], axis=0))[0])
    block = jnp.concatenate([edges[:4], pooled, edges[4:]], axis=0)
    gathered = gather_all(block, "zl")
    flat = jnp.concatenate(
        [gathered.reshape(4 * span, in_width), jnp.zeros((4, in_width), bf16)], axis=0
    )
    around = gather_all(gathered[:, 4 : 4 + rows].reshape(4 * rows, in_width), "y")

    cot = cotangent.T
    pairs = span // 2
    before = shift(cot[:, -1:], SEQ, 1)
    after = shift(cot[:, :1], SEQ, -1)
    place = jnp.arange(4)[:, None, None] + 4 * jnp.arange(4)[None, :, None]
    source = place * (rows // 2) + jnp.arange(pairs)[None, None, :] - 1
    source = jnp.where(jnp.arange(pairs)[None, None, :] < pairs - 2, source, -2)
    source = source.reshape(4, 1, 4 * pairs)
    pick = (source == jnp.arange(cot.shape[1])[None, :, None]).astype(bf16)
    spread = jnp.einsum("or,yrz->yoz", cot, pick, preferred_element_type=f32)
    spread = (
        spread
        + jnp.where(source == -1, before.astype(f32)[None], 0.0)
        + jnp.where(source == cot.shape[1], after.astype(f32)[None], 0.0)
    ).astype(bf16)
    cot_block = lax.all_to_all(spread, "y", 0, 0).reshape(group, 4 * pairs)
    lanes = 4 * span
    repeat = (jnp.arange(4 * pairs)[:, None] == jnp.arange(lanes)[None, :] // 2).astype(bf16)
    upstream = 0.5 * jnp.dot(cot_block, repeat, preferred_element_type=f32)

    conv_acc = jnp.zeros((group, lanes), f32)
    for k in range(tap_count):
        conv_acc = conv_acc + lax.dot_general(
            weights[k], flat[k : k + lanes], (((1,), (1,)), ((), ())),
            preferred_element_type=f32,
        )
    y_float = conv_acc.astype(bf16).astype(f32)
    square_sum = lax.psum(jnp.sum(y_float * y_float, axis=0), "zl")
    inv_second = lax.rsqrt(square_sum / full_out + EPSILON)[None, :]
    normed_second = y_float * inv_second
    slope_second = upstream * gelu_slope(normed_second)
    inner_second = lax.psum(jnp.sum(slope_second * normed_second, axis=0), "zl")
    conv_grad = inv_second * (slope_second - normed_second * (inner_second / full_out)[None, :])
    inside = (jnp.arange(lanes) % span < rows + 4)[None, :]
    conv_grad = jnp.where(inside, conv_grad, 0.0).astype(bf16)
    active = jax.nn.gelu(normed_second, approximate=False)
    features = 0.5 * lax.dot_general(
        active, repeat.astype(f32), (((1,), (1,)), ((), ())),
        precision=lax.Precision.HIGHEST, preferred_element_type=f32,
    )

    sent = jnp.concatenate([conv_grad, features.astype(bf16)], axis=1)
    back = lax.all_to_all(sent.reshape(4, out_width, -1), "y", 0, 0)
    feature_back = back[:, :, lanes:].reshape(4, out_width, 4, pairs)[..., 1 : 1 + rows // 2]
    features = feature_back.transpose(2, 0, 3, 1).reshape(-1, out_width)
    grad_back = back[:, :, :lanes].reshape(4, out_width, 4, span)

    grad_flat = jnp.concatenate([conv_grad, jnp.zeros((group, 4), bf16)], axis=1)
    running = jnp.zeros((lanes, in_width), f32)
    for k in range(tap_count):
        running = running + lax.dot_general(
            grad_flat[:, 4 - k : 4 - k + lanes], weights[k], (((0,), (0,)), ((), ())),
            preferred_element_type=f32,
        )
    running = running.astype(bf16).reshape(4, span, in_width)[:, :rows]
    parts = lax.all_to_all(running, "zl", 0, 0)
    pooled_grad = jnp.sum(parts.astype(f32), axis=0)
    slope_first = 0.5 * jnp.repeat(pooled_grad, 2, axis=0) * gelu_slope(normed_first)
    inner_first = jnp.mean(slope_first * normed_first, axis=1, keepdims=True)
    input_grad = (inv_first * (slope_first - normed_first * inner_first)).astype(bf16)

    windows = jnp.stack([grad_back[..., 4 - k : 4 - k + rows] for k in range(tap_count)])
    wide = windows.transpose(0, 2, 1, 3, 4).reshape(tap_count * out_width, -1)
    weight_part = lax.dot_general(
        around.reshape(-1, in_width), wide, (((0,), (1,)), ((), ())),
        preferred_element_type=f32,
    )
    halves = weight_part.reshape(16, 2, in_width // 32, tap_count * out_width)
    mine = jnp.where(core == 0, halves[:, 0], halves[:, 1])
    other = jnp.where(core == 0, halves[:, 1], halves[:, 0]).astype(bf16)
    total = mine + lax.ppermute(other, "core", [(0, 1), (1, 0)]).astype(f32)
    total = lax.all_to_all(total.astype(bf16), ("zh", "x"), 0, 0)
    weight_grad = jnp.sum(total.astype(f32), axis=0).reshape(-1, tap_count, out_width)
    return (features, input_grad, weight_grad)


def solution(mesh):
    split = Mesh(mesh.devices.reshape(4, 4, 2, 4, 4), AXES)
    return jax.shard_map(
        per_device,
        mesh=split,
        in_specs=(P(AXES, None), P(None, SUB, None), P(SEQ, SUB)),
        out_specs=(P(SEQ, SUB), P(AXES, None), P(SEQ, None, SUB)),
        check_vma=False,
    )
```

time: 232 us -> 216 us (0.931)
  the two profiles are of different devices: /device:TPU:64 before, /device:TPU:32 now
where the time goes in v2:
time: 216 us; the launch traced here: 214 us
  waiting for transfers between devices  77.8 us (36%)
  starting transfers between devices  59.2 us (27%)
  local copies, waits for them, and re-layouts  26.2 us (12%)
  blocking collectives  21.4 us (10%)
  matrix products  16.6 us (8%)
  other arithmetic  12 us (6%)
    all_to_all x3, waiting for transfers between devices, gather_all(): lax.all_to_all(jnp.broadcast_to(block, (count, *block.shape)), axis, 0, 0)  40.9 us
    all_to_all x1, waiting for transfers between devices, per_device(): total = lax.all_to_all(total.astype(bf16), ('zh', 'x'), 0, 0)  24.2 us
    all_to_all x3, starting transfers between devices, gather_all(): lax.all_to_all(jnp.broadcast_to(block, (count, *block.shape)), axis, 0, 0)  15.1 us
    all_to_all x1, starting transfers between devices, per_device(): total = lax.all_to_all(total.astype(bf16), ('zh', 'x'), 0, 0)  15 us
    psum x1, blocking collectives, per_device(): square_sum = lax.psum(jnp.sum(y_float * y_float, axis=0), 'zl')  11.6 us
    ppermute x4, starting transfers between devices, shift(): return lax.ppermute(block, axis, pairs)  10.7 us
    psum x1, blocking collectives, per_device(): inner_second = lax.psum(jnp.sum(slope_second * normed_second, axis=0), 'zl')  9.79 us
    dot_general x5, matrix products, per_device(): lax.dot_general(grad_flat[:, 4 - k:4 - k + lanes], weights[k], (((0,), (0...  7.69 us
  transfers between devices with their start and end apart: 13, of which 7 were waited for; matrix products, arithmetic and copies ran while one was open for 17% of the time, Pallas kernels for 0%

profile of v2, /device:TPU:32, one launch (start us, length us, event | category | flops | bytes accessed | tf_op | source)
XLA Modules:
  0.0 214.4 jit_solution(1401447146948551204)
XLA Ops:
  1.4 4.5 %collective-permute-start.2 = (bf16[8,1024]{1,0:T(8,128)(2,1)S(1)}, bf16[8,1024]{1,0:T(8,128)(2,1)S(1)}, u32[]{:S(2)}, u32[]{:S(2)}) collective-permute-start(bf16[8,1024]{1,0:T(8,128)(2,1)S(1)} %get-tuple-element.33), channel_id=1, source_target_pairs={{1,0},{2,1},{3,2},{4,3},{5,4},{6,5},{7,6},{8,7},{9,8},{10,9},{11,1... | collective-permute-start | bytes 49160 | tf_op jit(solution)/shard_map/ppermute | solution.py:29
  5.9 1.9 collective-permute-start.1
  10.0 3.0 %collective-permute-start.3 = (bf16[72,1]{1,0:T(8,128)(2,1)S(1)}, bf16[72,1]{1,0:T(8,128)(2,1)S(1)}, u32[]{:S(2)}, u32[]{:S(2)}) collective-permute-start(bf16[72,1]{1,0:T(8,128)(2,1)S(1)} %get-tuple-element.34), channel_id=1, source_target_pairs={{0,16},{16,32},{32,48},{48,64},{64,80},{80,96},{96,112},{112,128},... | collective-permute-start | bytes 440 | tf_op jit(solution)/shard_map/ppermute | solution.py:29
  14.1 2.2 %fusion.34 = f32[128,1024]{1,0:T(8,128)S(1)} fusion(bf16[128,1024]{1,0:T(8,128)(2,1)} %param.3, f32[128]{0:T(128)S(1)} %add_rsqrt_fusion.1), kind=kLoop, calls=%fused_computation.50 | loop fusion | flops 8650752 | bytes 786944 | tf_op jit(solution)/shard_map/mul | solution.py:44
  16.9 2.0 add_convert_fusion
  18.9 5.8 %all-to-all-start.2 = ((bf16[4,72,144]{1,2,0:T(8,128)(2,1)}), bf16[4,72,144]{1,2,0:T(8,128)(2,1)S(1)}, u32[]{:S(2)}, u32[]{:S(2)}) async-start(bf16[4,72,144]{1,2,0:T(8,128)(2,1)} %add_convert_fusion), calls=%async_computation.2 | async-start | bytes 294912 | tf_op jit(solution)/shard_map/all_to_all | solution.py:93
  25.7 5.7 %all-to-all-done.2 = bf16[4,72,144]{1,2,0:T(8,128)(2,1)S(1)} async-done(((bf16[4,72,144]{1,2,0:T(8,128)(2,1)}), bf16[4,72,144]{1,2,0:T(8,128)(2,1)S(1)}, u32[]{:S(2)}, u32[]{:S(2)}) %all-to-all-start.2) | async-done | bytes 82976 | tf_op jit(solution)/shard_map/all_to_all | solution.py:93
  32.7 3.6 %all-to-all-start = ((bf16[4,5,72,512]{3,2,1,0:T(8,128)(2,1)}), bf16[4,5,72,512]{3,2,1,0:T(8,128)(2,1)S(1)}, u32[]{:S(2)}, u32[]{:S(2)}) async-start(bf16[4,5,72,512]{3,2,1,0:T(8,128)(2,1)} %broadcast_in_dim.111), calls=%async_computation | async-start | bytes 2949120 | tf_op jit(solution)/shard_map/all_to_all | solution.py:34
  36.9 19.3 %all-to-all-done = bf16[4,5,72,512]{3,2,1,0:T(8,128)(2,1)S(1)} async-done(((bf16[4,5,72,512]{3,2,1,0:T(8,128)(2,1)}), bf16[4,5,72,512]{3,2,1,0:T(8,128)(2,1)S(1)}, u32[]{:S(2)}, u32[]{:S(2)}) %all-to-all-start) | async-done | bytes 1474592 | tf_op jit(solution)/shard_map/all_to_all | solution.py:34
  57.2 7.7 %all-to-all-start.1 = ((bf16[4,72,1024]{2,1,0:T(8,128)(2,1)}), bf16[4,72,1024]{2,1,0:T(8,128)(2,1)S(1)}, u32[]{:S(2)}, u32[]{:S(2)}) async-start(bf16[4,72,1024]{2,1,0:T(8,128)(2,1)} %broadcast_in_dim.112), calls=%async_computation.1 | async-start | bytes 1179648 | tf_op jit(solution)/shard_map/all_to_all | solution.py:34
  64.9 1.9 collective-permute-start
  67.0 10.1 %all-to-all-done.1 = bf16[4,72,1024]{2,1,0:T(8,128)(2,1)S(1)} async-done(((bf16[4,72,1024]{2,1,0:T(8,128)(2,1)}), bf16[4,72,1024]{2,1,0:T(8,128)(2,1)S(1)}, u32[]{:S(2)}, u32[]{:S(2)}) %all-to-all-start.1) | async-done | bytes 589856 | tf_op jit(solution)/shard_map/all_to_all | solution.py:34
  78.3 2.7 %fusion = bf16[5,4,72,1024]{3,2,0,1:T(8,128)(2,1)S(1)} fusion(bf16[4,5,72,512]{3,2,1,0:T(8,128)(2,1)} %collective-permute-done, bf16[4,5,72,512]{3,2,1,0:T(8,128)(2,1)S(1)} %all-to-all-done, pred[]{:T(512)S(6)} %eq.60), kind=kLoop, calls=%fused_computation.1 | loop fusion | flops 13271040 | bytes 5898241 | tf_op jit(solution)/shard_map/transpose | solution.py:64
  83.9 11.6 %psum.14 = f32[288]{0:T(512)S(1)} all-reduce(f32[288]{0:T(512)S(1)} %get-tuple-element.38), channel_id=1, replica_groups=mesh['zh'=4,'x'=4,'core'=2,'zl'=4,'y'=4] {'zl'}, use_global_device_ids=true, to_apply=%region_5.6 | all-reduce | flops 288 | bytes 2304 | tf_op jit(solution)/shard_map/psum | solution.py:105
  95.5 2.1 fusion.13
  98.7 9.8 %psum.15 = f32[288]{0:T(512)S(1)} all-reduce(f32[288]{0:T(512)S(1)} %get-tuple-element.40), channel_id=1, replica_groups=mesh['zh'=4,'x'=4,'core'=2,'zl'=4,'y'=4] {'zl'}, use_global_device_ids=true, to_apply=%region_7.8 | all-reduce | flops 288 | bytes 2304 | tf_op jit(solution)/shard_map/psum | solution.py:109
  109.7 1.5 fusion.255
  111.3 1.6 fusion.147
  113.8 3.5 %all-to-all-start.3 = ((bf16[4,72,432]{2,1,0:T(8,128)(2,1)}), bf16[4,72,432]{2,1,0:T(8,128)(2,1)S(1)}, u32[]{:S(2)}, u32[]{:S(2)}) async-start(bf16[4,72,432]{2,1,0:T(8,128)(2,1)} %bitcast.10), calls=%async_computation.3 | async-start | bytes 589824 | tf_op jit(solution)/shard_map/all_to_all | solution.py:120
  117.3 1.6 fusion.149
  118.9 5.2 %all-to-all-done.3 = bf16[4,72,432]{2,1,0:T(8,128)(2,1)S(1)} async-done(((bf16[4,72,432]{2,1,0:T(8,128)(2,1)}), bf16[4,72,432]{2,1,0:T(8,128)(2,1)S(1)}, u32[]{:S(2)}, u32[]{:S(2)}) %all-to-all-start.3) | async-done | bytes 248864 | tf_op jit(solution)/shard_map/all_to_all | solution.py:120
  125.6 3.8 %all-to-all-start.5 = ((bf16[4,256,1024]{1,2,0:T(8,128)(2,1)}), bf16[4,256,1024]{1,2,0:T(8,128)(2,1)S(1)}, u32[]{:S(2)}, u32[]{:S(2)}) async-start(bf16[4,256,1024]{1,2,0:T(8,128)(2,1)} %broadcast_in_dim.128), calls=%async_computation.5 | async-start | bytes 4194304 | tf_op jit(solution)/shard_map/all_to_all | solution.py:34
  130.7 2.4 %fusion.4 = bf16[288,1024]{1,0:T(8,128)(2,1)S(1)} fusion(f32[288,1024]{1,0:T(8,128)S(1)} %copy-done, f32[288,1024]{1,0:T(8,128)} %fusion.147, f32[288,1024]{1,0:T(8,128)} %fusion.149, f32[288,1024]{1,0:T(8,128)S(1)} %fusion.151, bf16[288,1024]{1,0:T(8,128)(2,1)S(1)} %bitcast.95, bf16[288,288]{1,0:T(8,128)(2,1)S(1)} %select_convert_fusion.1), kind=kOutput, calls=%fused_computation.6 | convolution fusion | flops 171343872 | bytes 6064128 | tf_op jit(solution)/shard_map/dot_general | solution.py:128
  137.5 11.5 %all-to-all-done.5 = bf16[4,256,1024]{1,2,0:T(8,128)(2,1)S(1)} async-done(((bf16[4,256,1024]{1,2,0:T(8,128)(2,1)}), bf16[4,256,1024]{1,2,0:T(8,128)(2,1)S(1)}, u32[]{:S(2)}, u32[]{:S(2)}) %all-to-all-start.5) | async-done | bytes 2097184 | tf_op jit(solution)/shard_map/all_to_all | solution.py:34
  149.0 5.2 %all-to-all-start.4 = ((bf16[4,64,1024]{2,1,0:T(8,128)(2,1)}), bf16[4,64,1024]{2,1,0:T(8,128)(2,1)S(1)}, u32[]{:S(2)}, u32[]{:S(2)}) async-start(bf16[4,64,1024]{2,1,0:T(8,128)(2,1)} %slice.155), calls=%async_computation.4 | async-start | bytes 1048576 | tf_op jit(solution)/shard_map/all_to_all | solution.py:133
  155.9 3.6 %reshape.294 = bf16[360,1024,1,1]{1,0,2,3:T(8,128)(2,1)} reshape(bf16[5,72,4,4,64]{4,3,2,1,0:T(4,128)(2,1)} %bitcast.24) | data formatting | bytes 1474560 | tf_op jit(solution)/shard_map/reshape | solution.py:140
  159.4 2.5 %copy.90 = bf16[4,256,1024]{2,1,0:T(8,128)(2,1)} copy(bf16[4,256,1024]{1,2,0:T(8,128)(2,1)S(1)} %all-to-all-done.5) | data formatting | bytes 4194304 | tf_op jit(solution)/shard_map/all_to_all | solution.py:34
  161.9 2.9 %copy.91 = bf16[1024,1024]{1,0:T(8,128)(2,1)S(1)} copy(bf16[1024,1024]{0,1:T(8,128)(2,1)} %bitcast.93) | data formatting | bytes 4194304 | tf_op jit(solution)/shard_map/dot_general | solution.py:141
  166.2 2.1 collective-permute-start.5
  168.3 1.7 collective-permute-done.5
  170.9 15.0 %all-to-all-start.6 = ((bf16[16,32,360]{2,1,0:T(8,128)(2,1)}), bf16[16,32,360]{2,1,0:T(8,128)(2,1)S(1)}, u32[]{:S(2)}, u32[]{:S(2)}) async-start(bf16[16,32,360]{2,1,0:T(8,128)(2,1)} %fusion.16), calls=%async_computation.6 | async-start | bytes 786432 | tf_op jit(solution)/shard_map/all_to_all | solution.py:149
  189.4 24.2 %all-to-all-done.6 = bf16[16,32,360]{2,1,0:T(8,128)(2,1)S(1)} async-done(((bf16[16,32,360]{2,1,0:T(8,128)(2,1)}), bf16[16,32,360]{2,1,0:T(8,128)(2,1)S(1)}, u32[]{:S(2)}, u32[]{:S(2)}) %all-to-all-start.6) | async-done | bytes 368672 | tf_op jit(solution)/shard_map/all_to_all | solution.py:149
  (110 shorter events, 31.1 us)
Async XLA Ops:
  0.6 24.1 %copy-start.8 = (bf16[5,72,1024]{2,1,0:T(8,128)(2,1)S(1)}, bf16[5,72,1024]{2,1,0:T(8,128)(2,1)}, u32[]{:S(2)}) copy-start(bf16[5,72,1024]{2,1,0:T(8,128)(2,1)} %param.4) | copy-start | bytes 2211844
  1.4 34.8 %collective-permute-start.2 = (bf16[8,1024]{1,0:T(8,128)(2,1)S(1)}, bf16[8,1024]{1,0:T(8,128)(2,1)S(1)}, u32[]{:S(2)}, u32[]{:S(2)}) collective-permute-start(bf16[8,1024]{1,0:T(8,128)(2,1)S(1)} %get-tuple-element.33), channel_id=1, source_target_pairs={{1,0},{2,1},{3,2},{4,3},{5,4},{6,5},{7,6},{8,7},{9,8},{10,9},{11,1... | collective-permute-start | bytes 49160 | tf_op jit(solution)/shard_map/ppermute | solution.py:29
  5.9 30.3 %collective-permute-start.1 = (bf16[8,1024]{1,0:T(8,128)(2,1)S(1)}, bf16[8,1024]{1,0:T(8,128)(2,1)S(1)}, u32[]{:S(2)}, u32[]{:S(2)}) collective-permute-start(bf16[8,1024]{1,0:T(8,128)(2,1)S(1)} %get-tuple-element.32), channel_id=1, source_target_pairs={{0,1},{1,2},{2,3},{3,4},{4,5},{5,6},{6,7},{7,8},{8,9},{9,10},{10,1... | collective-permute-start | bytes 49160 | tf_op jit(solution)/shard_map/ppermute | solution.py:29
  8.7 8.0 %collective-permute-start.4 = (bf16[72,1]{1,0:T(8,128)(2,1)S(1)}, bf16[72,1]{1,0:T(8,128)(2,1)S(1)}, u32[]{:S(2)}, u32[]{:S(2)}) collective-permute-start(bf16[72,1]{1,0:T(8,128)(2,1)S(1)} %get-tuple-element.35), channel_id=1, source_target_pairs={{16,0},{32,16},{48,32},{64,48},{80,64},{96,80},{112,96},{128,112},... | collective-permute-start | bytes 440 | tf_op jit(solution)/shard_map/ppermute | solution.py:29
  10.0 6.8 %collective-permute-start.3 = (bf16[72,1]{1,0:T(8,128)(2,1)S(1)}, bf16[72,1]{1,0:T(8,128)(2,1)S(1)}, u32[]{:S(2)}, u32[]{:S(2)}) collective-permute-start(bf16[72,1]{1,0:T(8,128)(2,1)S(1)} %get-tuple-element.34), channel_id=1, source_target_pairs={{0,16},{16,32},{32,48},{48,64},{64,80},{80,96},{96,112},{112,128},... | collective-permute-start | bytes 440 | tf_op jit(solution)/shard_map/ppermute | solution.py:29
  18.9 12.6 %all-to-all-start.2 = ((bf16[4,72,144]{1,2,0:T(8,128)(2,1)}), bf16[4,72,144]{1,2,0:T(8,128)(2,1)S(1)}, u32[]{:S(2)}, u32[]{:S(2)}) async-start(bf16[4,72,144]{1,2,0:T(8,128)(2,1)} %add_convert_fusion), calls=%async_computation.2 | async-start | bytes 294912 | tf_op jit(solution)/shard_map/all_to_all | solution.py:93
  32.7 23.6 %all-to-all-start = ((bf16[4,5,72,512]{3,2,1,0:T(8,128)(2,1)}), bf16[4,5,72,512]{3,2,1,0:T(8,128)(2,1)S(1)}, u32[]{:S(2)}, u32[]{:S(2)}) async-start(bf16[4,5,72,512]{3,2,1,0:T(8,128)(2,1)} %broadcast_in_dim.111), calls=%async_computation | async-start | bytes 2949120 | tf_op jit(solution)/shard_map/all_to_all | solution.py:34
  57.2 20.0 %all-to-all-start.1 = ((bf16[4,72,1024]{2,1,0:T(8,128)(2,1)}), bf16[4,72,1024]{2,1,0:T(8,128)(2,1)S(1)}, u32[]{:S(2)}, u32[]{:S(2)}) async-start(bf16[4,72,1024]{2,1,0:T(8,128)(2,1)} %broadcast_in_dim.112), calls=%async_computation.1 | async-start | bytes 1179648 | tf_op jit(solution)/shard_map/all_to_all | solution.py:34
  64.9 13.4 %collective-permute-start = (bf16[4,5,72,512]{3,2,1,0:T(8,128)(2,1)S(1)}, bf16[4,5,72,512]{3,2,1,0:T(8,128)(2,1)}, u32[]{:S(2)}, u32[]{:S(2)}) collective-permute-start(bf16[4,5,72,512]{3,2,1,0:T(8,128)(2,1)S(1)} %all-to-all-done), channel_id=1, source_target_pairs={{0,16},{16,0},{1,17},{17,1},{2,18},{18,2},{3,19},{19,3},{4,20},{20... | collective-permute-start | bytes 4423688 | tf_op jit(solution)/shard_map/ppermute | solution.py:58
  81.3 1.0 copy-start.2
  83.9 13.7 %copy-start.5 = (f32[288,288]{1,0:T(8,128)}, f32[288,288]{1,0:T(8,128)S(1)}, u32[]{:S(2)}) copy-start(f32[288,288]{1,0:T(8,128)S(1)} %get-tuple-element.39) | copy-start | bytes 995332
  97.6 12.2 %copy-start.3 = (bf16[1,4,72,1024]{3,2,0,1:T(8,128)(2,1)S(1)}, bf16[1,4,72,1024]{3,2,0,1:T(8,128)(2,1)}, u32[]{:S(2)}) copy-start(bf16[1,4,72,1024]{3,2,0,1:T(8,128)(2,1)} %copy-done.2) | copy-start | bytes 1769476
  111.3 1.6 copy-start.10
  113.0 11.1 %copy-start.4 = (bf16[256,1024]{0,1:T(8,128)(2,1)S(1)}, bf16[256,1024]{0,1:T(8,128)(2,1)}, u32[]{:S(2)}) copy-start(bf16[256,1024]{0,1:T(8,128)(2,1)} %copy.89) | copy-start | bytes 1572868
  113.8 10.3 %all-to-all-start.3 = ((bf16[4,72,432]{2,1,0:T(8,128)(2,1)}), bf16[4,72,432]{2,1,0:T(8,128)(2,1)S(1)}, u32[]{:S(2)}, u32[]{:S(2)}) async-start(bf16[4,72,432]{2,1,0:T(8,128)(2,1)} %bitcast.10), calls=%async_computation.3 | async-start | bytes 589824 | tf_op jit(solution)/shard_map/all_to_all | solution.py:120
  124.1 1.5 copy-start.6
  125.6 23.4 %all-to-all-start.5 = ((bf16[4,256,1024]{1,2,0:T(8,128)(2,1)}), bf16[4,256,1024]{1,2,0:T(8,128)(2,1)S(1)}, u32[]{:S(2)}, u32[]{:S(2)}) async-start(bf16[4,256,1024]{1,2,0:T(8,128)(2,1)} %broadcast_in_dim.128), calls=%async_computation.5 | async-start | bytes 4194304 | tf_op jit(solution)/shard_map/all_to_all | solution.py:34
  129.4 1.3 copy-start
  133.0 1.0 slice-start
  149.0 21.9 %all-to-all-start.4 = ((bf16[4,64,1024]{2,1,0:T(8,128)(2,1)}), bf16[4,64,1024]{2,1,0:T(8,128)(2,1)S(1)}, u32[]{:S(2)}, u32[]{:S(2)}) async-start(bf16[4,64,1024]{2,1,0:T(8,128)(2,1)} %slice.155), calls=%async_computation.4 | async-start | bytes 1048576 | tf_op jit(solution)/shard_map/all_to_all | solution.py:133
  161.9 2.9 %copy-start.9 = (bf16[360,1024,1,1]{1,0,2,3:T(8,128)(2,1)S(1)}, bf16[360,1024,1,1]{1,0,2,3:T(8,128)(2,1)}, u32[]{:S(2)}) copy-start(bf16[360,1024,1,1]{1,0,2,3:T(8,128)(2,1)} %reshape.294) | copy-start | bytes 2211844
  166.2 19.7 %copy-start.7 = (bf16[4,72,432]{2,1,0:T(8,128)(2,1)S(1)}, bf16[4,72,432]{2,1,0:T(8,128)(2,1)}, u32[]{:S(2)}) copy-start(bf16[4,72,432]{2,1,0:T(8,128)(2,1)} %copy-done.6) | copy-start | bytes 746500
  166.2 3.7 %collective-permute-start.5 = (bf16[16,32,360]{2,1,0:T(8,128)(2,1)S(1)}, bf16[16,32,360]{2,1,0:T(8,128)(2,1)S(1)}, u32[]{:S(2)}, u32[]{:S(2)}) collective-permute-start(bf16[16,32,360]{2,1,0:T(8,128)(2,1)S(1)} %fusion.140), channel_id=1, source_target_pairs={{0,16},{16,0},{1,17},{17,1},{2,18},{18,2},{3,19},{19,3},{4,20},{20... | collective-permute-start | bytes 1105928 | tf_op jit(solution)/shard_map/ppermute | solution.py:148
  170.9 42.7 %all-to-all-start.6 = ((bf16[16,32,360]{2,1,0:T(8,128)(2,1)}), bf16[16,32,360]{2,1,0:T(8,128)(2,1)S(1)}, u32[]{:S(2)}, u32[]{:S(2)}) async-start(bf16[16,32,360]{2,1,0:T(8,128)(2,1)} %fusion.16), calls=%async_computation.6 | async-start | bytes 786432 | tf_op jit(solution)/shard_map/all_to_all | solution.py:149
  187.0 0.9 copy-start.1

commit v3 on v1

v3 whole, which is shorter than its diff:
```python
import functools

import jax
import jax.numpy as jnp
from jax import lax
from jax.experimental import pallas as pl
from jax.experimental.pallas import tpu as pltpu
from jax.sharding import Mesh, PartitionSpec as P


EPSILON = 1e-06
AXES = ("zh", "x", "core", "zl", "y")
SEQ = ("zh", "x", "core")
SUB = ("zl", "y")
bf16 = jnp.bfloat16
f32 = jnp.float32


def half_erf(tensor):
    return 0.5 * (1.0 + lax.erf(tensor * 0.7071067811865476))


def gelu_slope(tensor, half):
    return half + tensor * jnp.exp(-0.5 * tensor * tensor) * 0.3989422804014327


def shift(block, axis, step):
    count = lax.axis_size(axis)
    pairs = [(i, i + step) for i in range(count) if 0 <= i + step < count]
    return lax.ppermute(block, axis, pairs)


def turn(block, axis, step):
    count = lax.axis_size(axis)
    return lax.ppermute(block, axis, [(i, (i + step) % count) for i in range(count)])


def gather_all(block, axis):
    count = lax.axis_size(axis)
    return lax.all_to_all(jnp.broadcast_to(block, (count, *block.shape)), axis, 0, 0)


def local_call(kernel, shapes, scratch, *args):
    vmem = pl.BlockSpec(memory_space=pltpu.VMEM)
    return pl.pallas_call(
        kernel,
        out_shape=shapes,
        in_specs=[vmem] * len(args),
        out_specs=jax.tree.map(lambda _: vmem, shapes),
        scratch_shapes=scratch,
        compiler_params=pltpu.CompilerParams(vmem_limit_bytes=12 << 20),
    )(*args)


def exact_dot(left, right):
    return jnp.dot(left, right, precision=lax.Precision.HIGHEST, preferred_element_type=f32)


def pair_mean(count, rows, first):
    pair = lax.broadcasted_iota(jnp.int32, (count, rows), 0)
    row = lax.broadcasted_iota(jnp.int32, (count, rows), 1)
    return jnp.where((row - first >= 2 * pair) & (row - first <= 2 * pair + 1), 0.5, 0.0)


def pooled_kernel(low_ref, own_ref, high_ref, out_ref, gelu_ref):
    at = 0
    for ref in (low_ref, own_ref, high_ref):
        count = ref.shape[0]
        wide = ref[...].astype(f32)
        inv = lax.rsqrt(jnp.mean(wide * wide, axis=1, keepdims=True) + EPSILON)
        normed = wide * inv
        gelu_ref[at : at + count, :] = normed * half_erf(normed)
        at += count
    out_ref[...] = exact_dot(pair_mean(at // 2, at, 0), gelu_ref[...]).astype(bf16)


def pooled_block(low, own, high):
    total = low.shape[0] + own.shape[0] + high.shape[0]
    width = own.shape[1]
    return local_call(
        pooled_kernel, jax.ShapeDtypeStruct((total // 2, width), bf16),
        [pltpu.VMEM((total, width), f32)], low, own, high,
    )


def windows_kernel(before_ref, cot_ref, after_ref, out_ref, wide_ref):
    count, rows, _ = out_ref.shape
    step = (cot_ref.shape[0]) // count
    wide_ref[...] = jnp.zeros_like(wide_ref)
    wide_ref[7:8, :] = before_ref[...].astype(f32)
    wide_ref[8 : 8 + cot_ref.shape[0], :] = cot_ref[...].astype(f32)
    wide_ref[8 + cot_ref.shape[0] : 9 + cot_ref.shape[0], :] = after_ref[...].astype(f32)
    for b in range(count):
        out_ref[b] = wide_ref[pl.ds(7 + step * b, rows), :].astype(bf16)


def cot_windows(before, cot, after, count):
    rows, width = cot.shape
    return local_call(
        windows_kernel,
        jax.ShapeDtypeStruct((count, rows // count + 8, width), bf16),
        [pltpu.VMEM((rows + 24, width), f32)], before, cot, after,
    )


def statistics_kernel(own, y_ref, cot_ref, grad_ref, back_ref):
    groups, rows, width = y_ref.shape
    full = groups * width
    pairs = cot_ref.shape[1]
    block = width // 4
    repeat = (
        lax.broadcasted_iota(jnp.int32, (rows, pairs), 0) // 2
        == lax.broadcasted_iota(jnp.int32, (rows, pairs), 1)
    ).astype(bf16)
    source = lax.broadcasted_iota(jnp.int32, (width, 512), 0)
    lane = lax.broadcasted_iota(jnp.int32, (width, 512), 1)
    spread = ((lane % 128 < block) & (source == lane // 128 * block + lane % 128)).astype(bf16)
    means = pair_mean(own // 2, rows, 2)
    keep = (
        lax.broadcasted_iota(jnp.int32, (own, rows), 0) + 2
        == lax.broadcasted_iota(jnp.int32, (own, rows), 1)
    ).astype(bf16)
    square = 0.0
    for g in range(groups):
        wide = y_ref[g].astype(f32)
        square = square + jnp.sum(wide * wide, axis=1, keepdims=True)
    inv = lax.rsqrt(square / full + EPSILON)
    slopes, inner = [], 0.0
    for g in range(groups):
        normed = y_ref[g].astype(f32) * inv
        half = half_erf(normed)
        features = exact_dot(means, normed * half).astype(bf16)
        placed = jnp.dot(features, spread, preferred_element_type=f32).astype(bf16)
        for i in range(4):
            back_ref[4 * g + i, : own // 2, :] = placed[:, 128 * i : 128 * i + 128]
        upstream = 0.5 * jnp.dot(repeat, cot_ref[g], preferred_element_type=f32)
        slope = upstream * gelu_slope(normed, half)
        inner = inner + jnp.sum(slope * normed, axis=1, keepdims=True)
        slopes.append(slope)
    mean = inner / full
    for g in range(groups):
        normed = y_ref[g].astype(f32) * inv
        grad = (inv * (slopes[g] - normed * mean)).astype(bf16)
        grad_ref[g] = grad
        mine = jnp.dot(keep, grad, preferred_element_type=f32).astype(bf16)
        placed = jnp.dot(mine, spread, preferred_element_type=f32).astype(bf16)
        for i in range(4):
            back_ref[4 * g + i, own // 2 :, :] = placed[:, 128 * i : 128 * i + 128]


def statistics(conv_out, cot, own):
    groups = conv_out.shape[0]
    shapes = (
        jax.ShapeDtypeStruct(conv_out.shape, bf16),
        jax.ShapeDtypeStruct((4 * groups, own + own // 2, 128), bf16),
    )
    kernel = functools.partial(statistics_kernel, own)
    return local_call(kernel, shapes, [], conv_out, cot)


def taps_kernel(taps, back_ref, wide_ref, feature_ref, stage_ref):
    count, rows, lanes = back_ref.shape
    own = 2 * rows // 3
    span = stage_ref.shape[0] // count
    width = wide_ref.shape[1]
    block = width // taps
    source = lax.broadcasted_iota(jnp.int32, (lanes, width), 0)
    lane = lax.broadcasted_iota(jnp.int32, (lanes, width), 1)
    total = jnp.zeros((count * span, width), f32)
    for k in range(taps):
        stage_ref[...] = jnp.zeros_like(stage_ref)
        for b in range(count):
            stage_ref[pl.ds(b * span + k + 2, own), :] = back_ref[b, own // 2 :, :].astype(f32)
        place = ((source < block) & (lane == source + k * block)).astype(bf16)
        total = total + jnp.dot(stage_ref[...].astype(bf16), place, preferred_element_type=f32)
    wide_ref[...] = total.astype(bf16)
    for b in range(count):
        feature_ref[pl.ds(b * (own // 2), own // 2), :] = back_ref[b, : own // 2, :block]


def spread_taps(back, taps, block, span):
    count, rows, lanes = back.shape
    shapes = (
        jax.ShapeDtypeStruct((count * span, taps * block), bf16),
        jax.ShapeDtypeStruct((count * (rows // 3), block), bf16),
    )
    kernel = functools.partial(taps_kernel, taps)
    return local_call(kernel, shapes, [pltpu.VMEM((count * span, lanes), f32)], back)


def per_device(activations, conv_weight, cotangent):
    tap_count, out_width, in_width = conv_weight.shape
    core = lax.axis_index("core")
    zl, y = lax.axis_index("zl"), lax.axis_index("y")
    half = in_width // 2
    rows = activations.shape[0] // 2
    span = rows + 8
    group = 4 * out_width
    lanes = 4 * span

    low = shift(activations[-8:], AXES, 1)
    high = shift(activations[:8], AXES, -1)

    own_half = jnp.where(core == 0, conv_weight[:, :, :half], conv_weight[:, :, half:])
    first = gather_all(own_half, "y")
    second = lax.ppermute(first, "core", [(0, 1), (1, 0)])
    weights = jnp.where(
        core == 0,
        jnp.concatenate([first, second], axis=3),
        jnp.concatenate([second, first], axis=3),
    )
    weights = weights.transpose(1, 0, 2, 3).reshape(tap_count, group, in_width)

    block = pooled_block(low, activations, high)
    blocks = [block] + [turn(block, "zl", j) for j in (1, 2, 3)]
    gathered = jnp.zeros((5, span, in_width), bf16)
    for j in range(4):
        gathered = lax.dynamic_update_index_in_dim(gathered, blocks[j], (zl - j) % 4, 0)
    flat = gathered.reshape(-1, in_width)

    cot, _ = lax.optimization_barrier((cotangent, block))
    before = shift(cot[-1:], SEQ, 1)
    after = shift(cot[:1], SEQ, -1)
    step = rows // 2
    windows = cot_windows(before, cot, after, 16)
    windows = lax.all_to_all(windows, SUB, 0, 0)
    cot_block = windows.reshape(4, 4, step + 8, out_width).transpose(0, 2, 1, 3)
    cot_block = cot_block.reshape(4, step + 8, group)

    conv_acc = jnp.zeros((lanes, group), f32)
    for k in range(tap_count):
        conv_acc = conv_acc + lax.dot_general(
            flat[k : k + lanes], weights[k], (((1,), (1,)), ((), ())),
            preferred_element_type=f32,
        )
    conv_out = conv_acc.astype(bf16).reshape(4, span, group)
    near = gathered[:4].reshape(lanes, in_width)
    ring = [near] + [turn(near, "y", j) for j in (1, 2, 3)]
    conv_out = lax.all_to_all(conv_out, "zl", 0, 0)
    grad, back = statistics(conv_out, cot_block, rows)
    back = lax.all_to_all(back, SUB, 0, 0)
    grad = lax.all_to_all(grad, "zl", 0, 0)

    grad_flat = jnp.concatenate([grad.reshape(lanes, group), jnp.zeros((8, group), bf16)], axis=0)
    running = jnp.zeros((lanes, in_width), f32)
    for k in range(tap_count):
        running = running + jnp.dot(
            grad_flat[4 - k : 4 - k + lanes], weights[k], preferred_element_type=f32
        )
    running = running.astype(bf16).reshape(4, span, in_width)
    own = [
        lax.dynamic_slice(running, ((zl + j) % 4, 0, 0), (1, rows, in_width))[0]
        for j in range(4)
    ]
    parts = own[:1] + [turn(own[j], "zl", j) for j in (1, 2, 3)]
    pooled_grad = sum(part.astype(f32) for part in parts)
    x_float = activations.astype(f32)
    inv_first = lax.rsqrt(jnp.mean(x_float * x_float, axis=1, keepdims=True) + EPSILON)
    normed_first = x_float * inv_first
    slope_first = 0.5 * jnp.repeat(pooled_grad, 2, axis=0)
    slope_first = slope_first * gelu_slope(normed_first, half_erf(normed_first))
    inner_first = jnp.mean(slope_first * normed_first, axis=1, keepdims=True)
    input_grad = (inv_first * (slope_first - normed_first * inner_first)).astype(bf16)

    around = jnp.zeros((4, 4, span, in_width), bf16)
    for j in range(4):
        piece = ring[j].reshape(4, 1, span, in_width)
        around = lax.dynamic_update_slice_in_dim(around, piece, (y - j) % 4, axis=1)
    wide, features = spread_taps(back, tap_count, out_width, span)
    weight_part = lax.dot_general(
        around.reshape(-1, in_width), wide, (((0,), (0,)), ((), ())),
        preferred_element_type=f32,
    )
    halves = weight_part.reshape(16, 2, in_width // 32, tap_count * out_width)
    mine = jnp.where(core == 0, halves[:, 0], halves[:, 1])
    other = jnp.where(core == 0, halves[:, 1], halves[:, 0]).astype(bf16)
    other = lax.ppermute(other, "core", [(0, 1), (1, 0)])
    total = (mine + other.astype(f32)).astype(bf16)
    total = lax.all_to_all(total, ("zh", "x"), 0, 0)
    weight_grad = jnp.sum(total.astype(f32), axis=0).reshape(-1, tap_count, out_width)
    return (features, input_grad, weight_grad)


def solution(mesh):
    split = Mesh(mesh.devices.reshape(4, 4, 2, 4, 4), AXES)
    return jax.shard_map(
        per_device,
        mesh=split,
        in_specs=(P(AXES, None), P(None, SUB, None), P(SEQ, SUB)),
        out_specs=(P(SEQ, SUB), P(AXES, None), P(SEQ, None, SUB)),
        check_vma=False,
    )
```

time: 232 us -> 206 us (0.89)
  the two profiles are of different devices: /device:TPU:64 before, /device:TPU:10 now
where the time goes in v3:
time: 206 us; the launch traced here: 205 us
  starting transfers between devices  90.7 us (44%)
  waiting for transfers between devices  51.1 us (25%)
  blocking collectives  22.9 us (11%)
  matrix products  16 us (8%)
  local copies, waits for them, and re-layouts  10.3 us (5%)
  other arithmetic  6.62 us (3%)
  Pallas kernels  5.67 us (3%)
    ppermute x9, waiting for transfers between devices, turn(): lax.ppermute(block, axis, [(i, (i + step) % count) for i in range(count)])  38.4 us
    ppermute x9, starting transfers between devices, turn(): lax.ppermute(block, axis, [(i, (i + step) % count) for i in range(count)])  33.1 us
    all_to_all x1, blocking collectives, gather_all(): lax.all_to_all(jnp.broadcast_to(block, (count, *block.shape)), axis, 0, 0)  22.9 us
    all_to_all x1, starting transfers between devices, per_device(): total = lax.all_to_all(total, ('zh', 'x'), 0, 0)  18.9 us
    ppermute x4, starting transfers between devices, shift(): return lax.ppermute(block, axis, pairs)  11.4 us
    all_to_all x1, starting transfers between devices, per_device(): windows = lax.all_to_all(windows, SUB, 0, 0)  8.98 us
    dot_general x5, matrix products, per_device(): jnp.dot(grad_flat[4 - k:4 - k + lanes], weights[k], preferred_element_typ...  8.64 us
    all_to_all x1, waiting for transfers between devices, per_device(): conv_out = lax.all_to_all(conv_out, 'zl', 0, 0)  7.6 us
  transfers between devices with their start and end apart: 20, of which 7 were waited for; matrix products, arithmetic and copies ran while one was open for 13% of the time, Pallas kernels for 1%

profile of v3, /device:TPU:10, one launch (start us, length us, event | category | flops | bytes accessed | tf_op | source)
XLA Modules:
  0.0 204.8 jit_solution(664943865870746433)
XLA Ops:
  1.9 22.9 %all_to_all.30 = bf16[4,5,72,512]{3,2,1,0:T(8,128)(2,1)S(1)} all-to-all(bf16[4,5,72,512]{3,2,1,0:T(8,128)(2,1)S(1)} %broadcast_in_dim.33), channel_id=1, replica_groups=mesh['zh'=4,'x'=4,'core'=2,'zl'=4,'y'=4] {'y'}, dimensions={0} | all-to-all | bytes 2949120 | tf_op jit(solution)/shard_map/all_to_all | solution.py:40
  26.8 2.4 %collective-permute-start = (bf16[8,1024]{1,0:T(8,128)(2,1)S(1)}, bf16[8,1024]{1,0:T(8,128)(2,1)S(1)}, u32[]{:S(2)}, u32[]{:S(2)}) collective-permute-start(bf16[8,1024]{1,0:T(8,128)(2,1)S(1)} %get-tuple-element.33), channel_id=1, source_target_pairs={{0,1},{1,2},{2,3},{3,4},{4,5},{5,6},{6,7},{7,8},{8,9},{9,10},{10,1... | collective-permute-start | bytes 49160 | tf_op jit(solution)/shard_map/ppermute | solution.py:30
  29.2 3.5 %collective-permute-start.1 = (bf16[8,1024]{1,0:T(8,128)(2,1)S(1)}, bf16[8,1024]{1,0:T(8,128)(2,1)S(1)}, u32[]{:S(2)}, u32[]{:S(2)}) collective-permute-start(bf16[8,1024]{1,0:T(8,128)(2,1)S(1)} %get-tuple-element.32), channel_id=1, source_target_pairs={{1,0},{2,1},{3,2},{4,3},{5,4},{6,5},{7,6},{8,7},{9,8},{10,9},{11,1... | collective-permute-start | bytes 49160 | tf_op jit(solution)/shard_map/ppermute | solution.py:30
  32.7 2.1 %collective-permute-done.1.high_ref = bf16[8,1024]{1,0:T(8,128)(2,1)S(1)} collective-permute-done((bf16[8,1024]{1,0:T(8,128)(2,1)S(1)}, bf16[8,1024]{1,0:T(8,128)(2,1)S(1)}, u32[]{:S(2)}, u32[]{:S(2)}) %collective-permute-start.1) | collective-permute-done | bytes 16416 | tf_op jit(solution)/shard_map/ppermute | solution.py:30
  35.4 3.8 %collective-permute-start.2 = (bf16[72,1024]{1,0:T(8,128)(2,1)S(1)}, bf16[72,1024]{1,0:T(8,128)(2,1)S(1)}, u32[]{:S(2)}, u32[]{:S(2)}) collective-permute-start(bf16[72,1024]{1,0:T(8,128)(2,1)S(1)} %shard_map.58), channel_id=1, source_target_pairs={{0,4},{4,8},{8,12},{12,0},{1,5},{5,9},{9,13},{13,1},{2,6},{6,10},{... | collective-permute-start | bytes 442376 | tf_op jit(solution)/shard_map/ppermute | solution.py:35
  39.2 5.2 %collective-permute-start.3 = (bf16[72,1024]{1,0:T(8,128)(2,1)S(1)}, bf16[72,1024]{1,0:T(8,128)(2,1)S(1)}, u32[]{:S(2)}, u32[]{:S(2)}) collective-permute-start(bf16[72,1024]{1,0:T(8,128)(2,1)S(1)} %shard_map.58), channel_id=1, source_target_pairs={{0,8},{4,12},{8,0},{12,4},{1,9},{5,13},{9,1},{13,5},{2,10},{6,14},... | collective-permute-start | bytes 442376 | tf_op jit(solution)/shard_map/ppermute | solution.py:35
  46.5 3.6 %collective-permute-start.7 = (bf16[1,72]{1,0:T(2,128)(2,1)S(1)}, bf16[1,72]{1,0:T(2,128)(2,1)S(1)}, u32[]{:S(2)}, u32[]{:S(2)}) collective-permute-start(bf16[1,72]{1,0:T(2,128)(2,1)S(1)} %get-tuple-element.34), channel_id=1, source_target_pairs={{16,0},{32,16},{48,32},{64,48},{80,64},{96,80},{112,96},{128,112},... | collective-permute-start | bytes 440 | tf_op jit(solution)/shard_map/ppermute | solution.py:30
  50.3 2.9 %collective-permute-start.4 = (bf16[72,1024]{1,0:T(8,128)(2,1)S(1)}, bf16[72,1024]{1,0:T(8,128)(2,1)S(1)}, u32[]{:S(2)}, u32[]{:S(2)}) collective-permute-start(bf16[72,1024]{1,0:T(8,128)(2,1)S(1)} %shard_map.58), channel_id=1, source_target_pairs={{0,12},{4,0},{8,4},{12,8},{1,13},{5,1},{9,5},{13,9},{2,14},{6,2},{... | collective-permute-start | bytes 442376 | tf_op jit(solution)/shard_map/ppermute | solution.py:35
  53.9 9.0 %all-to-all-start.2 = ((bf16[16,40,72]{2,1,0:T(8,128)(2,1)}), bf16[16,40,72]{2,1,0:T(8,128)(2,1)S(1)}, u32[]{:S(2)}, u32[]{:S(2)}) async-start(bf16[16,40,72]{2,1,0:T(8,128)(2,1)} %shard_map.59), calls=%async_computation.2 | async-start | bytes 327680 | tf_op jit(solution)/shard_map/all_to_all | solution.py:226
  63.9 2.8 %fusion = bf16[5,4,72,1024]{3,2,0,1:T(8,128)(2,1)S(1)} fusion(bf16[4,5,72,512]{3,2,1,0:T(8,128)(2,1)} %collective-permute-done.5, bf16[4,5,72,512]{3,2,1,0:T(8,128)(2,1)S(1)} %all_to_all.30, pred[]{:T(512)S(6)} %eq.19), kind=kLoop, calls=%fused_computation.1 | loop fusion | flops 13271040 | bytes 5898241 | tf_op jit(solution)/shard_map/transpose | solution.py:212
  69.4 2.3 %fusion.8 = bf16[288,288]{1,0:T(8,128)(2,1)} fusion(f32[288,288]{1,0:T(8,128)S(1)} %fusion.18, f32[288,288]{1,0:T(8,128)S(1)} %fusion.20, f32[288,288]{1,0:T(8,128)S(1)} %fusion.22, f32[288,288]{1,0:T(8,128)S(1)} %fusion.24, bf16[288,1024]{1,0:T(8,128)(2,1)} %bitcast.4, bf16[288,1024]{1,0:T(8,128)(2,1)S(1)} %bitcast.96), kind=kOutput, calls=%fused_computation.11 | convolution fusion | flops 170284032 | bytes 2672640 | tf_op jit(solution)/shard_map/dot_general | solution.py:232
  71.6 4.5 %all-to-all-start.1 = ((bf16[4,72,288]{2,1,0:T(8,128)(2,1)}), bf16[4,72,288]{2,1,0:T(8,128)(2,1)S(1)}, u32[]{:S(2)}, u32[]{:S(2)}) async-start(bf16[4,72,288]{2,1,0:T(8,128)(2,1)} %bitcast.12), calls=%async_computation.1 | async-start | bytes 442368 | tf_op jit(solution)/shard_map/all_to_all | solution.py:239
  76.4 7.6 %all-to-all-done.1.y_ref = bf16[4,72,288]{2,1,0:T(8,128)(2,1)S(1)} async-done(((bf16[4,72,288]{2,1,0:T(8,128)(2,1)}), bf16[4,72,288]{2,1,0:T(8,128)(2,1)S(1)}, u32[]{:S(2)}, u32[]{:S(2)}) %all-to-all-start.1) | async-done | bytes 165920 | tf_op jit(solution)/shard_map/all_to_all | solution.py:239
  84.0 2.8 %shard_map.60 = (bf16[4,72,288]{2,1,0:T(8,128)(2,1)}, bf16[16,96,128]{2,1,0:T(8,128)(2,1)}) custom-call(bf16[4,72,288]{2,1,0:T(8,128)(2,1)S(1)} %all-to-all-done.1.y_ref, bf16[4,40,288]{2,1,0:T(8,128)(2,1)S(1)} %reshape.79.cot_ref), custom_call_target="tpu_custom_call" | custom-call | tf_op jit(solution)/shard_map/pallas_call | solution.py:45
  86.8 3.4 %all-to-all-start.4 = ((bf16[4,72,288]{2,1,0:T(8,128)(2,1)}), bf16[4,72,288]{2,1,0:T(8,128)(2,1)S(1)}, u32[]{:S(2)}, u32[]{:S(2)}) async-start(bf16[4,72,288]{2,1,0:T(8,128)(2,1)} %get-tuple-element.11), calls=%async_computation.4 | async-start | bytes 442368 | tf_op jit(solution)/shard_map/all_to_all | solution.py:242
  90.2 3.4 %collective-permute-start.11 = (bf16[288,1024]{1,0:T(8,128)(2,1)}, bf16[288,1024]{1,0:T(8,128)(2,1)}, u32[]{:S(2)}, u32[]{:S(2)}) collective-permute-start(bf16[288,1024]{1,0:T(8,128)(2,1)} %bitcast.4), channel_id=1, source_target_pairs={{0,1},{1,2},{2,3},{3,0},{4,5},{5,6},{6,7},{7,4},{8,9},{9,10},{10,1... | collective-permute-start | bytes 1769480 | tf_op jit(solution)/shard_map/ppermute | solution.py:35
  93.6 3.1 %all-to-all-done.4 = bf16[4,72,288]{2,1,0:T(8,128)(2,1)S(1)} async-done(((bf16[4,72,288]{2,1,0:T(8,128)(2,1)}), bf16[4,72,288]{2,1,0:T(8,128)(2,1)S(1)}, u32[]{:S(2)}, u32[]{:S(2)}) %all-to-all-start.4) | async-done | bytes 165920 | tf_op jit(solution)/shard_map/all_to_all | solution.py:242
  96.6 6.3 %all-to-all-start.3 = ((bf16[16,96,128]{2,1,0:T(8,128)(2,1)}), bf16[16,96,128]{2,1,0:T(8,128)(2,1)S(1)}, u32[]{:S(2)}, u32[]{:S(2)}) async-start(bf16[16,96,128]{2,1,0:T(8,128)(2,1)} %get-tuple-element.9), calls=%async_computation.3 | async-start | bytes 786432 | tf_op jit(solution)/shard_map/all_to_all | solution.py:241
  102.9 4.0 %collective-permute-start.12 = (bf16[288,1024]{1,0:T(8,128)(2,1)}, bf16[288,1024]{1,0:T(8,128)(2,1)}, u32[]{:S(2)}, u32[]{:S(2)}) collective-permute-start(bf16[288,1024]{1,0:T(8,128)(2,1)} %bitcast.4), channel_id=1, source_target_pairs={{0,2},{1,3},{2,0},{3,1},{4,6},{5,7},{6,4},{7,5},{8,10},{9,11},{10,... | collective-permute-start | bytes 1769480 | tf_op jit(solution)/shard_map/ppermute | solution.py:35
  107.0 3.4 %collective-permute-start.13 = (bf16[288,1024]{1,0:T(8,128)(2,1)}, bf16[288,1024]{1,0:T(8,128)(2,1)S(1)}, u32[]{:S(2)}, u32[]{:S(2)}) collective-permute-start(bf16[288,1024]{1,0:T(8,128)(2,1)} %bitcast.4), channel_id=1, source_target_pairs={{0,3},{1,0},{2,1},{3,2},{4,7},{5,4},{6,5},{7,6},{8,11},{9,8},{10,9... | collective-permute-start | bytes 1769480 | tf_op jit(solution)/shard_map/ppermute | solution.py:35
  113.0 10.7 %collective-permute-done.12 = bf16[288,1024]{1,0:T(8,128)(2,1)} collective-permute-done((bf16[288,1024]{1,0:T(8,128)(2,1)}, bf16[288,1024]{1,0:T(8,128)(2,1)}, u32[]{:S(2)}, u32[]{:S(2)}) %collective-permute-start.12) | collective-permute-done | bytes 589856 | tf_op jit(solution)/shard_map/ppermute | solution.py:35
  124.9 9.0 %collective-permute-done.13 = bf16[288,1024]{1,0:T(8,128)(2,1)S(1)} collective-permute-done((bf16[288,1024]{1,0:T(8,128)(2,1)}, bf16[288,1024]{1,0:T(8,128)(2,1)S(1)}, u32[]{:S(2)}, u32[]{:S(2)}) %collective-permute-start.13) | collective-permute-done | bytes 589856 | tf_op jit(solution)/shard_map/ppermute | solution.py:35
  133.9 2.5 %copy.40 = bf16[1024,1152]{1,0:T(8,128)(2,1)} copy(bf16[1024,1152]{0,1:T(8,128)(2,1)S(1)} %bitcast.90) | data formatting | bytes 4718592 | tf_op jit(solution)/shard_map/dot_general | solution.py:270
  141.1 3.2 %fusion.9 = f32[16,2,32,360]{3,2,1,0:T(8,128)S(1)} fusion(bf16[16,2,32,1152]{3,2,1,0:T(8,128)(2,1)} %bitcast.110, bf16[1152,360]{1,0:T(8,128)(2,1)S(1)} %get-tuple-element.12), kind=kOutput, calls=%fused_computation.12 | convolution fusion | flops 849346560 | bytes 4663296 | tf_op jit(solution)/shard_map/dot_general | solution.py:270
  144.4 2.2 %collective-permute-start.14 = (bf16[16,32,360]{2,1,0:T(8,128)(2,1)S(1)}, bf16[16,32,360]{2,1,0:T(8,128)(2,1)S(1)}, u32[]{:S(2)}, u32[]{:S(2)}) collective-permute-start(bf16[16,32,360]{2,1,0:T(8,128)(2,1)S(1)} %fusion.38), channel_id=1, source_target_pairs={{0,16},{16,0},{1,17},{17,1},{2,18},{18,2},{3,19},{19,3},{4,20},{20... | collective-permute-start | bytes 1105928 | tf_op jit(solution)/shard_map/ppermute | solution.py:277
  150.6 18.9 %all-to-all-start.5 = ((bf16[16,32,360]{2,1,0:T(8,128)(2,1)}), bf16[16,32,360]{2,1,0:T(8,128)(2,1)S(1)}, u32[]{:S(2)}, u32[]{:S(2)}) async-start(bf16[16,32,360]{2,1,0:T(8,128)(2,1)} %fusion.13), calls=%async_computation.5 | async-start | bytes 786432 | tf_op jit(solution)/shard_map/all_to_all | solution.py:279
  169.5 2.6 %fusion.4 = bf16[288,1024]{1,0:T(8,128)(2,1)S(1)} fusion(f32[288,1024]{1,0:T(8,128)} %fusion.61, f32[288,1024]{1,0:T(8,128)S(1)} %fusion.42, f32[288,1024]{1,0:T(8,128)} %fusion.44, f32[288,1024]{1,0:T(8,128)} %fusion.46, bf16[288,1024]{1,0:T(8,128)(2,1)S(1)} %bitcast.97, bf16[288,288]{1,0:T(8,128)(2,1)S(1)} %bitcast.95), kind=kOutput, calls=%fused_computation.6 | convolution fusion | flops 171343872 | bytes 6064128 | tf_op jit(solution)/shard_map/dot_general | solution.py:247
  172.1 5.0 %collective-permute-start.10 = (bf16[64,1024]{1,0:T(8,128)(2,1)S(1)}, bf16[64,1024]{1,0:T(8,128)(2,1)S(1)}, u32[]{:S(2)}, u32[]{:S(2)}) collective-permute-start(bf16[64,1024]{1,0:T(8,128)(2,1)S(1)} %get-tuple-element.30), channel_id=1, source_target_pairs={{0,12},{4,0},{8,4},{12,8},{1,13},{5,1},{9,5},{13,9},{2,14},{6,2},{... | collective-permute-start | bytes 393224 | tf_op jit(solution)/shard_map/ppermute | solution.py:35
  177.0 2.2 %collective-permute-start.9 = (bf16[64,1024]{1,0:T(8,128)(2,1)S(1)}, bf16[64,1024]{1,0:T(8,128)(2,1)S(1)}, u32[]{:S(2)}, u32[]{:S(2)}) collective-permute-start(bf16[64,1024]{1,0:T(8,128)(2,1)S(1)} %get-tuple-element.31), channel_id=1, source_target_pairs={{0,8},{4,12},{8,0},{12,4},{1,9},{5,13},{9,1},{13,5},{2,10},{6,14},... | collective-permute-start | bytes 393224 | tf_op jit(solution)/shard_map/ppermute | solution.py:35
  179.2 3.3 %collective-permute-start.8 = (bf16[64,1024]{1,0:T(8,128)(2,1)S(1)}, bf16[64,1024]{1,0:T(8,128)(2,1)S(1)}, u32[]{:S(2)}, u32[]{:S(2)}) collective-permute-start(bf16[64,1024]{1,0:T(8,128)(2,1)S(1)} %get-tuple-element.29), channel_id=1, source_target_pairs={{0,4},{4,8},{8,12},{12,0},{1,5},{5,9},{9,13},{13,1},{2,6},{6,10},{... | collective-permute-start | bytes 393224 | tf_op jit(solution)/shard_map/ppermute | solution.py:35
  182.5 9.7 %collective-permute-done.10 = bf16[64,1024]{1,0:T(8,128)(2,1)S(1)} collective-permute-done((bf16[64,1024]{1,0:T(8,128)(2,1)S(1)}, bf16[64,1024]{1,0:T(8,128)(2,1)S(1)}, u32[]{:S(2)}, u32[]{:S(2)}) %collective-permute-start.10) | collective-permute-done | bytes 131104 | tf_op jit(solution)/shard_map/ppermute | solution.py:35
  192.3 8.9 %collective-permute-done.9 = bf16[64,1024]{1,0:T(8,128)(2,1)S(1)} collective-permute-done((bf16[64,1024]{1,0:T(8,128)(2,1)S(1)}, bf16[64,1024]{1,0:T(8,128)(2,1)S(1)}, u32[]{:S(2)}, u32[]{:S(2)}) %collective-permute-start.9) | collective-permute-done | bytes 131104 | tf_op jit(solution)/shard_map/ppermute | solution.py:35
  (84 shorter events, 26.4 us)
Async XLA Ops:
  1.8 25.0 %copy-start = (bf16[128,1024]{1,0:T(8,128)(2,1)S(1)}, bf16[128,1024]{1,0:T(8,128)(2,1)}, u32[]{:S(2)}) copy-start(bf16[128,1024]{1,0:T(8,128)(2,1)} %own_ref.1) | copy-start | bytes 786436
  1.8 42.6 %copy-start.11 = (bf16[512,72]{0,1:T(8,128)(2,1)S(1)}, bf16[512,72]{0,1:T(8,128)(2,1)}, u32[]{:S(2)}) copy-start(bf16[512,72]{0,1:T(8,128)(2,1)} %param.5) | copy-start | bytes 221188
  24.8 39.1 %collective-permute-start.5 = (bf16[4,5,72,512]{3,2,1,0:T(8,128)(2,1)S(1)}, bf16[4,5,72,512]{3,2,1,0:T(8,128)(2,1)}, u32[]{:S(2)}, u32[]{:S(2)}) collective-permute-start(bf16[4,5,72,512]{3,2,1,0:T(8,128)(2,1)S(1)} %all_to_all.30), channel_id=1, source_target_pairs={{0,16},{16,0},{1,17},{17,1},{2,18},{18,2},{3,19},{19,3},{4,20},{20... | collective-permute-start | bytes 4423688 | tf_op jit(solution)/shard_map/ppermute | solution.py:206
  26.8 5.9 %collective-permute-start = (bf16[8,1024]{1,0:T(8,128)(2,1)S(1)}, bf16[8,1024]{1,0:T(8,128)(2,1)S(1)}, u32[]{:S(2)}, u32[]{:S(2)}) collective-permute-start(bf16[8,1024]{1,0:T(8,128)(2,1)S(1)} %get-tuple-element.33), channel_id=1, source_target_pairs={{0,1},{1,2},{2,3},{3,4},{4,5},{5,6},{6,7},{7,8},{8,9},{9,10},{10,1... | collective-permute-start | bytes 49160 | tf_op jit(solution)/shard_map/ppermute | solution.py:30
  29.2 5.6 %collective-permute-start.1 = (bf16[8,1024]{1,0:T(8,128)(2,1)S(1)}, bf16[8,1024]{1,0:T(8,128)(2,1)S(1)}, u32[]{:S(2)}, u32[]{:S(2)}) collective-permute-start(bf16[8,1024]{1,0:T(8,128)(2,1)S(1)} %get-tuple-element.32), channel_id=1, source_target_pairs={{1,0},{2,1},{3,2},{4,3},{5,4},{6,5},{7,6},{8,7},{9,8},{10,9},{11,1... | collective-permute-start | bytes 49160 | tf_op jit(solution)/shard_map/ppermute | solution.py:30
  35.4 27.5 %collective-permute-start.2 = (bf16[72,1024]{1,0:T(8,128)(2,1)S(1)}, bf16[72,1024]{1,0:T(8,128)(2,1)S(1)}, u32[]{:S(2)}, u32[]{:S(2)}) collective-permute-start(bf16[72,1024]{1,0:T(8,128)(2,1)S(1)} %shard_map.58), channel_id=1, source_target_pairs={{0,4},{4,8},{8,12},{12,0},{1,5},{5,9},{9,13},{13,1},{2,6},{6,10},{... | collective-permute-start | bytes 442376 | tf_op jit(solution)/shard_map/ppermute | solution.py:35
  39.2 23.7 %collective-permute-start.3 = (bf16[72,1024]{1,0:T(8,128)(2,1)S(1)}, bf16[72,1024]{1,0:T(8,128)(2,1)S(1)}, u32[]{:S(2)}, u32[]{:S(2)}) collective-permute-start(bf16[72,1024]{1,0:T(8,128)(2,1)S(1)} %shard_map.58), channel_id=1, source_target_pairs={{0,8},{4,12},{8,0},{12,4},{1,9},{5,13},{9,1},{13,5},{2,10},{6,14},... | collective-permute-start | bytes 442376 | tf_op jit(solution)/shard_map/ppermute | solution.py:35
  44.6 5.7 %collective-permute-start.6 = (bf16[1,72]{1,0:T(2,128)(2,1)S(1)}, bf16[1,72]{1,0:T(2,128)(2,1)S(1)}, u32[]{:S(2)}, u32[]{:S(2)}) collective-permute-start(bf16[1,72]{1,0:T(2,128)(2,1)S(1)} %get-tuple-element.35), channel_id=1, source_target_pairs={{0,16},{16,32},{32,48},{48,64},{64,80},{80,96},{96,112},{112,128},... | collective-permute-start | bytes 440 | tf_op jit(solution)/shard_map/ppermute | solution.py:30
  46.5 6.7 %collective-permute-start.7 = (bf16[1,72]{1,0:T(2,128)(2,1)S(1)}, bf16[1,72]{1,0:T(2,128)(2,1)S(1)}, u32[]{:S(2)}, u32[]{:S(2)}) collective-permute-start(bf16[1,72]{1,0:T(2,128)(2,1)S(1)} %get-tuple-element.34), channel_id=1, source_target_pairs={{16,0},{32,16},{48,32},{64,48},{80,64},{96,80},{112,96},{128,112},... | collective-permute-start | bytes 440 | tf_op jit(solution)/shard_map/ppermute | solution.py:30
  50.3 12.7 %collective-permute-start.4 = (bf16[72,1024]{1,0:T(8,128)(2,1)S(1)}, bf16[72,1024]{1,0:T(8,128)(2,1)S(1)}, u32[]{:S(2)}, u32[]{:S(2)}) collective-permute-start(bf16[72,1024]{1,0:T(8,128)(2,1)S(1)} %shard_map.58), channel_id=1, source_target_pairs={{0,12},{4,0},{8,4},{12,8},{1,13},{5,1},{9,5},{13,9},{2,14},{6,2},{... | collective-permute-start | bytes 442376 | tf_op jit(solution)/shard_map/ppermute | solution.py:35
  53.9 17.7 %all-to-all-start.2 = ((bf16[16,40,72]{2,1,0:T(8,128)(2,1)}), bf16[16,40,72]{2,1,0:T(8,128)(2,1)S(1)}, u32[]{:S(2)}, u32[]{:S(2)}) async-start(bf16[16,40,72]{2,1,0:T(8,128)(2,1)} %shard_map.59), calls=%async_computation.2 | async-start | bytes 327680 | tf_op jit(solution)/shard_map/all_to_all | solution.py:226
  63.0 5.9 %copy-start.3 = (bf16[5,72,1024]{2,1,0:T(8,128)(2,1)}, bf16[5,72,1024]{2,1,0:T(8,128)(2,1)S(1)}, u32[]{:S(2)}) copy-start(bf16[5,72,1024]{2,1,0:T(8,128)(2,1)S(1)} %bitcast_dynamic-update-slice_fusion.1) | copy-start | bytes 2211844
  67.2 1.0 copy-start.4
  67.2 1.0 copy-start.10
  67.2 1.2 copy-start.8
  67.2 1.7 copy-start.6
  67.2 2.2 %copy-start.1 = (bf16[1,4,72,1024]{3,2,0,1:T(8,128)(2,1)}, bf16[1,4,72,1024]{3,2,0,1:T(8,128)(2,1)S(1)}, u32[]{:S(2)}) copy-start(bf16[1,4,72,1024]{3,2,0,1:T(8,128)(2,1)S(1)} %get-tuple-element.24) | copy-start | bytes 1769476
  71.6 12.4 %all-to-all-start.1 = ((bf16[4,72,288]{2,1,0:T(8,128)(2,1)}), bf16[4,72,288]{2,1,0:T(8,128)(2,1)S(1)}, u32[]{:S(2)}, u32[]{:S(2)}) async-start(bf16[4,72,288]{2,1,0:T(8,128)(2,1)} %bitcast.12), calls=%async_computation.1 | async-start | bytes 442368 | tf_op jit(solution)/shard_map/all_to_all | solution.py:239
  86.8 9.8 %all-to-all-start.4 = ((bf16[4,72,288]{2,1,0:T(8,128)(2,1)}), bf16[4,72,288]{2,1,0:T(8,128)(2,1)S(1)}, u32[]{:S(2)}, u32[]{:S(2)}) async-start(bf16[4,72,288]{2,1,0:T(8,128)(2,1)} %get-tuple-element.11), calls=%async_computation.4 | async-start | bytes 442368 | tf_op jit(solution)/shard_map/all_to_all | solution.py:242
  90.2 21.7 %collective-permute-start.11 = (bf16[288,1024]{1,0:T(8,128)(2,1)}, bf16[288,1024]{1,0:T(8,128)(2,1)}, u32[]{:S(2)}, u32[]{:S(2)}) collective-permute-start(bf16[288,1024]{1,0:T(8,128)(2,1)} %bitcast.4), channel_id=1, source_target_pairs={{0,1},{1,2},{2,3},{3,0},{4,5},{5,6},{6,7},{7,4},{8,9},{9,10},{10,1... | collective-permute-start | bytes 1769480 | tf_op jit(solution)/shard_map/ppermute | solution.py:35
  96.6 42.9 %all-to-all-start.3 = ((bf16[16,96,128]{2,1,0:T(8,128)(2,1)}), bf16[16,96,128]{2,1,0:T(8,128)(2,1)S(1)}, u32[]{:S(2)}, u32[]{:S(2)}) async-start(bf16[16,96,128]{2,1,0:T(8,128)(2,1)} %get-tuple-element.9), calls=%async_computation.3 | async-start | bytes 786432 | tf_op jit(solution)/shard_map/all_to_all | solution.py:241
  102.9 20.9 %collective-permute-start.12 = (bf16[288,1024]{1,0:T(8,128)(2,1)}, bf16[288,1024]{1,0:T(8,128)(2,1)}, u32[]{:S(2)}, u32[]{:S(2)}) collective-permute-start(bf16[288,1024]{1,0:T(8,128)(2,1)} %bitcast.4), channel_id=1, source_target_pairs={{0,2},{1,3},{2,0},{3,1},{4,6},{5,7},{6,4},{7,5},{8,10},{9,11},{10,... | collective-permute-start | bytes 1769480 | tf_op jit(solution)/shard_map/ppermute | solution.py:35
  107.0 26.9 %collective-permute-start.13 = (bf16[288,1024]{1,0:T(8,128)(2,1)}, bf16[288,1024]{1,0:T(8,128)(2,1)S(1)}, u32[]{:S(2)}, u32[]{:S(2)}) collective-permute-start(bf16[288,1024]{1,0:T(8,128)(2,1)} %bitcast.4), channel_id=1, source_target_pairs={{0,3},{1,0},{2,1},{3,2},{4,7},{5,4},{6,5},{7,6},{8,11},{9,8},{10,9... | collective-permute-start | bytes 1769480 | tf_op jit(solution)/shard_map/ppermute | solution.py:35
  136.5 1.6 copy-start.9
  141.1 5.5 %copy-start.7 = (bf16[1,4,72,1024]{3,2,0,1:T(8,128)(2,1)S(1)}, bf16[1,4,72,1024]{3,2,0,1:T(8,128)(2,1)}, u32[]{:S(2)}) copy-start(bf16[1,4,72,1024]{3,2,0,1:T(8,128)(2,1)} %copy-done.6) | copy-start | bytes 1769476
  144.3 3.9 %copy-start.5 = (bf16[1,4,72,1024]{3,2,0,1:T(8,128)(2,1)S(1)}, bf16[1,4,72,1024]{3,2,0,1:T(8,128)(2,1)}, u32[]{:S(2)}) copy-start(bf16[1,4,72,1024]{3,2,0,1:T(8,128)(2,1)} %copy-done.4) | copy-start | bytes 1769476
  144.4 5.3 %collective-permute-start.14 = (bf16[16,32,360]{2,1,0:T(8,128)(2,1)S(1)}, bf16[16,32,360]{2,1,0:T(8,128)(2,1)S(1)}, u32[]{:S(2)}, u32[]{:S(2)}) collective-permute-start(bf16[16,32,360]{2,1,0:T(8,128)(2,1)S(1)} %fusion.38), channel_id=1, source_target_pairs={{0,16},{16,0},{1,17},{17,1},{2,18},{18,2},{3,19},{19,3},{4,20},{20... | collective-permute-start | bytes 1105928 | tf_op jit(solution)/shard_map/ppermute | solution.py:277
  148.2 21.3 %copy-start.2 = (bf16[1,4,72,1024]{3,2,0,1:T(8,128)(2,1)S(1)}, bf16[1,4,72,1024]{3,2,0,1:T(8,128)(2,1)}, u32[]{:S(2)}) copy-start(bf16[1,4,72,1024]{3,2,0,1:T(8,128)(2,1)} %copy-done.1) | copy-start | bytes 1769476
  150.6 53.4 %all-to-all-start.5 = ((bf16[16,32,360]{2,1,0:T(8,128)(2,1)}), bf16[16,32,360]{2,1,0:T(8,128)(2,1)S(1)}, u32[]{:S(2)}, u32[]{:S(2)}) async-start(bf16[16,32,360]{2,1,0:T(8,128)(2,1)} %fusion.13), calls=%async_computation.5 | async-start | bytes 786432 | tf_op jit(solution)/shard_map/all_to_all | solution.py:279
  172.1 20.2 %collective-permute-start.10 = (bf16[64,1024]{1,0:T(8,128)(2,1)S(1)}, bf16[64,1024]{1,0:T(8,128)(2,1)S(1)}, u32[]{:S(2)}, u32[]{:S(2)}) collective-permute-start(bf16[64,1024]{1,0:T(8,128)(2,1)S(1)} %get-tuple-element.30), channel_id=1, source_target_pairs={{0,12},{4,0},{8,4},{12,8},{1,13},{5,1},{9,5},{13,9},{2,14},{6,2},{... | collective-permute-start | bytes 393224 | tf_op jit(solution)/shard_map/ppermute | solution.py:35
  177.0 24.2 %collective-permute-start.9 = (bf16[64,1024]{1,0:T(8,128)(2,1)S(1)}, bf16[64,1024]{1,0:T(8,128)(2,1)S(1)}, u32[]{:S(2)}, u32[]{:S(2)}) collective-permute-start(bf16[64,1024]{1,0:T(8,128)(2,1)S(1)} %get-tuple-element.31), channel_id=1, source_target_pairs={{0,8},{4,12},{8,0},{12,4},{1,9},{5,13},{9,1},{13,5},{2,10},{6,14},... | collective-permute-start | bytes 393224 | tf_op jit(solution)/shard_map/ppermute | solution.py:35
  179.2 22.0 %collective-permute-start.8 = (bf16[64,1024]{1,0:T(8,128)(2,1)S(1)}, bf16[64,1024]{1,0:T(8,128)(2,1)S(1)}, u32[]{:S(2)}, u32[]{:S(2)}) collective-permute-start(bf16[64,1024]{1,0:T(8,128)(2,1)S(1)} %get-tuple-element.29), channel_id=1, source_target_pairs={{0,4},{4,8},{8,12},{12,0},{1,5},{5,9},{9,13},{13,1},{2,6},{6,10},{... | collective-permute-start | bytes 393224 | tf_op jit(solution)/shard_map/ppermute | solution.py:35

commit v4 on v3

--- a/solution.py
+++ b/solution.py
@@ -116,10 +116,6 @@
     lane = lax.broadcasted_iota(jnp.int32, (width, 512), 1)
     spread = ((lane % 128 < block) & (source == lane // 128 * block + lane % 128)).astype(bf16)
     means = pair_mean(own // 2, rows, 2)
-    keep = (
-        lax.broadcasted_iota(jnp.int32, (own, rows), 0) + 2
-        == lax.broadcasted_iota(jnp.int32, (own, rows), 1)
-    ).astype(bf16)
     square = 0.0
     for g in range(groups):
         wide = y_ref[g].astype(f32)
@@ -142,8 +138,7 @@
         normed = y_ref[g].astype(f32) * inv
         grad = (inv * (slopes[g] - normed * mean)).astype(bf16)
         grad_ref[g] = grad
-        mine = jnp.dot(keep, grad, preferred_element_type=f32).astype(bf16)
-        placed = jnp.dot(mine, spread, preferred_element_type=f32).astype(bf16)
+        placed = jnp.dot(grad, spread, preferred_element_type=f32).astype(bf16)
         for i in range(4):
             back_ref[4 * g + i, own // 2 :, :] = placed[:, 128 * i : 128 * i + 128]
 
@@ -152,40 +147,45 @@
     groups = conv_out.shape[0]
     shapes = (
         jax.ShapeDtypeStruct(conv_out.shape, bf16),
-        jax.ShapeDtypeStruct((4 * groups, own + own // 2, 128), bf16),
+        jax.ShapeDtypeStruct((4 * groups, conv_out.shape[1] + own // 2, 128), bf16),
     )
     kernel = functools.partial(statistics_kernel, own)
     return local_call(kernel, shapes, [], conv_out, cot)
 
 
-def taps_kernel(taps, back_ref, wide_ref, feature_ref, stage_ref):
+def taps_kernel(taps, back_ref, wide_ref, feature_ref, frame_ref, stage_ref):
     count, rows, lanes = back_ref.shape
-    own = 2 * rows // 3
-    span = stage_ref.shape[0] // count
+    span = frame_ref.shape[1]
+    pooled = rows - span
+    own = 2 * pooled
     width = wide_ref.shape[1]
     block = width // taps
     source = lax.broadcasted_iota(jnp.int32, (lanes, width), 0)
     lane = lax.broadcasted_iota(jnp.int32, (lanes, width), 1)
-    total = jnp.zeros((count * span, width), f32)
+    for b in range(count):
+        frame_ref[b] = back_ref[b, pooled:, :].astype(f32)
+        feature_ref[pl.ds(b * pooled, pooled), :] = back_ref[b, :pooled, :block]
+    total = jnp.zeros((count * own, width), f32)
     for k in range(taps):
-        stage_ref[...] = jnp.zeros_like(stage_ref)
         for b in range(count):
-            stage_ref[pl.ds(b * span + k + 2, own), :] = back_ref[b, own // 2 :, :].astype(f32)
+            at = (b % 4 * 4 + b // 4) * own
+            stage_ref[pl.ds(at, own), :] = frame_ref[b, pl.ds(4 - k, own), :].astype(bf16)
         place = ((source < block) & (lane == source + k * block)).astype(bf16)
-        total = total + jnp.dot(stage_ref[...].astype(bf16), place, preferred_element_type=f32)
+        total = total + jnp.dot(stage_ref[...], place, preferred_element_type=f32)
     wide_ref[...] = total.astype(bf16)
-    for b in range(count):
-        feature_ref[pl.ds(b * (own // 2), own // 2), :] = back_ref[b, : own // 2, :block]
-
-
-def spread_taps(back, taps, block, span):
+
+
+def spread_taps(back, taps, block, own):
     count, rows, lanes = back.shape
     shapes = (
-        jax.ShapeDtypeStruct((count * span, taps * block), bf16),
-        jax.ShapeDtypeStruct((count * (rows // 3), block), bf16),
-    )
-    kernel = functools.partial(taps_kernel, taps)
-    return local_call(kernel, shapes, [pltpu.VMEM((count * span, lanes), f32)], back)
+        jax.ShapeDtypeStruct((count * own, taps * block), bf16),
+        jax.ShapeDtypeStruct((count * own // 2, block), bf16),
+    )
+    scratch = [
+        pltpu.VMEM((count, rows - own // 2, lanes), f32),
+        pltpu.VMEM((count * own, lanes), bf16),
+    ]
+    return local_call(functools.partial(taps_kernel, taps), shapes, scratch, back)
 
 
 def per_device(activations, conv_weight, cotangent):
@@ -197,57 +197,67 @@
     span = rows + 8
     group = 4 * out_width
     lanes = 4 * span
+    step = rows // 2
 
     low = shift(activations[-8:], AXES, 1)
     high = shift(activations[:8], AXES, -1)
 
     own_half = jnp.where(core == 0, conv_weight[:, :, :half], conv_weight[:, :, half:])
-    first = gather_all(own_half, "y")
+    own_half = lax.optimization_barrier(own_half)
+    shards = [own_half] + [turn(own_half, "y", j) for j in (1, 2, 3)]
+    first = jnp.zeros((tap_count, 4, out_width, half), bf16)
+    first = lax.dynamic_update_slice_in_dim(first, shards[0][:, None], y, axis=1)
+    for j in range(1, 4):
+        first = lax.dynamic_update_slice_in_dim(first, shards[j][:, None], (y - j) % 4, axis=1)
+    first = first.reshape(tap_count, group, half)
     second = lax.ppermute(first, "core", [(0, 1), (1, 0)])
-    weights = jnp.where(
-        core == 0,
-        jnp.concatenate([first, second], axis=3),
-        jnp.concatenate([second, first], axis=3),
-    )
-    weights = weights.transpose(1, 0, 2, 3).reshape(tap_count, group, in_width)
 
     block = pooled_block(low, activations, high)
-    blocks = [block] + [turn(block, "zl", j) for j in (1, 2, 3)]
-    gathered = jnp.zeros((5, span, in_width), bf16)
-    for j in range(4):
-        gathered = lax.dynamic_update_index_in_dim(gathered, blocks[j], (zl - j) % 4, 0)
-    flat = gathered.reshape(-1, in_width)
+    gathered = gather_all(block, "zl")
+    flat = jnp.concatenate(
+        [gathered.reshape(lanes, in_width), jnp.zeros((8, in_width), bf16)], axis=0
+    )
+    flat_first = jnp.where(core == 0, flat[:, :half], flat[:, half:])
+    flat_second = jnp.where(core == 0, flat[:, half:], flat[:, :half])
 
     cot, _ = lax.optimization_barrier((cotangent, block))
     before = shift(cot[-1:], SEQ, 1)
     after = shift(cot[:1], SEQ, -1)
-    step = rows // 2
     windows = cot_windows(before, cot, after, 16)
     windows = lax.all_to_all(windows, SUB, 0, 0)
     cot_block = windows.reshape(4, 4, step + 8, out_width).transpose(0, 2, 1, 3)
     cot_block = cot_block.reshape(4, step + 8, group)
 
     conv_acc = jnp.zeros((lanes, group), f32)
-    for k in range(tap_count):
-        conv_acc = conv_acc + lax.dot_general(
-            flat[k : k + lanes], weights[k], (((1,), (1,)), ((), ())),
-            preferred_element_type=f32,
-        )
+    for columns, weight in ((flat_first, first), (flat_second, second)):
+        for k in range(tap_count):
+            conv_acc = conv_acc + lax.dot_general(
+                columns[k : k + lanes], weight[k], (((1,), (1,)), ((), ())),
+                preferred_element_type=f32,
+            )
     conv_out = conv_acc.astype(bf16).reshape(4, span, group)
-    near = gathered[:4].reshape(lanes, in_width)
+    near = gathered[:, 4 : 4 + rows].reshape(4 * rows, in_width)
     ring = [near] + [turn(near, "y", j) for j in (1, 2, 3)]
+    ring = [lax.optimization_barrier(piece.T) for piece in ring]
     conv_out = lax.all_to_all(conv_out, "zl", 0, 0)
     grad, back = statistics(conv_out, cot_block, rows)
     back = lax.all_to_all(back, SUB, 0, 0)
     grad = lax.all_to_all(grad, "zl", 0, 0)
 
     grad_flat = jnp.concatenate([grad.reshape(lanes, group), jnp.zeros((8, group), bf16)], axis=0)
-    running = jnp.zeros((lanes, in_width), f32)
-    for k in range(tap_count):
-        running = running + jnp.dot(
-            grad_flat[4 - k : 4 - k + lanes], weights[k], preferred_element_type=f32
-        )
-    running = running.astype(bf16).reshape(4, span, in_width)
+    sides = []
+    for weight in (first, second):
+        side = jnp.zeros((lanes, half), f32)
+        for k in range(tap_count):
+            side = side + jnp.dot(
+                grad_flat[4 - k : 4 - k + lanes], weight[k], preferred_element_type=f32
+            )
+        sides.append(side.astype(bf16))
+    running = jnp.where(
+        core == 0,
+        jnp.concatenate(sides, axis=1),
+        jnp.concatenate(sides[::-1], axis=1),
+    ).reshape(4, span, in_width)
     own = [
         lax.dynamic_slice(running, ((zl + j) % 4, 0, 0), (1, rows, in_width))[0]
         for j in range(4)
@@ -262,15 +272,14 @@
     inner_first = jnp.mean(slope_first * normed_first, axis=1, keepdims=True)
     input_grad = (inv_first * (slope_first - normed_first * inner_first)).astype(bf16)
 
-    around = jnp.zeros((4, 4, span, in_width), bf16)
+    wide, features = spread_taps(back, tap_count, out_width, rows)
+    wide = wide.reshape(4, 4 * rows, tap_count * out_width)
+    weight_part = 0.0
     for j in range(4):
-        piece = ring[j].reshape(4, 1, span, in_width)
-        around = lax.dynamic_update_slice_in_dim(around, piece, (y - j) % 4, axis=1)
-    wide, features = spread_taps(back, tap_count, out_width, span)
-    weight_part = lax.dot_general(
-        around.reshape(-1, in_width), wide, (((0,), (0,)), ((), ())),
-        preferred_element_type=f32,
-    )
+        weight_part = weight_part + lax.dot_general(
+            ring[j], lax.dynamic_index_in_dim(wide, (y - j) % 4, keepdims=False),
+            (((1,), (0,)), ((), ())), preferred_element_type=f32,
+        )
     halves = weight_part.reshape(16, 2, in_width // 32, tap_count * out_width)
     mine = jnp.where(core == 0, halves[:, 0], halves[:, 1])
     other = jnp.where(core == 0, halves[:, 1], halves[:, 0]).astype(bf16)

time: 206 us -> 191 us (0.927)
  the two profiles are of different devices: /device:TPU:10 before, /device:TPU:1 now
where the time goes in v4:
time: 191 us; the launch traced here: 189 us
  starting transfers between devices  100 us (52%)
  waiting for transfers between devices  43.9 us (23%)
  matrix products  26.1 us (14%)
  local copies, waits for them, and re-layouts  9.72 us (5%)
  Pallas kernels  4.94 us (3%)
  other arithmetic  2.97 us (2%)
    ppermute x9, waiting for transfers between devices, turn(): lax.ppermute(block, axis, [(i, (i + step) % count) for i in range(count)])  35.3 us
    ppermute x9, starting transfers between devices, turn(): lax.ppermute(block, axis, [(i, (i + step) % count) for i in range(count)])  31.4 us
    all_to_all x1, starting transfers between devices, per_device(): total = lax.all_to_all(total, ('zh', 'x'), 0, 0)  18 us
    ppermute x4, starting transfers between devices, shift(): return lax.ppermute(block, axis, pairs)  17.5 us
    dot_general x10, matrix products, per_device(): jnp.dot(grad_flat[4 - k:4 - k + lanes], weight[k], preferred_element_type...  10.4 us
    dot_general x10, matrix products, per_device(): lax.dot_general(columns[k:k + lanes], weight[k], (((1,), (1,)), ((), ()))...  9.83 us
    all_to_all x1, starting transfers between devices, per_device(): back = lax.all_to_all(back, SUB, 0, 0)  7.05 us
    all_to_all x1, starting transfers between devices, per_device(): windows = lax.all_to_all(windows, SUB, 0, 0)  6.71 us
  transfers between devices with their start and end apart: 21, of which 8 were waited for; matrix products, arithmetic and copies ran while one was open for 14% of the time, Pallas kernels for 2%

profile of v4, /device:TPU:1, one launch (start us, length us, event | category | flops | bytes accessed | tf_op | source)
XLA Modules:
  0.0 189.3 jit_solution(7490801226432763997)
XLA Ops:
  1.4 4.0 %collective-permute-start = (bf16[8,1024]{1,0:T(8,128)(2,1)S(1)}, bf16[8,1024]{1,0:T(8,128)(2,1)S(1)}, u32[]{:S(2)}, u32[]{:S(2)}) collective-permute-start(bf16[8,1024]{1,0:T(8,128)(2,1)S(1)} %get-tuple-element.32), channel_id=1, source_target_pairs={{0,1},{1,2},{2,3},{3,4},{4,5},{5,6},{6,7},{7,8},{8,9},{9,10},{10,1... | collective-permute-start | bytes 49160 | tf_op jit(solution)/shard_map/ppermute | solution.py:30
  5.4 8.0 %collective-permute-start.1 = (bf16[8,1024]{1,0:T(8,128)(2,1)S(1)}, bf16[8,1024]{1,0:T(8,128)(2,1)S(1)}, u32[]{:S(2)}, u32[]{:S(2)}) collective-permute-start(bf16[8,1024]{1,0:T(8,128)(2,1)S(1)} %get-tuple-element.31), channel_id=1, source_target_pairs={{1,0},{2,1},{3,2},{4,3},{5,4},{6,5},{7,6},{8,7},{9,8},{10,9},{11,1... | collective-permute-start | bytes 49160 | tf_op jit(solution)/shard_map/ppermute | solution.py:30
  16.7 3.5 %all-to-all-start = ((bf16[4,72,1024]{2,1,0:T(8,128)(2,1)}), bf16[4,72,1024]{2,1,0:T(8,128)(2,1)S(1)}, u32[]{:S(2)}, u32[]{:S(2)}) async-start(bf16[4,72,1024]{2,1,0:T(8,128)(2,1)} %broadcast_in_dim.25), calls=%async_computation | async-start | bytes 1179648 | tf_op jit(solution)/shard_map/all_to_all | solution.py:40
  20.2 1.9 %collective-permute-start.2 = (bf16[5,72,512]{2,1,0:T(8,128)(2,1)S(1)}, bf16[5,72,512]{2,1,0:T(8,128)(2,1)}, u32[]{:S(2)}, u32[]{:S(2)}) collective-permute-start(bf16[5,72,512]{2,1,0:T(8,128)(2,1)S(1)} %slice_select_fusion), channel_id=1, source_target_pairs={{0,1},{1,2},{2,3},{3,0},{4,5},{5,6},{6,7},{7,4},{8,9},{9,10},{10,1... | collective-permute-start | bytes 1105928 | tf_op jit(solution)/shard_map/ppermute | solution.py:35
  22.2 7.8 %collective-permute-start.3 = (bf16[5,72,512]{2,1,0:T(8,128)(2,1)S(1)}, bf16[5,72,512]{2,1,0:T(8,128)(2,1)S(1)}, u32[]{:S(2)}, u32[]{:S(2)}) collective-permute-start(bf16[5,72,512]{2,1,0:T(8,128)(2,1)S(1)} %slice_select_fusion), channel_id=1, source_target_pairs={{0,2},{1,3},{2,0},{3,1},{4,6},{5,7},{6,4},{7,5},{8,10},{9,11},{10,... | collective-permute-start | bytes 1105928 | tf_op jit(solution)/shard_map/ppermute | solution.py:35
  30.0 1.9 %collective-permute-start.4 = (bf16[5,72,512]{2,1,0:T(8,128)(2,1)S(1)}, bf16[5,72,512]{2,1,0:T(8,128)(2,1)S(1)}, u32[]{:S(2)}, u32[]{:S(2)}) collective-permute-start(bf16[5,72,512]{2,1,0:T(8,128)(2,1)S(1)} %slice_select_fusion), channel_id=1, source_target_pairs={{0,3},{1,0},{2,1},{3,2},{4,7},{5,4},{6,5},{7,6},{8,11},{9,8},{10,9... | collective-permute-start | bytes 1105928 | tf_op jit(solution)/shard_map/ppermute | solution.py:35
  32.4 3.6 %collective-permute-start.6 = (bf16[1,72]{1,0:T(2,128)(2,1)S(1)}, bf16[1,72]{1,0:T(2,128)(2,1)S(1)}, u32[]{:S(2)}, u32[]{:S(2)}) collective-permute-start(bf16[1,72]{1,0:T(2,128)(2,1)S(1)} %get-tuple-element.34), channel_id=1, source_target_pairs={{0,16},{16,32},{32,48},{48,64},{64,80},{80,96},{96,112},{112,128},... | collective-permute-start | bytes 440 | tf_op jit(solution)/shard_map/ppermute | solution.py:30
  37.9 3.2 %collective-permute-done.7.after_ref = bf16[1,72]{1,0:T(2,128)(2,1)S(1)} collective-permute-done((bf16[1,72]{1,0:T(2,128)(2,1)S(1)}, bf16[1,72]{1,0:T(2,128)(2,1)S(1)}, u32[]{:S(2)}, u32[]{:S(2)}) %collective-permute-start.7) | collective-permute-done | bytes 176 | tf_op jit(solution)/shard_map/ppermute | solution.py:30
  42.9 1.9 %collective-permute-done.3 = bf16[5,72,512]{2,1,0:T(8,128)(2,1)S(1)} collective-permute-done((bf16[5,72,512]{2,1,0:T(8,128)(2,1)S(1)}, bf16[5,72,512]{2,1,0:T(8,128)(2,1)S(1)}, u32[]{:S(2)}, u32[]{:S(2)}) %collective-permute-start.3) | collective-permute-done | bytes 368672 | tf_op jit(solution)/shard_map/ppermute | solution.py:35
  46.2 2.6 %collective-permute-start.5 = (bf16[5,288,512]{2,1,0:T(8,128)(2,1)S(1)}, bf16[5,288,512]{2,1,0:T(8,128)(2,1)}, u32[]{:S(2)}, u32[]{:S(2)}) collective-permute-start(bf16[5,288,512]{2,1,0:T(8,128)(2,1)S(1)} %bitcast.118), channel_id=1, source_target_pairs={{0,16},{16,0},{1,17},{17,1},{2,18},{18,2},{3,19},{19,3},{4,20},{20... | collective-permute-start | bytes 4423688 | tf_op jit(solution)/shard_map/ppermute | solution.py:213
  49.7 6.7 %all-to-all-start.2 = ((bf16[16,40,72]{2,1,0:T(8,128)(2,1)}), bf16[16,40,72]{2,1,0:T(8,128)(2,1)S(1)}, u32[]{:S(2)}, u32[]{:S(2)}) async-start(bf16[16,40,72]{2,1,0:T(8,128)(2,1)} %shard_map.59), calls=%async_computation.2 | async-start | bytes 327680 | tf_op jit(solution)/shard_map/all_to_all | solution.py:227
  64.4 2.0 %fusion.9 = bf16[288,288]{1,0:T(8,128)(2,1)} fusion(f32[288,288]{1,0:T(8,128)S(1)} %fusion.28, f32[288,288]{1,0:T(8,128)S(1)} %fusion.30, f32[288,288]{1,0:T(8,128)S(1)} %fusion.32, f32[288,288]{1,0:T(8,128)S(1)} %fusion.34, f32[288,288]{1,0:T(8,128)S(1)} %convolution_add_fusion.6, bf16[296,512]{1,0:T(8,128)(2,1)S(1)} %get-tuple-element.30, ...), kind=kOutput, calls=%fused_computation.20 | convolution fusion | flops 85432320 | bytes 2967552 | tf_op jit(solution)/shard_map/dot_general | solution.py:234
  67.1 4.6 %all-to-all-start.1 = ((bf16[4,72,288]{2,1,0:T(8,128)(2,1)}), bf16[4,72,288]{2,1,0:T(8,128)(2,1)S(1)}, u32[]{:S(2)}, u32[]{:S(2)}) async-start(bf16[4,72,288]{2,1,0:T(8,128)(2,1)} %bitcast.19), calls=%async_computation.1 | async-start | bytes 442368 | tf_op jit(solution)/shard_map/all_to_all | solution.py:242
  71.8 4.7 %collective-permute-start.12 = (bf16[256,1024]{1,0:T(8,128)(2,1)S(1)}, bf16[256,1024]{1,0:T(8,128)(2,1)}, u32[]{:S(2)}, u32[]{:S(2)}) collective-permute-start(bf16[256,1024]{1,0:T(8,128)(2,1)S(1)} %bitcast.130), channel_id=1, source_target_pairs={{0,2},{1,3},{2,0},{3,1},{4,6},{5,7},{6,4},{7,5},{8,10},{9,11},{10,... | collective-permute-start | bytes 1572872 | tf_op jit(solution)/shard_map/ppermute | solution.py:35
  76.6 2.2 %collective-permute-start.11 = (bf16[256,1024]{1,0:T(8,128)(2,1)S(1)}, bf16[256,1024]{1,0:T(8,128)(2,1)}, u32[]{:S(2)}, u32[]{:S(2)}) collective-permute-start(bf16[256,1024]{1,0:T(8,128)(2,1)S(1)} %bitcast.131), channel_id=1, source_target_pairs={{0,1},{1,2},{2,3},{3,0},{4,5},{5,6},{6,7},{7,4},{8,9},{9,10},{10,1... | collective-permute-start | bytes 1572872 | tf_op jit(solution)/shard_map/ppermute | solution.py:35
  78.8 4.3 %collective-permute-start.13 = (bf16[256,1024]{1,0:T(8,128)(2,1)S(1)}, bf16[256,1024]{1,0:T(8,128)(2,1)}, u32[]{:S(2)}, u32[]{:S(2)}) collective-permute-start(bf16[256,1024]{1,0:T(8,128)(2,1)S(1)} %bitcast.132), channel_id=1, source_target_pairs={{0,3},{1,0},{2,1},{3,2},{4,7},{5,4},{6,5},{7,6},{8,11},{9,8},{10,9... | collective-permute-start | bytes 1572872 | tf_op jit(solution)/shard_map/ppermute | solution.py:35
  83.3 2.4 %shard_map.60 = (bf16[4,72,288]{2,1,0:T(8,128)(2,1)}, bf16[16,104,128]{2,1,0:T(8,128)(2,1)}) custom-call(bf16[4,72,288]{2,1,0:T(8,128)(2,1)S(1)} %all-to-all-done.1.y_ref, bf16[4,40,288]{2,1,0:T(8,128)(2,1)S(1)} %reshape.77.cot_ref), custom_call_target="tpu_custom_call" | custom-call | tf_op jit(solution)/shard_map/pallas_call | solution.py:45
  85.7 4.5 %all-to-all-start.4 = ((bf16[4,72,288]{2,1,0:T(8,128)(2,1)}), bf16[4,72,288]{2,1,0:T(8,128)(2,1)S(1)}, u32[]{:S(2)}, u32[]{:S(2)}) async-start(bf16[4,72,288]{2,1,0:T(8,128)(2,1)} %get-tuple-element.11), calls=%async_computation.4 | async-start | bytes 442368 | tf_op jit(solution)/shard_map/all_to_all | solution.py:245
  90.4 10.2 %collective-permute-done.11 = bf16[256,1024]{1,0:T(8,128)(2,1)} collective-permute-done((bf16[256,1024]{1,0:T(8,128)(2,1)S(1)}, bf16[256,1024]{1,0:T(8,128)(2,1)}, u32[]{:S(2)}, u32[]{:S(2)}) %collective-permute-start.11) | collective-permute-done | bytes 524320 | tf_op jit(solution)/shard_map/ppermute | solution.py:35
  100.6 7.0 %all-to-all-start.3 = ((bf16[16,104,128]{2,1,0:T(8,128)(2,1)}), bf16[16,104,128]{2,1,0:T(8,128)(2,1)S(1)}, u32[]{:S(2)}, u32[]{:S(2)}) async-start(bf16[16,104,128]{2,1,0:T(8,128)(2,1)} %get-tuple-element.9), calls=%async_computation.3 | async-start | bytes 851968 | tf_op jit(solution)/shard_map/all_to_all | solution.py:244
  107.9 2.1 %fusion.48 = f32[288,512]{1,0:T(8,128)} fusion(bf16[5,288,512]{2,1,0:T(8,128)(2,1)} %collective-permute-done.5, bf16[288,288]{1,0:T(8,128)(2,1)S(1)} %bitcast.107), kind=kOutput, calls=%fused_computation.81 | convolution fusion | flops 84934656 | bytes 1050624 | tf_op jit(solution)/shard_map/dot_general | solution.py:252
  110.0 2.1 %fusion.47 = f32[288,512]{1,0:T(8,128)} fusion(bf16[5,288,512]{2,1,0:T(8,128)(2,1)} %collective-permute-done.5, bf16[288,288]{1,0:T(8,128)(2,1)S(1)} %bitcast.108), kind=kOutput, calls=%fused_computation.80 | convolution fusion | flops 84934656 | bytes 1050624 | tf_op jit(solution)/shard_map/dot_general | solution.py:252
  112.1 2.1 %fusion.49 = f32[288,512]{1,0:T(8,128)} fusion(bf16[288,288]{1,0:T(8,128)(2,1)S(1)} %bitcast.109, bf16[5,288,512]{2,1,0:T(8,128)(2,1)} %collective-permute-done.5), kind=kOutput, calls=%fused_computation.82 | convolution fusion | flops 84934656 | bytes 1050624 | tf_op jit(solution)/shard_map/dot_general | solution.py:252
  115.5 4.4 %all-to-all-done.3.back_ref = bf16[16,104,128]{2,1,0:T(8,128)(2,1)S(1)} async-done(((bf16[16,104,128]{2,1,0:T(8,128)(2,1)}), bf16[16,104,128]{2,1,0:T(8,128)(2,1)S(1)}, u32[]{:S(2)}, u32[]{:S(2)}) %all-to-all-start.3) | async-done | bytes 426016 | tf_op jit(solution)/shard_map/all_to_all | solution.py:244
  124.5 2.6 %add_add_fusion = f32[1024,360]{0,1:T(8,128)} fusion(f32[1024,360]{0,1:T(8,128)S(1)} %fusion.54, f32[1024,360]{0,1:T(8,128)S(1)} %fusion.58, f32[1024,360]{0,1:T(8,128)S(1)} %fusion.56, bf16[1024,256]{0,1:T(8,128)(2,1)} %bitcast.37, bf16[4,256,360]{2,1,0:T(8,128)(2,1)S(1)} %bitcast.105, s32[]{:T(128)S(6)} %select_n.127), kind=kOutput, calls=%fused_computation | convolution fusion | flops 189849600 | bytes 6619140 | tf_op jit(solution)/shard_map/dot_general | solution.py:279
  129.0 4.5 %collective-permute-start.14 = (bf16[16,32,360]{2,1,0:T(8,128)(2,1)S(1)}, bf16[16,32,360]{2,1,0:T(8,128)(2,1)S(1)}, u32[]{:S(2)}, u32[]{:S(2)}) collective-permute-start(bf16[16,32,360]{2,1,0:T(8,128)(2,1)S(1)} %fusion.27), channel_id=1, source_target_pairs={{0,16},{16,0},{1,17},{17,1},{2,18},{18,2},{3,19},{19,3},{4,20},{20... | collective-permute-start | bytes 1105928 | tf_op jit(solution)/shard_map/ppermute | solution.py:286
  137.1 18.0 %all-to-all-start.5 = ((bf16[16,32,360]{2,1,0:T(8,128)(2,1)}), bf16[16,32,360]{2,1,0:T(8,128)(2,1)S(1)}, u32[]{:S(2)}, u32[]{:S(2)}) async-start(bf16[16,32,360]{2,1,0:T(8,128)(2,1)} %fusion.10), calls=%async_computation.5 | async-start | bytes 786432 | tf_op jit(solution)/shard_map/all_to_all | solution.py:288
  155.3 3.0 %collective-permute-start.10 = (bf16[64,1024]{1,0:T(8,128)(2,1)S(1)}, bf16[64,1024]{1,0:T(8,128)(2,1)S(1)}, u32[]{:S(2)}, u32[]{:S(2)}) collective-permute-start(bf16[64,1024]{1,0:T(8,128)(2,1)S(1)} %get-tuple-element.27), channel_id=1, source_target_pairs={{0,12},{4,0},{8,4},{12,8},{1,13},{5,1},{9,5},{13,9},{2,14},{6,2},{... | collective-permute-start | bytes 393224 | tf_op jit(solution)/shard_map/ppermute | solution.py:35
  158.3 2.7 %collective-permute-start.9 = (bf16[64,1024]{1,0:T(8,128)(2,1)S(1)}, bf16[64,1024]{1,0:T(8,128)(2,1)S(1)}, u32[]{:S(2)}, u32[]{:S(2)}) collective-permute-start(bf16[64,1024]{1,0:T(8,128)(2,1)S(1)} %get-tuple-element.28), channel_id=1, source_target_pairs={{0,8},{4,12},{8,0},{12,4},{1,9},{5,13},{9,1},{13,5},{2,10},{6,14},... | collective-permute-start | bytes 393224 | tf_op jit(solution)/shard_map/ppermute | solution.py:35
  161.0 2.8 %collective-permute-start.8 = (bf16[64,1024]{1,0:T(8,128)(2,1)S(1)}, bf16[64,1024]{1,0:T(8,128)(2,1)S(1)}, u32[]{:S(2)}, u32[]{:S(2)}) collective-permute-start(bf16[64,1024]{1,0:T(8,128)(2,1)S(1)} %get-tuple-element.26), channel_id=1, source_target_pairs={{0,4},{4,8},{8,12},{12,0},{1,5},{5,9},{9,13},{13,1},{2,6},{6,10},{... | collective-permute-start | bytes 393224 | tf_op jit(solution)/shard_map/ppermute | solution.py:35
  163.8 11.6 %collective-permute-done.10 = bf16[64,1024]{1,0:T(8,128)(2,1)S(1)} collective-permute-done((bf16[64,1024]{1,0:T(8,128)(2,1)S(1)}, bf16[64,1024]{1,0:T(8,128)(2,1)S(1)}, u32[]{:S(2)}, u32[]{:S(2)}) %collective-permute-start.10) | collective-permute-done | bytes 131104 | tf_op jit(solution)/shard_map/ppermute | solution.py:35
  175.4 10.2 %collective-permute-done.9 = bf16[64,1024]{1,0:T(8,128)(2,1)S(1)} collective-permute-done((bf16[64,1024]{1,0:T(8,128)(2,1)S(1)}, bf16[64,1024]{1,0:T(8,128)(2,1)S(1)}, u32[]{:S(2)}, u32[]{:S(2)}) %collective-permute-start.9) | collective-permute-done | bytes 131104 | tf_op jit(solution)/shard_map/ppermute | solution.py:35
  (90 shorter events, 34.6 us)
Async XLA Ops:
  1.4 12.0 %collective-permute-start = (bf16[8,1024]{1,0:T(8,128)(2,1)S(1)}, bf16[8,1024]{1,0:T(8,128)(2,1)S(1)}, u32[]{:S(2)}, u32[]{:S(2)}) collective-permute-start(bf16[8,1024]{1,0:T(8,128)(2,1)S(1)} %get-tuple-element.32), channel_id=1, source_target_pairs={{0,1},{1,2},{2,3},{3,4},{4,5},{5,6},{6,7},{7,8},{8,9},{9,10},{10,1... | collective-permute-start | bytes 49160 | tf_op jit(solution)/shard_map/ppermute | solution.py:30
  5.4 8.8 %collective-permute-start.1 = (bf16[8,1024]{1,0:T(8,128)(2,1)S(1)}, bf16[8,1024]{1,0:T(8,128)(2,1)S(1)}, u32[]{:S(2)}, u32[]{:S(2)}) collective-permute-start(bf16[8,1024]{1,0:T(8,128)(2,1)S(1)} %get-tuple-element.31), channel_id=1, source_target_pairs={{1,0},{2,1},{3,2},{4,3},{5,4},{6,5},{7,6},{8,7},{9,8},{10,9},{11,1... | collective-permute-start | bytes 49160 | tf_op jit(solution)/shard_map/ppermute | solution.py:30
  14.2 0.9 copy-start
  15.2 5.0 %copy-start.6 = (bf16[5,72,1024]{2,1,0:T(8,128)(2,1)S(1)}, bf16[5,72,1024]{2,1,0:T(8,128)(2,1)}, u32[]{:S(2)}) copy-start(bf16[5,72,1024]{2,1,0:T(8,128)(2,1)} %param.4) | copy-start | bytes 2211844
  16.7 33.0 %all-to-all-start = ((bf16[4,72,1024]{2,1,0:T(8,128)(2,1)}), bf16[4,72,1024]{2,1,0:T(8,128)(2,1)S(1)}, u32[]{:S(2)}, u32[]{:S(2)}) async-start(bf16[4,72,1024]{2,1,0:T(8,128)(2,1)} %broadcast_in_dim.25), calls=%async_computation | async-start | bytes 1179648 | tf_op jit(solution)/shard_map/all_to_all | solution.py:40
  20.2 12.0 %copy-start.9 = (bf16[512,72]{0,1:T(8,128)(2,1)S(1)}, bf16[512,72]{0,1:T(8,128)(2,1)}, u32[]{:S(2)}) copy-start(bf16[512,72]{0,1:T(8,128)(2,1)} %param.5) | copy-start | bytes 221188
  20.2 21.6 %collective-permute-start.2 = (bf16[5,72,512]{2,1,0:T(8,128)(2,1)S(1)}, bf16[5,72,512]{2,1,0:T(8,128)(2,1)}, u32[]{:S(2)}, u32[]{:S(2)}) collective-permute-start(bf16[5,72,512]{2,1,0:T(8,128)(2,1)S(1)} %slice_select_fusion), channel_id=1, source_target_pairs={{0,1},{1,2},{2,3},{3,0},{4,5},{5,6},{6,7},{7,4},{8,9},{9,10},{10,1... | collective-permute-start | bytes 1105928 | tf_op jit(solution)/shard_map/ppermute | solution.py:35
  22.2 22.6 %collective-permute-start.3 = (bf16[5,72,512]{2,1,0:T(8,128)(2,1)S(1)}, bf16[5,72,512]{2,1,0:T(8,128)(2,1)S(1)}, u32[]{:S(2)}, u32[]{:S(2)}) collective-permute-start(bf16[5,72,512]{2,1,0:T(8,128)(2,1)S(1)} %slice_select_fusion), channel_id=1, source_target_pairs={{0,2},{1,3},{2,0},{3,1},{4,6},{5,7},{6,4},{7,5},{8,10},{9,11},{10,... | collective-permute-start | bytes 1105928 | tf_op jit(solution)/shard_map/ppermute | solution.py:35
  30.0 16.1 %collective-permute-start.4 = (bf16[5,72,512]{2,1,0:T(8,128)(2,1)S(1)}, bf16[5,72,512]{2,1,0:T(8,128)(2,1)S(1)}, u32[]{:S(2)}, u32[]{:S(2)}) collective-permute-start(bf16[5,72,512]{2,1,0:T(8,128)(2,1)S(1)} %slice_select_fusion), channel_id=1, source_target_pairs={{0,3},{1,0},{2,1},{3,2},{4,7},{5,4},{6,5},{7,6},{8,11},{9,8},{10,9... | collective-permute-start | bytes 1105928 | tf_op jit(solution)/shard_map/ppermute | solution.py:35
  32.4 5.5 %collective-permute-start.6 = (bf16[1,72]{1,0:T(2,128)(2,1)S(1)}, bf16[1,72]{1,0:T(2,128)(2,1)S(1)}, u32[]{:S(2)}, u32[]{:S(2)}) collective-permute-start(bf16[1,72]{1,0:T(2,128)(2,1)S(1)} %get-tuple-element.34), channel_id=1, source_target_pairs={{0,16},{16,32},{32,48},{48,64},{64,80},{80,96},{96,112},{112,128},... | collective-permute-start | bytes 440 | tf_op jit(solution)/shard_map/ppermute | solution.py:30
  35.9 5.2 %collective-permute-start.7 = (bf16[1,72]{1,0:T(2,128)(2,1)S(1)}, bf16[1,72]{1,0:T(2,128)(2,1)S(1)}, u32[]{:S(2)}, u32[]{:S(2)}) collective-permute-start(bf16[1,72]{1,0:T(2,128)(2,1)S(1)} %get-tuple-element.33), channel_id=1, source_target_pairs={{16,0},{32,16},{48,32},{64,48},{80,64},{96,80},{112,96},{128,112},... | collective-permute-start | bytes 440 | tf_op jit(solution)/shard_map/ppermute | solution.py:30
  46.2 13.0 %collective-permute-start.5 = (bf16[5,288,512]{2,1,0:T(8,128)(2,1)S(1)}, bf16[5,288,512]{2,1,0:T(8,128)(2,1)}, u32[]{:S(2)}, u32[]{:S(2)}) collective-permute-start(bf16[5,288,512]{2,1,0:T(8,128)(2,1)S(1)} %bitcast.118), channel_id=1, source_target_pairs={{0,16},{16,0},{1,17},{17,1},{2,18},{18,2},{3,19},{19,3},{4,20},{20... | collective-permute-start | bytes 4423688 | tf_op jit(solution)/shard_map/ppermute | solution.py:213
  49.7 16.7 %all-to-all-start.2 = ((bf16[16,40,72]{2,1,0:T(8,128)(2,1)}), bf16[16,40,72]{2,1,0:T(8,128)(2,1)S(1)}, u32[]{:S(2)}, u32[]{:S(2)}) async-start(bf16[16,40,72]{2,1,0:T(8,128)(2,1)} %shard_map.59), calls=%async_computation.2 | async-start | bytes 327680 | tf_op jit(solution)/shard_map/all_to_all | solution.py:227
  66.4 0.7 copy-start.7
  67.1 16.0 %copy-start.8 = (bf16[16,40,72]{2,1,0:T(8,128)(2,1)S(1)}, bf16[16,40,72]{2,1,0:T(8,128)(2,1)}, u32[]{:S(2)}) copy-start(bf16[16,40,72]{2,1,0:T(8,128)(2,1)} %copy-done.7) | copy-start | bytes 276484
  67.1 23.1 %copy-start.1 = (bf16[128,1024]{1,0:T(8,128)(2,1)S(1)}, bf16[128,1024]{1,0:T(8,128)(2,1)}, u32[]{:S(2)}) copy-start(bf16[128,1024]{1,0:T(8,128)(2,1)} %own_ref.1) | copy-start | bytes 786436
  67.1 16.2 %all-to-all-start.1 = ((bf16[4,72,288]{2,1,0:T(8,128)(2,1)}), bf16[4,72,288]{2,1,0:T(8,128)(2,1)S(1)}, u32[]{:S(2)}, u32[]{:S(2)}) async-start(bf16[4,72,288]{2,1,0:T(8,128)(2,1)} %bitcast.19), calls=%async_computation.1 | async-start | bytes 442368 | tf_op jit(solution)/shard_map/all_to_all | solution.py:242
  71.8 35.8 %copy-start.2 = (bf16[1,4,72,512]{3,2,1,0:T(8,128)(2,1)S(1)}, bf16[1,4,72,512]{3,2,1,0:T(8,128)(2,1)}, u32[]{:S(2)}) copy-start(bf16[1,4,72,512]{3,2,1,0:T(8,128)(2,1)} %get-tuple-element.24) | copy-start | bytes 884740
  71.8 18.5 %collective-permute-start.12 = (bf16[256,1024]{1,0:T(8,128)(2,1)S(1)}, bf16[256,1024]{1,0:T(8,128)(2,1)}, u32[]{:S(2)}, u32[]{:S(2)}) collective-permute-start(bf16[256,1024]{1,0:T(8,128)(2,1)S(1)} %bitcast.130), channel_id=1, source_target_pairs={{0,2},{1,3},{2,0},{3,1},{4,6},{5,7},{6,4},{7,5},{8,10},{9,11},{10,... | collective-permute-start | bytes 1572872 | tf_op jit(solution)/shard_map/ppermute | solution.py:35
  76.6 24.0 %collective-permute-start.11 = (bf16[256,1024]{1,0:T(8,128)(2,1)S(1)}, bf16[256,1024]{1,0:T(8,128)(2,1)}, u32[]{:S(2)}, u32[]{:S(2)}) collective-permute-start(bf16[256,1024]{1,0:T(8,128)(2,1)S(1)} %bitcast.131), channel_id=1, source_target_pairs={{0,1},{1,2},{2,3},{3,0},{4,5},{5,6},{6,7},{7,4},{8,9},{9,10},{10,1... | collective-permute-start | bytes 1572872 | tf_op jit(solution)/shard_map/ppermute | solution.py:35
  78.8 21.8 %collective-permute-start.13 = (bf16[256,1024]{1,0:T(8,128)(2,1)S(1)}, bf16[256,1024]{1,0:T(8,128)(2,1)}, u32[]{:S(2)}, u32[]{:S(2)}) collective-permute-start(bf16[256,1024]{1,0:T(8,128)(2,1)S(1)} %bitcast.132), channel_id=1, source_target_pairs={{0,3},{1,0},{2,1},{3,2},{4,7},{5,4},{6,5},{7,6},{8,11},{9,8},{10,9... | collective-permute-start | bytes 1572872 | tf_op jit(solution)/shard_map/ppermute | solution.py:35
  85.7 14.9 %all-to-all-start.4 = ((bf16[4,72,288]{2,1,0:T(8,128)(2,1)}), bf16[4,72,288]{2,1,0:T(8,128)(2,1)S(1)}, u32[]{:S(2)}, u32[]{:S(2)}) async-start(bf16[4,72,288]{2,1,0:T(8,128)(2,1)} %get-tuple-element.11), calls=%async_computation.4 | async-start | bytes 442368 | tf_op jit(solution)/shard_map/all_to_all | solution.py:245
  100.6 19.4 %all-to-all-start.3 = ((bf16[16,104,128]{2,1,0:T(8,128)(2,1)}), bf16[16,104,128]{2,1,0:T(8,128)(2,1)S(1)}, u32[]{:S(2)}, u32[]{:S(2)}) async-start(bf16[16,104,128]{2,1,0:T(8,128)(2,1)} %get-tuple-element.9), calls=%async_computation.3 | async-start | bytes 851968 | tf_op jit(solution)/shard_map/all_to_all | solution.py:244
  128.9 5.9 %copy-start.3 = (f32[288,512]{1,0:T(8,128)S(1)}, f32[288,512]{1,0:T(8,128)}, u32[]{:S(2)}) copy-start(f32[288,512]{1,0:T(8,128)} %fusion.48) | copy-start | bytes 1769476
  128.9 5.9 %copy-start.4 = (f32[288,512]{1,0:T(8,128)S(1)}, f32[288,512]{1,0:T(8,128)}, u32[]{:S(2)}) copy-start(f32[288,512]{1,0:T(8,128)} %fusion.47) | copy-start | bytes 1769476
  128.9 5.9 %copy-start.5 = (f32[288,512]{1,0:T(8,128)S(1)}, f32[288,512]{1,0:T(8,128)}, u32[]{:S(2)}) copy-start(f32[288,512]{1,0:T(8,128)} %fusion.49) | copy-start | bytes 1769476
  129.0 7.1 %collective-permute-start.14 = (bf16[16,32,360]{2,1,0:T(8,128)(2,1)S(1)}, bf16[16,32,360]{2,1,0:T(8,128)(2,1)S(1)}, u32[]{:S(2)}, u32[]{:S(2)}) collective-permute-start(bf16[16,32,360]{2,1,0:T(8,128)(2,1)S(1)} %fusion.27), channel_id=1, source_target_pairs={{0,16},{16,0},{1,17},{17,1},{2,18},{18,2},{3,19},{19,3},{4,20},{20... | collective-permute-start | bytes 1105928 | tf_op jit(solution)/shard_map/ppermute | solution.py:286
  137.1 51.4 %all-to-all-start.5 = ((bf16[16,32,360]{2,1,0:T(8,128)(2,1)}), bf16[16,32,360]{2,1,0:T(8,128)(2,1)S(1)}, u32[]{:S(2)}, u32[]{:S(2)}) async-start(bf16[16,32,360]{2,1,0:T(8,128)(2,1)} %fusion.10), calls=%async_computation.5 | async-start | bytes 786432 | tf_op jit(solution)/shard_map/all_to_all | solution.py:288
  155.3 20.1 %collective-permute-start.10 = (bf16[64,1024]{1,0:T(8,128)(2,1)S(1)}, bf16[64,1024]{1,0:T(8,128)(2,1)S(1)}, u32[]{:S(2)}, u32[]{:S(2)}) collective-permute-start(bf16[64,1024]{1,0:T(8,128)(2,1)S(1)} %get-tuple-element.27), channel_id=1, source_target_pairs={{0,12},{4,0},{8,4},{12,8},{1,13},{5,1},{9,5},{13,9},{2,14},{6,2},{... | collective-permute-start | bytes 393224 | tf_op jit(solution)/shard_map/ppermute | solution.py:35
  158.3 27.3 %collective-permute-start.9 = (bf16[64,1024]{1,0:T(8,128)(2,1)S(1)}, bf16[64,1024]{1,0:T(8,128)(2,1)S(1)}, u32[]{:S(2)}, u32[]{:S(2)}) collective-permute-start(bf16[64,1024]{1,0:T(8,128)(2,1)S(1)} %get-tuple-element.28), channel_id=1, source_target_pairs={{0,8},{4,12},{8,0},{12,4},{1,9},{5,13},{9,1},{13,5},{2,10},{6,14},... | collective-permute-start | bytes 393224 | tf_op jit(solution)/shard_map/ppermute | solution.py:35
  161.0 24.7 %collective-permute-start.8 = (bf16[64,1024]{1,0:T(8,128)(2,1)S(1)}, bf16[64,1024]{1,0:T(8,128)(2,1)S(1)}, u32[]{:S(2)}, u32[]{:S(2)}) collective-permute-start(bf16[64,1024]{1,0:T(8,128)(2,1)S(1)} %get-tuple-element.26), channel_id=1, source_target_pairs={{0,4},{4,8},{8,12},{12,0},{1,5},{5,9},{9,13},{13,1},{2,6},{6,10},{... | collective-permute-start | bytes 393224 | tf_op jit(solution)/shard_map/ppermute | solution.py:35

commit v5 on v4

v5 whole, which is shorter than its diff:
```python
import functools

import jax
import jax.numpy as jnp
from jax import lax
from jax.experimental import pallas as pl
from jax.experimental.pallas import tpu as pltpu
from jax.sharding import Mesh, PartitionSpec as P


EPSILON = 1e-06
AXES = ("zh", "x", "core", "zl", "y")
SEQ = ("zh", "x", "core")
SUB = ("zl", "y")
bf16 = jnp.bfloat16
f32 = jnp.float32


def half_erf(tensor):
    return 0.5 * (1.0 + lax.erf(tensor * 0.7071067811865476))


def gelu_slope(tensor, half):
    return half + tensor * jnp.exp(-0.5 * tensor * tensor) * 0.3989422804014327


def shift(block, axis, step):
    count = lax.axis_size(axis)
    pairs = [(i, i + step) for i in range(count) if 0 <= i + step < count]
    return lax.ppermute(block, axis, pairs)


def turn(block, axis, step):
    count = lax.axis_size(axis)
    return lax.ppermute(block, axis, [(i, (i + step) % count) for i in range(count)])


def gather_all(block, axis):
    count = lax.axis_size(axis)
    return lax.all_to_all(jnp.broadcast_to(block, (count, *block.shape)), axis, 0, 0)


def local_call(kernel, shapes, scratch, *args):
    vmem = pl.BlockSpec(memory_space=pltpu.VMEM)
    return pl.pallas_call(
        kernel,
        out_shape=shapes,
        in_specs=[pl.BlockSpec(memory_space=pltpu.SMEM) if a.dtype == jnp.int32 else vmem for a in args],
        out_specs=jax.tree.map(lambda _: vmem, shapes),
        scratch_shapes=scratch,
        compiler_params=pltpu.CompilerParams(vmem_limit_bytes=20 << 20),
    )(*args)


def exact_dot(left, right):
    return jnp.dot(left, right, precision=lax.Precision.HIGHEST, preferred_element_type=f32)


def pair_mean(count, rows, first):
    pair = lax.broadcasted_iota(jnp.int32, (count, rows), 0)
    row = lax.broadcasted_iota(jnp.int32, (count, rows), 1)
    return jnp.where((row - first >= 2 * pair) & (row - first <= 2 * pair + 1), 0.5, 0.0)


def pooled_kernel(low_ref, own_ref, high_ref, out_ref, gelu_ref):
    at = 0
    for ref in (low_ref, own_ref, high_ref):
        count = ref.shape[0]
        wide = ref[...].astype(f32)
        inv = lax.rsqrt(jnp.mean(wide * wide, axis=1, keepdims=True) + EPSILON)
        normed = wide * inv
        gelu_ref[at : at + count, :] = normed * half_erf(normed)
        at += count
    out_ref[...] = exact_dot(pair_mean(at // 2, at, 0), gelu_ref[...]).astype(bf16)


def pooled_block(low, own, high):
    total = low.shape[0] + own.shape[0] + high.shape[0]
    width = own.shape[1]
    return local_call(
        pooled_kernel, jax.ShapeDtypeStruct((total // 2, width), bf16),
        [pltpu.VMEM((total, width), f32)], low, own, high,
    )


def conv_kernel(where_ref, flat_ref, first_ref, second_ref, out_ref, tap_ref):
    lanes = flat_ref.shape[0]
    taps, _, half = first_ref.shape
    core = where_ref[0]
    near = flat_ref[:, pl.ds(pl.multiple_of(core * half, 128), half)]
    far = flat_ref[:, pl.ds(pl.multiple_of((1 - core) * half, 128), half)]
    contract = (((1,), (1,)), ((), ()))
    for k in range(taps):
        tap_ref[k, lanes:, :] = jnp.zeros_like(tap_ref[k, lanes:, :])
        tap_ref[k, :lanes, :] = lax.dot_general(
            near, first_ref[k], contract, preferred_element_type=f32
        ) + lax.dot_general(far, second_ref[k], contract, preferred_element_type=f32)
    total = tap_ref[0, pl.ds(2, lanes), :]
    for k in range(1, taps):
        total = total + tap_ref[k, pl.ds(2 + k, lanes), :]
    out_ref[...] = total.astype(bf16)


def conv_forward(where, flat, first, second):
    taps, group, _ = first.shape
    shape = jax.ShapeDtypeStruct((flat.shape[0], group), bf16)
    scratch = [pltpu.VMEM((taps, flat.shape[0] + 8, group), f32)]
    return local_call(conv_kernel, shape, scratch, where, flat, first, second)


def backward_kernel(rows, where_ref, flat_ref, first_ref, second_ref, *refs):
    out_refs, tap_ref = refs[:4], refs[4]
    taps, _, half = first_ref.shape
    frame = flat_ref.shape[0] // 4
    core, zl = where_ref[0], where_ref[1]
    for side, weight_ref in ((core, first_ref), (1 - core, second_ref)):
        for k in range(taps):
            spread = jnp.dot(flat_ref[...], weight_ref[k], preferred_element_type=f32)
            for f in range(4):
                tap_ref[k, f] = spread[f * frame : (f + 1) * frame]
        for j in range(4):
            f = lax.rem(zl + j, 4)
            total = tap_ref[0, f, pl.ds(10, rows), :]
            for k in range(1, taps):
                total = total + tap_ref[k, f, pl.ds(10 - k, rows), :]
            columns = pl.ds(pl.multiple_of(side * half, 128), half)
            out_refs[j][:, columns] = total.astype(bf16)


def conv_backward(where, flat, first, second, rows):
    taps, _, half = first.shape
    shapes = (jax.ShapeDtypeStruct((rows, 2 * half), bf16),) * 4
    scratch = [pltpu.VMEM((taps, 4, flat.shape[0] // 4, half), f32)]
    kernel = functools.partial(backward_kernel, rows)
    return local_call(kernel, shapes, scratch, where, flat, first, second)


def statistics_kernel(own, y_ref, cot_ref, grad_ref, back_ref):
    groups, _, width = y_ref.shape
    full = groups * width
    pairs = cot_ref.shape[1]
    block = width // 4
    repeat = (
        lax.broadcasted_iota(jnp.int32, (own, pairs), 0) // 2
        == lax.broadcasted_iota(jnp.int32, (own, pairs), 1)
    ).astype(bf16)
    source = lax.broadcasted_iota(jnp.int32, (width, 512), 0)
    lane = lax.broadcasted_iota(jnp.int32, (width, 512), 1)
    spread = ((lane % 128 < block) & (source == lane // 128 * block + lane % 128)).astype(bf16)
    means = pair_mean(pairs, own, 0)
    square = 0.0
    for g in range(groups):
        wide = y_ref[g, :own, :].astype(f32)
        square = square + jnp.sum(wide * wide, axis=1, keepdims=True)
    inv = lax.rsqrt(square / full + EPSILON)
    slopes, inner = [], 0.0
    for g in range(groups):
        normed = y_ref[g, :own, :].astype(f32) * inv
        half = half_erf(normed)
        features = exact_dot(means, normed * half).astype(bf16)
        placed = jnp.dot(features, spread, preferred_element_type=f32).astype(bf16)
        for i in range(4):
            back_ref[4 * g + i, :pairs, :] = placed[:, 128 * i : 128 * i + 128]
        upstream = 0.5 * jnp.dot(repeat, cot_ref[g], preferred_element_type=f32)
        slope = upstream * gelu_slope(normed, half)
        inner = inner + jnp.sum(slope * normed, axis=1, keepdims=True)
        slopes.append(slope)
    mean = inner / full
    for g in range(groups):
        normed = y_ref[g, :own, :].astype(f32) * inv
        grad = (inv * (slopes[g] - normed * mean)).astype(bf16)
        grad_ref[g] = grad
        placed = jnp.dot(grad, spread, preferred_element_type=f32).astype(bf16)
        for i in range(4):
            back_ref[4 * g + i, pairs:, :] = placed[:, 128 * i : 128 * i + 128]


def statistics(conv_out, cot, own):
    groups, _, width = conv_out.shape
    shapes = (
        jax.ShapeDtypeStruct((groups, own, width), bf16),
        jax.ShapeDtypeStruct((4 * groups, own + own // 2, 128), bf16),
    )
    kernel = functools.partial(statistics_kernel, own)
    return local_call(kernel, shapes, [], conv_out, cot)


def weight_kernel(taps, block, where_ref, back_ref, *refs):
    ring_refs, (mine_ref, other_ref, feature_ref, stage_ref, wide_ref, part_ref) = refs[:4], refs[4:]
    count, rows, lanes = back_ref.shape
    pooled = rows // 3
    own = 2 * pooled
    span = wide_ref.shape[1] // 4
    width = wide_ref.shape[2]
    core, y = where_ref[0], where_ref[2]
    source = lax.broadcasted_iota(jnp.int32, (lanes, width), 0)
    lane = lax.broadcasted_iota(jnp.int32, (lanes, width), 1)
    for b in range(count):
        feature_ref[pl.ds(b * pooled, pooled), :] = back_ref[b, :pooled, :block]
    stage_ref[...] = jnp.zeros_like(stage_ref)
    for i in range(4):
        total = jnp.zeros((4 * span, width), f32)
        for k in range(taps):
            for z in range(4):
                stage_ref[pl.ds(z * span + k + 2, own), :] = back_ref[
                    4 * z + i, pooled:, :
                ].astype(f32)
                stage_ref[pl.ds(z * span + k + 1, 1), :] = jnp.zeros((1, lanes), f32)
            place = ((source < block) & (lane == source + k * block)).astype(bf16)
            total = total + jnp.dot(
                stage_ref[...].astype(bf16), place, preferred_element_type=f32
            )
        for z in range(4):
            stage_ref[pl.ds(z * span + taps + 1, own), :] = jnp.zeros((own, lanes), f32)
        wide_ref[i] = total.astype(bf16)
    contract = (((0,), (0,)), ((), ()))
    for j in range(4):
        term = lax.dot_general(
            ring_refs[j][...], wide_ref[lax.rem(y - j + 4, 4)], contract,
            preferred_element_type=f32,
        )
        part_ref[...] = term if j == 0 else part_ref[...] + term
    for c in range(mine_ref.shape[0]):
        step = mine_ref.shape[1]
        near = pl.ds(pl.multiple_of(c * 2 * step + core * step, step), step)
        far = pl.ds(pl.multiple_of(c * 2 * step + (1 - core) * step, step), step)
        mine_ref[c] = part_ref[near, : taps * block]
        other_ref[c] = part_ref[far, : taps * block].astype(bf16)


def weight_partial(where, back, ring, taps, block):
    count, rows, lanes = back.shape
    total, width = ring[0].shape
    lot = (16, width // 32, taps * block)
    wide = (taps * block + 127) // 128 * 128
    shapes = (
        jax.ShapeDtypeStruct(lot, f32),
        jax.ShapeDtypeStruct(lot, bf16),
        jax.ShapeDtypeStruct((count * (rows // 3), block), bf16),
    )
    scratch = [
        pltpu.VMEM((total, lanes), f32),
        pltpu.VMEM((4, total, wide), bf16),
        pltpu.VMEM((width, wide), f32),
    ]
    kernel = functools.partial(weight_kernel, taps, block)
    return local_call(kernel, shapes, scratch, where, back, *ring)


def per_device(activations, conv_weight, cotangent):
    tap_count, out_width, in_width = conv_weight.shape
    core = lax.axis_index("core")
    zl, y = lax.axis_index("zl"), lax.axis_index("y")
    half = in_width // 2
    rows = activations.shape[0] // 2
    span = rows + 8
    group = 4 * out_width
    lanes = 4 * span
    step = rows // 2

    low = shift(activations[-8:], AXES, 1)
    high = shift(activations[:8], AXES, -1)

    own_half = jnp.where(core == 0, conv_weight[:, :, :half], conv_weight[:, :, half:])
    own_half = lax.optimization_barrier(own_half)
    shards = [own_half] + [turn(own_half, "y", j) for j in (1, 2, 3)]
    first = jnp.zeros((tap_count, 4, out_width, half), bf16)
    first = lax.dynamic_update_slice_in_dim(first, shards[0][:, None], y, axis=1)
    for j in range(1, 4):
        first = lax.dynamic_update_slice_in_dim(first, shards[j][:, None], (y - j) % 4, axis=1)
    first = first.reshape(tap_count, group, half)
    second = lax.ppermute(first, "core", [(0, 1), (1, 0)])

    block = pooled_block(low, activations, high)
    gathered = gather_all(block, "zl")
    flat = gathered.reshape(lanes, in_width)
    where = jnp.stack([core, zl, y]).astype(jnp.int32)

    cot, _ = lax.optimization_barrier((cotangent, block))
    cot = lax.all_to_all(cot.reshape(16, step, out_width), SUB, 0, 0)
    cot_block = cot.reshape(4, 4, step, out_width).transpose(0, 2, 1, 3)
    cot_block = cot_block.reshape(4, step, group)

    conv_out = conv_forward(where, flat, first, second).reshape(4, span, group)
    ring = [flat] + [turn(flat, "y", j) for j in (1, 2, 3)]
    conv_out = lax.all_to_all(conv_out, "zl", 0, 0)
    grad, back = statistics(conv_out, cot_block, rows)
    back = lax.all_to_all(back, SUB, 0, 0)
    framed = jnp.concatenate(
        [shift(grad[:, -8:], AXES, 1), grad, shift(grad[:, :8], AXES, -1)], axis=1
    )
    framed = lax.all_to_all(framed, "zl", 0, 0)

    own = conv_backward(where, framed.reshape(-1, group), first, second, rows)
    parts = [own[0]] + [turn(own[j], "zl", j) for j in (1, 2, 3)]
    pooled_grad = sum(part.astype(f32) for part in parts)
    x_float = activations.astype(f32)
    inv_first = lax.rsqrt(jnp.mean(x_float * x_float, axis=1, keepdims=True) + EPSILON)
    normed_first = x_float * inv_first
    slope_first = 0.5 * jnp.repeat(pooled_grad, 2, axis=0)
    slope_first = slope_first * gelu_slope(normed_first, half_erf(normed_first))
    inner_first = jnp.mean(slope_first * normed_first, axis=1, keepdims=True)
    input_grad = (inv_first * (slope_first - normed_first * inner_first)).astype(bf16)

    mine, other, features = weight_partial(where, back, ring, tap_count, out_width)
    other = lax.ppermute(other, "core", [(0, 1), (1, 0)])
    total = (mine + other.astype(f32)).astype(bf16)
    total = lax.all_to_all(total, ("zh", "x"), 0, 0)
    weight_grad = jnp.sum(total.astype(f32), axis=0).reshape(-1, tap_count, out_width)
    return (features, input_grad, weight_grad)


def solution(mesh):
    split = Mesh(mesh.devices.reshape(4, 4, 2, 4, 4), AXES)
    return jax.shard_map(
        per_device,
        mesh=split,
        in_specs=(P(AXES, None), P(None, SUB, None), P(SEQ, SUB)),
        out_specs=(P(SEQ, SUB), P(AXES, None), P(SEQ, None, SUB)),
        check_vma=False,
    )
```

time: 191 us -> 195 us (1.021)
  the two profiles are of different devices: /device:TPU:1 before, /device:TPU:34 now
where the time goes in v5:
time: 195 us; the launch traced here: 193 us
  starting transfers between devices  98.1 us (50%)
  waiting for transfers between devices  51.6 us (26%)
  local copies, waits for them, and re-layouts  21.5 us (11%)
  Pallas kernels  13.7 us (7%)
  other arithmetic  7.47 us (4%)
    ppermute x9, starting transfers between devices, turn(): lax.ppermute(block, axis, [(i, (i + step) % count) for i in range(count)])  32.9 us
    ppermute x9, waiting for transfers between devices, turn(): lax.ppermute(block, axis, [(i, (i + step) % count) for i in range(count)])  29.1 us
    all_to_all x1, starting transfers between devices, per_device(): total = lax.all_to_all(total, ('zh', 'x'), 0, 0)  16.7 us
    ppermute x4, starting transfers between devices, shift(): return lax.ppermute(block, axis, pairs)  13.8 us
    pallas_call x5, Pallas kernels, local_call(): pl.pallas_call(kernel, out_shape=shapes, in_specs=[pl.BlockSpec(memory_sp...  13.7 us
    unnamed x34, local copies, waits for them, and re-layouts  11.7 us
    all_to_all x1, starting transfers between devices, per_device(): cot = lax.all_to_all(cot.reshape(16, step, out_width), SUB, 0, 0)  9.19 us
    all_to_all x1, waiting for transfers between devices, gather_all(): lax.all_to_all(jnp.broadcast_to(block, (count, *block.shape)), axis, 0, 0)  6.86 us
  transfers between devices with their start and end apart: 21, of which 10 were waited for; matrix products, arithmetic and copies ran while one was open for 8% of the time, Pallas kernels for 6%

profile of v5, /device:TPU:34, one launch (start us, length us, event | category | flops | bytes accessed | tf_op | source)
XLA Modules:
  0.0 193.4 jit_solution(16002251252024903043)
XLA Ops:
  1.8 3.5 %collective-permute-start.2 = (bf16[5,72,512]{2,1,0:T(8,128)(2,1)S(1)}, bf16[5,72,512]{2,1,0:T(8,128)(2,1)}, u32[]{:S(2)}, u32[]{:S(2)}) collective-permute-start(bf16[5,72,512]{2,1,0:T(8,128)(2,1)S(1)} %slice_select_fusion), channel_id=1, source_target_pairs={{0,1},{1,2},{2,3},{3,0},{4,5},{5,6},{6,7},{7,4},{8,9},{9,10},{10,1... | collective-permute-start | bytes 1105928 | tf_op jit(solution)/shard_map/ppermute | solution.py:35
  5.3 4.8 %collective-permute-start.3 = (bf16[5,72,512]{2,1,0:T(8,128)(2,1)S(1)}, bf16[5,72,512]{2,1,0:T(8,128)(2,1)S(1)}, u32[]{:S(2)}, u32[]{:S(2)}) collective-permute-start(bf16[5,72,512]{2,1,0:T(8,128)(2,1)S(1)} %slice_select_fusion), channel_id=1, source_target_pairs={{0,2},{1,3},{2,0},{3,1},{4,6},{5,7},{6,4},{7,5},{8,10},{9,11},{10,... | collective-permute-start | bytes 1105928 | tf_op jit(solution)/shard_map/ppermute | solution.py:35
  10.1 3.3 %collective-permute-start.4 = (bf16[5,72,512]{2,1,0:T(8,128)(2,1)S(1)}, bf16[5,72,512]{2,1,0:T(8,128)(2,1)S(1)}, u32[]{:S(2)}, u32[]{:S(2)}) collective-permute-start(bf16[5,72,512]{2,1,0:T(8,128)(2,1)S(1)} %slice_select_fusion), channel_id=1, source_target_pairs={{0,3},{1,0},{2,1},{3,2},{4,7},{5,4},{6,5},{7,6},{8,11},{9,8},{10,9... | collective-permute-start | bytes 1105928 | tf_op jit(solution)/shard_map/ppermute | solution.py:35
  14.2 2.6 %collective-permute-start = (bf16[8,1024]{1,0:T(8,128)(2,1)S(1)}, bf16[8,1024]{1,0:T(8,128)(2,1)S(1)}, u32[]{:S(2)}, u32[]{:S(2)}) collective-permute-start(bf16[8,1024]{1,0:T(8,128)(2,1)S(1)} %get-tuple-element.32), channel_id=1, source_target_pairs={{0,1},{1,2},{2,3},{3,4},{4,5},{5,6},{6,7},{7,8},{8,9},{9,10},{10,1... | collective-permute-start | bytes 49160 | tf_op jit(solution)/shard_map/ppermute | solution.py:30
  16.7 5.4 %collective-permute-start.1 = (bf16[8,1024]{1,0:T(8,128)(2,1)S(1)}, bf16[8,1024]{1,0:T(8,128)(2,1)S(1)}, u32[]{:S(2)}, u32[]{:S(2)}) collective-permute-start(bf16[8,1024]{1,0:T(8,128)(2,1)S(1)} %get-tuple-element.31), channel_id=1, source_target_pairs={{1,0},{2,1},{3,2},{4,3},{5,4},{6,5},{7,6},{8,7},{9,8},{10,9},{11,1... | collective-permute-start | bytes 49160 | tf_op jit(solution)/shard_map/ppermute | solution.py:30
  22.4 3.8 %collective-permute-done.1.high_ref = bf16[8,1024]{1,0:T(8,128)(2,1)S(1)} collective-permute-done((bf16[8,1024]{1,0:T(8,128)(2,1)S(1)}, bf16[8,1024]{1,0:T(8,128)(2,1)S(1)}, u32[]{:S(2)}, u32[]{:S(2)}) %collective-permute-start.1) | collective-permute-done | bytes 16416 | tf_op jit(solution)/shard_map/ppermute | solution.py:30
  27.7 6.0 %all-to-all-start = ((bf16[4,72,1024]{2,1,0:T(8,128)(2,1)}), bf16[4,72,1024]{2,1,0:T(8,128)(2,1)S(1)}, u32[]{:S(2)}, u32[]{:S(2)}) async-start(bf16[4,72,1024]{2,1,0:T(8,128)(2,1)} %broadcast_in_dim.23), calls=%async_computation | async-start | bytes 1179648 | tf_op jit(solution)/shard_map/all_to_all | solution.py:40
  34.8 1.9 collective-permute-start.5
  38.3 6.9 %all-to-all-done = bf16[4,72,1024]{2,1,0:T(8,128)(2,1)S(1)} async-done(((bf16[4,72,1024]{2,1,0:T(8,128)(2,1)}), bf16[4,72,1024]{2,1,0:T(8,128)(2,1)S(1)}, u32[]{:S(2)}, u32[]{:S(2)}) %all-to-all-start) | async-done | bytes 589856 | tf_op jit(solution)/shard_map/all_to_all | solution.py:40
  45.2 9.2 %all-to-all-start.2 = ((bf16[16,32,72]{2,1,0:T(8,128)(2,1)}), bf16[16,32,72]{2,1,0:T(8,128)(2,1)}, u32[]{:S(2)}, u32[]{:S(2)}) async-start(bf16[16,32,72]{2,1,0:T(8,128)(2,1)} %bitcast.37), calls=%async_computation.2 | async-start | bytes 262144 | tf_op jit(solution)/shard_map/all_to_all | solution.py:280
  54.5 2.3 %shard_map.59 = bf16[288,288]{1,0:T(8,128)(2,1)S(1)} custom-call(s32[3]{0:T(128)S(1)} %pad_add_fusion.where_ref, bf16[288,1024]{1,0:T(8,128)(2,1)S(1)} %bitcast.30, bf16[5,288,512]{2,1,0:T(8,128)(2,1)S(1)} %bitcast.28, bf16[5,288,512]{2,1,0:T(8,128)(2,1)S(1)} %collective-permute-done.5.second_ref), custom_call_target="tpu_custom_call" | custom-call | tf_op jit(solution)/shard_map/pallas_call | solution.py:45
  57.4 4.0 %all-to-all-done.2 = bf16[16,32,72]{2,1,0:T(8,128)(2,1)} async-done(((bf16[16,32,72]{2,1,0:T(8,128)(2,1)}), bf16[16,32,72]{2,1,0:T(8,128)(2,1)}, u32[]{:S(2)}, u32[]{:S(2)}) %all-to-all-start.2) | async-done | bytes 73760 | tf_op jit(solution)/shard_map/all_to_all | solution.py:280
  61.4 6.1 %all-to-all-start.1 = ((bf16[4,72,288]{2,1,0:T(8,128)(2,1)}), bf16[4,72,288]{2,1,0:T(8,128)(2,1)}, u32[]{:S(2)}, u32[]{:S(2)}) async-start(bf16[4,72,288]{2,1,0:T(8,128)(2,1)} %bitcast.36), calls=%async_computation.1 | async-start | bytes 442368 | tf_op jit(solution)/shard_map/all_to_all | solution.py:286
  70.8 2.7 %all-to-all-done.1.y_ref = bf16[4,72,288]{2,1,0:T(8,128)(2,1)} async-done(((bf16[4,72,288]{2,1,0:T(8,128)(2,1)}), bf16[4,72,288]{2,1,0:T(8,128)(2,1)}, u32[]{:S(2)}, u32[]{:S(2)}) %all-to-all-start.1) | async-done | bytes 165920 | tf_op jit(solution)/shard_map/all_to_all | solution.py:286
  74.4 2.5 %shard_map.60 = (bf16[4,64,288]{2,1,0:T(8,128)(2,1)S(1)}, bf16[16,96,128]{2,1,0:T(8,128)(2,1)S(1)}) custom-call(bf16[4,72,288]{2,1,0:T(8,128)(2,1)} %all-to-all-done.1.y_ref, bf16[4,32,288]{2,1,0:T(8,128)(2,1)S(1)} %copy-done.11), custom_call_target="tpu_custom_call" | custom-call | tf_op jit(solution)/shard_map/pallas_call | solution.py:45
  78.3 4.7 %all-to-all-start.3 = ((bf16[16,96,128]{2,1,0:T(8,128)(2,1)}), bf16[16,96,128]{2,1,0:T(8,128)(2,1)}, u32[]{:S(2)}, u32[]{:S(2)}) async-start(bf16[16,96,128]{2,1,0:T(8,128)(2,1)} %copy-done.10), calls=%async_computation.3 | async-start | bytes 786432 | tf_op jit(solution)/shard_map/all_to_all | solution.py:288
  83.0 3.4 %collective-permute-start.6 = (bf16[288,1024]{1,0:T(8,128)(2,1)S(1)}, bf16[288,1024]{1,0:T(8,128)(2,1)S(1)}, u32[]{:S(2)}, u32[]{:S(2)}) collective-permute-start(bf16[288,1024]{1,0:T(8,128)(2,1)S(1)} %bitcast.31), channel_id=1, source_target_pairs={{0,1},{1,2},{2,3},{3,0},{4,5},{5,6},{6,7},{7,4},{8,9},{9,10},{10,1... | collective-permute-start | bytes 1769480 | tf_op jit(solution)/shard_map/ppermute | solution.py:35
  86.4 4.6 %collective-permute-start.7 = (bf16[288,1024]{1,0:T(8,128)(2,1)S(1)}, bf16[288,1024]{1,0:T(8,128)(2,1)S(1)}, u32[]{:S(2)}, u32[]{:S(2)}) collective-permute-start(bf16[288,1024]{1,0:T(8,128)(2,1)S(1)} %bitcast.32), channel_id=1, source_target_pairs={{0,2},{1,3},{2,0},{3,1},{4,6},{5,7},{6,4},{7,5},{8,10},{9,11},{10,... | collective-permute-start | bytes 1769480 | tf_op jit(solution)/shard_map/ppermute | solution.py:35
  91.0 3.4 %collective-permute-start.8 = (bf16[288,1024]{1,0:T(8,128)(2,1)S(1)}, bf16[288,1024]{1,0:T(8,128)(2,1)S(1)}, u32[]{:S(2)}, u32[]{:S(2)}) collective-permute-start(bf16[288,1024]{1,0:T(8,128)(2,1)S(1)} %bitcast.33), channel_id=1, source_target_pairs={{0,3},{1,0},{2,1},{3,2},{4,7},{5,4},{6,5},{7,6},{8,11},{9,8},{10,9... | collective-permute-start | bytes 1769480 | tf_op jit(solution)/shard_map/ppermute | solution.py:35
  97.6 3.9 %collective-permute-start.9 = (bf16[4,8,288]{2,1,0:T(8,128)(2,1)}, bf16[4,8,288]{2,1,0:T(8,128)(2,1)}, u32[]{:S(2)}, u32[]{:S(2)}) collective-permute-start(bf16[4,8,288]{2,1,0:T(8,128)(2,1)} %get-tuple-element.33), channel_id=1, source_target_pairs={{0,1},{1,2},{2,3},{3,4},{4,5},{5,6},{6,7},{7,8},{8,9},{9,10},{10,1... | collective-permute-start | bytes 55304 | tf_op jit(solution)/shard_map/ppermute | solution.py:30
  101.6 2.3 %collective-permute-done.6.refs_1_ = bf16[288,1024]{1,0:T(8,128)(2,1)S(1)} collective-permute-done((bf16[288,1024]{1,0:T(8,128)(2,1)S(1)}, bf16[288,1024]{1,0:T(8,128)(2,1)S(1)}, u32[]{:S(2)}, u32[]{:S(2)}) %collective-permute-start.6) | collective-permute-done | bytes 589856 | tf_op jit(solution)/shard_map/ppermute | solution.py:35
  104.7 11.1 %collective-permute-done.7.refs_2_ = bf16[288,1024]{1,0:T(8,128)(2,1)S(1)} collective-permute-done((bf16[288,1024]{1,0:T(8,128)(2,1)S(1)}, bf16[288,1024]{1,0:T(8,128)(2,1)S(1)}, u32[]{:S(2)}, u32[]{:S(2)}) %collective-permute-start.7) | collective-permute-done | bytes 589856 | tf_op jit(solution)/shard_map/ppermute | solution.py:35
  120.7 5.4 %shard_map.61 = (f32[16,32,360]{2,1,0:T(8,128)S(1)}, bf16[16,32,360]{2,1,0:T(8,128)(2,1)}, bf16[512,72]{1,0:T(8,128)(2,1)S(1)}) custom-call(s32[3]{0:T(128)S(1)} %pad_add_fusion.where_ref, bf16[16,96,128]{2,1,0:T(8,128)(2,1)} %all-to-all-done.3.back_ref, bf16[288,1024]{1,0:T(8,128)(2,1)S(1)} %bitcast.34, bf16[288,1024]{1,0:T(8,128)(2,1)S(1)} %copy-done.5, ...), custom_call_target="tpu_custom_call" | custom-call | tf_op jit(solution)/shard_map/pallas_call | solution.py:45
  131.1 5.0 %all-to-all-start.4 = ((bf16[4,80,288]{2,1,0:T(8,128)(2,1)}), bf16[4,80,288]{2,1,0:T(8,128)(2,1)S(1)}, u32[]{:S(2)}, u32[]{:S(2)}) async-start(bf16[4,80,288]{2,1,0:T(8,128)(2,1)} %pad_maximum_fusion), calls=%async_computation.4 | async-start | bytes 491520 | tf_op jit(solution)/shard_map/all_to_all | solution.py:292
  136.1 2.1 %add_convert_fusion = bf16[16,32,360]{2,1,0:T(8,128)(2,1)} fusion(f32[16,32,360]{2,1,0:T(8,128)} %copy-done.3, bf16[16,32,360]{2,1,0:T(8,128)(2,1)} %collective-permute-done.14), kind=kLoop, calls=%fused_computation.1 | loop fusion | flops 552960 | bytes 1474560 | tf_op jit(solution)/shard_map/convert_element_type | solution.py:307
  138.2 5.2 %all-to-all-done.4 = bf16[4,80,288]{2,1,0:T(8,128)(2,1)S(1)} async-done(((bf16[4,80,288]{2,1,0:T(8,128)(2,1)}), bf16[4,80,288]{2,1,0:T(8,128)(2,1)S(1)}, u32[]{:S(2)}, u32[]{:S(2)}) %all-to-all-start.4) | async-done | bytes 184352 | tf_op jit(solution)/shard_map/all_to_all | solution.py:292
  143.4 16.7 %all-to-all-start.5 = ((bf16[16,32,360]{2,1,0:T(8,128)(2,1)}), bf16[16,32,360]{2,1,0:T(8,128)(2,1)}, u32[]{:S(2)}, u32[]{:S(2)}) async-start(bf16[16,32,360]{2,1,0:T(8,128)(2,1)} %add_convert_fusion), calls=%async_computation.5 | async-start | bytes 786432 | tf_op jit(solution)/shard_map/all_to_all | solution.py:308
  160.3 3.0 %shard_map.62 = (bf16[64,1024]{1,0:T(8,128)(2,1)S(1)}, bf16[64,1024]{1,0:T(8,128)(2,1)S(1)}, bf16[64,1024]{1,0:T(8,128)(2,1)S(1)}, bf16[64,1024]{1,0:T(8,128)(2,1)S(1)}) custom-call(s32[3]{0:T(128)S(1)} %pad_add_fusion.where_ref, bf16[320,288]{1,0:T(8,128)(2,1)S(1)} %bitcast.35, bf16[5,288,512]{2,1,0:T(8,128)(2,1)S(1)} %bitcast.29, ...), custom_call_target="tpu_custom_call" | custom-call | tf_op jit(solution)/shard_map/pallas_call | solution.py:45
  163.2 2.2 %collective-permute-start.11 = (bf16[64,1024]{1,0:T(8,128)(2,1)S(1)}, bf16[64,1024]{1,0:T(8,128)(2,1)S(1)}, u32[]{:S(2)}, u32[]{:S(2)}) collective-permute-start(bf16[64,1024]{1,0:T(8,128)(2,1)S(1)} %get-tuple-element.18), channel_id=1, source_target_pairs={{0,4},{4,8},{8,12},{12,0},{1,5},{5,9},{9,13},{13,1},{2,6},{6,10},{... | collective-permute-start | bytes 393224 | tf_op jit(solution)/shard_map/ppermute | solution.py:35
  165.5 5.8 %collective-permute-start.12 = (bf16[64,1024]{1,0:T(8,128)(2,1)S(1)}, bf16[64,1024]{1,0:T(8,128)(2,1)S(1)}, u32[]{:S(2)}, u32[]{:S(2)}) collective-permute-start(bf16[64,1024]{1,0:T(8,128)(2,1)S(1)} %get-tuple-element.19), channel_id=1, source_target_pairs={{0,8},{4,12},{8,0},{12,4},{1,9},{5,13},{9,1},{13,5},{2,10},{6,14},... | collective-permute-start | bytes 393224 | tf_op jit(solution)/shard_map/ppermute | solution.py:35
  173.3 8.9 %collective-permute-done.11 = bf16[64,1024]{1,0:T(8,128)(2,1)S(1)} collective-permute-done((bf16[64,1024]{1,0:T(8,128)(2,1)S(1)}, bf16[64,1024]{1,0:T(8,128)(2,1)S(1)}, u32[]{:S(2)}, u32[]{:S(2)}) %collective-permute-start.11) | collective-permute-done | bytes 131104 | tf_op jit(solution)/shard_map/ppermute | solution.py:35
  182.1 5.3 %collective-permute-done.12 = bf16[64,1024]{1,0:T(8,128)(2,1)S(1)} collective-permute-done((bf16[64,1024]{1,0:T(8,128)(2,1)S(1)}, bf16[64,1024]{1,0:T(8,128)(2,1)S(1)}, u32[]{:S(2)}, u32[]{:S(2)}) %collective-permute-start.12) | collective-permute-done | bytes 131104 | tf_op jit(solution)/shard_map/ppermute | solution.py:35
  (74 shorter events, 34.8 us)
Async XLA Ops:
  0.6 25.5 %copy-start = (bf16[128,1024]{1,0:T(8,128)(2,1)S(1)}, bf16[128,1024]{1,0:T(8,128)(2,1)}, u32[]{:S(2)}) copy-start(bf16[128,1024]{1,0:T(8,128)(2,1)} %own_ref.1) | copy-start | bytes 786436
  1.8 31.8 %collective-permute-start.2 = (bf16[5,72,512]{2,1,0:T(8,128)(2,1)S(1)}, bf16[5,72,512]{2,1,0:T(8,128)(2,1)}, u32[]{:S(2)}, u32[]{:S(2)}) collective-permute-start(bf16[5,72,512]{2,1,0:T(8,128)(2,1)S(1)} %slice_select_fusion), channel_id=1, source_target_pairs={{0,1},{1,2},{2,3},{3,0},{4,5},{5,6},{6,7},{7,4},{8,9},{9,10},{10,1... | collective-permute-start | bytes 1105928 | tf_op jit(solution)/shard_map/ppermute | solution.py:35
  5.3 29.4 %collective-permute-start.3 = (bf16[5,72,512]{2,1,0:T(8,128)(2,1)S(1)}, bf16[5,72,512]{2,1,0:T(8,128)(2,1)S(1)}, u32[]{:S(2)}, u32[]{:S(2)}) collective-permute-start(bf16[5,72,512]{2,1,0:T(8,128)(2,1)S(1)} %slice_select_fusion), channel_id=1, source_target_pairs={{0,2},{1,3},{2,0},{3,1},{4,6},{5,7},{6,4},{7,5},{8,10},{9,11},{10,... | collective-permute-start | bytes 1105928 | tf_op jit(solution)/shard_map/ppermute | solution.py:35
  10.1 24.6 %collective-permute-start.4 = (bf16[5,72,512]{2,1,0:T(8,128)(2,1)S(1)}, bf16[5,72,512]{2,1,0:T(8,128)(2,1)S(1)}, u32[]{:S(2)}, u32[]{:S(2)}) collective-permute-start(bf16[5,72,512]{2,1,0:T(8,128)(2,1)S(1)} %slice_select_fusion), channel_id=1, source_target_pairs={{0,3},{1,0},{2,1},{3,2},{4,7},{5,4},{6,5},{7,6},{8,11},{9,8},{10,9... | collective-permute-start | bytes 1105928 | tf_op jit(solution)/shard_map/ppermute | solution.py:35
  14.2 8.2 %collective-permute-start = (bf16[8,1024]{1,0:T(8,128)(2,1)S(1)}, bf16[8,1024]{1,0:T(8,128)(2,1)S(1)}, u32[]{:S(2)}, u32[]{:S(2)}) collective-permute-start(bf16[8,1024]{1,0:T(8,128)(2,1)S(1)} %get-tuple-element.32), channel_id=1, source_target_pairs={{0,1},{1,2},{2,3},{3,4},{4,5},{5,6},{6,7},{7,8},{8,9},{9,10},{10,1... | collective-permute-start | bytes 49160 | tf_op jit(solution)/shard_map/ppermute | solution.py:30
  16.7 9.4 %collective-permute-start.1 = (bf16[8,1024]{1,0:T(8,128)(2,1)S(1)}, bf16[8,1024]{1,0:T(8,128)(2,1)S(1)}, u32[]{:S(2)}, u32[]{:S(2)}) collective-permute-start(bf16[8,1024]{1,0:T(8,128)(2,1)S(1)} %get-tuple-element.31), channel_id=1, source_target_pairs={{1,0},{2,1},{3,2},{4,3},{5,4},{6,5},{7,6},{8,7},{9,8},{10,9},{11,1... | collective-permute-start | bytes 49160 | tf_op jit(solution)/shard_map/ppermute | solution.py:30
  27.7 17.6 %all-to-all-start = ((bf16[4,72,1024]{2,1,0:T(8,128)(2,1)}), bf16[4,72,1024]{2,1,0:T(8,128)(2,1)S(1)}, u32[]{:S(2)}, u32[]{:S(2)}) async-start(bf16[4,72,1024]{2,1,0:T(8,128)(2,1)} %broadcast_in_dim.23), calls=%async_computation | async-start | bytes 1179648 | tf_op jit(solution)/shard_map/all_to_all | solution.py:40
  34.8 19.7 %collective-permute-start.5 = (bf16[5,288,512]{2,1,0:T(8,128)(2,1)S(1)}, bf16[5,288,512]{2,1,0:T(8,128)(2,1)S(1)}, u32[]{:S(2)}, u32[]{:S(2)}) collective-permute-start(bf16[5,288,512]{2,1,0:T(8,128)(2,1)S(1)} %bitcast.27), channel_id=1, source_target_pairs={{0,16},{16,0},{1,17},{17,1},{2,18},{18,2},{3,19},{19,3},{4,20},{20... | collective-permute-start | bytes 4423688 | tf_op jit(solution)/shard_map/ppermute | solution.py:272
  45.2 16.2 %all-to-all-start.2 = ((bf16[16,32,72]{2,1,0:T(8,128)(2,1)}), bf16[16,32,72]{2,1,0:T(8,128)(2,1)}, u32[]{:S(2)}, u32[]{:S(2)}) async-start(bf16[16,32,72]{2,1,0:T(8,128)(2,1)} %bitcast.37), calls=%async_computation.2 | async-start | bytes 262144 | tf_op jit(solution)/shard_map/all_to_all | solution.py:280
  61.4 12.1 %all-to-all-start.1 = ((bf16[4,72,288]{2,1,0:T(8,128)(2,1)}), bf16[4,72,288]{2,1,0:T(8,128)(2,1)}, u32[]{:S(2)}, u32[]{:S(2)}) async-start(bf16[4,72,288]{2,1,0:T(8,128)(2,1)} %bitcast.36), calls=%async_computation.1 | async-start | bytes 442368 | tf_op jit(solution)/shard_map/all_to_all | solution.py:286
  73.5 0.9 copy-start.11
  78.3 39.2 %all-to-all-start.3 = ((bf16[16,96,128]{2,1,0:T(8,128)(2,1)}), bf16[16,96,128]{2,1,0:T(8,128)(2,1)}, u32[]{:S(2)}, u32[]{:S(2)}) async-start(bf16[16,96,128]{2,1,0:T(8,128)(2,1)} %copy-done.10), calls=%async_computation.3 | async-start | bytes 786432 | tf_op jit(solution)/shard_map/all_to_all | solution.py:288
  83.0 20.9 %collective-permute-start.6 = (bf16[288,1024]{1,0:T(8,128)(2,1)S(1)}, bf16[288,1024]{1,0:T(8,128)(2,1)S(1)}, u32[]{:S(2)}, u32[]{:S(2)}) collective-permute-start(bf16[288,1024]{1,0:T(8,128)(2,1)S(1)} %bitcast.31), channel_id=1, source_target_pairs={{0,1},{1,2},{2,3},{3,0},{4,5},{5,6},{6,7},{7,4},{8,9},{9,10},{10,1... | collective-permute-start | bytes 1769480 | tf_op jit(solution)/shard_map/ppermute | solution.py:35
  86.4 29.5 %collective-permute-start.7 = (bf16[288,1024]{1,0:T(8,128)(2,1)S(1)}, bf16[288,1024]{1,0:T(8,128)(2,1)S(1)}, u32[]{:S(2)}, u32[]{:S(2)}) collective-permute-start(bf16[288,1024]{1,0:T(8,128)(2,1)S(1)} %bitcast.32), channel_id=1, source_target_pairs={{0,2},{1,3},{2,0},{3,1},{4,6},{5,7},{6,4},{7,5},{8,10},{9,11},{10,... | collective-permute-start | bytes 1769480 | tf_op jit(solution)/shard_map/ppermute | solution.py:35
  91.0 25.7 %collective-permute-start.8 = (bf16[288,1024]{1,0:T(8,128)(2,1)S(1)}, bf16[288,1024]{1,0:T(8,128)(2,1)S(1)}, u32[]{:S(2)}, u32[]{:S(2)}) collective-permute-start(bf16[288,1024]{1,0:T(8,128)(2,1)S(1)} %bitcast.33), channel_id=1, source_target_pairs={{0,3},{1,0},{2,1},{3,2},{4,7},{5,4},{6,5},{7,6},{8,11},{9,8},{10,9... | collective-permute-start | bytes 1769480 | tf_op jit(solution)/shard_map/ppermute | solution.py:35
  95.7 33.9 %collective-permute-start.10 = (bf16[4,8,288]{2,1,0:T(8,128)(2,1)}, bf16[4,8,288]{2,1,0:T(8,128)(2,1)}, u32[]{:S(2)}, u32[]{:S(2)}) collective-permute-start(bf16[4,8,288]{2,1,0:T(8,128)(2,1)} %get-tuple-element.34), channel_id=1, source_target_pairs={{1,0},{2,1},{3,2},{4,3},{5,4},{6,5},{7,6},{8,7},{9,8},{10,9},{11,1... | collective-permute-start | bytes 55304 | tf_op jit(solution)/shard_map/ppermute | solution.py:30
  97.6 32.0 %collective-permute-start.9 = (bf16[4,8,288]{2,1,0:T(8,128)(2,1)}, bf16[4,8,288]{2,1,0:T(8,128)(2,1)}, u32[]{:S(2)}, u32[]{:S(2)}) collective-permute-start(bf16[4,8,288]{2,1,0:T(8,128)(2,1)} %get-tuple-element.33), channel_id=1, source_target_pairs={{0,1},{1,2},{2,3},{3,4},{4,5},{5,6},{6,7},{7,8},{8,9},{9,10},{10,1... | collective-permute-start | bytes 55304 | tf_op jit(solution)/shard_map/ppermute | solution.py:30
  115.9 0.8 copy-start.6
  116.7 0.8 copy-start.8
  117.6 1.1 copy-start.5
  118.6 1.1 copy-start.7
  119.7 1.1 copy-start.9
  120.7 8.9 %copy-start.13 = (bf16[4,64,288]{2,1,0:T(8,128)(2,1)S(1)}, bf16[4,64,288]{2,1,0:T(8,128)(2,1)}, u32[]{:S(2)}) copy-start(bf16[4,64,288]{2,1,0:T(8,128)(2,1)} %copy-done.12) | copy-start | bytes 442372
  126.2 0.9 copy-start.3
  127.7 8.4 %collective-permute-start.14 = (bf16[16,32,360]{2,1,0:T(8,128)(2,1)}, bf16[16,32,360]{2,1,0:T(8,128)(2,1)}, u32[]{:S(2)}, u32[]{:S(2)}) collective-permute-start(bf16[16,32,360]{2,1,0:T(8,128)(2,1)} %get-tuple-element.22), channel_id=1, source_target_pairs={{0,16},{16,0},{1,17},{17,1},{2,18},{18,2},{3,19},{19,3},{4,20},{20... | collective-permute-start | bytes 1105928 | tf_op jit(solution)/shard_map/ppermute | solution.py:306
  131.1 29.0 %copy-start.1 = (bf16[128,1024]{1,0:T(8,128)(2,1)S(1)}, bf16[128,1024]{1,0:T(8,128)(2,1)}, u32[]{:S(2)}) copy-start(bf16[128,1024]{1,0:T(8,128)(2,1)} %own_ref.1) | copy-start | bytes 786436
  131.1 12.3 %all-to-all-start.4 = ((bf16[4,80,288]{2,1,0:T(8,128)(2,1)}), bf16[4,80,288]{2,1,0:T(8,128)(2,1)S(1)}, u32[]{:S(2)}, u32[]{:S(2)}) async-start(bf16[4,80,288]{2,1,0:T(8,128)(2,1)} %pad_maximum_fusion), calls=%async_computation.4 | async-start | bytes 491520 | tf_op jit(solution)/shard_map/all_to_all | solution.py:292
  143.4 48.2 %all-to-all-start.5 = ((bf16[16,32,360]{2,1,0:T(8,128)(2,1)}), bf16[16,32,360]{2,1,0:T(8,128)(2,1)}, u32[]{:S(2)}, u32[]{:S(2)}) async-start(bf16[16,32,360]{2,1,0:T(8,128)(2,1)} %add_convert_fusion), calls=%async_computation.5 | async-start | bytes 786432 | tf_op jit(solution)/shard_map/all_to_all | solution.py:308
  163.2 18.9 %collective-permute-start.11 = (bf16[64,1024]{1,0:T(8,128)(2,1)S(1)}, bf16[64,1024]{1,0:T(8,128)(2,1)S(1)}, u32[]{:S(2)}, u32[]{:S(2)}) collective-permute-start(bf16[64,1024]{1,0:T(8,128)(2,1)S(1)} %get-tuple-element.18), channel_id=1, source_target_pairs={{0,4},{4,8},{8,12},{12,0},{1,5},{5,9},{9,13},{13,1},{2,6},{6,10},{... | collective-permute-start | bytes 393224 | tf_op jit(solution)/shard_map/ppermute | solution.py:35
  165.5 21.9 %collective-permute-start.12 = (bf16[64,1024]{1,0:T(8,128)(2,1)S(1)}, bf16[64,1024]{1,0:T(8,128)(2,1)S(1)}, u32[]{:S(2)}, u32[]{:S(2)}) collective-permute-start(bf16[64,1024]{1,0:T(8,128)(2,1)S(1)} %get-tuple-element.19), channel_id=1, source_target_pairs={{0,8},{4,12},{8,0},{12,4},{1,9},{5,13},{9,1},{13,5},{2,10},{6,14},... | collective-permute-start | bytes 393224 | tf_op jit(solution)/shard_map/ppermute | solution.py:35
  171.3 17.5 %collective-permute-start.13 = (bf16[64,1024]{1,0:T(8,128)(2,1)S(1)}, bf16[64,1024]{1,0:T(8,128)(2,1)S(1)}, u32[]{:S(2)}, u32[]{:S(2)}) collective-permute-start(bf16[64,1024]{1,0:T(8,128)(2,1)S(1)} %get-tuple-element.20), channel_id=1, source_target_pairs={{0,12},{4,0},{8,4},{12,8},{1,13},{5,1},{9,5},{13,9},{2,14},{6,2},{... | collective-permute-start | bytes 393224 | tf_op jit(solution)/shard_map/ppermute | solution.py:35
  189.1 1.8 copy-start.15
  (5 other events, 3.6 us)

commit v6 on v5

--- a/solution.py
+++ b/solution.py
@@ -40,15 +40,17 @@
     return lax.all_to_all(jnp.broadcast_to(block, (count, *block.shape)), axis, 0, 0)
 
 
-def local_call(kernel, shapes, scratch, *args):
+def local_call(kernel, shapes, scratch, *args, limit=12):
     vmem = pl.BlockSpec(memory_space=pltpu.VMEM)
     return pl.pallas_call(
         kernel,
         out_shape=shapes,
-        in_specs=[pl.BlockSpec(memory_space=pltpu.SMEM) if a.dtype == jnp.int32 else vmem for a in args],
+        in_specs=[
+            pl.BlockSpec(memory_space=pltpu.SMEM) if a.dtype == jnp.int32 else vmem for a in args
+        ],
         out_specs=jax.tree.map(lambda _: vmem, shapes),
         scratch_shapes=scratch,
-        compiler_params=pltpu.CompilerParams(vmem_limit_bytes=20 << 20),
+        compiler_params=pltpu.CompilerParams(vmem_limit_bytes=limit << 20),
     )(*args)
 
 
@@ -83,10 +85,14 @@
     )
 
 
-def conv_kernel(where_ref, flat_ref, first_ref, second_ref, out_ref, tap_ref):
+def conv_kernel(where_ref, flat_ref, first_ref, second_ref, *refs):
+    cot_refs, out_ref, tap_ref = refs[:4], refs[4], refs[5]
     lanes = flat_ref.shape[0]
-    taps, _, half = first_ref.shape
-    core = where_ref[0]
+    taps, group, half = first_ref.shape
+    core, y = where_ref[0], where_ref[2]
+    span = lanes // 4
+    own = span - 8
+    step, block = cot_refs[0].shape[1:]
     near = flat_ref[:, pl.ds(pl.multiple_of(core * half, 128), half)]
     far = flat_ref[:, pl.ds(pl.multiple_of((1 - core) * half, 128), half)]
     contract = (((1,), (1,)), ((), ()))
@@ -95,17 +101,26 @@
         tap_ref[k, :lanes, :] = lax.dot_general(
             near, first_ref[k], contract, preferred_element_type=f32
         ) + lax.dot_general(far, second_ref[k], contract, preferred_element_type=f32)
-    total = tap_ref[0, pl.ds(2, lanes), :]
-    for k in range(1, taps):
-        total = total + tap_ref[k, pl.ds(2 + k, lanes), :]
-    out_ref[...] = total.astype(bf16)
-
-
-def conv_forward(where, flat, first, second):
+    source = lax.broadcasted_iota(jnp.int32, (block, group), 0)
+    lane = lax.broadcasted_iota(jnp.int32, (block, group), 1)
+    for f in range(4):
+        total = tap_ref[0, pl.ds(f * span + 2, own), :]
+        for k in range(1, taps):
+            total = total + tap_ref[k, pl.ds(f * span + 2 + k, own), :]
+        out_ref[f, :own, :] = total.astype(bf16)
+        placed = jnp.zeros((step, group), f32)
+        for j in range(4):
+            place = (lane == source + lax.rem(y - j + 4, 4) * block).astype(bf16)
+            placed = placed + jnp.dot(cot_refs[j][f], place, preferred_element_type=f32)
+        out_ref[f, own:, :] = placed.astype(bf16)
+
+
+def conv_forward(where, flat, first, second, cots):
     taps, group, _ = first.shape
-    shape = jax.ShapeDtypeStruct((flat.shape[0], group), bf16)
+    span = flat.shape[0] // 4
+    shape = jax.ShapeDtypeStruct((4, span - 8 + cots[0].shape[1], group), bf16)
     scratch = [pltpu.VMEM((taps, flat.shape[0] + 8, group), f32)]
-    return local_call(conv_kernel, shape, scratch, where, flat, first, second)
+    return local_call(conv_kernel, shape, scratch, where, flat, first, second, *cots)
 
 
 def backward_kernel(rows, where_ref, flat_ref, first_ref, second_ref, *refs):
@@ -132,13 +147,13 @@
     shapes = (jax.ShapeDtypeStruct((rows, 2 * half), bf16),) * 4
     scratch = [pltpu.VMEM((taps, 4, flat.shape[0] // 4, half), f32)]
     kernel = functools.partial(backward_kernel, rows)
-    return local_call(kernel, shapes, scratch, where, flat, first, second)
-
-
-def statistics_kernel(own, y_ref, cot_ref, grad_ref, back_ref):
+    return local_call(kernel, shapes, scratch, where, flat, first, second, limit=16)
+
+
+def statistics_kernel(own, y_ref, grad_ref, back_ref, head_ref, tail_ref):
     groups, _, width = y_ref.shape
     full = groups * width
-    pairs = cot_ref.shape[1]
+    pairs = own // 2
     block = width // 4
     repeat = (
         lax.broadcasted_iota(jnp.int32, (own, pairs), 0) // 2
@@ -161,7 +176,7 @@
         placed = jnp.dot(features, spread, preferred_element_type=f32).astype(bf16)
         for i in range(4):
             back_ref[4 * g + i, :pairs, :] = placed[:, 128 * i : 128 * i + 128]
-        upstream = 0.5 * jnp.dot(repeat, cot_ref[g], preferred_element_type=f32)
+        upstream = 0.5 * jnp.dot(repeat, y_ref[g, own:, :], preferred_element_type=f32)
         slope = upstream * gelu_slope(normed, half)
         inner = inner + jnp.sum(slope * normed, axis=1, keepdims=True)
         slopes.append(slope)
@@ -170,23 +185,47 @@
         normed = y_ref[g, :own, :].astype(f32) * inv
         grad = (inv * (slopes[g] - normed * mean)).astype(bf16)
         grad_ref[g] = grad
+        head_ref[g] = grad_ref[g, :8, :]
+        tail_ref[g] = grad_ref[g, own - 8 :, :]
         placed = jnp.dot(grad, spread, preferred_element_type=f32).astype(bf16)
         for i in range(4):
             back_ref[4 * g + i, pairs:, :] = placed[:, 128 * i : 128 * i + 128]
 
 
-def statistics(conv_out, cot, own):
+def statistics(conv_out, own):
     groups, _, width = conv_out.shape
     shapes = (
         jax.ShapeDtypeStruct((groups, own, width), bf16),
         jax.ShapeDtypeStruct((4 * groups, own + own // 2, 128), bf16),
+        jax.ShapeDtypeStruct((groups, 8, width), bf16),
+        jax.ShapeDtypeStruct((groups, 8, width), bf16),
     )
     kernel = functools.partial(statistics_kernel, own)
-    return local_call(kernel, shapes, [], conv_out, cot)
+    return local_call(kernel, shapes, [], conv_out)
+
+
+def input_kernel(act_ref, *refs):
+    part_refs, out_ref = refs[:4], refs[4]
+    rows = act_ref.shape[0]
+    pooled_grad = sum(ref[...].astype(f32) for ref in part_refs)
+    pair = lax.broadcasted_iota(jnp.int32, (rows, rows // 2), 1)
+    row = lax.broadcasted_iota(jnp.int32, (rows, rows // 2), 0)
+    upstream = exact_dot(jnp.where(row // 2 == pair, 0.5, 0.0), pooled_grad)
+    wide = act_ref[...].astype(f32)
+    inv = lax.rsqrt(jnp.mean(wide * wide, axis=1, keepdims=True) + EPSILON)
+    normed = wide * inv
+    slope = upstream * gelu_slope(normed, half_erf(normed))
+    inner = jnp.mean(slope * normed, axis=1, keepdims=True)
+    out_ref[...] = (inv * (slope - normed * inner)).astype(bf16)
+
+
+def input_gradient(activations, parts):
+    shape = jax.ShapeDtypeStruct(activations.shape, bf16)
+    return local_call(input_kernel, shape, [], activations, *parts)
 
 
 def weight_kernel(taps, block, where_ref, back_ref, *refs):
-    ring_refs, (mine_ref, other_ref, feature_ref, stage_ref, wide_ref, part_ref) = refs[:4], refs[4:]
+    ring_refs, (mine_ref, other_ref, feature_ref, stage_ref, wide_ref, part_ref) = refs[:5], refs[5:]
     count, rows, lanes = back_ref.shape
     pooled = rows // 3
     own = 2 * pooled
@@ -214,12 +253,14 @@
             stage_ref[pl.ds(z * span + taps + 1, own), :] = jnp.zeros((own, lanes), f32)
         wide_ref[i] = total.astype(bf16)
     contract = (((0,), (0,)), ((), ()))
-    for j in range(4):
+    middle = 2 * span
+    pieces = ((0, slice(None)), (3, slice(None)), (1, slice(None)), (2, slice(0, middle)), (2, slice(middle, None)))
+    for ref, (turns, some) in zip(ring_refs, pieces, strict=True):
         term = lax.dot_general(
-            ring_refs[j][...], wide_ref[lax.rem(y - j + 4, 4)], contract,
+            ref[...], wide_ref[lax.rem(y + turns, 4), some], contract,
             preferred_element_type=f32,
         )
-        part_ref[...] = term if j == 0 else part_ref[...] + term
+        part_ref[...] = term if ref is ring_refs[0] else part_ref[...] + term
     for c in range(mine_ref.shape[0]):
         step = mine_ref.shape[1]
         near = pl.ds(pl.multiple_of(c * 2 * step + core * step, step), step)
@@ -244,7 +285,7 @@
         pltpu.VMEM((width, wide), f32),
     ]
     kernel = functools.partial(weight_kernel, taps, block)
-    return local_call(kernel, shapes, scratch, where, back, *ring)
+    return local_call(kernel, shapes, scratch, where, back, *ring, limit=16)
 
 
 def per_device(activations, conv_weight, cotangent):
@@ -277,32 +318,28 @@
     where = jnp.stack([core, zl, y]).astype(jnp.int32)
 
     cot, _ = lax.optimization_barrier((cotangent, block))
-    cot = lax.all_to_all(cot.reshape(16, step, out_width), SUB, 0, 0)
-    cot_block = cot.reshape(4, 4, step, out_width).transpose(0, 2, 1, 3)
-    cot_block = cot_block.reshape(4, step, group)
-
-    conv_out = conv_forward(where, flat, first, second).reshape(4, span, group)
-    ring = [flat] + [turn(flat, "y", j) for j in (1, 2, 3)]
+    cot = cot.reshape(4, 4, step, out_width)
+    cots = [lax.dynamic_index_in_dim(cot, (y + j) % 4, 1, keepdims=False) for j in range(4)]
+    cots = cots[:1] + [turn(cots[j], "y", j) for j in (1, 2, 3)]
+
+    conv_out = conv_forward(where, flat, first, second, cots)
+    up, down = turn(flat, "y", 1), turn(flat, "y", -1)
+    far = [turn(up[: 2 * span], "y", 1), turn(down[2 * span :], "y", -1)]
     conv_out = lax.all_to_all(conv_out, "zl", 0, 0)
-    grad, back = statistics(conv_out, cot_block, rows)
+    grad, back, head, tail = statistics(conv_out, rows)
     back = lax.all_to_all(back, SUB, 0, 0)
-    framed = jnp.concatenate(
-        [shift(grad[:, -8:], AXES, 1), grad, shift(grad[:, :8], AXES, -1)], axis=1
-    )
+    tail, head = shift(tail, AXES, 1), shift(head, AXES, -1)
+    framed = jnp.concatenate([tail, grad, head], axis=1)
     framed = lax.all_to_all(framed, "zl", 0, 0)
 
     own = conv_backward(where, framed.reshape(-1, group), first, second, rows)
-    parts = [own[0]] + [turn(own[j], "zl", j) for j in (1, 2, 3)]
-    pooled_grad = sum(part.astype(f32) for part in parts)
-    x_float = activations.astype(f32)
-    inv_first = lax.rsqrt(jnp.mean(x_float * x_float, axis=1, keepdims=True) + EPSILON)
-    normed_first = x_float * inv_first
-    slope_first = 0.5 * jnp.repeat(pooled_grad, 2, axis=0)
-    slope_first = slope_first * gelu_slope(normed_first, half_erf(normed_first))
-    inner_first = jnp.mean(slope_first * normed_first, axis=1, keepdims=True)
-    input_grad = (inv_first * (slope_first - normed_first * inner_first)).astype(bf16)
-
-    mine, other, features = weight_partial(where, back, ring, tap_count, out_width)
+    parts = [own[0], turn(own[2], "zl", 2)]
+    parts = parts + [turn(own[1], "zl", 1), turn(own[3], "zl", 3)]
+    input_grad = input_gradient(activations, parts)
+
+    mine, other, features = weight_partial(
+        where, back, [flat, up, down, *far], tap_count, out_width
+    )
     other = lax.ppermute(other, "core", [(0, 1), (1, 0)])
     total = (mine + other.astype(f32)).astype(bf16)
     total = lax.all_to_all(total, ("zh", "x"), 0, 0)

time: 195 us -> 198 us (1.015)
  the two profiles are of different devices: /device:TPU:34 before, /device:TPU:35 now
where the time goes in v6:
time: 198 us; the launch traced here: 196 us
  starting transfers between devices  96.1 us (49%)
  waiting for transfers between devices  44.5 us (22%)
  local copies, waits for them, and re-layouts  23.8 us (12%)
  Pallas kernels  14.6 us (7%)
  blocking collectives  10.5 us (5%)
  other arithmetic  5.89 us (3%)
    ppermute x13, starting transfers between devices, turn(): lax.ppermute(block, axis, [(i, (i + step) % count) for i in range(count)])  38.8 us
    ppermute x13, waiting for transfers between devices, turn(): lax.ppermute(block, axis, [(i, (i + step) % count) for i in range(count)])  33.4 us
    unnamed x52, local copies, waits for them, and re-layouts  16.7 us
    all_to_all x1, starting transfers between devices, per_device(): total = lax.all_to_all(total, ('zh', 'x'), 0, 0)  15.1 us
    pallas_call x6, Pallas kernels, local_call(): pl.pallas_call(kernel, out_shape=shapes, in_specs=[pl.BlockSpec(memory_sp...  14.6 us
    ppermute x4, starting transfers between devices, shift(): return lax.ppermute(block, axis, pairs)  12.8 us
    all_to_all x1, blocking collectives, per_device(): conv_out = lax.all_to_all(conv_out, 'zl', 0, 0)  10.5 us
    all_to_all x1, starting transfers between devices, gather_all(): lax.all_to_all(jnp.broadcast_to(block, (count, *block.shape)), axis, 0, 0)  9.67 us
  transfers between devices with their start and end apart: 23, of which 9 were waited for; matrix products, arithmetic and copies ran while one was open for 6% of the time, Pallas kernels for 5%

profile of v6, /device:TPU:35, one launch (start us, length us, event | category | flops | bytes accessed | tf_op | source)
XLA Modules:
  0.0 196.5 jit_solution(5405545206972995285)
XLA Ops:
  1.8 4.6 %collective-permute-start.4 = (bf16[5,72,512]{2,1,0:T(8,128)(2,1)S(1)}, bf16[5,72,512]{2,1,0:T(8,128)(2,1)S(1)}, u32[]{:S(2)}, u32[]{:S(2)}) collective-permute-start(bf16[5,72,512]{2,1,0:T(8,128)(2,1)S(1)} %slice_select_fusion), channel_id=1, source_target_pairs={{0,3},{1,0},{2,1},{3,2},{4,7},{5,4},{6,5},{7,6},{8,11},{9,8},{10,9... | collective-permute-start | bytes 1105928 | tf_op jit(solution)/shard_map/ppermute | solution.py:35
  6.5 2.3 %collective-permute-start.3 = (bf16[5,72,512]{2,1,0:T(8,128)(2,1)S(1)}, bf16[5,72,512]{2,1,0:T(8,128)(2,1)}, u32[]{:S(2)}, u32[]{:S(2)}) collective-permute-start(bf16[5,72,512]{2,1,0:T(8,128)(2,1)S(1)} %slice_select_fusion), channel_id=1, source_target_pairs={{0,2},{1,3},{2,0},{3,1},{4,6},{5,7},{6,4},{7,5},{8,10},{9,11},{10,... | collective-permute-start | bytes 1105928 | tf_op jit(solution)/shard_map/ppermute | solution.py:35
  8.8 2.6 %collective-permute-start.2 = (bf16[5,72,512]{2,1,0:T(8,128)(2,1)S(1)}, bf16[5,72,512]{2,1,0:T(8,128)(2,1)}, u32[]{:S(2)}, u32[]{:S(2)}) collective-permute-start(bf16[5,72,512]{2,1,0:T(8,128)(2,1)S(1)} %slice_select_fusion), channel_id=1, source_target_pairs={{0,1},{1,2},{2,3},{3,0},{4,5},{5,6},{6,7},{7,4},{8,9},{9,10},{10,1... | collective-permute-start | bytes 1105928 | tf_op jit(solution)/shard_map/ppermute | solution.py:35
  12.1 3.4 %collective-permute-start.1 = (bf16[8,1024]{1,0:T(8,128)(2,1)S(1)}, bf16[8,1024]{1,0:T(8,128)(2,1)S(1)}, u32[]{:S(2)}, u32[]{:S(2)}) collective-permute-start(bf16[8,1024]{1,0:T(8,128)(2,1)S(1)} %get-tuple-element.33), channel_id=1, source_target_pairs={{1,0},{2,1},{3,2},{4,3},{5,4},{6,5},{7,6},{8,7},{9,8},{10,9},{11,1... | collective-permute-start | bytes 49160 | tf_op jit(solution)/shard_map/ppermute | solution.py:30
  15.5 2.0 %collective-permute-start = (bf16[8,1024]{1,0:T(8,128)(2,1)S(1)}, bf16[8,1024]{1,0:T(8,128)(2,1)S(1)}, u32[]{:S(2)}, u32[]{:S(2)}) collective-permute-start(bf16[8,1024]{1,0:T(8,128)(2,1)S(1)} %get-tuple-element.34), channel_id=1, source_target_pairs={{0,1},{1,2},{2,3},{3,4},{4,5},{5,6},{6,7},{7,8},{8,9},{9,10},{10,1... | collective-permute-start | bytes 49160 | tf_op jit(solution)/shard_map/ppermute | solution.py:30
  17.8 4.0 %collective-permute-done.1.high_ref = bf16[8,1024]{1,0:T(8,128)(2,1)S(1)} collective-permute-done((bf16[8,1024]{1,0:T(8,128)(2,1)S(1)}, bf16[8,1024]{1,0:T(8,128)(2,1)S(1)}, u32[]{:S(2)}, u32[]{:S(2)}) %collective-permute-start.1) | collective-permute-done | bytes 16416 | tf_op jit(solution)/shard_map/ppermute | solution.py:30
  21.8 2.2 %collective-permute-done.low_ref = bf16[8,1024]{1,0:T(8,128)(2,1)S(1)} collective-permute-done((bf16[8,1024]{1,0:T(8,128)(2,1)S(1)}, bf16[8,1024]{1,0:T(8,128)(2,1)S(1)}, u32[]{:S(2)}, u32[]{:S(2)}) %collective-permute-start) | collective-permute-done | bytes 16416 | tf_op jit(solution)/shard_map/ppermute | solution.py:30
  25.5 9.7 %all-to-all-start = ((bf16[4,72,1024]{2,1,0:T(8,128)(2,1)}), bf16[4,72,1024]{2,1,0:T(8,128)(2,1)S(1)}, u32[]{:S(2)}, u32[]{:S(2)}) async-start(bf16[4,72,1024]{2,1,0:T(8,128)(2,1)} %broadcast_in_dim.18), calls=%async_computation | async-start | bytes 1179648 | tf_op jit(solution)/shard_map/all_to_all | solution.py:40
  37.3 2.1 %collective-permute-start.5 = (bf16[5,288,512]{2,1,0:T(8,128)(2,1)S(1)}, bf16[5,288,512]{2,1,0:T(8,128)(2,1)S(1)}, u32[]{:S(2)}, u32[]{:S(2)}) collective-permute-start(bf16[5,288,512]{2,1,0:T(8,128)(2,1)S(1)} %bitcast.31), channel_id=1, source_target_pairs={{0,16},{16,0},{1,17},{17,1},{2,18},{18,2},{3,19},{19,3},{4,20},{20... | collective-permute-start | bytes 4423688 | tf_op jit(solution)/shard_map/ppermute | solution.py:313
  42.5 3.5 %collective-permute-start.8 = (bf16[4,32,72]{2,1,0:T(8,128)(2,1)S(1)}, bf16[4,32,72]{2,1,0:T(8,128)(2,1)S(1)}, u32[]{:S(2)}, u32[]{:S(2)}) collective-permute-start(bf16[4,32,72]{2,1,0:T(8,128)(2,1)S(1)} %get-tuple-element.35), channel_id=1, source_target_pairs={{0,3},{1,0},{2,1},{3,2},{4,7},{5,4},{6,5},{7,6},{8,11},{9,8},{10,9... | collective-permute-start | bytes 55304 | tf_op jit(solution)/shard_map/ppermute | solution.py:35
  46.1 2.3 %collective-permute-start.7 = (bf16[4,32,72]{2,1,0:T(8,128)(2,1)S(1)}, bf16[4,32,72]{2,1,0:T(8,128)(2,1)S(1)}, u32[]{:S(2)}, u32[]{:S(2)}) collective-permute-start(bf16[4,32,72]{2,1,0:T(8,128)(2,1)S(1)} %get-tuple-element.36), channel_id=1, source_target_pairs={{0,2},{1,3},{2,0},{3,1},{4,6},{5,7},{6,4},{7,5},{8,10},{9,11},{10,... | collective-permute-start | bytes 55304 | tf_op jit(solution)/shard_map/ppermute | solution.py:35
  48.3 2.4 %collective-permute-start.6 = (bf16[4,32,72]{2,1,0:T(8,128)(2,1)S(1)}, bf16[4,32,72]{2,1,0:T(8,128)(2,1)S(1)}, u32[]{:S(2)}, u32[]{:S(2)}) collective-permute-start(bf16[4,32,72]{2,1,0:T(8,128)(2,1)S(1)} %get-tuple-element.37), channel_id=1, source_target_pairs={{0,1},{1,2},{2,3},{3,0},{4,5},{5,6},{6,7},{7,4},{8,9},{9,10},{10,1... | collective-permute-start | bytes 55304 | tf_op jit(solution)/shard_map/ppermute | solution.py:35
  57.8 2.5 %shard_map.59 = bf16[4,96,288]{2,1,0:T(8,128)(2,1)S(1)} custom-call(s32[3]{0:T(128)S(1)} %pad_add_fusion.where_ref, bf16[288,1024]{1,0:T(8,128)(2,1)S(1)} %bitcast.34, bf16[5,288,512]{2,1,0:T(8,128)(2,1)S(1)} %bitcast.32, bf16[5,288,512]{2,1,0:T(8,128)(2,1)S(1)} %collective-permute-done.5.second_ref, bf16[4,32,72]{2,1,0:T(8,128)(2,1)S(1)} %copy-done.14, ...), custom_call_target="tpu_custom_call" | custom-call | tf_op jit(solution)/shard_map/pallas_call | solution.py:45
  60.4 10.5 %all_to_all.25.y_ref = bf16[4,96,288]{2,1,0:T(8,128)(2,1)S(1)} all-to-all(bf16[4,96,288]{2,1,0:T(8,128)(2,1)S(1)} %shard_map.59), channel_id=1, replica_groups=mesh['zh'=4,'x'=4,'core'=2,'zl'=4,'y'=4] {'zl'}, dimensions={0} | all-to-all | bytes 442368 | tf_op jit(solution)/shard_map/all_to_all | solution.py:328
  75.0 6.7 %all-to-all-start.2 = ((bf16[16,96,128]{2,1,0:T(8,128)(2,1)}), bf16[16,96,128]{2,1,0:T(8,128)(2,1)}, u32[]{:S(2)}, u32[]{:S(2)}) async-start(bf16[16,96,128]{2,1,0:T(8,128)(2,1)} %copy-done.7), calls=%async_computation.2 | async-start | bytes 786432 | tf_op jit(solution)/shard_map/all_to_all | solution.py:330
  81.7 4.3 %collective-permute-start.10 = (bf16[288,1024]{1,0:T(8,128)(2,1)S(1)}, bf16[288,1024]{1,0:T(8,128)(2,1)S(1)}, u32[]{:S(2)}, u32[]{:S(2)}) collective-permute-start(bf16[288,1024]{1,0:T(8,128)(2,1)S(1)} %bitcast.35), channel_id=1, source_target_pairs={{0,3},{1,0},{2,1},{3,2},{4,7},{5,4},{6,5},{7,6},{8,11},{9,8},{10,9... | collective-permute-start | bytes 1769480 | tf_op jit(solution)/shard_map/ppermute | solution.py:35
  87.9 13.1 %collective-permute-done.10.refs_2_ = bf16[288,1024]{1,0:T(8,128)(2,1)S(1)} collective-permute-done((bf16[288,1024]{1,0:T(8,128)(2,1)S(1)}, bf16[288,1024]{1,0:T(8,128)(2,1)S(1)}, u32[]{:S(2)}, u32[]{:S(2)}) %collective-permute-start.10) | collective-permute-done | bytes 589856 | tf_op jit(solution)/shard_map/ppermute | solution.py:35
  101.0 4.2 %collective-permute-start.12 = (bf16[144,1024]{1,0:T(8,128)(2,1)S(1)}, bf16[144,1024]{1,0:T(8,128)(2,1)S(1)}, u32[]{:S(2)}, u32[]{:S(2)}) collective-permute-start(bf16[144,1024]{1,0:T(8,128)(2,1)S(1)} %slice.25), channel_id=1, source_target_pairs={{0,3},{1,0},{2,1},{3,2},{4,7},{5,4},{6,5},{7,6},{8,11},{9,8},{10,9... | collective-permute-start | bytes 884744 | tf_op jit(solution)/shard_map/ppermute | solution.py:35
  108.0 2.6 %collective-permute-start.13 = (bf16[4,8,288]{2,1,0:T(8,128)(2,1)}, bf16[4,8,288]{2,1,0:T(8,128)(2,1)}, u32[]{:S(2)}, u32[]{:S(2)}) collective-permute-start(bf16[4,8,288]{2,1,0:T(8,128)(2,1)} %copy-done.24), channel_id=1, source_target_pairs={{0,1},{1,2},{2,3},{3,4},{4,5},{5,6},{6,7},{7,8},{8,9},{9,10},{10,1... | collective-permute-start | bytes 55304 | tf_op jit(solution)/shard_map/ppermute | solution.py:30
  110.5 4.8 %collective-permute-start.14 = (bf16[4,8,288]{2,1,0:T(8,128)(2,1)}, bf16[4,8,288]{2,1,0:T(8,128)(2,1)}, u32[]{:S(2)}, u32[]{:S(2)}) collective-permute-start(bf16[4,8,288]{2,1,0:T(8,128)(2,1)} %copy-done.23), channel_id=1, source_target_pairs={{1,0},{2,1},{3,2},{4,3},{5,4},{6,5},{7,6},{8,7},{9,8},{10,9},{11,1... | collective-permute-start | bytes 55304 | tf_op jit(solution)/shard_map/ppermute | solution.py:30
  120.9 5.5 %shard_map.61 = (f32[16,32,360]{2,1,0:T(8,128)S(1)}, bf16[16,32,360]{2,1,0:T(8,128)(2,1)}, bf16[512,72]{1,0:T(8,128)(2,1)S(1)}) custom-call(s32[3]{0:T(128)S(1)} %pad_add_fusion.where_ref, bf16[16,96,128]{2,1,0:T(8,128)(2,1)} %all-to-all-done.2.back_ref, bf16[288,1024]{1,0:T(8,128)(2,1)S(1)} %bitcast.37, bf16[288,1024]{1,0:T(8,128)(2,1)S(1)} %copy-done.3, ...), custom_call_target="tpu_custom_call" | custom-call | tf_op jit(solution)/shard_map/pallas_call | solution.py:45
  127.9 4.9 %collective-permute-start.18 = (bf16[16,32,360]{2,1,0:T(8,128)(2,1)}, bf16[16,32,360]{2,1,0:T(8,128)(2,1)}, u32[]{:S(2)}, u32[]{:S(2)}) collective-permute-start(bf16[16,32,360]{2,1,0:T(8,128)(2,1)} %get-tuple-element.26), channel_id=1, source_target_pairs={{0,16},{16,0},{1,17},{17,1},{2,18},{18,2},{3,19},{19,3},{4,20},{20... | collective-permute-start | bytes 1105928 | tf_op jit(solution)/shard_map/ppermute | solution.py:343
  134.3 6.1 %all-to-all-start.3 = ((bf16[4,80,288]{2,1,0:T(8,128)(2,1)}), bf16[4,80,288]{2,1,0:T(8,128)(2,1)S(1)}, u32[]{:S(2)}, u32[]{:S(2)}) async-start(bf16[4,80,288]{2,1,0:T(8,128)(2,1)} %pad_maximum_fusion), calls=%async_computation.3 | async-start | bytes 491520 | tf_op jit(solution)/shard_map/all_to_all | solution.py:333
  140.4 2.1 %add_convert_fusion = bf16[16,32,360]{2,1,0:T(8,128)(2,1)} fusion(f32[16,32,360]{2,1,0:T(8,128)} %copy-done.6, bf16[16,32,360]{2,1,0:T(8,128)(2,1)} %collective-permute-done.18), kind=kLoop, calls=%fused_computation.1 | loop fusion | flops 552960 | bytes 1474560 | tf_op jit(solution)/shard_map/convert_element_type | solution.py:344
  142.5 4.9 %all-to-all-done.3 = bf16[4,80,288]{2,1,0:T(8,128)(2,1)S(1)} async-done(((bf16[4,80,288]{2,1,0:T(8,128)(2,1)}), bf16[4,80,288]{2,1,0:T(8,128)(2,1)S(1)}, u32[]{:S(2)}, u32[]{:S(2)}) %all-to-all-start.3) | async-done | bytes 184352 | tf_op jit(solution)/shard_map/all_to_all | solution.py:333
  147.4 15.1 %all-to-all-start.4 = ((bf16[16,32,360]{2,1,0:T(8,128)(2,1)}), bf16[16,32,360]{2,1,0:T(8,128)(2,1)}, u32[]{:S(2)}, u32[]{:S(2)}) async-start(bf16[16,32,360]{2,1,0:T(8,128)(2,1)} %add_convert_fusion), calls=%async_computation.4 | async-start | bytes 786432 | tf_op jit(solution)/shard_map/all_to_all | solution.py:345
  162.5 3.0 %shard_map.62 = (bf16[64,1024]{1,0:T(8,128)(2,1)S(1)}, bf16[64,1024]{1,0:T(8,128)(2,1)S(1)}, bf16[64,1024]{1,0:T(8,128)(2,1)S(1)}, bf16[64,1024]{1,0:T(8,128)(2,1)S(1)}) custom-call(s32[3]{0:T(128)S(1)} %pad_add_fusion.where_ref, bf16[320,288]{1,0:T(8,128)(2,1)S(1)} %bitcast.38, bf16[5,288,512]{2,1,0:T(8,128)(2,1)S(1)} %bitcast.33, ...), custom_call_target="tpu_custom_call" | custom-call | tf_op jit(solution)/shard_map/pallas_call | solution.py:45
  165.5 3.5 %collective-permute-start.15 = (bf16[64,1024]{1,0:T(8,128)(2,1)S(1)}, bf16[64,1024]{1,0:T(8,128)(2,1)S(1)}, u32[]{:S(2)}, u32[]{:S(2)}) collective-permute-start(bf16[64,1024]{1,0:T(8,128)(2,1)S(1)} %get-tuple-element.22), channel_id=1, source_target_pairs={{0,8},{4,12},{8,0},{12,4},{1,9},{5,13},{9,1},{13,5},{2,10},{6,14},... | collective-permute-start | bytes 393224 | tf_op jit(solution)/shard_map/ppermute | solution.py:35
  169.0 2.2 %collective-permute-start.16 = (bf16[64,1024]{1,0:T(8,128)(2,1)S(1)}, bf16[64,1024]{1,0:T(8,128)(2,1)S(1)}, u32[]{:S(2)}, u32[]{:S(2)}) collective-permute-start(bf16[64,1024]{1,0:T(8,128)(2,1)S(1)} %get-tuple-element.23), channel_id=1, source_target_pairs={{0,4},{4,8},{8,12},{12,0},{1,5},{5,9},{9,13},{13,1},{2,6},{6,10},{... | collective-permute-start | bytes 393224 | tf_op jit(solution)/shard_map/ppermute | solution.py:35
  171.2 3.1 %collective-permute-start.17 = (bf16[64,1024]{1,0:T(8,128)(2,1)S(1)}, bf16[64,1024]{1,0:T(8,128)(2,1)S(1)}, u32[]{:S(2)}, u32[]{:S(2)}) collective-permute-start(bf16[64,1024]{1,0:T(8,128)(2,1)S(1)} %get-tuple-element.24), channel_id=1, source_target_pairs={{0,12},{4,0},{8,4},{12,8},{1,13},{5,1},{9,5},{13,9},{2,14},{6,2},{... | collective-permute-start | bytes 393224 | tf_op jit(solution)/shard_map/ppermute | solution.py:35
  174.3 9.3 %collective-permute-done.15.refs_1_ = bf16[64,1024]{1,0:T(8,128)(2,1)S(1)} collective-permute-done((bf16[64,1024]{1,0:T(8,128)(2,1)S(1)}, bf16[64,1024]{1,0:T(8,128)(2,1)S(1)}, u32[]{:S(2)}, u32[]{:S(2)}) %collective-permute-start.15) | collective-permute-done | bytes 131104 | tf_op jit(solution)/shard_map/ppermute | solution.py:35
  183.6 7.3 %collective-permute-done.16.refs_2_ = bf16[64,1024]{1,0:T(8,128)(2,1)S(1)} collective-permute-done((bf16[64,1024]{1,0:T(8,128)(2,1)S(1)}, bf16[64,1024]{1,0:T(8,128)(2,1)S(1)}, u32[]{:S(2)}, u32[]{:S(2)}) %collective-permute-start.16) | collective-permute-done | bytes 131104 | tf_op jit(solution)/shard_map/ppermute | solution.py:35
  (90 shorter events, 38.7 us)
Async XLA Ops:
  0.6 23.4 %copy-start.4 = (bf16[128,1024]{1,0:T(8,128)(2,1)S(1)}, bf16[128,1024]{1,0:T(8,128)(2,1)}, u32[]{:S(2)}) copy-start(bf16[128,1024]{1,0:T(8,128)(2,1)} %act_ref.1) | copy-start | bytes 786436
  1.8 35.4 %collective-permute-start.4 = (bf16[5,72,512]{2,1,0:T(8,128)(2,1)S(1)}, bf16[5,72,512]{2,1,0:T(8,128)(2,1)S(1)}, u32[]{:S(2)}, u32[]{:S(2)}) collective-permute-start(bf16[5,72,512]{2,1,0:T(8,128)(2,1)S(1)} %slice_select_fusion), channel_id=1, source_target_pairs={{0,3},{1,0},{2,1},{3,2},{4,7},{5,4},{6,5},{7,6},{8,11},{9,8},{10,9... | collective-permute-start | bytes 1105928 | tf_op jit(solution)/shard_map/ppermute | solution.py:35
  6.5 29.8 %collective-permute-start.3 = (bf16[5,72,512]{2,1,0:T(8,128)(2,1)S(1)}, bf16[5,72,512]{2,1,0:T(8,128)(2,1)}, u32[]{:S(2)}, u32[]{:S(2)}) collective-permute-start(bf16[5,72,512]{2,1,0:T(8,128)(2,1)S(1)} %slice_select_fusion), channel_id=1, source_target_pairs={{0,2},{1,3},{2,0},{3,1},{4,6},{5,7},{6,4},{7,5},{8,10},{9,11},{10,... | collective-permute-start | bytes 1105928 | tf_op jit(solution)/shard_map/ppermute | solution.py:35
  8.8 26.5 %collective-permute-start.2 = (bf16[5,72,512]{2,1,0:T(8,128)(2,1)S(1)}, bf16[5,72,512]{2,1,0:T(8,128)(2,1)}, u32[]{:S(2)}, u32[]{:S(2)}) collective-permute-start(bf16[5,72,512]{2,1,0:T(8,128)(2,1)S(1)} %slice_select_fusion), channel_id=1, source_target_pairs={{0,1},{1,2},{2,3},{3,0},{4,5},{5,6},{6,7},{7,4},{8,9},{9,10},{10,1... | collective-permute-start | bytes 1105928 | tf_op jit(solution)/shard_map/ppermute | solution.py:35
  12.1 9.7 %collective-permute-start.1 = (bf16[8,1024]{1,0:T(8,128)(2,1)S(1)}, bf16[8,1024]{1,0:T(8,128)(2,1)S(1)}, u32[]{:S(2)}, u32[]{:S(2)}) collective-permute-start(bf16[8,1024]{1,0:T(8,128)(2,1)S(1)} %get-tuple-element.33), channel_id=1, source_target_pairs={{1,0},{2,1},{3,2},{4,3},{5,4},{6,5},{7,6},{8,7},{9,8},{10,9},{11,1... | collective-permute-start | bytes 49160 | tf_op jit(solution)/shard_map/ppermute | solution.py:30
  15.5 8.5 %collective-permute-start = (bf16[8,1024]{1,0:T(8,128)(2,1)S(1)}, bf16[8,1024]{1,0:T(8,128)(2,1)S(1)}, u32[]{:S(2)}, u32[]{:S(2)}) collective-permute-start(bf16[8,1024]{1,0:T(8,128)(2,1)S(1)} %get-tuple-element.34), channel_id=1, source_target_pairs={{0,1},{1,2},{2,3},{3,4},{4,5},{5,6},{6,7},{7,8},{8,9},{9,10},{10,1... | collective-permute-start | bytes 49160 | tf_op jit(solution)/shard_map/ppermute | solution.py:30
  25.5 29.3 %all-to-all-start = ((bf16[4,72,1024]{2,1,0:T(8,128)(2,1)}), bf16[4,72,1024]{2,1,0:T(8,128)(2,1)S(1)}, u32[]{:S(2)}, u32[]{:S(2)}) async-start(bf16[4,72,1024]{2,1,0:T(8,128)(2,1)} %broadcast_in_dim.18), calls=%async_computation | async-start | bytes 1179648 | tf_op jit(solution)/shard_map/all_to_all | solution.py:40
  37.3 17.5 %collective-permute-start.5 = (bf16[5,288,512]{2,1,0:T(8,128)(2,1)S(1)}, bf16[5,288,512]{2,1,0:T(8,128)(2,1)S(1)}, u32[]{:S(2)}, u32[]{:S(2)}) collective-permute-start(bf16[5,288,512]{2,1,0:T(8,128)(2,1)S(1)} %bitcast.31), channel_id=1, source_target_pairs={{0,16},{16,0},{1,17},{17,1},{2,18},{18,2},{3,19},{19,3},{4,20},{20... | collective-permute-start | bytes 4423688 | tf_op jit(solution)/shard_map/ppermute | solution.py:313
  42.5 8.3 %collective-permute-start.8 = (bf16[4,32,72]{2,1,0:T(8,128)(2,1)S(1)}, bf16[4,32,72]{2,1,0:T(8,128)(2,1)S(1)}, u32[]{:S(2)}, u32[]{:S(2)}) collective-permute-start(bf16[4,32,72]{2,1,0:T(8,128)(2,1)S(1)} %get-tuple-element.35), channel_id=1, source_target_pairs={{0,3},{1,0},{2,1},{3,2},{4,7},{5,4},{6,5},{7,6},{8,11},{9,8},{10,9... | collective-permute-start | bytes 55304 | tf_op jit(solution)/shard_map/ppermute | solution.py:35
  46.1 6.2 %collective-permute-start.7 = (bf16[4,32,72]{2,1,0:T(8,128)(2,1)S(1)}, bf16[4,32,72]{2,1,0:T(8,128)(2,1)S(1)}, u32[]{:S(2)}, u32[]{:S(2)}) collective-permute-start(bf16[4,32,72]{2,1,0:T(8,128)(2,1)S(1)} %get-tuple-element.36), channel_id=1, source_target_pairs={{0,2},{1,3},{2,0},{3,1},{4,6},{5,7},{6,4},{7,5},{8,10},{9,11},{10,... | collective-permute-start | bytes 55304 | tf_op jit(solution)/shard_map/ppermute | solution.py:35
  48.3 5.9 %collective-permute-start.6 = (bf16[4,32,72]{2,1,0:T(8,128)(2,1)S(1)}, bf16[4,32,72]{2,1,0:T(8,128)(2,1)S(1)}, u32[]{:S(2)}, u32[]{:S(2)}) collective-permute-start(bf16[4,32,72]{2,1,0:T(8,128)(2,1)S(1)} %get-tuple-element.37), channel_id=1, source_target_pairs={{0,1},{1,2},{2,3},{3,0},{4,5},{5,6},{6,7},{7,4},{8,9},{9,10},{10,1... | collective-permute-start | bytes 55304 | tf_op jit(solution)/shard_map/ppermute | solution.py:35
  75.0 41.8 %all-to-all-start.2 = ((bf16[16,96,128]{2,1,0:T(8,128)(2,1)}), bf16[16,96,128]{2,1,0:T(8,128)(2,1)}, u32[]{:S(2)}, u32[]{:S(2)}) async-start(bf16[16,96,128]{2,1,0:T(8,128)(2,1)} %copy-done.7), calls=%async_computation.2 | async-start | bytes 786432 | tf_op jit(solution)/shard_map/all_to_all | solution.py:330
  81.7 19.3 %collective-permute-start.10 = (bf16[288,1024]{1,0:T(8,128)(2,1)S(1)}, bf16[288,1024]{1,0:T(8,128)(2,1)S(1)}, u32[]{:S(2)}, u32[]{:S(2)}) collective-permute-start(bf16[288,1024]{1,0:T(8,128)(2,1)S(1)} %bitcast.35), channel_id=1, source_target_pairs={{0,3},{1,0},{2,1},{3,2},{4,7},{5,4},{6,5},{7,6},{8,11},{9,8},{10,9... | collective-permute-start | bytes 1769480 | tf_op jit(solution)/shard_map/ppermute | solution.py:35
  86.0 19.2 %collective-permute-start.9 = (bf16[288,1024]{1,0:T(8,128)(2,1)S(1)}, bf16[288,1024]{1,0:T(8,128)(2,1)S(1)}, u32[]{:S(2)}, u32[]{:S(2)}) collective-permute-start(bf16[288,1024]{1,0:T(8,128)(2,1)S(1)} %bitcast.36), channel_id=1, source_target_pairs={{0,1},{1,2},{2,3},{3,0},{4,5},{5,6},{6,7},{7,4},{8,9},{9,10},{10,1... | collective-permute-start | bytes 1769480 | tf_op jit(solution)/shard_map/ppermute | solution.py:35
  101.0 4.2 %copy-start = (bf16[288,1024]{1,0:T(8,128)(2,1)}, bf16[288,1024]{1,0:T(8,128)(2,1)S(1)}, u32[]{:S(2)}) copy-start(bf16[288,1024]{1,0:T(8,128)(2,1)S(1)} %collective-permute-done.10.refs_2_) | copy-start | bytes 1769476
  101.0 14.3 %collective-permute-start.12 = (bf16[144,1024]{1,0:T(8,128)(2,1)S(1)}, bf16[144,1024]{1,0:T(8,128)(2,1)S(1)}, u32[]{:S(2)}, u32[]{:S(2)}) collective-permute-start(bf16[144,1024]{1,0:T(8,128)(2,1)S(1)} %slice.25), channel_id=1, source_target_pairs={{0,3},{1,0},{2,1},{3,2},{4,7},{5,4},{6,5},{7,6},{8,11},{9,8},{10,9... | collective-permute-start | bytes 884744 | tf_op jit(solution)/shard_map/ppermute | solution.py:35
  106.0 10.1 %collective-permute-start.11 = (bf16[144,1024]{1,0:T(8,128)(2,1)S(1)}, bf16[144,1024]{1,0:T(8,128)(2,1)S(1)}, u32[]{:S(2)}, u32[]{:S(2)}) collective-permute-start(bf16[144,1024]{1,0:T(8,128)(2,1)S(1)} %slice.24), channel_id=1, source_target_pairs={{0,1},{1,2},{2,3},{3,0},{4,5},{5,6},{6,7},{7,4},{8,9},{9,10},{10,1... | collective-permute-start | bytes 884744 | tf_op jit(solution)/shard_map/ppermute | solution.py:35
  108.0 24.8 %collective-permute-start.13 = (bf16[4,8,288]{2,1,0:T(8,128)(2,1)}, bf16[4,8,288]{2,1,0:T(8,128)(2,1)}, u32[]{:S(2)}, u32[]{:S(2)}) collective-permute-start(bf16[4,8,288]{2,1,0:T(8,128)(2,1)} %copy-done.24), channel_id=1, source_target_pairs={{0,1},{1,2},{2,3},{3,4},{4,5},{5,6},{6,7},{7,8},{8,9},{9,10},{10,1... | collective-permute-start | bytes 55304 | tf_op jit(solution)/shard_map/ppermute | solution.py:30
  110.5 22.3 %collective-permute-start.14 = (bf16[4,8,288]{2,1,0:T(8,128)(2,1)}, bf16[4,8,288]{2,1,0:T(8,128)(2,1)}, u32[]{:S(2)}, u32[]{:S(2)}) collective-permute-start(bf16[4,8,288]{2,1,0:T(8,128)(2,1)} %copy-done.23), channel_id=1, source_target_pairs={{1,0},{2,1},{3,2},{4,3},{5,4},{6,5},{7,6},{8,7},{9,8},{10,9},{11,1... | collective-permute-start | bytes 55304 | tf_op jit(solution)/shard_map/ppermute | solution.py:30
  116.8 1.1 copy-start.1
  117.9 1.1 copy-start.3
  119.0 1.0 copy-start.9
  119.9 1.0 copy-start.11
  120.9 11.9 %copy-start.13 = (bf16[4,64,288]{2,1,0:T(8,128)(2,1)S(1)}, bf16[4,64,288]{2,1,0:T(8,128)(2,1)}, u32[]{:S(2)}) copy-start(bf16[4,64,288]{2,1,0:T(8,128)(2,1)} %copy-done.12) | copy-start | bytes 442372
  127.9 12.5 %collective-permute-start.18 = (bf16[16,32,360]{2,1,0:T(8,128)(2,1)}, bf16[16,32,360]{2,1,0:T(8,128)(2,1)}, u32[]{:S(2)}, u32[]{:S(2)}) collective-permute-start(bf16[16,32,360]{2,1,0:T(8,128)(2,1)} %get-tuple-element.26), channel_id=1, source_target_pairs={{0,16},{16,0},{1,17},{17,1},{2,18},{18,2},{3,19},{19,3},{4,20},{20... | collective-permute-start | bytes 1105928 | tf_op jit(solution)/shard_map/ppermute | solution.py:343
  134.3 13.1 %all-to-all-start.3 = ((bf16[4,80,288]{2,1,0:T(8,128)(2,1)}), bf16[4,80,288]{2,1,0:T(8,128)(2,1)S(1)}, u32[]{:S(2)}, u32[]{:S(2)}) async-start(bf16[4,80,288]{2,1,0:T(8,128)(2,1)} %pad_maximum_fusion), calls=%async_computation.3 | async-start | bytes 491520 | tf_op jit(solution)/shard_map/all_to_all | solution.py:333
  147.4 47.3 %all-to-all-start.4 = ((bf16[16,32,360]{2,1,0:T(8,128)(2,1)}), bf16[16,32,360]{2,1,0:T(8,128)(2,1)}, u32[]{:S(2)}, u32[]{:S(2)}) async-start(bf16[16,32,360]{2,1,0:T(8,128)(2,1)} %add_convert_fusion), calls=%async_computation.4 | async-start | bytes 786432 | tf_op jit(solution)/shard_map/all_to_all | solution.py:345
  162.5 30.0 %copy-start.5 = (bf16[128,1024]{1,0:T(8,128)(2,1)S(1)}, bf16[128,1024]{1,0:T(8,128)(2,1)}, u32[]{:S(2)}) copy-start(bf16[128,1024]{1,0:T(8,128)(2,1)} %act_ref.1) | copy-start | bytes 786436
  162.5 31.4 %copy-start.16 = (bf16[512,72]{1,0:T(8,128)(2,1)S(1)}, bf16[512,72]{1,0:T(8,128)(2,1)}, u32[]{:S(2)}) copy-start(bf16[512,72]{1,0:T(8,128)(2,1)} %copy-done.15) | copy-start | bytes 221188
  165.5 18.1 %collective-permute-start.15 = (bf16[64,1024]{1,0:T(8,128)(2,1)S(1)}, bf16[64,1024]{1,0:T(8,128)(2,1)S(1)}, u32[]{:S(2)}, u32[]{:S(2)}) collective-permute-start(bf16[64,1024]{1,0:T(8,128)(2,1)S(1)} %get-tuple-element.22), channel_id=1, source_target_pairs={{0,8},{4,12},{8,0},{12,4},{1,9},{5,13},{9,1},{13,5},{2,10},{6,14},... | collective-permute-start | bytes 393224 | tf_op jit(solution)/shard_map/ppermute | solution.py:35
  169.0 21.9 %collective-permute-start.16 = (bf16[64,1024]{1,0:T(8,128)(2,1)S(1)}, bf16[64,1024]{1,0:T(8,128)(2,1)S(1)}, u32[]{:S(2)}, u32[]{:S(2)}) collective-permute-start(bf16[64,1024]{1,0:T(8,128)(2,1)S(1)} %get-tuple-element.23), channel_id=1, source_target_pairs={{0,4},{4,8},{8,12},{12,0},{1,5},{5,9},{9,13},{13,1},{2,6},{6,10},{... | collective-permute-start | bytes 393224 | tf_op jit(solution)/shard_map/ppermute | solution.py:35
  171.2 21.3 %collective-permute-start.17 = (bf16[64,1024]{1,0:T(8,128)(2,1)S(1)}, bf16[64,1024]{1,0:T(8,128)(2,1)S(1)}, u32[]{:S(2)}, u32[]{:S(2)}) collective-permute-start(bf16[64,1024]{1,0:T(8,128)(2,1)S(1)} %get-tuple-element.24), channel_id=1, source_target_pairs={{0,12},{4,0},{8,4},{12,8},{1,13},{5,1},{9,5},{13,9},{2,14},{6,2},{... | collective-permute-start | bytes 393224 | tf_op jit(solution)/shard_map/ppermute | solution.py:35
  (16 other events, 11.3 us)

commit v7 on v6

--- a/solution.py
+++ b/solution.py
@@ -225,7 +225,7 @@
 
 
 def weight_kernel(taps, block, where_ref, back_ref, *refs):
-    ring_refs, (mine_ref, other_ref, feature_ref, stage_ref, wide_ref, part_ref) = refs[:5], refs[5:]
+    ring_refs, (mine_ref, other_ref, feature_ref, stage_ref, wide_ref, part_ref) = refs[:4], refs[4:]
     count, rows, lanes = back_ref.shape
     pooled = rows // 3
     own = 2 * pooled
@@ -253,14 +253,12 @@
             stage_ref[pl.ds(z * span + taps + 1, own), :] = jnp.zeros((own, lanes), f32)
         wide_ref[i] = total.astype(bf16)
     contract = (((0,), (0,)), ((), ()))
-    middle = 2 * span
-    pieces = ((0, slice(None)), (3, slice(None)), (1, slice(None)), (2, slice(0, middle)), (2, slice(middle, None)))
-    for ref, (turns, some) in zip(ring_refs, pieces, strict=True):
+    for j, turns in enumerate((0, 3, 1, 2)):
         term = lax.dot_general(
-            ref[...], wide_ref[lax.rem(y + turns, 4), some], contract,
+            ring_refs[j][...], wide_ref[lax.rem(y + turns, 4)], contract,
             preferred_element_type=f32,
         )
-        part_ref[...] = term if ref is ring_refs[0] else part_ref[...] + term
+        part_ref[...] = term if j == 0 else part_ref[...] + term
     for c in range(mine_ref.shape[0]):
         step = mine_ref.shape[1]
         near = pl.ds(pl.multiple_of(c * 2 * step + core * step, step), step)
@@ -324,7 +322,7 @@
 
     conv_out = conv_forward(where, flat, first, second, cots)
     up, down = turn(flat, "y", 1), turn(flat, "y", -1)
-    far = [turn(up[: 2 * span], "y", 1), turn(down[2 * span :], "y", -1)]
+    far = turn(flat, "y", 2)
     conv_out = lax.all_to_all(conv_out, "zl", 0, 0)
     grad, back, head, tail = statistics(conv_out, rows)
     back = lax.all_to_all(back, SUB, 0, 0)
@@ -338,7 +336,7 @@
     input_grad = input_gradient(activations, parts)
 
     mine, other, features = weight_partial(
-        where, back, [flat, up, down, *far], tap_count, out_width
+        where, back, [flat, up, down, far], tap_count, out_width
     )
     other = lax.ppermute(other, "core", [(0, 1), (1, 0)])
     total = (mine + other.astype(f32)).astype(bf16)

time: 198 us -> 193 us (0.975)
  the two profiles are of different devices: /device:TPU:35 before, /device:TPU:34 now
where the time goes in v7:
time: 193 us; the launch traced here: 191 us
  starting transfers between devices  91.3 us (47%)
  waiting for transfers between devices  43.5 us (23%)
  local copies, waits for them, and re-layouts  23.1 us (12%)
  Pallas kernels  14.5 us (8%)
  blocking collectives  11.9 us (6%)
  other arithmetic  5.87 us (3%)
    ppermute x12, starting transfers between devices, turn(): lax.ppermute(block, axis, [(i, (i + step) % count) for i in range(count)])  39.4 us
    ppermute x12, waiting for transfers between devices, turn(): lax.ppermute(block, axis, [(i, (i + step) % count) for i in range(count)])  32.2 us
    unnamed x48, local copies, waits for them, and re-layouts  16.1 us
    all_to_all x1, starting transfers between devices, per_device(): total = lax.all_to_all(total, ('zh', 'x'), 0, 0)  15.7 us
    pallas_call x6, Pallas kernels, local_call(): pl.pallas_call(kernel, out_shape=shapes, in_specs=[pl.BlockSpec(memory_sp...  14.5 us
    ppermute x4, starting transfers between devices, shift(): return lax.ppermute(block, axis, pairs)  13.8 us
    all_to_all x1, blocking collectives, per_device(): conv_out = lax.all_to_all(conv_out, 'zl', 0, 0)  11.9 us
    all_to_all x1, starting transfers between devices, gather_all(): lax.all_to_all(jnp.broadcast_to(block, (count, *block.shape)), axis, 0, 0)  8.01 us
  transfers between devices with their start and end apart: 22, of which 11 were waited for; matrix products, arithmetic and copies ran while one was open for 6% of the time, Pallas kernels for 5%

profile of v7, /device:TPU:34, one launch (start us, length us, event | category | flops | bytes accessed | tf_op | source)
XLA Modules:
  0.0 191.3 jit_solution(9001991758663281031)
XLA Ops:
  1.8 4.9 %collective-permute-start.4 = (bf16[5,72,512]{2,1,0:T(8,128)(2,1)S(1)}, bf16[5,72,512]{2,1,0:T(8,128)(2,1)S(1)}, u32[]{:S(2)}, u32[]{:S(2)}) collective-permute-start(bf16[5,72,512]{2,1,0:T(8,128)(2,1)S(1)} %slice_select_fusion), channel_id=1, source_target_pairs={{0,3},{1,0},{2,1},{3,2},{4,7},{5,4},{6,5},{7,6},{8,11},{9,8},{10,9... | collective-permute-start | bytes 1105928 | tf_op jit(solution)/shard_map/ppermute | solution.py:35
  6.8 2.5 %collective-permute-start.3 = (bf16[5,72,512]{2,1,0:T(8,128)(2,1)S(1)}, bf16[5,72,512]{2,1,0:T(8,128)(2,1)}, u32[]{:S(2)}, u32[]{:S(2)}) collective-permute-start(bf16[5,72,512]{2,1,0:T(8,128)(2,1)S(1)} %slice_select_fusion), channel_id=1, source_target_pairs={{0,2},{1,3},{2,0},{3,1},{4,6},{5,7},{6,4},{7,5},{8,10},{9,11},{10,... | collective-permute-start | bytes 1105928 | tf_op jit(solution)/shard_map/ppermute | solution.py:35
  9.3 2.9 %collective-permute-start.2 = (bf16[5,72,512]{2,1,0:T(8,128)(2,1)S(1)}, bf16[5,72,512]{2,1,0:T(8,128)(2,1)}, u32[]{:S(2)}, u32[]{:S(2)}) collective-permute-start(bf16[5,72,512]{2,1,0:T(8,128)(2,1)S(1)} %slice_select_fusion), channel_id=1, source_target_pairs={{0,1},{1,2},{2,3},{3,0},{4,5},{5,6},{6,7},{7,4},{8,9},{9,10},{10,1... | collective-permute-start | bytes 1105928 | tf_op jit(solution)/shard_map/ppermute | solution.py:35
  12.9 3.7 %collective-permute-start.1 = (bf16[8,1024]{1,0:T(8,128)(2,1)S(1)}, bf16[8,1024]{1,0:T(8,128)(2,1)S(1)}, u32[]{:S(2)}, u32[]{:S(2)}) collective-permute-start(bf16[8,1024]{1,0:T(8,128)(2,1)S(1)} %get-tuple-element.33), channel_id=1, source_target_pairs={{1,0},{2,1},{3,2},{4,3},{5,4},{6,5},{7,6},{8,7},{9,8},{10,9},{11,1... | collective-permute-start | bytes 49160 | tf_op jit(solution)/shard_map/ppermute | solution.py:30
  16.7 2.1 %collective-permute-start = (bf16[8,1024]{1,0:T(8,128)(2,1)S(1)}, bf16[8,1024]{1,0:T(8,128)(2,1)S(1)}, u32[]{:S(2)}, u32[]{:S(2)}) collective-permute-start(bf16[8,1024]{1,0:T(8,128)(2,1)S(1)} %get-tuple-element.34), channel_id=1, source_target_pairs={{0,1},{1,2},{2,3},{3,4},{4,5},{5,6},{6,7},{7,8},{8,9},{9,10},{10,1... | collective-permute-start | bytes 49160 | tf_op jit(solution)/shard_map/ppermute | solution.py:30
  19.0 3.5 %collective-permute-done.1.high_ref = bf16[8,1024]{1,0:T(8,128)(2,1)S(1)} collective-permute-done((bf16[8,1024]{1,0:T(8,128)(2,1)S(1)}, bf16[8,1024]{1,0:T(8,128)(2,1)S(1)}, u32[]{:S(2)}, u32[]{:S(2)}) %collective-permute-start.1) | collective-permute-done | bytes 16416 | tf_op jit(solution)/shard_map/ppermute | solution.py:30
  22.5 2.6 %collective-permute-done.low_ref = bf16[8,1024]{1,0:T(8,128)(2,1)S(1)} collective-permute-done((bf16[8,1024]{1,0:T(8,128)(2,1)S(1)}, bf16[8,1024]{1,0:T(8,128)(2,1)S(1)}, u32[]{:S(2)}, u32[]{:S(2)}) %collective-permute-start) | collective-permute-done | bytes 16416 | tf_op jit(solution)/shard_map/ppermute | solution.py:30
  26.7 8.0 %all-to-all-start = ((bf16[4,72,1024]{2,1,0:T(8,128)(2,1)}), bf16[4,72,1024]{2,1,0:T(8,128)(2,1)S(1)}, u32[]{:S(2)}, u32[]{:S(2)}) async-start(bf16[4,72,1024]{2,1,0:T(8,128)(2,1)} %broadcast_in_dim.18), calls=%async_computation | async-start | bytes 1179648 | tf_op jit(solution)/shard_map/all_to_all | solution.py:40
  36.8 2.3 %collective-permute-start.5 = (bf16[5,288,512]{2,1,0:T(8,128)(2,1)S(1)}, bf16[5,288,512]{2,1,0:T(8,128)(2,1)S(1)}, u32[]{:S(2)}, u32[]{:S(2)}) collective-permute-start(bf16[5,288,512]{2,1,0:T(8,128)(2,1)S(1)} %bitcast.31), channel_id=1, source_target_pairs={{0,16},{16,0},{1,17},{17,1},{2,18},{18,2},{3,19},{19,3},{4,20},{20... | collective-permute-start | bytes 4423688 | tf_op jit(solution)/shard_map/ppermute | solution.py:311
  42.2 3.5 %collective-permute-start.8 = (bf16[4,32,72]{2,1,0:T(8,128)(2,1)S(1)}, bf16[4,32,72]{2,1,0:T(8,128)(2,1)S(1)}, u32[]{:S(2)}, u32[]{:S(2)}) collective-permute-start(bf16[4,32,72]{2,1,0:T(8,128)(2,1)S(1)} %get-tuple-element.35), channel_id=1, source_target_pairs={{0,3},{1,0},{2,1},{3,2},{4,7},{5,4},{6,5},{7,6},{8,11},{9,8},{10,9... | collective-permute-start | bytes 55304 | tf_op jit(solution)/shard_map/ppermute | solution.py:35
  45.7 2.5 %collective-permute-start.7 = (bf16[4,32,72]{2,1,0:T(8,128)(2,1)S(1)}, bf16[4,32,72]{2,1,0:T(8,128)(2,1)S(1)}, u32[]{:S(2)}, u32[]{:S(2)}) collective-permute-start(bf16[4,32,72]{2,1,0:T(8,128)(2,1)S(1)} %get-tuple-element.36), channel_id=1, source_target_pairs={{0,2},{1,3},{2,0},{3,1},{4,6},{5,7},{6,4},{7,5},{8,10},{9,11},{10,... | collective-permute-start | bytes 55304 | tf_op jit(solution)/shard_map/ppermute | solution.py:35
  48.2 2.7 %collective-permute-start.6 = (bf16[4,32,72]{2,1,0:T(8,128)(2,1)S(1)}, bf16[4,32,72]{2,1,0:T(8,128)(2,1)S(1)}, u32[]{:S(2)}, u32[]{:S(2)}) collective-permute-start(bf16[4,32,72]{2,1,0:T(8,128)(2,1)S(1)} %get-tuple-element.37), channel_id=1, source_target_pairs={{0,1},{1,2},{2,3},{3,0},{4,5},{5,6},{6,7},{7,4},{8,9},{9,10},{10,1... | collective-permute-start | bytes 55304 | tf_op jit(solution)/shard_map/ppermute | solution.py:35
  58.9 2.5 %shard_map.59 = bf16[4,96,288]{2,1,0:T(8,128)(2,1)S(1)} custom-call(s32[3]{0:T(128)S(1)} %pad_add_fusion.where_ref, bf16[288,1024]{1,0:T(8,128)(2,1)S(1)} %bitcast.34, bf16[5,288,512]{2,1,0:T(8,128)(2,1)S(1)} %bitcast.32, bf16[5,288,512]{2,1,0:T(8,128)(2,1)S(1)} %collective-permute-done.5.second_ref, bf16[4,32,72]{2,1,0:T(8,128)(2,1)S(1)} %copy-done.12, ...), custom_call_target="tpu_custom_call" | custom-call | tf_op jit(solution)/shard_map/pallas_call | solution.py:45
  61.4 11.9 %all_to_all.25.y_ref = bf16[4,96,288]{2,1,0:T(8,128)(2,1)S(1)} all-to-all(bf16[4,96,288]{2,1,0:T(8,128)(2,1)S(1)} %shard_map.59), channel_id=1, replica_groups=mesh['zh'=4,'x'=4,'core'=2,'zl'=4,'y'=4] {'zl'}, dimensions={0} | all-to-all | bytes 442368 | tf_op jit(solution)/shard_map/all_to_all | solution.py:326
  77.5 5.5 %all-to-all-start.2 = ((bf16[16,96,128]{2,1,0:T(8,128)(2,1)}), bf16[16,96,128]{2,1,0:T(8,128)(2,1)}, u32[]{:S(2)}, u32[]{:S(2)}) async-start(bf16[16,96,128]{2,1,0:T(8,128)(2,1)} %copy-done.9), calls=%async_computation.2 | async-start | bytes 786432 | tf_op jit(solution)/shard_map/all_to_all | solution.py:328
  83.0 4.9 %collective-permute-start.11 = (bf16[288,1024]{1,0:T(8,128)(2,1)S(1)}, bf16[288,1024]{1,0:T(8,128)(2,1)S(1)}, u32[]{:S(2)}, u32[]{:S(2)}) collective-permute-start(bf16[288,1024]{1,0:T(8,128)(2,1)S(1)} %bitcast.35), channel_id=1, source_target_pairs={{0,2},{1,3},{2,0},{3,1},{4,6},{5,7},{6,4},{7,5},{8,10},{9,11},{10,... | collective-permute-start | bytes 1769480 | tf_op jit(solution)/shard_map/ppermute | solution.py:35
  87.9 3.1 %collective-permute-start.10 = (bf16[288,1024]{1,0:T(8,128)(2,1)S(1)}, bf16[288,1024]{1,0:T(8,128)(2,1)S(1)}, u32[]{:S(2)}, u32[]{:S(2)}) collective-permute-start(bf16[288,1024]{1,0:T(8,128)(2,1)S(1)} %bitcast.36), channel_id=1, source_target_pairs={{0,3},{1,0},{2,1},{3,2},{4,7},{5,4},{6,5},{7,6},{8,11},{9,8},{10,9... | collective-permute-start | bytes 1769480 | tf_op jit(solution)/shard_map/ppermute | solution.py:35
  90.9 2.8 %collective-permute-start.9 = (bf16[288,1024]{1,0:T(8,128)(2,1)S(1)}, bf16[288,1024]{1,0:T(8,128)(2,1)S(1)}, u32[]{:S(2)}, u32[]{:S(2)}) collective-permute-start(bf16[288,1024]{1,0:T(8,128)(2,1)S(1)} %bitcast.37), channel_id=1, source_target_pairs={{0,1},{1,2},{2,3},{3,0},{4,5},{5,6},{6,7},{7,4},{8,9},{9,10},{10,1... | collective-permute-start | bytes 1769480 | tf_op jit(solution)/shard_map/ppermute | solution.py:35
  93.7 2.5 %collective-permute-start.12 = (bf16[4,8,288]{2,1,0:T(8,128)(2,1)}, bf16[4,8,288]{2,1,0:T(8,128)(2,1)}, u32[]{:S(2)}, u32[]{:S(2)}) collective-permute-start(bf16[4,8,288]{2,1,0:T(8,128)(2,1)} %copy-done.22), channel_id=1, source_target_pairs={{0,1},{1,2},{2,3},{3,4},{4,5},{5,6},{6,7},{7,8},{8,9},{9,10},{10,1... | collective-permute-start | bytes 55304 | tf_op jit(solution)/shard_map/ppermute | solution.py:30
  96.2 5.5 %collective-permute-start.13 = (bf16[4,8,288]{2,1,0:T(8,128)(2,1)}, bf16[4,8,288]{2,1,0:T(8,128)(2,1)}, u32[]{:S(2)}, u32[]{:S(2)}) collective-permute-start(bf16[4,8,288]{2,1,0:T(8,128)(2,1)} %copy-done.21), channel_id=1, source_target_pairs={{1,0},{2,1},{3,2},{4,3},{5,4},{6,5},{7,6},{8,7},{9,8},{10,9},{11,1... | collective-permute-start | bytes 55304 | tf_op jit(solution)/shard_map/ppermute | solution.py:30
  101.7 3.1 %collective-permute-done.11.refs_3_ = bf16[288,1024]{1,0:T(8,128)(2,1)S(1)} collective-permute-done((bf16[288,1024]{1,0:T(8,128)(2,1)S(1)}, bf16[288,1024]{1,0:T(8,128)(2,1)S(1)}, u32[]{:S(2)}, u32[]{:S(2)}) %collective-permute-start.11) | collective-permute-done | bytes 589856 | tf_op jit(solution)/shard_map/ppermute | solution.py:35
  105.6 9.4 %collective-permute-done.10.refs_2_ = bf16[288,1024]{1,0:T(8,128)(2,1)S(1)} collective-permute-done((bf16[288,1024]{1,0:T(8,128)(2,1)S(1)}, bf16[288,1024]{1,0:T(8,128)(2,1)S(1)}, u32[]{:S(2)}, u32[]{:S(2)}) %collective-permute-start.10) | collective-permute-done | bytes 589856 | tf_op jit(solution)/shard_map/ppermute | solution.py:35
  120.6 5.4 %shard_map.61 = (f32[16,32,360]{2,1,0:T(8,128)S(1)}, bf16[16,32,360]{2,1,0:T(8,128)(2,1)}, bf16[512,72]{1,0:T(8,128)(2,1)S(1)}) custom-call(s32[3]{0:T(128)S(1)} %pad_add_fusion.where_ref, bf16[16,96,128]{2,1,0:T(8,128)(2,1)} %all-to-all-done.2.back_ref, bf16[288,1024]{1,0:T(8,128)(2,1)S(1)} %bitcast.38, bf16[288,1024]{1,0:T(8,128)(2,1)S(1)} %copy-done.8, ...), custom_call_target="tpu_custom_call" | custom-call | tf_op jit(solution)/shard_map/pallas_call | solution.py:45
  131.1 4.7 %all-to-all-start.3 = ((bf16[4,80,288]{2,1,0:T(8,128)(2,1)}), bf16[4,80,288]{2,1,0:T(8,128)(2,1)S(1)}, u32[]{:S(2)}, u32[]{:S(2)}) async-start(bf16[4,80,288]{2,1,0:T(8,128)(2,1)} %pad_maximum_fusion), calls=%async_computation.3 | async-start | bytes 491520 | tf_op jit(solution)/shard_map/all_to_all | solution.py:331
  137.8 5.1 %all-to-all-done.3 = bf16[4,80,288]{2,1,0:T(8,128)(2,1)S(1)} async-done(((bf16[4,80,288]{2,1,0:T(8,128)(2,1)}), bf16[4,80,288]{2,1,0:T(8,128)(2,1)S(1)}, u32[]{:S(2)}, u32[]{:S(2)}) %all-to-all-start.3) | async-done | bytes 184352 | tf_op jit(solution)/shard_map/all_to_all | solution.py:331
  143.0 15.7 %all-to-all-start.4 = ((bf16[16,32,360]{2,1,0:T(8,128)(2,1)}), bf16[16,32,360]{2,1,0:T(8,128)(2,1)}, u32[]{:S(2)}, u32[]{:S(2)}) async-start(bf16[16,32,360]{2,1,0:T(8,128)(2,1)} %add_convert_fusion), calls=%async_computation.4 | async-start | bytes 786432 | tf_op jit(solution)/shard_map/all_to_all | solution.py:343
  158.6 3.0 %shard_map.62 = (bf16[64,1024]{1,0:T(8,128)(2,1)S(1)}, bf16[64,1024]{1,0:T(8,128)(2,1)S(1)}, bf16[64,1024]{1,0:T(8,128)(2,1)S(1)}, bf16[64,1024]{1,0:T(8,128)(2,1)S(1)}) custom-call(s32[3]{0:T(128)S(1)} %pad_add_fusion.where_ref, bf16[320,288]{1,0:T(8,128)(2,1)S(1)} %bitcast.39, bf16[5,288,512]{2,1,0:T(8,128)(2,1)S(1)} %bitcast.33, ...), custom_call_target="tpu_custom_call" | custom-call | tf_op jit(solution)/shard_map/pallas_call | solution.py:45
  161.6 3.8 %collective-permute-start.14 = (bf16[64,1024]{1,0:T(8,128)(2,1)S(1)}, bf16[64,1024]{1,0:T(8,128)(2,1)S(1)}, u32[]{:S(2)}, u32[]{:S(2)}) collective-permute-start(bf16[64,1024]{1,0:T(8,128)(2,1)S(1)} %get-tuple-element.22), channel_id=1, source_target_pairs={{0,8},{4,12},{8,0},{12,4},{1,9},{5,13},{9,1},{13,5},{2,10},{6,14},... | collective-permute-start | bytes 393224 | tf_op jit(solution)/shard_map/ppermute | solution.py:35
  165.4 3.4 %collective-permute-start.15 = (bf16[64,1024]{1,0:T(8,128)(2,1)S(1)}, bf16[64,1024]{1,0:T(8,128)(2,1)S(1)}, u32[]{:S(2)}, u32[]{:S(2)}) collective-permute-start(bf16[64,1024]{1,0:T(8,128)(2,1)S(1)} %get-tuple-element.23), channel_id=1, source_target_pairs={{0,4},{4,8},{8,12},{12,0},{1,5},{5,9},{9,13},{13,1},{2,6},{6,10},{... | collective-permute-start | bytes 393224 | tf_op jit(solution)/shard_map/ppermute | solution.py:35
  168.8 2.5 %collective-permute-start.16 = (bf16[64,1024]{1,0:T(8,128)(2,1)S(1)}, bf16[64,1024]{1,0:T(8,128)(2,1)S(1)}, u32[]{:S(2)}, u32[]{:S(2)}) collective-permute-start(bf16[64,1024]{1,0:T(8,128)(2,1)S(1)} %get-tuple-element.24), channel_id=1, source_target_pairs={{0,12},{4,0},{8,4},{12,8},{1,13},{5,1},{9,5},{13,9},{2,14},{6,2},{... | collective-permute-start | bytes 393224 | tf_op jit(solution)/shard_map/ppermute | solution.py:35
  171.3 9.8 %collective-permute-done.14.refs_1_ = bf16[64,1024]{1,0:T(8,128)(2,1)S(1)} collective-permute-done((bf16[64,1024]{1,0:T(8,128)(2,1)S(1)}, bf16[64,1024]{1,0:T(8,128)(2,1)S(1)}, u32[]{:S(2)}, u32[]{:S(2)}) %collective-permute-start.14) | collective-permute-done | bytes 131104 | tf_op jit(solution)/shard_map/ppermute | solution.py:35
  181.1 4.7 %collective-permute-done.15.refs_2_ = bf16[64,1024]{1,0:T(8,128)(2,1)S(1)} collective-permute-done((bf16[64,1024]{1,0:T(8,128)(2,1)S(1)}, bf16[64,1024]{1,0:T(8,128)(2,1)S(1)}, u32[]{:S(2)}, u32[]{:S(2)}) %collective-permute-start.15) | collective-permute-done | bytes 131104 | tf_op jit(solution)/shard_map/ppermute | solution.py:35
  (82 shorter events, 39.8 us)
Async XLA Ops:
  0.6 24.5 %copy-start = (bf16[128,1024]{1,0:T(8,128)(2,1)S(1)}, bf16[128,1024]{1,0:T(8,128)(2,1)}, u32[]{:S(2)}) copy-start(bf16[128,1024]{1,0:T(8,128)(2,1)} %act_ref.1) | copy-start | bytes 786436
  1.8 34.9 %collective-permute-start.4 = (bf16[5,72,512]{2,1,0:T(8,128)(2,1)S(1)}, bf16[5,72,512]{2,1,0:T(8,128)(2,1)S(1)}, u32[]{:S(2)}, u32[]{:S(2)}) collective-permute-start(bf16[5,72,512]{2,1,0:T(8,128)(2,1)S(1)} %slice_select_fusion), channel_id=1, source_target_pairs={{0,3},{1,0},{2,1},{3,2},{4,7},{5,4},{6,5},{7,6},{8,11},{9,8},{10,9... | collective-permute-start | bytes 1105928 | tf_op jit(solution)/shard_map/ppermute | solution.py:35
  6.8 28.9 %collective-permute-start.3 = (bf16[5,72,512]{2,1,0:T(8,128)(2,1)S(1)}, bf16[5,72,512]{2,1,0:T(8,128)(2,1)}, u32[]{:S(2)}, u32[]{:S(2)}) collective-permute-start(bf16[5,72,512]{2,1,0:T(8,128)(2,1)S(1)} %slice_select_fusion), channel_id=1, source_target_pairs={{0,2},{1,3},{2,0},{3,1},{4,6},{5,7},{6,4},{7,5},{8,10},{9,11},{10,... | collective-permute-start | bytes 1105928 | tf_op jit(solution)/shard_map/ppermute | solution.py:35
  9.3 25.4 %collective-permute-start.2 = (bf16[5,72,512]{2,1,0:T(8,128)(2,1)S(1)}, bf16[5,72,512]{2,1,0:T(8,128)(2,1)}, u32[]{:S(2)}, u32[]{:S(2)}) collective-permute-start(bf16[5,72,512]{2,1,0:T(8,128)(2,1)S(1)} %slice_select_fusion), channel_id=1, source_target_pairs={{0,1},{1,2},{2,3},{3,0},{4,5},{5,6},{6,7},{7,4},{8,9},{9,10},{10,1... | collective-permute-start | bytes 1105928 | tf_op jit(solution)/shard_map/ppermute | solution.py:35
  12.9 9.6 %collective-permute-start.1 = (bf16[8,1024]{1,0:T(8,128)(2,1)S(1)}, bf16[8,1024]{1,0:T(8,128)(2,1)S(1)}, u32[]{:S(2)}, u32[]{:S(2)}) collective-permute-start(bf16[8,1024]{1,0:T(8,128)(2,1)S(1)} %get-tuple-element.33), channel_id=1, source_target_pairs={{1,0},{2,1},{3,2},{4,3},{5,4},{6,5},{7,6},{8,7},{9,8},{10,9},{11,1... | collective-permute-start | bytes 49160 | tf_op jit(solution)/shard_map/ppermute | solution.py:30
  16.7 8.5 %collective-permute-start = (bf16[8,1024]{1,0:T(8,128)(2,1)S(1)}, bf16[8,1024]{1,0:T(8,128)(2,1)S(1)}, u32[]{:S(2)}, u32[]{:S(2)}) collective-permute-start(bf16[8,1024]{1,0:T(8,128)(2,1)S(1)} %get-tuple-element.34), channel_id=1, source_target_pairs={{0,1},{1,2},{2,3},{3,4},{4,5},{5,6},{6,7},{7,8},{8,9},{9,10},{10,1... | collective-permute-start | bytes 49160 | tf_op jit(solution)/shard_map/ppermute | solution.py:30
  26.7 29.2 %all-to-all-start = ((bf16[4,72,1024]{2,1,0:T(8,128)(2,1)}), bf16[4,72,1024]{2,1,0:T(8,128)(2,1)S(1)}, u32[]{:S(2)}, u32[]{:S(2)}) async-start(bf16[4,72,1024]{2,1,0:T(8,128)(2,1)} %broadcast_in_dim.18), calls=%async_computation | async-start | bytes 1179648 | tf_op jit(solution)/shard_map/all_to_all | solution.py:40
  36.8 19.1 %collective-permute-start.5 = (bf16[5,288,512]{2,1,0:T(8,128)(2,1)S(1)}, bf16[5,288,512]{2,1,0:T(8,128)(2,1)S(1)}, u32[]{:S(2)}, u32[]{:S(2)}) collective-permute-start(bf16[5,288,512]{2,1,0:T(8,128)(2,1)S(1)} %bitcast.31), channel_id=1, source_target_pairs={{0,16},{16,0},{1,17},{17,1},{2,18},{18,2},{3,19},{19,3},{4,20},{20... | collective-permute-start | bytes 4423688 | tf_op jit(solution)/shard_map/ppermute | solution.py:311
  42.2 8.8 %collective-permute-start.8 = (bf16[4,32,72]{2,1,0:T(8,128)(2,1)S(1)}, bf16[4,32,72]{2,1,0:T(8,128)(2,1)S(1)}, u32[]{:S(2)}, u32[]{:S(2)}) collective-permute-start(bf16[4,32,72]{2,1,0:T(8,128)(2,1)S(1)} %get-tuple-element.35), channel_id=1, source_target_pairs={{0,3},{1,0},{2,1},{3,2},{4,7},{5,4},{6,5},{7,6},{8,11},{9,8},{10,9... | collective-permute-start | bytes 55304 | tf_op jit(solution)/shard_map/ppermute | solution.py:35
  45.7 7.3 %collective-permute-start.7 = (bf16[4,32,72]{2,1,0:T(8,128)(2,1)S(1)}, bf16[4,32,72]{2,1,0:T(8,128)(2,1)S(1)}, u32[]{:S(2)}, u32[]{:S(2)}) collective-permute-start(bf16[4,32,72]{2,1,0:T(8,128)(2,1)S(1)} %get-tuple-element.36), channel_id=1, source_target_pairs={{0,2},{1,3},{2,0},{3,1},{4,6},{5,7},{6,4},{7,5},{8,10},{9,11},{10,... | collective-permute-start | bytes 55304 | tf_op jit(solution)/shard_map/ppermute | solution.py:35
  48.2 7.0 %collective-permute-start.6 = (bf16[4,32,72]{2,1,0:T(8,128)(2,1)S(1)}, bf16[4,32,72]{2,1,0:T(8,128)(2,1)S(1)}, u32[]{:S(2)}, u32[]{:S(2)}) collective-permute-start(bf16[4,32,72]{2,1,0:T(8,128)(2,1)S(1)} %get-tuple-element.37), channel_id=1, source_target_pairs={{0,1},{1,2},{2,3},{3,0},{4,5},{5,6},{6,7},{7,4},{8,9},{9,10},{10,1... | collective-permute-start | bytes 55304 | tf_op jit(solution)/shard_map/ppermute | solution.py:35
  77.5 39.9 %all-to-all-start.2 = ((bf16[16,96,128]{2,1,0:T(8,128)(2,1)}), bf16[16,96,128]{2,1,0:T(8,128)(2,1)}, u32[]{:S(2)}, u32[]{:S(2)}) async-start(bf16[16,96,128]{2,1,0:T(8,128)(2,1)} %copy-done.9), calls=%async_computation.2 | async-start | bytes 786432 | tf_op jit(solution)/shard_map/all_to_all | solution.py:328
  83.0 21.8 %collective-permute-start.11 = (bf16[288,1024]{1,0:T(8,128)(2,1)S(1)}, bf16[288,1024]{1,0:T(8,128)(2,1)S(1)}, u32[]{:S(2)}, u32[]{:S(2)}) collective-permute-start(bf16[288,1024]{1,0:T(8,128)(2,1)S(1)} %bitcast.35), channel_id=1, source_target_pairs={{0,2},{1,3},{2,0},{3,1},{4,6},{5,7},{6,4},{7,5},{8,10},{9,11},{10,... | collective-permute-start | bytes 1769480 | tf_op jit(solution)/shard_map/ppermute | solution.py:35
  87.9 27.2 %collective-permute-start.10 = (bf16[288,1024]{1,0:T(8,128)(2,1)S(1)}, bf16[288,1024]{1,0:T(8,128)(2,1)S(1)}, u32[]{:S(2)}, u32[]{:S(2)}) collective-permute-start(bf16[288,1024]{1,0:T(8,128)(2,1)S(1)} %bitcast.36), channel_id=1, source_target_pairs={{0,3},{1,0},{2,1},{3,2},{4,7},{5,4},{6,5},{7,6},{8,11},{9,8},{10,9... | collective-permute-start | bytes 1769480 | tf_op jit(solution)/shard_map/ppermute | solution.py:35
  90.9 25.7 %collective-permute-start.9 = (bf16[288,1024]{1,0:T(8,128)(2,1)S(1)}, bf16[288,1024]{1,0:T(8,128)(2,1)S(1)}, u32[]{:S(2)}, u32[]{:S(2)}) collective-permute-start(bf16[288,1024]{1,0:T(8,128)(2,1)S(1)} %bitcast.37), channel_id=1, source_target_pairs={{0,1},{1,2},{2,3},{3,0},{4,5},{5,6},{6,7},{7,4},{8,9},{9,10},{10,1... | collective-permute-start | bytes 1769480 | tf_op jit(solution)/shard_map/ppermute | solution.py:35
  93.7 35.8 %collective-permute-start.12 = (bf16[4,8,288]{2,1,0:T(8,128)(2,1)}, bf16[4,8,288]{2,1,0:T(8,128)(2,1)}, u32[]{:S(2)}, u32[]{:S(2)}) collective-permute-start(bf16[4,8,288]{2,1,0:T(8,128)(2,1)} %copy-done.22), channel_id=1, source_target_pairs={{0,1},{1,2},{2,3},{3,4},{4,5},{5,6},{6,7},{7,8},{8,9},{9,10},{10,1... | collective-permute-start | bytes 55304 | tf_op jit(solution)/shard_map/ppermute | solution.py:30
  96.2 33.4 %collective-permute-start.13 = (bf16[4,8,288]{2,1,0:T(8,128)(2,1)}, bf16[4,8,288]{2,1,0:T(8,128)(2,1)}, u32[]{:S(2)}, u32[]{:S(2)}) collective-permute-start(bf16[4,8,288]{2,1,0:T(8,128)(2,1)} %copy-done.21), channel_id=1, source_target_pairs={{1,0},{2,1},{3,2},{4,3},{5,4},{6,5},{7,6},{8,7},{9,8},{10,9},{11,1... | collective-permute-start | bytes 55304 | tf_op jit(solution)/shard_map/ppermute | solution.py:30
  104.8 0.8 copy-start.3
  115.1 0.8 copy-start.5
  117.4 1.1 copy-start.4
  118.5 1.1 copy-start.6
  119.5 1.1 copy-start.8
  120.6 9.0 %copy-start.11 = (bf16[4,64,288]{2,1,0:T(8,128)(2,1)S(1)}, bf16[4,64,288]{2,1,0:T(8,128)(2,1)}, u32[]{:S(2)}) copy-start(bf16[4,64,288]{2,1,0:T(8,128)(2,1)} %copy-done.10) | copy-start | bytes 442372
  126.0 0.9 copy-start.2
  127.5 8.2 %collective-permute-start.17 = (bf16[16,32,360]{2,1,0:T(8,128)(2,1)}, bf16[16,32,360]{2,1,0:T(8,128)(2,1)}, u32[]{:S(2)}, u32[]{:S(2)}) collective-permute-start(bf16[16,32,360]{2,1,0:T(8,128)(2,1)} %get-tuple-element.26), channel_id=1, source_target_pairs={{0,16},{16,0},{1,17},{17,1},{2,18},{18,2},{3,19},{19,3},{4,20},{20... | collective-permute-start | bytes 1105928 | tf_op jit(solution)/shard_map/ppermute | solution.py:341
  131.1 11.9 %all-to-all-start.3 = ((bf16[4,80,288]{2,1,0:T(8,128)(2,1)}), bf16[4,80,288]{2,1,0:T(8,128)(2,1)S(1)}, u32[]{:S(2)}, u32[]{:S(2)}) async-start(bf16[4,80,288]{2,1,0:T(8,128)(2,1)} %pad_maximum_fusion), calls=%async_computation.3 | async-start | bytes 491520 | tf_op jit(solution)/shard_map/all_to_all | solution.py:331
  143.0 46.5 %all-to-all-start.4 = ((bf16[16,32,360]{2,1,0:T(8,128)(2,1)}), bf16[16,32,360]{2,1,0:T(8,128)(2,1)}, u32[]{:S(2)}, u32[]{:S(2)}) async-start(bf16[16,32,360]{2,1,0:T(8,128)(2,1)} %add_convert_fusion), calls=%async_computation.4 | async-start | bytes 786432 | tf_op jit(solution)/shard_map/all_to_all | solution.py:343
  158.6 28.7 %copy-start.1 = (bf16[128,1024]{1,0:T(8,128)(2,1)S(1)}, bf16[128,1024]{1,0:T(8,128)(2,1)}, u32[]{:S(2)}) copy-start(bf16[128,1024]{1,0:T(8,128)(2,1)} %act_ref.1) | copy-start | bytes 786436
  158.6 30.1 %copy-start.14 = (bf16[512,72]{1,0:T(8,128)(2,1)S(1)}, bf16[512,72]{1,0:T(8,128)(2,1)}, u32[]{:S(2)}) copy-start(bf16[512,72]{1,0:T(8,128)(2,1)} %copy-done.13) | copy-start | bytes 221188
  161.6 19.5 %collective-permute-start.14 = (bf16[64,1024]{1,0:T(8,128)(2,1)S(1)}, bf16[64,1024]{1,0:T(8,128)(2,1)S(1)}, u32[]{:S(2)}, u32[]{:S(2)}) collective-permute-start(bf16[64,1024]{1,0:T(8,128)(2,1)S(1)} %get-tuple-element.22), channel_id=1, source_target_pairs={{0,8},{4,12},{8,0},{12,4},{1,9},{5,13},{9,1},{13,5},{2,10},{6,14},... | collective-permute-start | bytes 393224 | tf_op jit(solution)/shard_map/ppermute | solution.py:35
  165.4 20.4 %collective-permute-start.15 = (bf16[64,1024]{1,0:T(8,128)(2,1)S(1)}, bf16[64,1024]{1,0:T(8,128)(2,1)S(1)}, u32[]{:S(2)}, u32[]{:S(2)}) collective-permute-start(bf16[64,1024]{1,0:T(8,128)(2,1)S(1)} %get-tuple-element.23), channel_id=1, source_target_pairs={{0,4},{4,8},{8,12},{12,0},{1,5},{5,9},{9,13},{13,1},{2,6},{6,10},{... | collective-permute-start | bytes 393224 | tf_op jit(solution)/shard_map/ppermute | solution.py:35
  168.8 18.5 %collective-permute-start.16 = (bf16[64,1024]{1,0:T(8,128)(2,1)S(1)}, bf16[64,1024]{1,0:T(8,128)(2,1)S(1)}, u32[]{:S(2)}, u32[]{:S(2)}) collective-permute-start(bf16[64,1024]{1,0:T(8,128)(2,1)S(1)} %get-tuple-element.24), channel_id=1, source_target_pairs={{0,12},{4,0},{8,4},{12,8},{1,13},{5,1},{9,5},{13,9},{2,14},{6,2},{... | collective-permute-start | bytes 393224 | tf_op jit(solution)/shard_map/ppermute | solution.py:35
  (13 other events, 9.0 us)

commit v8 on v7

--- a/solution.py
+++ b/solution.py
@@ -150,7 +150,7 @@
     return local_call(kernel, shapes, scratch, where, flat, first, second, limit=16)
 
 
-def statistics_kernel(own, y_ref, grad_ref, back_ref, head_ref, tail_ref):
+def statistics_kernel(own, y_ref, grad_ref, back_ref, edge_ref):
     groups, _, width = y_ref.shape
     full = groups * width
     pairs = own // 2
@@ -185,8 +185,8 @@
         normed = y_ref[g, :own, :].astype(f32) * inv
         grad = (inv * (slopes[g] - normed * mean)).astype(bf16)
         grad_ref[g] = grad
-        head_ref[g] = grad_ref[g, :8, :]
-        tail_ref[g] = grad_ref[g, own - 8 :, :]
+        edge_ref[0, g] = grad_ref[g, :8, :]
+        edge_ref[1, g] = grad_ref[g, own - 8 :, :]
         placed = jnp.dot(grad, spread, preferred_element_type=f32).astype(bf16)
         for i in range(4):
             back_ref[4 * g + i, pairs:, :] = placed[:, 128 * i : 128 * i + 128]
@@ -197,8 +197,7 @@
     shapes = (
         jax.ShapeDtypeStruct((groups, own, width), bf16),
         jax.ShapeDtypeStruct((4 * groups, own + own // 2, 128), bf16),
-        jax.ShapeDtypeStruct((groups, 8, width), bf16),
-        jax.ShapeDtypeStruct((groups, 8, width), bf16),
+        jax.ShapeDtypeStruct((2, groups, 8, width), bf16),
     )
     kernel = functools.partial(statistics_kernel, own)
     return local_call(kernel, shapes, [], conv_out)
@@ -324,10 +323,10 @@
     up, down = turn(flat, "y", 1), turn(flat, "y", -1)
     far = turn(flat, "y", 2)
     conv_out = lax.all_to_all(conv_out, "zl", 0, 0)
-    grad, back, head, tail = statistics(conv_out, rows)
+    grad, back, edge = statistics(conv_out, rows)
     back = lax.all_to_all(back, SUB, 0, 0)
-    tail, head = shift(tail, AXES, 1), shift(head, AXES, -1)
-    framed = jnp.concatenate([tail, grad, head], axis=1)
+    low, high = shift(edge, AXES, 1), shift(edge, AXES, -1)
+    framed = jnp.concatenate([low[1], grad, high[0]], axis=1)
     framed = lax.all_to_all(framed, "zl", 0, 0)
 
     own = conv_backward(where, framed.reshape(-1, group), first, second, rows)

time: 193 us -> 195 us (1.010)
  the two profiles are of different devices: /device:TPU:34 before, /device:TPU:35 now
where the time goes in v8:
time: 195 us; the launch traced here: 193 us
  starting transfers between devices  89.2 us (46%)
  waiting for transfers between devices  48.7 us (25%)
  local copies, waits for them, and re-layouts  23.8 us (12%)
  Pallas kernels  14.5 us (7%)
  blocking collectives  10.5 us (5%)
  other arithmetic  5.11 us (3%)
    ppermute x12, starting transfers between devices, turn(): lax.ppermute(block, axis, [(i, (i + step) % count) for i in range(count)])  36.4 us
    ppermute x4, waiting for transfers between devices, shift(): return lax.ppermute(block, axis, pairs)  23.6 us
    ppermute x12, waiting for transfers between devices, turn(): lax.ppermute(block, axis, [(i, (i + step) % count) for i in range(count)])  20.3 us
    unnamed x50, local copies, waits for them, and re-layouts  15.6 us
    all_to_all x1, starting transfers between devices, per_device(): total = lax.all_to_all(total, ('zh', 'x'), 0, 0)  15.1 us
    pallas_call x6, Pallas kernels, local_call(): pl.pallas_call(kernel, out_shape=shapes, in_specs=[pl.BlockSpec(memory_sp...  14.5 us
    ppermute x4, starting transfers between devices, shift(): return lax.ppermute(block, axis, pairs)  11.3 us
    all_to_all x1, blocking collectives, per_device(): conv_out = lax.all_to_all(conv_out, 'zl', 0, 0)  10.5 us
  transfers between devices with their start and end apart: 22, of which 9 were waited for; matrix products, arithmetic and copies ran while one was open for 6% of the time, Pallas kernels for 3%

profile of v8, /device:TPU:35, one launch (start us, length us, event | category | flops | bytes accessed | tf_op | source)
XLA Modules:
  0.0 192.9 jit_solution(6477243942121331650)
XLA Ops:
  1.8 4.6 %collective-permute-start.4 = (bf16[5,72,512]{2,1,0:T(8,128)(2,1)S(1)}, bf16[5,72,512]{2,1,0:T(8,128)(2,1)S(1)}, u32[]{:S(2)}, u32[]{:S(2)}) collective-permute-start(bf16[5,72,512]{2,1,0:T(8,128)(2,1)S(1)} %slice_select_fusion), channel_id=1, source_target_pairs={{0,3},{1,0},{2,1},{3,2},{4,7},{5,4},{6,5},{7,6},{8,11},{9,8},{10,9... | collective-permute-start | bytes 1105928 | tf_op jit(solution)/shard_map/ppermute | solution.py:35
  6.5 2.3 %collective-permute-start.3 = (bf16[5,72,512]{2,1,0:T(8,128)(2,1)S(1)}, bf16[5,72,512]{2,1,0:T(8,128)(2,1)}, u32[]{:S(2)}, u32[]{:S(2)}) collective-permute-start(bf16[5,72,512]{2,1,0:T(8,128)(2,1)S(1)} %slice_select_fusion), channel_id=1, source_target_pairs={{0,2},{1,3},{2,0},{3,1},{4,6},{5,7},{6,4},{7,5},{8,10},{9,11},{10,... | collective-permute-start | bytes 1105928 | tf_op jit(solution)/shard_map/ppermute | solution.py:35
  8.8 2.6 %collective-permute-start.2 = (bf16[5,72,512]{2,1,0:T(8,128)(2,1)S(1)}, bf16[5,72,512]{2,1,0:T(8,128)(2,1)}, u32[]{:S(2)}, u32[]{:S(2)}) collective-permute-start(bf16[5,72,512]{2,1,0:T(8,128)(2,1)S(1)} %slice_select_fusion), channel_id=1, source_target_pairs={{0,1},{1,2},{2,3},{3,0},{4,5},{5,6},{6,7},{7,4},{8,9},{9,10},{10,1... | collective-permute-start | bytes 1105928 | tf_op jit(solution)/shard_map/ppermute | solution.py:35
  12.1 3.4 %collective-permute-start.1 = (bf16[8,1024]{1,0:T(8,128)(2,1)S(1)}, bf16[8,1024]{1,0:T(8,128)(2,1)S(1)}, u32[]{:S(2)}, u32[]{:S(2)}) collective-permute-start(bf16[8,1024]{1,0:T(8,128)(2,1)S(1)} %get-tuple-element.31), channel_id=1, source_target_pairs={{1,0},{2,1},{3,2},{4,3},{5,4},{6,5},{7,6},{8,7},{9,8},{10,9},{11,1... | collective-permute-start | bytes 49160 | tf_op jit(solution)/shard_map/ppermute | solution.py:30
  15.5 2.0 %collective-permute-start = (bf16[8,1024]{1,0:T(8,128)(2,1)S(1)}, bf16[8,1024]{1,0:T(8,128)(2,1)S(1)}, u32[]{:S(2)}, u32[]{:S(2)}) collective-permute-start(bf16[8,1024]{1,0:T(8,128)(2,1)S(1)} %get-tuple-element.32), channel_id=1, source_target_pairs={{0,1},{1,2},{2,3},{3,4},{4,5},{5,6},{6,7},{7,8},{8,9},{9,10},{10,1... | collective-permute-start | bytes 49160 | tf_op jit(solution)/shard_map/ppermute | solution.py:30
  17.8 4.0 %collective-permute-done.1.high_ref = bf16[8,1024]{1,0:T(8,128)(2,1)S(1)} collective-permute-done((bf16[8,1024]{1,0:T(8,128)(2,1)S(1)}, bf16[8,1024]{1,0:T(8,128)(2,1)S(1)}, u32[]{:S(2)}, u32[]{:S(2)}) %collective-permute-start.1) | collective-permute-done | bytes 16416 | tf_op jit(solution)/shard_map/ppermute | solution.py:30
  21.8 2.2 %collective-permute-done.low_ref = bf16[8,1024]{1,0:T(8,128)(2,1)S(1)} collective-permute-done((bf16[8,1024]{1,0:T(8,128)(2,1)S(1)}, bf16[8,1024]{1,0:T(8,128)(2,1)S(1)}, u32[]{:S(2)}, u32[]{:S(2)}) %collective-permute-start) | collective-permute-done | bytes 16416 | tf_op jit(solution)/shard_map/ppermute | solution.py:30
  25.5 9.7 %all-to-all-start = ((bf16[4,72,1024]{2,1,0:T(8,128)(2,1)}), bf16[4,72,1024]{2,1,0:T(8,128)(2,1)S(1)}, u32[]{:S(2)}, u32[]{:S(2)}) async-start(bf16[4,72,1024]{2,1,0:T(8,128)(2,1)} %broadcast_in_dim.18), calls=%async_computation | async-start | bytes 1179648 | tf_op jit(solution)/shard_map/all_to_all | solution.py:40
  37.3 2.1 %collective-permute-start.5 = (bf16[5,288,512]{2,1,0:T(8,128)(2,1)S(1)}, bf16[5,288,512]{2,1,0:T(8,128)(2,1)S(1)}, u32[]{:S(2)}, u32[]{:S(2)}) collective-permute-start(bf16[5,288,512]{2,1,0:T(8,128)(2,1)S(1)} %bitcast.35), channel_id=1, source_target_pairs={{0,16},{16,0},{1,17},{17,1},{2,18},{18,2},{3,19},{19,3},{4,20},{20... | collective-permute-start | bytes 4423688 | tf_op jit(solution)/shard_map/ppermute | solution.py:310
  42.5 3.5 %collective-permute-start.8 = (bf16[4,32,72]{2,1,0:T(8,128)(2,1)S(1)}, bf16[4,32,72]{2,1,0:T(8,128)(2,1)S(1)}, u32[]{:S(2)}, u32[]{:S(2)}) collective-permute-start(bf16[4,32,72]{2,1,0:T(8,128)(2,1)S(1)} %get-tuple-element.33), channel_id=1, source_target_pairs={{0,3},{1,0},{2,1},{3,2},{4,7},{5,4},{6,5},{7,6},{8,11},{9,8},{10,9... | collective-permute-start | bytes 55304 | tf_op jit(solution)/shard_map/ppermute | solution.py:35
  46.1 2.3 %collective-permute-start.7 = (bf16[4,32,72]{2,1,0:T(8,128)(2,1)S(1)}, bf16[4,32,72]{2,1,0:T(8,128)(2,1)S(1)}, u32[]{:S(2)}, u32[]{:S(2)}) collective-permute-start(bf16[4,32,72]{2,1,0:T(8,128)(2,1)S(1)} %get-tuple-element.34), channel_id=1, source_target_pairs={{0,2},{1,3},{2,0},{3,1},{4,6},{5,7},{6,4},{7,5},{8,10},{9,11},{10,... | collective-permute-start | bytes 55304 | tf_op jit(solution)/shard_map/ppermute | solution.py:35
  48.3 2.4 %collective-permute-start.6 = (bf16[4,32,72]{2,1,0:T(8,128)(2,1)S(1)}, bf16[4,32,72]{2,1,0:T(8,128)(2,1)S(1)}, u32[]{:S(2)}, u32[]{:S(2)}) collective-permute-start(bf16[4,32,72]{2,1,0:T(8,128)(2,1)S(1)} %get-tuple-element.35), channel_id=1, source_target_pairs={{0,1},{1,2},{2,3},{3,0},{4,5},{5,6},{6,7},{7,4},{8,9},{9,10},{10,1... | collective-permute-start | bytes 55304 | tf_op jit(solution)/shard_map/ppermute | solution.py:35
  57.8 2.5 %shard_map.59 = bf16[4,96,288]{2,1,0:T(8,128)(2,1)S(1)} custom-call(s32[3]{0:T(128)S(1)} %pad_add_fusion.where_ref, bf16[288,1024]{1,0:T(8,128)(2,1)S(1)} %bitcast.38, bf16[5,288,512]{2,1,0:T(8,128)(2,1)S(1)} %bitcast.36, bf16[5,288,512]{2,1,0:T(8,128)(2,1)S(1)} %collective-permute-done.5.second_ref, bf16[4,32,72]{2,1,0:T(8,128)(2,1)S(1)} %copy-done.12, ...), custom_call_target="tpu_custom_call" | custom-call | tf_op jit(solution)/shard_map/pallas_call | solution.py:45
  60.4 10.5 %all_to_all.25.y_ref = bf16[4,96,288]{2,1,0:T(8,128)(2,1)S(1)} all-to-all(bf16[4,96,288]{2,1,0:T(8,128)(2,1)S(1)} %shard_map.59), channel_id=1, replica_groups=mesh['zh'=4,'x'=4,'core'=2,'zl'=4,'y'=4] {'zl'}, dimensions={0} | all-to-all | bytes 442368 | tf_op jit(solution)/shard_map/all_to_all | solution.py:325
  74.5 6.7 %all-to-all-start.2 = ((bf16[16,96,128]{2,1,0:T(8,128)(2,1)}), bf16[16,96,128]{2,1,0:T(8,128)(2,1)}, u32[]{:S(2)}, u32[]{:S(2)}) async-start(bf16[16,96,128]{2,1,0:T(8,128)(2,1)} %copy-done.9), calls=%async_computation.2 | async-start | bytes 786432 | tf_op jit(solution)/shard_map/all_to_all | solution.py:327
  81.1 4.6 %collective-permute-start.11 = (bf16[288,1024]{1,0:T(8,128)(2,1)S(1)}, bf16[288,1024]{1,0:T(8,128)(2,1)S(1)}, u32[]{:S(2)}, u32[]{:S(2)}) collective-permute-start(bf16[288,1024]{1,0:T(8,128)(2,1)S(1)} %bitcast.39), channel_id=1, source_target_pairs={{0,2},{1,3},{2,0},{3,1},{4,6},{5,7},{6,4},{7,5},{8,10},{9,11},{10,... | collective-permute-start | bytes 1769480 | tf_op jit(solution)/shard_map/ppermute | solution.py:35
  85.7 2.8 %collective-permute-start.10 = (bf16[288,1024]{1,0:T(8,128)(2,1)S(1)}, bf16[288,1024]{1,0:T(8,128)(2,1)S(1)}, u32[]{:S(2)}, u32[]{:S(2)}) collective-permute-start(bf16[288,1024]{1,0:T(8,128)(2,1)S(1)} %bitcast.40), channel_id=1, source_target_pairs={{0,3},{1,0},{2,1},{3,2},{4,7},{5,4},{6,5},{7,6},{8,11},{9,8},{10,9... | collective-permute-start | bytes 1769480 | tf_op jit(solution)/shard_map/ppermute | solution.py:35
  88.5 2.5 %collective-permute-start.9 = (bf16[288,1024]{1,0:T(8,128)(2,1)S(1)}, bf16[288,1024]{1,0:T(8,128)(2,1)S(1)}, u32[]{:S(2)}, u32[]{:S(2)}) collective-permute-start(bf16[288,1024]{1,0:T(8,128)(2,1)S(1)} %bitcast.41), channel_id=1, source_target_pairs={{0,1},{1,2},{2,3},{3,0},{4,5},{5,6},{6,7},{7,4},{8,9},{9,10},{10,1... | collective-permute-start | bytes 1769480 | tf_op jit(solution)/shard_map/ppermute | solution.py:35
  91.0 4.0 %collective-permute-start.13 = (bf16[2,4,8,288]{3,2,1,0:T(8,128)(2,1)}, bf16[2,4,8,288]{3,2,1,0:T(8,128)(2,1)S(1)}, u32[]{:S(2)}, u32[]{:S(2)}) collective-permute-start(bf16[2,4,8,288]{3,2,1,0:T(8,128)(2,1)} %copy-done.21), channel_id=1, source_target_pairs={{1,0},{2,1},{3,2},{4,3},{5,4},{6,5},{7,6},{8,7},{9,8},{10,9},{11,1... | collective-permute-start | bytes 110600 | tf_op jit(solution)/shard_map/ppermute | solution.py:30
  97.0 17.4 %collective-permute-done.13 = bf16[2,4,8,288]{3,2,1,0:T(8,128)(2,1)S(1)} collective-permute-done((bf16[2,4,8,288]{3,2,1,0:T(8,128)(2,1)}, bf16[2,4,8,288]{3,2,1,0:T(8,128)(2,1)S(1)}, u32[]{:S(2)}, u32[]{:S(2)}) %collective-permute-start.13) | collective-permute-done | bytes 36896 | tf_op jit(solution)/shard_map/ppermute | solution.py:30
  121.2 5.4 %shard_map.61 = (f32[16,32,360]{2,1,0:T(8,128)S(1)}, bf16[16,32,360]{2,1,0:T(8,128)(2,1)}, bf16[512,72]{1,0:T(8,128)(2,1)S(1)}) custom-call(s32[3]{0:T(128)S(1)} %pad_add_fusion.where_ref, bf16[16,96,128]{2,1,0:T(8,128)(2,1)} %all-to-all-done.2.back_ref, bf16[288,1024]{1,0:T(8,128)(2,1)S(1)} %bitcast.42, bf16[288,1024]{1,0:T(8,128)(2,1)S(1)} %copy-done.8, ...), custom_call_target="tpu_custom_call" | custom-call | tf_op jit(solution)/shard_map/pallas_call | solution.py:45
  128.2 4.1 %collective-permute-start.17 = (bf16[16,32,360]{2,1,0:T(8,128)(2,1)}, bf16[16,32,360]{2,1,0:T(8,128)(2,1)}, u32[]{:S(2)}, u32[]{:S(2)}) collective-permute-start(bf16[16,32,360]{2,1,0:T(8,128)(2,1)} %get-tuple-element.24), channel_id=1, source_target_pairs={{0,16},{16,0},{1,17},{17,1},{2,18},{18,2},{3,19},{19,3},{4,20},{20... | collective-permute-start | bytes 1105928 | tf_op jit(solution)/shard_map/ppermute | solution.py:340
  133.0 3.9 %all-to-all-start.3 = ((bf16[4,80,288]{2,1,0:T(8,128)(2,1)}), bf16[4,80,288]{2,1,0:T(8,128)(2,1)S(1)}, u32[]{:S(2)}, u32[]{:S(2)}) async-start(bf16[4,80,288]{2,1,0:T(8,128)(2,1)} %pad_maximum_fusion), calls=%async_computation.3 | async-start | bytes 491520 | tf_op jit(solution)/shard_map/all_to_all | solution.py:330
  136.9 2.1 %add_convert_fusion = bf16[16,32,360]{2,1,0:T(8,128)(2,1)} fusion(f32[16,32,360]{2,1,0:T(8,128)} %copy-done.2, bf16[16,32,360]{2,1,0:T(8,128)(2,1)} %collective-permute-done.17), kind=kLoop, calls=%fused_computation.1 | loop fusion | flops 552960 | bytes 1474560 | tf_op jit(solution)/shard_map/convert_element_type | solution.py:341
  139.0 4.8 %all-to-all-done.3 = bf16[4,80,288]{2,1,0:T(8,128)(2,1)S(1)} async-done(((bf16[4,80,288]{2,1,0:T(8,128)(2,1)}), bf16[4,80,288]{2,1,0:T(8,128)(2,1)S(1)}, u32[]{:S(2)}, u32[]{:S(2)}) %all-to-all-start.3) | async-done | bytes 184352 | tf_op jit(solution)/shard_map/all_to_all | solution.py:330
  143.8 15.1 %all-to-all-start.4 = ((bf16[16,32,360]{2,1,0:T(8,128)(2,1)}), bf16[16,32,360]{2,1,0:T(8,128)(2,1)}, u32[]{:S(2)}, u32[]{:S(2)}) async-start(bf16[16,32,360]{2,1,0:T(8,128)(2,1)} %add_convert_fusion), calls=%async_computation.4 | async-start | bytes 786432 | tf_op jit(solution)/shard_map/all_to_all | solution.py:342
  158.9 3.0 %shard_map.62 = (bf16[64,1024]{1,0:T(8,128)(2,1)S(1)}, bf16[64,1024]{1,0:T(8,128)(2,1)S(1)}, bf16[64,1024]{1,0:T(8,128)(2,1)S(1)}, bf16[64,1024]{1,0:T(8,128)(2,1)S(1)}) custom-call(s32[3]{0:T(128)S(1)} %pad_add_fusion.where_ref, bf16[320,288]{1,0:T(8,128)(2,1)S(1)} %bitcast.43, bf16[5,288,512]{2,1,0:T(8,128)(2,1)S(1)} %bitcast.37, ...), custom_call_target="tpu_custom_call" | custom-call | tf_op jit(solution)/shard_map/pallas_call | solution.py:45
  161.9 3.5 %collective-permute-start.14 = (bf16[64,1024]{1,0:T(8,128)(2,1)S(1)}, bf16[64,1024]{1,0:T(8,128)(2,1)S(1)}, u32[]{:S(2)}, u32[]{:S(2)}) collective-permute-start(bf16[64,1024]{1,0:T(8,128)(2,1)S(1)} %get-tuple-element.20), channel_id=1, source_target_pairs={{0,8},{4,12},{8,0},{12,4},{1,9},{5,13},{9,1},{13,5},{2,10},{6,14},... | collective-permute-start | bytes 393224 | tf_op jit(solution)/shard_map/ppermute | solution.py:35
  165.4 2.2 %collective-permute-start.15 = (bf16[64,1024]{1,0:T(8,128)(2,1)S(1)}, bf16[64,1024]{1,0:T(8,128)(2,1)S(1)}, u32[]{:S(2)}, u32[]{:S(2)}) collective-permute-start(bf16[64,1024]{1,0:T(8,128)(2,1)S(1)} %get-tuple-element.21), channel_id=1, source_target_pairs={{0,4},{4,8},{8,12},{12,0},{1,5},{5,9},{9,13},{13,1},{2,6},{6,10},{... | collective-permute-start | bytes 393224 | tf_op jit(solution)/shard_map/ppermute | solution.py:35
  167.6 3.1 %collective-permute-start.16 = (bf16[64,1024]{1,0:T(8,128)(2,1)S(1)}, bf16[64,1024]{1,0:T(8,128)(2,1)S(1)}, u32[]{:S(2)}, u32[]{:S(2)}) collective-permute-start(bf16[64,1024]{1,0:T(8,128)(2,1)S(1)} %get-tuple-element.22), channel_id=1, source_target_pairs={{0,12},{4,0},{8,4},{12,8},{1,13},{5,1},{9,5},{13,9},{2,14},{6,2},{... | collective-permute-start | bytes 393224 | tf_op jit(solution)/shard_map/ppermute | solution.py:35
  170.7 9.1 %collective-permute-done.14.refs_1_ = bf16[64,1024]{1,0:T(8,128)(2,1)S(1)} collective-permute-done((bf16[64,1024]{1,0:T(8,128)(2,1)S(1)}, bf16[64,1024]{1,0:T(8,128)(2,1)S(1)}, u32[]{:S(2)}, u32[]{:S(2)}) %collective-permute-start.14) | collective-permute-done | bytes 131104 | tf_op jit(solution)/shard_map/ppermute | solution.py:35
  179.8 7.6 %collective-permute-done.15.refs_2_ = bf16[64,1024]{1,0:T(8,128)(2,1)S(1)} collective-permute-done((bf16[64,1024]{1,0:T(8,128)(2,1)S(1)}, bf16[64,1024]{1,0:T(8,128)(2,1)S(1)}, u32[]{:S(2)}, u32[]{:S(2)}) %collective-permute-start.15) | collective-permute-done | bytes 131104 | tf_op jit(solution)/shard_map/ppermute | solution.py:35
  (86 shorter events, 36.1 us)
Async XLA Ops:
  0.6 23.4 %copy-start = (bf16[128,1024]{1,0:T(8,128)(2,1)S(1)}, bf16[128,1024]{1,0:T(8,128)(2,1)}, u32[]{:S(2)}) copy-start(bf16[128,1024]{1,0:T(8,128)(2,1)} %act_ref.1) | copy-start | bytes 786436
  1.8 35.4 %collective-permute-start.4 = (bf16[5,72,512]{2,1,0:T(8,128)(2,1)S(1)}, bf16[5,72,512]{2,1,0:T(8,128)(2,1)S(1)}, u32[]{:S(2)}, u32[]{:S(2)}) collective-permute-start(bf16[5,72,512]{2,1,0:T(8,128)(2,1)S(1)} %slice_select_fusion), channel_id=1, source_target_pairs={{0,3},{1,0},{2,1},{3,2},{4,7},{5,4},{6,5},{7,6},{8,11},{9,8},{10,9... | collective-permute-start | bytes 1105928 | tf_op jit(solution)/shard_map/ppermute | solution.py:35
  6.5 29.8 %collective-permute-start.3 = (bf16[5,72,512]{2,1,0:T(8,128)(2,1)S(1)}, bf16[5,72,512]{2,1,0:T(8,128)(2,1)}, u32[]{:S(2)}, u32[]{:S(2)}) collective-permute-start(bf16[5,72,512]{2,1,0:T(8,128)(2,1)S(1)} %slice_select_fusion), channel_id=1, source_target_pairs={{0,2},{1,3},{2,0},{3,1},{4,6},{5,7},{6,4},{7,5},{8,10},{9,11},{10,... | collective-permute-start | bytes 1105928 | tf_op jit(solution)/shard_map/ppermute | solution.py:35
  8.8 26.5 %collective-permute-start.2 = (bf16[5,72,512]{2,1,0:T(8,128)(2,1)S(1)}, bf16[5,72,512]{2,1,0:T(8,128)(2,1)}, u32[]{:S(2)}, u32[]{:S(2)}) collective-permute-start(bf16[5,72,512]{2,1,0:T(8,128)(2,1)S(1)} %slice_select_fusion), channel_id=1, source_target_pairs={{0,1},{1,2},{2,3},{3,0},{4,5},{5,6},{6,7},{7,4},{8,9},{9,10},{10,1... | collective-permute-start | bytes 1105928 | tf_op jit(solution)/shard_map/ppermute | solution.py:35
  12.1 9.7 %collective-permute-start.1 = (bf16[8,1024]{1,0:T(8,128)(2,1)S(1)}, bf16[8,1024]{1,0:T(8,128)(2,1)S(1)}, u32[]{:S(2)}, u32[]{:S(2)}) collective-permute-start(bf16[8,1024]{1,0:T(8,128)(2,1)S(1)} %get-tuple-element.31), channel_id=1, source_target_pairs={{1,0},{2,1},{3,2},{4,3},{5,4},{6,5},{7,6},{8,7},{9,8},{10,9},{11,1... | collective-permute-start | bytes 49160 | tf_op jit(solution)/shard_map/ppermute | solution.py:30
  15.5 8.5 %collective-permute-start = (bf16[8,1024]{1,0:T(8,128)(2,1)S(1)}, bf16[8,1024]{1,0:T(8,128)(2,1)S(1)}, u32[]{:S(2)}, u32[]{:S(2)}) collective-permute-start(bf16[8,1024]{1,0:T(8,128)(2,1)S(1)} %get-tuple-element.32), channel_id=1, source_target_pairs={{0,1},{1,2},{2,3},{3,4},{4,5},{5,6},{6,7},{7,8},{8,9},{9,10},{10,1... | collective-permute-start | bytes 49160 | tf_op jit(solution)/shard_map/ppermute | solution.py:30
  25.5 29.3 %all-to-all-start = ((bf16[4,72,1024]{2,1,0:T(8,128)(2,1)}), bf16[4,72,1024]{2,1,0:T(8,128)(2,1)S(1)}, u32[]{:S(2)}, u32[]{:S(2)}) async-start(bf16[4,72,1024]{2,1,0:T(8,128)(2,1)} %broadcast_in_dim.18), calls=%async_computation | async-start | bytes 1179648 | tf_op jit(solution)/shard_map/all_to_all | solution.py:40
  37.3 17.5 %collective-permute-start.5 = (bf16[5,288,512]{2,1,0:T(8,128)(2,1)S(1)}, bf16[5,288,512]{2,1,0:T(8,128)(2,1)S(1)}, u32[]{:S(2)}, u32[]{:S(2)}) collective-permute-start(bf16[5,288,512]{2,1,0:T(8,128)(2,1)S(1)} %bitcast.35), channel_id=1, source_target_pairs={{0,16},{16,0},{1,17},{17,1},{2,18},{18,2},{3,19},{19,3},{4,20},{20... | collective-permute-start | bytes 4423688 | tf_op jit(solution)/shard_map/ppermute | solution.py:310
  42.5 8.3 %collective-permute-start.8 = (bf16[4,32,72]{2,1,0:T(8,128)(2,1)S(1)}, bf16[4,32,72]{2,1,0:T(8,128)(2,1)S(1)}, u32[]{:S(2)}, u32[]{:S(2)}) collective-permute-start(bf16[4,32,72]{2,1,0:T(8,128)(2,1)S(1)} %get-tuple-element.33), channel_id=1, source_target_pairs={{0,3},{1,0},{2,1},{3,2},{4,7},{5,4},{6,5},{7,6},{8,11},{9,8},{10,9... | collective-permute-start | bytes 55304 | tf_op jit(solution)/shard_map/ppermute | solution.py:35
  46.1 6.2 %collective-permute-start.7 = (bf16[4,32,72]{2,1,0:T(8,128)(2,1)S(1)}, bf16[4,32,72]{2,1,0:T(8,128)(2,1)S(1)}, u32[]{:S(2)}, u32[]{:S(2)}) collective-permute-start(bf16[4,32,72]{2,1,0:T(8,128)(2,1)S(1)} %get-tuple-element.34), channel_id=1, source_target_pairs={{0,2},{1,3},{2,0},{3,1},{4,6},{5,7},{6,4},{7,5},{8,10},{9,11},{10,... | collective-permute-start | bytes 55304 | tf_op jit(solution)/shard_map/ppermute | solution.py:35
  48.3 5.9 %collective-permute-start.6 = (bf16[4,32,72]{2,1,0:T(8,128)(2,1)S(1)}, bf16[4,32,72]{2,1,0:T(8,128)(2,1)S(1)}, u32[]{:S(2)}, u32[]{:S(2)}) collective-permute-start(bf16[4,32,72]{2,1,0:T(8,128)(2,1)S(1)} %get-tuple-element.35), channel_id=1, source_target_pairs={{0,1},{1,2},{2,3},{3,0},{4,5},{5,6},{6,7},{7,4},{8,9},{9,10},{10,1... | collective-permute-start | bytes 55304 | tf_op jit(solution)/shard_map/ppermute | solution.py:35
  74.5 43.6 %all-to-all-start.2 = ((bf16[16,96,128]{2,1,0:T(8,128)(2,1)}), bf16[16,96,128]{2,1,0:T(8,128)(2,1)}, u32[]{:S(2)}, u32[]{:S(2)}) async-start(bf16[16,96,128]{2,1,0:T(8,128)(2,1)} %copy-done.9), calls=%async_computation.2 | async-start | bytes 786432 | tf_op jit(solution)/shard_map/all_to_all | solution.py:327
  81.1 34.4 %collective-permute-start.11 = (bf16[288,1024]{1,0:T(8,128)(2,1)S(1)}, bf16[288,1024]{1,0:T(8,128)(2,1)S(1)}, u32[]{:S(2)}, u32[]{:S(2)}) collective-permute-start(bf16[288,1024]{1,0:T(8,128)(2,1)S(1)} %bitcast.39), channel_id=1, source_target_pairs={{0,2},{1,3},{2,0},{3,1},{4,6},{5,7},{6,4},{7,5},{8,10},{9,11},{10,... | collective-permute-start | bytes 1769480 | tf_op jit(solution)/shard_map/ppermute | solution.py:35
  85.7 30.7 %collective-permute-start.10 = (bf16[288,1024]{1,0:T(8,128)(2,1)S(1)}, bf16[288,1024]{1,0:T(8,128)(2,1)S(1)}, u32[]{:S(2)}, u32[]{:S(2)}) collective-permute-start(bf16[288,1024]{1,0:T(8,128)(2,1)S(1)} %bitcast.40), channel_id=1, source_target_pairs={{0,3},{1,0},{2,1},{3,2},{4,7},{5,4},{6,5},{7,6},{8,11},{9,8},{10,9... | collective-permute-start | bytes 1769480 | tf_op jit(solution)/shard_map/ppermute | solution.py:35
  88.5 28.7 %collective-permute-start.9 = (bf16[288,1024]{1,0:T(8,128)(2,1)S(1)}, bf16[288,1024]{1,0:T(8,128)(2,1)S(1)}, u32[]{:S(2)}, u32[]{:S(2)}) collective-permute-start(bf16[288,1024]{1,0:T(8,128)(2,1)S(1)} %bitcast.41), channel_id=1, source_target_pairs={{0,1},{1,2},{2,3},{3,0},{4,5},{5,6},{6,7},{7,4},{8,9},{9,10},{10,1... | collective-permute-start | bytes 1769480 | tf_op jit(solution)/shard_map/ppermute | solution.py:35
  91.0 23.3 %collective-permute-start.13 = (bf16[2,4,8,288]{3,2,1,0:T(8,128)(2,1)}, bf16[2,4,8,288]{3,2,1,0:T(8,128)(2,1)S(1)}, u32[]{:S(2)}, u32[]{:S(2)}) collective-permute-start(bf16[2,4,8,288]{3,2,1,0:T(8,128)(2,1)} %copy-done.21), channel_id=1, source_target_pairs={{1,0},{2,1},{3,2},{4,3},{5,4},{6,5},{7,6},{8,7},{9,8},{10,9},{11,1... | collective-permute-start | bytes 110600 | tf_op jit(solution)/shard_map/ppermute | solution.py:30
  95.0 19.9 %collective-permute-start.12 = (bf16[2,4,8,288]{3,2,1,0:T(8,128)(2,1)}, bf16[2,4,8,288]{3,2,1,0:T(8,128)(2,1)S(1)}, u32[]{:S(2)}, u32[]{:S(2)}) collective-permute-start(bf16[2,4,8,288]{3,2,1,0:T(8,128)(2,1)} %copy-done.21), channel_id=1, source_target_pairs={{0,1},{1,2},{2,3},{3,4},{4,5},{5,6},{6,7},{7,8},{8,9},{9,10},{10,1... | collective-permute-start | bytes 110600 | tf_op jit(solution)/shard_map/ppermute | solution.py:30
  118.0 1.1 copy-start.4
  119.1 1.1 copy-start.6
  120.2 1.1 copy-start.8
  121.2 11.0 %copy-start.11 = (bf16[4,64,288]{2,1,0:T(8,128)(2,1)S(1)}, bf16[4,64,288]{2,1,0:T(8,128)(2,1)}, u32[]{:S(2)}) copy-start(bf16[4,64,288]{2,1,0:T(8,128)(2,1)} %copy-done.10) | copy-start | bytes 442372
  121.2 11.0 %copy-start.22 = (bf16[4,8,288]{2,1,0:T(8,128)(2,1)S(1)}, bf16[4,8,288]{2,1,0:T(8,128)(2,1)}, u32[]{:S(2)}) copy-start(bf16[4,8,288]{2,1,0:T(8,128)(2,1)} %slice_bitcast_fusion) | copy-start | bytes 55300
  121.2 11.0 %copy-start.23 = (bf16[4,8,288]{2,1,0:T(8,128)(2,1)S(1)}, bf16[4,8,288]{2,1,0:T(8,128)(2,1)}, u32[]{:S(2)}) copy-start(bf16[4,8,288]{2,1,0:T(8,128)(2,1)} %slice_bitcast_fusion.1) | copy-start | bytes 55300
  126.6 0.9 copy-start.2
  128.2 8.7 %collective-permute-start.17 = (bf16[16,32,360]{2,1,0:T(8,128)(2,1)}, bf16[16,32,360]{2,1,0:T(8,128)(2,1)}, u32[]{:S(2)}, u32[]{:S(2)}) collective-permute-start(bf16[16,32,360]{2,1,0:T(8,128)(2,1)} %get-tuple-element.24), channel_id=1, source_target_pairs={{0,16},{16,0},{1,17},{17,1},{2,18},{18,2},{3,19},{19,3},{4,20},{20... | collective-permute-start | bytes 1105928 | tf_op jit(solution)/shard_map/ppermute | solution.py:340
  133.0 10.8 %all-to-all-start.3 = ((bf16[4,80,288]{2,1,0:T(8,128)(2,1)}), bf16[4,80,288]{2,1,0:T(8,128)(2,1)S(1)}, u32[]{:S(2)}, u32[]{:S(2)}) async-start(bf16[4,80,288]{2,1,0:T(8,128)(2,1)} %pad_maximum_fusion), calls=%async_computation.3 | async-start | bytes 491520 | tf_op jit(solution)/shard_map/all_to_all | solution.py:330
  143.8 47.3 %all-to-all-start.4 = ((bf16[16,32,360]{2,1,0:T(8,128)(2,1)}), bf16[16,32,360]{2,1,0:T(8,128)(2,1)}, u32[]{:S(2)}, u32[]{:S(2)}) async-start(bf16[16,32,360]{2,1,0:T(8,128)(2,1)} %add_convert_fusion), calls=%async_computation.4 | async-start | bytes 786432 | tf_op jit(solution)/shard_map/all_to_all | solution.py:342
  158.9 30.0 %copy-start.1 = (bf16[128,1024]{1,0:T(8,128)(2,1)S(1)}, bf16[128,1024]{1,0:T(8,128)(2,1)}, u32[]{:S(2)}) copy-start(bf16[128,1024]{1,0:T(8,128)(2,1)} %act_ref.1) | copy-start | bytes 786436
  158.9 31.4 %copy-start.14 = (bf16[512,72]{1,0:T(8,128)(2,1)S(1)}, bf16[512,72]{1,0:T(8,128)(2,1)}, u32[]{:S(2)}) copy-start(bf16[512,72]{1,0:T(8,128)(2,1)} %copy-done.13) | copy-start | bytes 221188
  161.9 17.9 %collective-permute-start.14 = (bf16[64,1024]{1,0:T(8,128)(2,1)S(1)}, bf16[64,1024]{1,0:T(8,128)(2,1)S(1)}, u32[]{:S(2)}, u32[]{:S(2)}) collective-permute-start(bf16[64,1024]{1,0:T(8,128)(2,1)S(1)} %get-tuple-element.20), channel_id=1, source_target_pairs={{0,8},{4,12},{8,0},{12,4},{1,9},{5,13},{9,1},{13,5},{2,10},{6,14},... | collective-permute-start | bytes 393224 | tf_op jit(solution)/shard_map/ppermute | solution.py:35
  165.4 21.9 %collective-permute-start.15 = (bf16[64,1024]{1,0:T(8,128)(2,1)S(1)}, bf16[64,1024]{1,0:T(8,128)(2,1)S(1)}, u32[]{:S(2)}, u32[]{:S(2)}) collective-permute-start(bf16[64,1024]{1,0:T(8,128)(2,1)S(1)} %get-tuple-element.21), channel_id=1, source_target_pairs={{0,4},{4,8},{8,12},{12,0},{1,5},{5,9},{9,13},{13,1},{2,6},{6,10},{... | collective-permute-start | bytes 393224 | tf_op jit(solution)/shard_map/ppermute | solution.py:35
  167.6 21.3 %collective-permute-start.16 = (bf16[64,1024]{1,0:T(8,128)(2,1)S(1)}, bf16[64,1024]{1,0:T(8,128)(2,1)S(1)}, u32[]{:S(2)}, u32[]{:S(2)}) collective-permute-start(bf16[64,1024]{1,0:T(8,128)(2,1)S(1)} %get-tuple-element.22), channel_id=1, source_target_pairs={{0,12},{4,0},{8,4},{12,8},{1,13},{5,1},{9,5},{13,9},{2,14},{6,2},{... | collective-permute-start | bytes 393224 | tf_op jit(solution)/shard_map/ppermute | solution.py:35
  (14 other events, 10.1 us)

commit v9 on v7

--- a/solution.py
+++ b/solution.py
@@ -263,8 +263,9 @@
         step = mine_ref.shape[1]
         near = pl.ds(pl.multiple_of(c * 2 * step + core * step, step), step)
         far = pl.ds(pl.multiple_of(c * 2 * step + (1 - core) * step, step), step)
-        mine_ref[c] = part_ref[near, : taps * block]
-        other_ref[c] = part_ref[far, : taps * block].astype(bf16)
+        at = c % 4 * 4 + c // 4
+        mine_ref[at] = part_ref[near, : taps * block]
+        other_ref[at] = part_ref[far, : taps * block].astype(bf16)
 
 
 def weight_partial(where, back, ring, taps, block):
@@ -335,13 +336,21 @@
     parts = parts + [turn(own[1], "zl", 1), turn(own[3], "zl", 3)]
     input_grad = input_gradient(activations, parts)
 
-    mine, other, features = weight_partial(
-        where, back, [flat, up, down, far], tap_count, out_width
-    )
+    mine, other, features = weight_partial(where, back, [flat, up, down, far], tap_count, out_width)
     other = lax.ppermute(other, "core", [(0, 1), (1, 0)])
     total = (mine + other.astype(f32)).astype(bf16)
-    total = lax.all_to_all(total, ("zh", "x"), 0, 0)
-    weight_grad = jnp.sum(total.astype(f32), axis=0).reshape(-1, tap_count, out_width)
+    zh = lax.axis_index("zh")
+    total = lax.all_to_all(total.reshape(4, 4, *total.shape[1:]), "x", 0, 0)
+    total = jnp.sum(total.astype(f32), axis=0)
+    upper = zh // 2
+    away = lax.dynamic_slice_in_dim(total, 2 - 2 * upper, 2).astype(bf16)
+    away = lax.ppermute(away, "zh", [(i, i ^ 2) for i in range(4)])
+    total = lax.dynamic_slice_in_dim(total, 2 * upper, 2) + away.astype(f32)
+    lower = zh % 2
+    away = lax.dynamic_index_in_dim(total, 1 - lower, keepdims=False).astype(bf16)
+    away = lax.ppermute(away, "zh", [(i, i ^ 1) for i in range(4)])
+    total = lax.dynamic_index_in_dim(total, lower, keepdims=False) + away.astype(f32)
+    weight_grad = total.reshape(-1, tap_count, out_width)
     return (features, input_grad, weight_grad)
 
 

time: 193 us -> 198 us (1.026)
  the two profiles are of different devices: /device:TPU:34 before, /device:TPU:25 now
where the time goes in v9:
time: 198 us; the launch traced here: 196 us
  starting transfers between devices  103 us (52%)
  waiting for transfers between devices  36.8 us (19%)
  local copies, waits for them, and re-layouts  24.1 us (12%)
  Pallas kernels  14.4 us (7%)
  blocking collectives  11.8 us (6%)
  other arithmetic  4.73 us (2%)
    ppermute x12, starting transfers between devices, turn(): lax.ppermute(block, axis, [(i, (i + step) % count) for i in range(count)])  37.8 us
    ppermute x12, waiting for transfers between devices, turn(): lax.ppermute(block, axis, [(i, (i + step) % count) for i in range(count)])  25.1 us
    unnamed x56, local copies, waits for them, and re-layouts  17 us
    pallas_call x6, Pallas kernels, local_call(): pl.pallas_call(kernel, out_shape=shapes, in_specs=[pl.BlockSpec(memory_sp...  14.4 us
    ppermute x4, starting transfers between devices, shift(): return lax.ppermute(block, axis, pairs)  14.4 us
    ppermute x1, starting transfers between devices, per_device(): away = lax.ppermute(away, 'zh', [(i, i ^ 2) for i in range(4)])  12.1 us
    all_to_all x1, blocking collectives, per_device(): conv_out = lax.all_to_all(conv_out, 'zl', 0, 0)  11.8 us
    ppermute x4, waiting for transfers between devices, shift(): return lax.ppermute(block, axis, pairs)  9.26 us
  transfers between devices with their start and end apart: 24, of which 9 were waited for; matrix products, arithmetic and copies ran while one was open for 6% of the time, Pallas kernels for 3%

profile of v9, /device:TPU:25, one launch (start us, length us, event | category | flops | bytes accessed | tf_op | source)
XLA Modules:
  0.0 196.2 jit_solution(982405822019961320)
XLA Ops:
  1.8 1.9 collective-permute-start.2
  3.8 4.1 %collective-permute-start.3 = (bf16[5,72,512]{2,1,0:T(8,128)(2,1)S(1)}, bf16[5,72,512]{2,1,0:T(8,128)(2,1)}, u32[]{:S(2)}, u32[]{:S(2)}) collective-permute-start(bf16[5,72,512]{2,1,0:T(8,128)(2,1)S(1)} %slice_select_fusion), channel_id=1, source_target_pairs={{0,2},{1,3},{2,0},{3,1},{4,6},{5,7},{6,4},{7,5},{8,10},{9,11},{10,... | collective-permute-start | bytes 1105928 | tf_op jit(solution)/shard_map/ppermute | solution.py:35
  7.9 1.9 collective-permute-start.4
  10.6 5.9 %collective-permute-start = (bf16[8,1024]{1,0:T(8,128)(2,1)S(1)}, bf16[8,1024]{1,0:T(8,128)(2,1)S(1)}, u32[]{:S(2)}, u32[]{:S(2)}) collective-permute-start(bf16[8,1024]{1,0:T(8,128)(2,1)S(1)} %get-tuple-element.34), channel_id=1, source_target_pairs={{0,1},{1,2},{2,3},{3,4},{4,5},{5,6},{6,7},{7,8},{8,9},{9,10},{10,1... | collective-permute-start | bytes 49160 | tf_op jit(solution)/shard_map/ppermute | solution.py:30
  16.5 1.9 collective-permute-start.1
  18.7 3.1 %collective-permute-done.low_ref = bf16[8,1024]{1,0:T(8,128)(2,1)S(1)} collective-permute-done((bf16[8,1024]{1,0:T(8,128)(2,1)S(1)}, bf16[8,1024]{1,0:T(8,128)(2,1)S(1)}, u32[]{:S(2)}, u32[]{:S(2)}) %collective-permute-start) | collective-permute-done | bytes 16416 | tf_op jit(solution)/shard_map/ppermute | solution.py:30
  24.7 8.4 %all-to-all-start = ((bf16[4,72,1024]{2,1,0:T(8,128)(2,1)}), bf16[4,72,1024]{2,1,0:T(8,128)(2,1)S(1)}, u32[]{:S(2)}, u32[]{:S(2)}) async-start(bf16[4,72,1024]{2,1,0:T(8,128)(2,1)} %broadcast_in_dim.18), calls=%async_computation | async-start | bytes 1179648 | tf_op jit(solution)/shard_map/all_to_all | solution.py:40
  35.2 1.9 collective-permute-start.5
  40.3 2.9 %collective-permute-start.6 = (bf16[4,32,72]{2,1,0:T(8,128)(2,1)S(1)}, bf16[4,32,72]{2,1,0:T(8,128)(2,1)S(1)}, u32[]{:S(2)}, u32[]{:S(2)}) collective-permute-start(bf16[4,32,72]{2,1,0:T(8,128)(2,1)S(1)} %get-tuple-element.37), channel_id=1, source_target_pairs={{0,1},{1,2},{2,3},{3,0},{4,5},{5,6},{6,7},{7,4},{8,9},{9,10},{10,1... | collective-permute-start | bytes 55304 | tf_op jit(solution)/shard_map/ppermute | solution.py:35
  43.2 4.1 %collective-permute-start.7 = (bf16[4,32,72]{2,1,0:T(8,128)(2,1)S(1)}, bf16[4,32,72]{2,1,0:T(8,128)(2,1)S(1)}, u32[]{:S(2)}, u32[]{:S(2)}) collective-permute-start(bf16[4,32,72]{2,1,0:T(8,128)(2,1)S(1)} %get-tuple-element.36), channel_id=1, source_target_pairs={{0,2},{1,3},{2,0},{3,1},{4,6},{5,7},{6,4},{7,5},{8,10},{9,11},{10,... | collective-permute-start | bytes 55304 | tf_op jit(solution)/shard_map/ppermute | solution.py:35
  47.4 2.4 %collective-permute-start.8 = (bf16[4,32,72]{2,1,0:T(8,128)(2,1)S(1)}, bf16[4,32,72]{2,1,0:T(8,128)(2,1)S(1)}, u32[]{:S(2)}, u32[]{:S(2)}) collective-permute-start(bf16[4,32,72]{2,1,0:T(8,128)(2,1)S(1)} %get-tuple-element.35), channel_id=1, source_target_pairs={{0,3},{1,0},{2,1},{3,2},{4,7},{5,4},{6,5},{7,6},{8,11},{9,8},{10,9... | collective-permute-start | bytes 55304 | tf_op jit(solution)/shard_map/ppermute | solution.py:35
  51.2 2.1 %collective-permute-done.8.refs_3_ = bf16[4,32,72]{2,1,0:T(8,128)(2,1)S(1)} collective-permute-done((bf16[4,32,72]{2,1,0:T(8,128)(2,1)S(1)}, bf16[4,32,72]{2,1,0:T(8,128)(2,1)S(1)}, u32[]{:S(2)}, u32[]{:S(2)}) %collective-permute-start.8) | collective-permute-done | bytes 18464 | tf_op jit(solution)/shard_map/ppermute | solution.py:35
  56.9 2.5 %shard_map.59 = bf16[4,96,288]{2,1,0:T(8,128)(2,1)S(1)} custom-call(s32[3]{0:T(128)S(1)} %pad_add_fusion.where_ref, bf16[288,1024]{1,0:T(8,128)(2,1)S(1)} %bitcast.39, bf16[5,288,512]{2,1,0:T(8,128)(2,1)S(1)} %bitcast.37, bf16[5,288,512]{2,1,0:T(8,128)(2,1)S(1)} %collective-permute-done.5.second_ref, bf16[4,32,72]{2,1,0:T(8,128)(2,1)S(1)} %copy-done.11, ...), custom_call_target="tpu_custom_call" | custom-call | tf_op jit(solution)/shard_map/pallas_call | solution.py:45
  59.4 11.8 %all_to_all.25.y_ref = bf16[4,96,288]{2,1,0:T(8,128)(2,1)S(1)} all-to-all(bf16[4,96,288]{2,1,0:T(8,128)(2,1)S(1)} %shard_map.59), channel_id=1, replica_groups=mesh['zh'=4,'x'=4,'core'=2,'zl'=4,'y'=4] {'zl'}, dimensions={0} | all-to-all | bytes 442368 | tf_op jit(solution)/shard_map/all_to_all | solution.py:327
  75.4 7.0 %all-to-all-start.2 = ((bf16[16,96,128]{2,1,0:T(8,128)(2,1)}), bf16[16,96,128]{2,1,0:T(8,128)(2,1)}, u32[]{:S(2)}, u32[]{:S(2)}) async-start(bf16[16,96,128]{2,1,0:T(8,128)(2,1)} %copy-done.8), calls=%async_computation.2 | async-start | bytes 786432 | tf_op jit(solution)/shard_map/all_to_all | solution.py:329
  82.3 2.5 %collective-permute-start.10 = (bf16[288,1024]{1,0:T(8,128)(2,1)S(1)}, bf16[288,1024]{1,0:T(8,128)(2,1)S(1)}, u32[]{:S(2)}, u32[]{:S(2)}) collective-permute-start(bf16[288,1024]{1,0:T(8,128)(2,1)S(1)} %bitcast.40), channel_id=1, source_target_pairs={{0,3},{1,0},{2,1},{3,2},{4,7},{5,4},{6,5},{7,6},{8,11},{9,8},{10,9... | collective-permute-start | bytes 1769480 | tf_op jit(solution)/shard_map/ppermute | solution.py:35
  84.8 2.7 %collective-permute-start.11 = (bf16[288,1024]{1,0:T(8,128)(2,1)S(1)}, bf16[288,1024]{1,0:T(8,128)(2,1)S(1)}, u32[]{:S(2)}, u32[]{:S(2)}) collective-permute-start(bf16[288,1024]{1,0:T(8,128)(2,1)S(1)} %bitcast.41), channel_id=1, source_target_pairs={{0,2},{1,3},{2,0},{3,1},{4,6},{5,7},{6,4},{7,5},{8,10},{9,11},{10,... | collective-permute-start | bytes 1769480 | tf_op jit(solution)/shard_map/ppermute | solution.py:35
  87.5 3.8 %collective-permute-start.9 = (bf16[288,1024]{1,0:T(8,128)(2,1)S(1)}, bf16[288,1024]{1,0:T(8,128)(2,1)S(1)}, u32[]{:S(2)}, u32[]{:S(2)}) collective-permute-start(bf16[288,1024]{1,0:T(8,128)(2,1)S(1)} %bitcast.42), channel_id=1, source_target_pairs={{0,1},{1,2},{2,3},{3,0},{4,5},{5,6},{6,7},{7,4},{8,9},{9,10},{10,1... | collective-permute-start | bytes 1769480 | tf_op jit(solution)/shard_map/ppermute | solution.py:35
  91.3 11.1 %collective-permute-done.10.refs_2_ = bf16[288,1024]{1,0:T(8,128)(2,1)S(1)} collective-permute-done((bf16[288,1024]{1,0:T(8,128)(2,1)S(1)}, bf16[288,1024]{1,0:T(8,128)(2,1)S(1)}, u32[]{:S(2)}, u32[]{:S(2)}) %collective-permute-start.10) | collective-permute-done | bytes 589856 | tf_op jit(solution)/shard_map/ppermute | solution.py:35
  103.2 11.3 %collective-permute-done.11.refs_3_ = bf16[288,1024]{1,0:T(8,128)(2,1)S(1)} collective-permute-done((bf16[288,1024]{1,0:T(8,128)(2,1)S(1)}, bf16[288,1024]{1,0:T(8,128)(2,1)S(1)}, u32[]{:S(2)}, u32[]{:S(2)}) %collective-permute-start.11) | collective-permute-done | bytes 589856 | tf_op jit(solution)/shard_map/ppermute | solution.py:35
  120.0 4.6 %shard_map.61 = (f32[16,32,360]{2,1,0:T(8,128)S(1)}, bf16[16,32,360]{2,1,0:T(8,128)(2,1)S(1)}, bf16[512,72]{1,0:T(8,128)(2,1)S(1)}) custom-call(s32[3]{0:T(128)S(1)} %pad_add_fusion.where_ref, bf16[16,96,128]{2,1,0:T(8,128)(2,1)} %all-to-all-done.2.back_ref, bf16[288,1024]{1,0:T(8,128)(2,1)S(1)} %bitcast.43, bf16[288,1024]{1,0:T(8,128)(2,1)S(1)} %copy-done.7, ...), custom_call_target="tpu_custom_call" | custom-call | tf_op jit(solution)/shard_map/pallas_call | solution.py:45
  124.7 4.0 %collective-permute-start.17 = (bf16[16,32,360]{2,1,0:T(8,128)(2,1)S(1)}, bf16[16,32,360]{2,1,0:T(8,128)(2,1)S(1)}, u32[]{:S(2)}, u32[]{:S(2)}) collective-permute-start(bf16[16,32,360]{2,1,0:T(8,128)(2,1)S(1)} %get-tuple-element.26), channel_id=1, source_target_pairs={{0,16},{16,0},{1,17},{17,1},{2,18},{18,2},{3,19},{19,3},{4,20},{20... | collective-permute-start | bytes 1105928 | tf_op jit(solution)/shard_map/ppermute | solution.py:340
  130.8 5.1 %all-to-all-start.4 = ((bf16[4,4,32,360]{3,2,1,0:T(8,128)(2,1)}), bf16[4,4,32,360]{3,2,1,0:T(8,128)(2,1)}, u32[]{:S(2)}, u32[]{:S(2)}) async-start(bf16[4,4,32,360]{3,2,1,0:T(8,128)(2,1)} %bitcast.45), calls=%async_computation.4 | async-start | bytes 786432 | tf_op jit(solution)/shard_map/all_to_all | solution.py:343
  135.9 4.6 %collective-permute-start.12 = (bf16[4,8,288]{2,1,0:T(8,128)(2,1)S(1)}, bf16[4,8,288]{2,1,0:T(8,128)(2,1)S(1)}, u32[]{:S(2)}, u32[]{:S(2)}) collective-permute-start(bf16[4,8,288]{2,1,0:T(8,128)(2,1)S(1)} %copy-done.24), channel_id=1, source_target_pairs={{0,1},{1,2},{2,3},{3,4},{4,5},{5,6},{6,7},{7,8},{8,9},{9,10},{10,1... | collective-permute-start | bytes 55304 | tf_op jit(solution)/shard_map/ppermute | solution.py:30
  142.5 4.7 %collective-permute-done.13 = bf16[4,8,288]{2,1,0:T(8,128)(2,1)S(1)} collective-permute-done((bf16[4,8,288]{2,1,0:T(8,128)(2,1)S(1)}, bf16[4,8,288]{2,1,0:T(8,128)(2,1)S(1)}, u32[]{:S(2)}, u32[]{:S(2)}) %collective-permute-start.13) | collective-permute-done | bytes 18464 | tf_op jit(solution)/shard_map/ppermute | solution.py:30
  147.9 8.5 %all-to-all-start.3 = ((bf16[4,80,288]{2,1,0:T(8,128)(2,1)}), bf16[4,80,288]{2,1,0:T(8,128)(2,1)S(1)}, u32[]{:S(2)}, u32[]{:S(2)}) async-start(bf16[4,80,288]{2,1,0:T(8,128)(2,1)} %pad_maximum_fusion), calls=%async_computation.3 | async-start | bytes 491520 | tf_op jit(solution)/shard_map/all_to_all | solution.py:332
  157.5 12.1 %collective-permute-start.18 = (bf16[2,32,360]{2,1,0:T(8,128)(2,1)S(1)}, bf16[2,32,360]{2,1,0:T(8,128)(2,1)}, u32[]{:S(2)}, u32[]{:S(2)}) collective-permute-start(bf16[2,32,360]{2,1,0:T(8,128)(2,1)S(1)} %dynamic-slice_convert_fusion), channel_id=1, source_target_pairs={{0,256},{128,384},{256,0},{384,128},{1,257},{129,385},{257,1},{385... | collective-permute-start | bytes 138248 | tf_op jit(solution)/shard_map/ppermute | solution.py:347
  169.7 3.7 %shard_map.62 = (bf16[64,1024]{1,0:T(8,128)(2,1)S(1)}, bf16[64,1024]{1,0:T(8,128)(2,1)}, bf16[64,1024]{1,0:T(8,128)(2,1)}, bf16[64,1024]{1,0:T(8,128)(2,1)}) custom-call(s32[3]{0:T(128)S(1)} %pad_add_fusion.where_ref, bf16[320,288]{1,0:T(8,128)(2,1)S(1)} %bitcast.44, bf16[5,288,512]{2,1,0:T(8,128)(2,1)S(1)} %bitcast.38, ...), custom_call_target="tpu_custom_call" | custom-call | tf_op jit(solution)/shard_map/pallas_call | solution.py:45
  174.1 4.2 %collective-permute-start.14 = (bf16[64,1024]{1,0:T(8,128)(2,1)}, bf16[64,1024]{1,0:T(8,128)(2,1)S(1)}, u32[]{:S(2)}, u32[]{:S(2)}) collective-permute-start(bf16[64,1024]{1,0:T(8,128)(2,1)} %get-tuple-element.22), channel_id=1, source_target_pairs={{0,8},{4,12},{8,0},{12,4},{1,9},{5,13},{9,1},{13,5},{2,10},{6,14},... | collective-permute-start | bytes 393224 | tf_op jit(solution)/shard_map/ppermute | solution.py:35
  178.3 3.1 %collective-permute-start.15 = (bf16[64,1024]{1,0:T(8,128)(2,1)}, bf16[64,1024]{1,0:T(8,128)(2,1)S(1)}, u32[]{:S(2)}, u32[]{:S(2)}) collective-permute-start(bf16[64,1024]{1,0:T(8,128)(2,1)} %get-tuple-element.23), channel_id=1, source_target_pairs={{0,4},{4,8},{8,12},{12,0},{1,5},{5,9},{9,13},{13,1},{2,6},{6,10},{... | collective-permute-start | bytes 393224 | tf_op jit(solution)/shard_map/ppermute | solution.py:35
  181.4 4.0 %collective-permute-start.16 = (bf16[64,1024]{1,0:T(8,128)(2,1)}, bf16[64,1024]{1,0:T(8,128)(2,1)S(1)}, u32[]{:S(2)}, u32[]{:S(2)}) collective-permute-start(bf16[64,1024]{1,0:T(8,128)(2,1)} %get-tuple-element.24), channel_id=1, source_target_pairs={{0,12},{4,0},{8,4},{12,8},{1,13},{5,1},{9,5},{13,9},{2,14},{6,2},{... | collective-permute-start | bytes 393224 | tf_op jit(solution)/shard_map/ppermute | solution.py:35
  186.3 4.0 %collective-permute-start.19 = (bf16[32,360]{1,0:T(8,128)(2,1)S(1)}, bf16[32,360]{1,0:T(8,128)(2,1)S(1)}, u32[]{:S(2)}, u32[]{:S(2)}) collective-permute-start(bf16[32,360]{1,0:T(8,128)(2,1)S(1)} %fusion), channel_id=1, source_target_pairs={{0,128},{128,0},{256,384},{384,256},{1,129},{129,1},{257,385},{385... | collective-permute-start | bytes 69128 | tf_op jit(solution)/shard_map/ppermute | solution.py:351
  (98 shorter events, 38.9 us)
Async XLA Ops:
  0.6 22.6 %copy-start = (bf16[128,1024]{1,0:T(8,128)(2,1)S(1)}, bf16[128,1024]{1,0:T(8,128)(2,1)}, u32[]{:S(2)}) copy-start(bf16[128,1024]{1,0:T(8,128)(2,1)} %act_ref.1) | copy-start | bytes 786436
  1.8 31.3 %collective-permute-start.2 = (bf16[5,72,512]{2,1,0:T(8,128)(2,1)S(1)}, bf16[5,72,512]{2,1,0:T(8,128)(2,1)}, u32[]{:S(2)}, u32[]{:S(2)}) collective-permute-start(bf16[5,72,512]{2,1,0:T(8,128)(2,1)S(1)} %slice_select_fusion), channel_id=1, source_target_pairs={{0,1},{1,2},{2,3},{3,0},{4,5},{5,6},{6,7},{7,4},{8,9},{9,10},{10,1... | collective-permute-start | bytes 1105928 | tf_op jit(solution)/shard_map/ppermute | solution.py:35
  3.8 30.4 %collective-permute-start.3 = (bf16[5,72,512]{2,1,0:T(8,128)(2,1)S(1)}, bf16[5,72,512]{2,1,0:T(8,128)(2,1)}, u32[]{:S(2)}, u32[]{:S(2)}) collective-permute-start(bf16[5,72,512]{2,1,0:T(8,128)(2,1)S(1)} %slice_select_fusion), channel_id=1, source_target_pairs={{0,2},{1,3},{2,0},{3,1},{4,6},{5,7},{6,4},{7,5},{8,10},{9,11},{10,... | collective-permute-start | bytes 1105928 | tf_op jit(solution)/shard_map/ppermute | solution.py:35
  7.9 27.3 %collective-permute-start.4 = (bf16[5,72,512]{2,1,0:T(8,128)(2,1)S(1)}, bf16[5,72,512]{2,1,0:T(8,128)(2,1)S(1)}, u32[]{:S(2)}, u32[]{:S(2)}) collective-permute-start(bf16[5,72,512]{2,1,0:T(8,128)(2,1)S(1)} %slice_select_fusion), channel_id=1, source_target_pairs={{0,3},{1,0},{2,1},{3,2},{4,7},{5,4},{6,5},{7,6},{8,11},{9,8},{10,9... | collective-permute-start | bytes 1105928 | tf_op jit(solution)/shard_map/ppermute | solution.py:35
  10.6 11.2 %collective-permute-start = (bf16[8,1024]{1,0:T(8,128)(2,1)S(1)}, bf16[8,1024]{1,0:T(8,128)(2,1)S(1)}, u32[]{:S(2)}, u32[]{:S(2)}) collective-permute-start(bf16[8,1024]{1,0:T(8,128)(2,1)S(1)} %get-tuple-element.34), channel_id=1, source_target_pairs={{0,1},{1,2},{2,3},{3,4},{4,5},{5,6},{6,7},{7,8},{8,9},{9,10},{10,1... | collective-permute-start | bytes 49160 | tf_op jit(solution)/shard_map/ppermute | solution.py:30
  16.5 6.7 %collective-permute-start.1 = (bf16[8,1024]{1,0:T(8,128)(2,1)S(1)}, bf16[8,1024]{1,0:T(8,128)(2,1)S(1)}, u32[]{:S(2)}, u32[]{:S(2)}) collective-permute-start(bf16[8,1024]{1,0:T(8,128)(2,1)S(1)} %get-tuple-element.33), channel_id=1, source_target_pairs={{1,0},{2,1},{3,2},{4,3},{5,4},{6,5},{7,6},{8,7},{9,8},{10,9},{11,1... | collective-permute-start | bytes 49160 | tf_op jit(solution)/shard_map/ppermute | solution.py:30
  24.7 29.1 %all-to-all-start = ((bf16[4,72,1024]{2,1,0:T(8,128)(2,1)}), bf16[4,72,1024]{2,1,0:T(8,128)(2,1)S(1)}, u32[]{:S(2)}, u32[]{:S(2)}) async-start(bf16[4,72,1024]{2,1,0:T(8,128)(2,1)} %broadcast_in_dim.18), calls=%async_computation | async-start | bytes 1179648 | tf_op jit(solution)/shard_map/all_to_all | solution.py:40
  35.2 18.6 %collective-permute-start.5 = (bf16[5,288,512]{2,1,0:T(8,128)(2,1)S(1)}, bf16[5,288,512]{2,1,0:T(8,128)(2,1)S(1)}, u32[]{:S(2)}, u32[]{:S(2)}) collective-permute-start(bf16[5,288,512]{2,1,0:T(8,128)(2,1)S(1)} %bitcast.36), channel_id=1, source_target_pairs={{0,16},{16,0},{1,17},{17,1},{2,18},{18,2},{3,19},{19,3},{4,20},{20... | collective-permute-start | bytes 4423688 | tf_op jit(solution)/shard_map/ppermute | solution.py:312
  40.3 9.6 %collective-permute-start.6 = (bf16[4,32,72]{2,1,0:T(8,128)(2,1)S(1)}, bf16[4,32,72]{2,1,0:T(8,128)(2,1)S(1)}, u32[]{:S(2)}, u32[]{:S(2)}) collective-permute-start(bf16[4,32,72]{2,1,0:T(8,128)(2,1)S(1)} %get-tuple-element.37), channel_id=1, source_target_pairs={{0,1},{1,2},{2,3},{3,0},{4,5},{5,6},{6,7},{7,4},{8,9},{9,10},{10,1... | collective-permute-start | bytes 55304 | tf_op jit(solution)/shard_map/ppermute | solution.py:35
  43.2 7.3 %collective-permute-start.7 = (bf16[4,32,72]{2,1,0:T(8,128)(2,1)S(1)}, bf16[4,32,72]{2,1,0:T(8,128)(2,1)S(1)}, u32[]{:S(2)}, u32[]{:S(2)}) collective-permute-start(bf16[4,32,72]{2,1,0:T(8,128)(2,1)S(1)} %get-tuple-element.36), channel_id=1, source_target_pairs={{0,2},{1,3},{2,0},{3,1},{4,6},{5,7},{6,4},{7,5},{8,10},{9,11},{10,... | collective-permute-start | bytes 55304 | tf_op jit(solution)/shard_map/ppermute | solution.py:35
  47.4 5.9 %collective-permute-start.8 = (bf16[4,32,72]{2,1,0:T(8,128)(2,1)S(1)}, bf16[4,32,72]{2,1,0:T(8,128)(2,1)S(1)}, u32[]{:S(2)}, u32[]{:S(2)}) collective-permute-start(bf16[4,32,72]{2,1,0:T(8,128)(2,1)S(1)} %get-tuple-element.35), channel_id=1, source_target_pairs={{0,3},{1,0},{2,1},{3,2},{4,7},{5,4},{6,5},{7,6},{8,11},{9,8},{10,9... | collective-permute-start | bytes 55304 | tf_op jit(solution)/shard_map/ppermute | solution.py:35
  75.4 41.4 %all-to-all-start.2 = ((bf16[16,96,128]{2,1,0:T(8,128)(2,1)}), bf16[16,96,128]{2,1,0:T(8,128)(2,1)}, u32[]{:S(2)}, u32[]{:S(2)}) async-start(bf16[16,96,128]{2,1,0:T(8,128)(2,1)} %copy-done.8), calls=%async_computation.2 | async-start | bytes 786432 | tf_op jit(solution)/shard_map/all_to_all | solution.py:329
  82.3 20.1 %collective-permute-start.10 = (bf16[288,1024]{1,0:T(8,128)(2,1)S(1)}, bf16[288,1024]{1,0:T(8,128)(2,1)S(1)}, u32[]{:S(2)}, u32[]{:S(2)}) collective-permute-start(bf16[288,1024]{1,0:T(8,128)(2,1)S(1)} %bitcast.40), channel_id=1, source_target_pairs={{0,3},{1,0},{2,1},{3,2},{4,7},{5,4},{6,5},{7,6},{8,11},{9,8},{10,9... | collective-permute-start | bytes 1769480 | tf_op jit(solution)/shard_map/ppermute | solution.py:35
  84.8 29.7 %collective-permute-start.11 = (bf16[288,1024]{1,0:T(8,128)(2,1)S(1)}, bf16[288,1024]{1,0:T(8,128)(2,1)S(1)}, u32[]{:S(2)}, u32[]{:S(2)}) collective-permute-start(bf16[288,1024]{1,0:T(8,128)(2,1)S(1)} %bitcast.41), channel_id=1, source_target_pairs={{0,2},{1,3},{2,0},{3,1},{4,6},{5,7},{6,4},{7,5},{8,10},{9,11},{10,... | collective-permute-start | bytes 1769480 | tf_op jit(solution)/shard_map/ppermute | solution.py:35
  87.5 28.5 %collective-permute-start.9 = (bf16[288,1024]{1,0:T(8,128)(2,1)S(1)}, bf16[288,1024]{1,0:T(8,128)(2,1)S(1)}, u32[]{:S(2)}, u32[]{:S(2)}) collective-permute-start(bf16[288,1024]{1,0:T(8,128)(2,1)S(1)} %bitcast.42), channel_id=1, source_target_pairs={{0,1},{1,2},{2,3},{3,0},{4,5},{5,6},{6,7},{7,4},{8,9},{9,10},{10,1... | collective-permute-start | bytes 1769480 | tf_op jit(solution)/shard_map/ppermute | solution.py:35
  124.6 6.2 %copy-start.12 = (bf16[512,72]{1,0:T(8,128)(2,1)}, bf16[512,72]{1,0:T(8,128)(2,1)S(1)}, u32[]{:S(2)}) copy-start(bf16[512,72]{1,0:T(8,128)(2,1)S(1)} %get-tuple-element.30) | copy-start | bytes 221188
  124.6 11.3 %copy-start.24 = (bf16[4,8,288]{2,1,0:T(8,128)(2,1)S(1)}, bf16[4,8,288]{2,1,0:T(8,128)(2,1)}, u32[]{:S(2)}) copy-start(bf16[4,8,288]{2,1,0:T(8,128)(2,1)} %copy-done.23) | copy-start | bytes 55300
  124.6 15.9 %copy-start.22 = (bf16[4,8,288]{2,1,0:T(8,128)(2,1)S(1)}, bf16[4,8,288]{2,1,0:T(8,128)(2,1)}, u32[]{:S(2)}) copy-start(bf16[4,8,288]{2,1,0:T(8,128)(2,1)} %copy-done.21) | copy-start | bytes 55300
  124.6 22.6 %copy-start.10 = (bf16[4,64,288]{2,1,0:T(8,128)(2,1)S(1)}, bf16[4,64,288]{2,1,0:T(8,128)(2,1)}, u32[]{:S(2)}) copy-start(bf16[4,64,288]{2,1,0:T(8,128)(2,1)} %copy-done.9) | copy-start | bytes 442372
  124.7 5.3 %collective-permute-start.17 = (bf16[16,32,360]{2,1,0:T(8,128)(2,1)S(1)}, bf16[16,32,360]{2,1,0:T(8,128)(2,1)S(1)}, u32[]{:S(2)}, u32[]{:S(2)}) collective-permute-start(bf16[16,32,360]{2,1,0:T(8,128)(2,1)S(1)} %get-tuple-element.26), channel_id=1, source_target_pairs={{0,16},{16,0},{1,17},{17,1},{2,18},{18,2},{3,19},{19,3},{4,20},{20... | collective-permute-start | bytes 1105928 | tf_op jit(solution)/shard_map/ppermute | solution.py:340
  130.8 17.1 %all-to-all-start.4 = ((bf16[4,4,32,360]{3,2,1,0:T(8,128)(2,1)}), bf16[4,4,32,360]{3,2,1,0:T(8,128)(2,1)}, u32[]{:S(2)}, u32[]{:S(2)}) async-start(bf16[4,4,32,360]{3,2,1,0:T(8,128)(2,1)} %bitcast.45), calls=%async_computation.4 | async-start | bytes 786432 | tf_op jit(solution)/shard_map/all_to_all | solution.py:343
  135.9 6.6 %collective-permute-start.12 = (bf16[4,8,288]{2,1,0:T(8,128)(2,1)S(1)}, bf16[4,8,288]{2,1,0:T(8,128)(2,1)S(1)}, u32[]{:S(2)}, u32[]{:S(2)}) collective-permute-start(bf16[4,8,288]{2,1,0:T(8,128)(2,1)S(1)} %copy-done.24), channel_id=1, source_target_pairs={{0,1},{1,2},{2,3},{3,4},{4,5},{5,6},{6,7},{7,8},{8,9},{9,10},{10,1... | collective-permute-start | bytes 55304 | tf_op jit(solution)/shard_map/ppermute | solution.py:30
  140.5 6.7 %collective-permute-start.13 = (bf16[4,8,288]{2,1,0:T(8,128)(2,1)S(1)}, bf16[4,8,288]{2,1,0:T(8,128)(2,1)S(1)}, u32[]{:S(2)}, u32[]{:S(2)}) collective-permute-start(bf16[4,8,288]{2,1,0:T(8,128)(2,1)S(1)} %copy-done.22), channel_id=1, source_target_pairs={{1,0},{2,1},{3,2},{4,3},{5,4},{6,5},{7,6},{8,7},{9,8},{10,9},{11,1... | collective-permute-start | bytes 55304 | tf_op jit(solution)/shard_map/ppermute | solution.py:30
  147.9 21.7 %all-to-all-start.3 = ((bf16[4,80,288]{2,1,0:T(8,128)(2,1)}), bf16[4,80,288]{2,1,0:T(8,128)(2,1)S(1)}, u32[]{:S(2)}, u32[]{:S(2)}) async-start(bf16[4,80,288]{2,1,0:T(8,128)(2,1)} %pad_maximum_fusion), calls=%async_computation.3 | async-start | bytes 491520 | tf_op jit(solution)/shard_map/all_to_all | solution.py:332
  157.5 12.2 %copy-start.25 = (f32[4,32,360]{2,1,0:T(8,128)}, f32[4,32,360]{2,1,0:T(8,128)S(1)}, u32[]{:S(2)}) copy-start(f32[4,32,360]{2,1,0:T(8,128)S(1)} %convert_reduce_fusion) | copy-start | bytes 552964
  157.5 27.9 %collective-permute-start.18 = (bf16[2,32,360]{2,1,0:T(8,128)(2,1)S(1)}, bf16[2,32,360]{2,1,0:T(8,128)(2,1)}, u32[]{:S(2)}, u32[]{:S(2)}) collective-permute-start(bf16[2,32,360]{2,1,0:T(8,128)(2,1)S(1)} %dynamic-slice_convert_fusion), channel_id=1, source_target_pairs={{0,256},{128,384},{256,0},{384,128},{1,257},{129,385},{257,1},{385... | collective-permute-start | bytes 138248 | tf_op jit(solution)/shard_map/ppermute | solution.py:347
  169.7 15.7 %copy-start.26 = (f32[4,32,360]{2,1,0:T(8,128)S(1)}, f32[4,32,360]{2,1,0:T(8,128)}, u32[]{:S(2)}) copy-start(f32[4,32,360]{2,1,0:T(8,128)} %copy-done.25) | copy-start | bytes 552964
  169.7 20.7 %copy-start.1 = (bf16[128,1024]{1,0:T(8,128)(2,1)S(1)}, bf16[128,1024]{1,0:T(8,128)(2,1)}, u32[]{:S(2)}) copy-start(bf16[128,1024]{1,0:T(8,128)(2,1)} %act_ref.1) | copy-start | bytes 786436
  174.1 16.3 %collective-permute-start.14 = (bf16[64,1024]{1,0:T(8,128)(2,1)}, bf16[64,1024]{1,0:T(8,128)(2,1)S(1)}, u32[]{:S(2)}, u32[]{:S(2)}) collective-permute-start(bf16[64,1024]{1,0:T(8,128)(2,1)} %get-tuple-element.22), channel_id=1, source_target_pairs={{0,8},{4,12},{8,0},{12,4},{1,9},{5,13},{9,1},{13,5},{2,10},{6,14},... | collective-permute-start | bytes 393224 | tf_op jit(solution)/shard_map/ppermute | solution.py:35
  178.3 12.0 %collective-permute-start.15 = (bf16[64,1024]{1,0:T(8,128)(2,1)}, bf16[64,1024]{1,0:T(8,128)(2,1)S(1)}, u32[]{:S(2)}, u32[]{:S(2)}) collective-permute-start(bf16[64,1024]{1,0:T(8,128)(2,1)} %get-tuple-element.23), channel_id=1, source_target_pairs={{0,4},{4,8},{8,12},{12,0},{1,5},{5,9},{9,13},{13,1},{2,6},{6,10},{... | collective-permute-start | bytes 393224 | tf_op jit(solution)/shard_map/ppermute | solution.py:35
  181.4 8.9 %collective-permute-start.16 = (bf16[64,1024]{1,0:T(8,128)(2,1)}, bf16[64,1024]{1,0:T(8,128)(2,1)S(1)}, u32[]{:S(2)}, u32[]{:S(2)}) collective-permute-start(bf16[64,1024]{1,0:T(8,128)(2,1)} %get-tuple-element.24), channel_id=1, source_target_pairs={{0,12},{4,0},{8,4},{12,8},{1,13},{5,1},{9,5},{13,9},{2,14},{6,2},{... | collective-permute-start | bytes 393224 | tf_op jit(solution)/shard_map/ppermute | solution.py:35
  186.3 9.2 %collective-permute-start.19 = (bf16[32,360]{1,0:T(8,128)(2,1)S(1)}, bf16[32,360]{1,0:T(8,128)(2,1)S(1)}, u32[]{:S(2)}, u32[]{:S(2)}) collective-permute-start(bf16[32,360]{1,0:T(8,128)(2,1)S(1)} %fusion), channel_id=1, source_target_pairs={{0,128},{128,0},{256,384},{384,256},{1,129},{129,1},{257,385},{385... | collective-permute-start | bytes 69128 | tf_op jit(solution)/shard_map/ppermute | solution.py:351
  (19 other events, 14.7 us)

commit v10 on v7

--- a/solution.py
+++ b/solution.py
@@ -85,14 +85,45 @@
     )
 
 
+def pack_kernel(where_ref, weight_ref, cot_ref, own_ref, *pack_refs):
+    taps, block, width = weight_ref.shape
+    step = own_ref.shape[0]
+    half = width // 2
+    core, y = where_ref[0], where_ref[2]
+    for j, ref in enumerate((own_ref, *pack_refs)):
+        ref[:step, :] = jnp.zeros((step, half), bf16)
+        for f in range(4):
+            at = pl.multiple_of((f * 4 + lax.rem(y + j, 4)) * step, step)
+            ref[:step, 128 * f : 128 * f + block] = cot_ref[pl.ds(at, step), :]
+    for k in range(taps):
+        piece = weight_ref[k, :, pl.ds(pl.multiple_of(core * half, 128), half)]
+        for ref in pack_refs:
+            ref[step + k * block : step + (k + 1) * block, :] = piece
+
+
+def pack_shards(where, weight, cot):
+    taps, block, width = weight.shape
+    step = cot.shape[0] // 16
+    shapes = (jax.ShapeDtypeStruct((step, width // 2), bf16),) + (
+        jax.ShapeDtypeStruct((step + taps * block, width // 2), bf16),
+    ) * 3
+    return local_call(pack_kernel, shapes, [], where, weight, cot)
+
+
 def conv_kernel(where_ref, flat_ref, first_ref, second_ref, *refs):
-    cot_refs, out_ref, tap_ref = refs[:4], refs[4], refs[5]
+    own_ref, pack_refs, (out_ref, tap_ref, cot_ref, done) = refs[0], refs[1:4], refs[4:]
     lanes = flat_ref.shape[0]
     taps, group, half = first_ref.shape
     core, y = where_ref[0], where_ref[2]
     span = lanes // 4
     own = span - 8
-    step, block = cot_refs[0].shape[1:]
+    step, block = own_ref.shape[0], group // 4
+    copies = [
+        pltpu.make_async_copy(pack_refs[j].at[pl.ds(0, step), :], cot_ref.at[j], done.at[j])
+        for j in range(3)
+    ]
+    for copy in copies:
+        copy.start()
     near = flat_ref[:, pl.ds(pl.multiple_of(core * half, 128), half)]
     far = flat_ref[:, pl.ds(pl.multiple_of((1 - core) * half, 128), half)]
     contract = (((1,), (1,)), ((), ()))
@@ -101,6 +132,9 @@
         tap_ref[k, :lanes, :] = lax.dot_general(
             near, first_ref[k], contract, preferred_element_type=f32
         ) + lax.dot_general(far, second_ref[k], contract, preferred_element_type=f32)
+    for copy in copies:
+        copy.wait()
+    cots = [own_ref[...]] + [cot_ref[j] for j in range(3)]
     source = lax.broadcasted_iota(jnp.int32, (block, group), 0)
     lane = lax.broadcasted_iota(jnp.int32, (block, group), 1)
     for f in range(4):
@@ -111,16 +145,29 @@
         placed = jnp.zeros((step, group), f32)
         for j in range(4):
             place = (lane == source + lax.rem(y - j + 4, 4) * block).astype(bf16)
-            placed = placed + jnp.dot(cot_refs[j][f], place, preferred_element_type=f32)
+            placed = placed + jnp.dot(
+                cots[j][:, 128 * f : 128 * f + block], place, preferred_element_type=f32
+            )
         out_ref[f, own:, :] = placed.astype(bf16)
 
 
-def conv_forward(where, flat, first, second, cots):
+def conv_forward(where, flat, first, second, own, packs):
     taps, group, _ = first.shape
     span = flat.shape[0] // 4
-    shape = jax.ShapeDtypeStruct((4, span - 8 + cots[0].shape[1], group), bf16)
-    scratch = [pltpu.VMEM((taps, flat.shape[0] + 8, group), f32)]
-    return local_call(conv_kernel, shape, scratch, where, flat, first, second, *cots)
+    vmem, hbm = pl.BlockSpec(memory_space=pltpu.VMEM), pl.BlockSpec(memory_space=pl.ANY)
+    return pl.pallas_call(
+        conv_kernel,
+        out_shape=jax.ShapeDtypeStruct((4, span - 8 + own.shape[0], group), bf16),
+        in_specs=[pl.BlockSpec(memory_space=pltpu.SMEM)] + [vmem] * 4 + [hbm] * 3,
+        out_specs=vmem,
+        scratch_shapes=[
+            pltpu.VMEM((taps, flat.shape[0] + 8, group), f32),
+            pltpu.VMEM((3, *own.shape), bf16),
+            pltpu.SemaphoreType.DMA((3,)),
+        ],
+        compiler_params=pltpu.CompilerParams(vmem_limit_bytes=12 << 20),
+        name="conv_forward",
+    )(where, flat, first, second, own, *packs)
 
 
 def backward_kernel(rows, where_ref, flat_ref, first_ref, second_ref, *refs):
@@ -263,8 +310,9 @@
         step = mine_ref.shape[1]
         near = pl.ds(pl.multiple_of(c * 2 * step + core * step, step), step)
         far = pl.ds(pl.multiple_of(c * 2 * step + (1 - core) * step, step), step)
-        mine_ref[c] = part_ref[near, : taps * block]
-        other_ref[c] = part_ref[far, : taps * block].astype(bf16)
+        at = c % 4 * 4 + c // 4
+        mine_ref[at] = part_ref[near, : taps * block]
+        other_ref[at] = part_ref[far, : taps * block].astype(bf16)
 
 
 def weight_partial(where, back, ring, taps, block):
@@ -300,9 +348,11 @@
     low = shift(activations[-8:], AXES, 1)
     high = shift(activations[:8], AXES, -1)
 
-    own_half = jnp.where(core == 0, conv_weight[:, :, :half], conv_weight[:, :, half:])
-    own_half = lax.optimization_barrier(own_half)
-    shards = [own_half] + [turn(own_half, "y", j) for j in (1, 2, 3)]
+    where = jnp.stack([core, zl, y]).astype(jnp.int32)
+    own_cot, *packs = pack_shards(where, conv_weight, cotangent)
+    packs = [turn(packs[j], "y", j + 1) for j in range(3)]
+    shards = [jnp.where(core == 0, conv_weight[:, :, :half], conv_weight[:, :, half:])]
+    shards += [pack[step:].reshape(tap_count, out_width, half) for pack in packs]
     first = jnp.zeros((tap_count, 4, out_width, half), bf16)
     first = lax.dynamic_update_slice_in_dim(first, shards[0][:, None], y, axis=1)
     for j in range(1, 4):
@@ -313,14 +363,8 @@
     block = pooled_block(low, activations, high)
     gathered = gather_all(block, "zl")
     flat = gathered.reshape(lanes, in_width)
-    where = jnp.stack([core, zl, y]).astype(jnp.int32)
-
-    cot, _ = lax.optimization_barrier((cotangent, block))
-    cot = cot.reshape(4, 4, step, out_width)
-    cots = [lax.dynamic_index_in_dim(cot, (y + j) % 4, 1, keepdims=False) for j in range(4)]
-    cots = cots[:1] + [turn(cots[j], "y", j) for j in (1, 2, 3)]
-
-    conv_out = conv_forward(where, flat, first, second, cots)
+
+    conv_out = conv_forward(where, flat, first, second, own_cot, packs)
     up, down = turn(flat, "y", 1), turn(flat, "y", -1)
     far = turn(flat, "y", 2)
     conv_out = lax.all_to_all(conv_out, "zl", 0, 0)
@@ -340,7 +384,9 @@
     )
     other = lax.ppermute(other, "core", [(0, 1), (1, 0)])
     total = (mine + other.astype(f32)).astype(bf16)
-    total = lax.all_to_all(total, ("zh", "x"), 0, 0)
+    total = lax.all_to_all(total.reshape(4, 4, *total.shape[1:]), "x", 0, 0)
+    total = jnp.sum(total.astype(f32), axis=0).astype(bf16)
+    total = lax.all_to_all(total, "zh", 0, 0)
     weight_grad = jnp.sum(total.astype(f32), axis=0).reshape(-1, tap_count, out_width)
     return (features, input_grad, weight_grad)
 

time: 193 us -> 199 us (1.031)
  the two profiles are of different devices: /device:TPU:34 before, /device:TPU:4 now
where the time goes in v10:
time: 199 us; the launch traced here: 197 us
  starting transfers between devices  89 us (45%)
  waiting for transfers between devices  57.3 us (29%)
  local copies, waits for them, and re-layouts  18.3 us (9%)
  Pallas kernels  16.3 us (8%)
  blocking collectives  11.5 us (6%)
  other arithmetic  3.51 us (2%)
    ppermute x9, starting transfers between devices, turn(): lax.ppermute(block, axis, [(i, (i + step) % count) for i in range(count)])  32.4 us
    ppermute x9, waiting for transfers between devices, turn(): lax.ppermute(block, axis, [(i, (i + step) % count) for i in range(count)])  26.7 us
    ppermute x4, starting transfers between devices, shift(): return lax.ppermute(block, axis, pairs)  18.5 us
    unnamed x49, local copies, waits for them, and re-layouts  14.2 us
    all_to_all x1, starting transfers between devices, per_device(): total = lax.all_to_all(total, 'zh', 0, 0)  13.1 us
    pallas_call x6, Pallas kernels, local_call(): pl.pallas_call(kernel, out_shape=shapes, in_specs=[pl.BlockSpec(memory_sp...  12.9 us
    all_to_all x1, blocking collectives, per_device(): conv_out = lax.all_to_all(conv_out, 'zl', 0, 0)  11.5 us
    ppermute x4, waiting for transfers between devices, shift(): return lax.ppermute(block, axis, pairs)  10.9 us
  transfers between devices with their start and end apart: 20, of which 10 were waited for; matrix products, arithmetic and copies ran while one was open for 4% of the time, Pallas kernels for 3%

profile of v10, /device:TPU:4, one launch (start us, length us, event | category | flops | bytes accessed | tf_op | source)
XLA Modules:
  0.0 197.0 jit_solution(1610041960075942607)
XLA Ops:
  5.1 3.6 %collective-permute-start.2 = (bf16[392,512]{1,0:T(8,128)(2,1)}, bf16[392,512]{1,0:T(8,128)(2,1)S(1)}, u32[]{:S(2)}, u32[]{:S(2)}) collective-permute-start(bf16[392,512]{1,0:T(8,128)(2,1)} %get-tuple-element.18), channel_id=1, source_target_pairs={{0,1},{1,2},{2,3},{3,0},{4,5},{5,6},{6,7},{7,4},{8,9},{9,10},{10,1... | collective-permute-start | bytes 1204232 | tf_op jit(solution)/shard_map/ppermute | solution.py:35
  8.7 4.8 %collective-permute-start.3 = (bf16[392,512]{1,0:T(8,128)(2,1)}, bf16[392,512]{1,0:T(8,128)(2,1)}, u32[]{:S(2)}, u32[]{:S(2)}) collective-permute-start(bf16[392,512]{1,0:T(8,128)(2,1)} %get-tuple-element.19), channel_id=1, source_target_pairs={{0,2},{1,3},{2,0},{3,1},{4,6},{5,7},{6,4},{7,5},{8,10},{9,11},{10,... | collective-permute-start | bytes 1204232 | tf_op jit(solution)/shard_map/ppermute | solution.py:35
  13.5 3.3 %collective-permute-start.4 = (bf16[392,512]{1,0:T(8,128)(2,1)}, bf16[392,512]{1,0:T(8,128)(2,1)}, u32[]{:S(2)}, u32[]{:S(2)}) collective-permute-start(bf16[392,512]{1,0:T(8,128)(2,1)} %get-tuple-element.20), channel_id=1, source_target_pairs={{0,3},{1,0},{2,1},{3,2},{4,7},{5,4},{6,5},{7,6},{8,11},{9,8},{10,9... | collective-permute-start | bytes 1204232 | tf_op jit(solution)/shard_map/ppermute | solution.py:35
  17.5 2.6 %collective-permute-start = (bf16[8,1024]{1,0:T(8,128)(2,1)S(1)}, bf16[8,1024]{1,0:T(8,128)(2,1)S(1)}, u32[]{:S(2)}, u32[]{:S(2)}) collective-permute-start(bf16[8,1024]{1,0:T(8,128)(2,1)S(1)} %get-tuple-element.43), channel_id=1, source_target_pairs={{0,1},{1,2},{2,3},{3,4},{4,5},{5,6},{6,7},{7,8},{8,9},{9,10},{10,1... | collective-permute-start | bytes 49160 | tf_op jit(solution)/shard_map/ppermute | solution.py:30
  20.1 7.8 %collective-permute-start.1 = (bf16[8,1024]{1,0:T(8,128)(2,1)S(1)}, bf16[8,1024]{1,0:T(8,128)(2,1)S(1)}, u32[]{:S(2)}, u32[]{:S(2)}) collective-permute-start(bf16[8,1024]{1,0:T(8,128)(2,1)S(1)} %get-tuple-element.42), channel_id=1, source_target_pairs={{1,0},{2,1},{3,2},{4,3},{5,4},{6,5},{7,6},{8,7},{9,8},{10,9},{11,1... | collective-permute-start | bytes 49160 | tf_op jit(solution)/shard_map/ppermute | solution.py:30
  28.3 2.9 %collective-permute-done.1.high_ref = bf16[8,1024]{1,0:T(8,128)(2,1)S(1)} collective-permute-done((bf16[8,1024]{1,0:T(8,128)(2,1)S(1)}, bf16[8,1024]{1,0:T(8,128)(2,1)S(1)}, u32[]{:S(2)}, u32[]{:S(2)}) %collective-permute-start.1) | collective-permute-done | bytes 16416 | tf_op jit(solution)/shard_map/ppermute | solution.py:30
  32.6 5.9 %all-to-all-start = ((bf16[4,72,1024]{2,1,0:T(8,128)(2,1)}), bf16[4,72,1024]{2,1,0:T(8,128)(2,1)S(1)}, u32[]{:S(2)}, u32[]{:S(2)}) async-start(bf16[4,72,1024]{2,1,0:T(8,128)(2,1)} %broadcast_in_dim.9), calls=%async_computation | async-start | bytes 1179648 | tf_op jit(solution)/shard_map/all_to_all | solution.py:40
  40.8 1.9 collective-permute-start.5
  42.8 10.7 %all-to-all-done = bf16[4,72,1024]{2,1,0:T(8,128)(2,1)S(1)} async-done(((bf16[4,72,1024]{2,1,0:T(8,128)(2,1)}), bf16[4,72,1024]{2,1,0:T(8,128)(2,1)S(1)}, u32[]{:S(2)}, u32[]{:S(2)}) %all-to-all-start) | async-done | bytes 589856 | tf_op jit(solution)/shard_map/all_to_all | solution.py:40
  55.2 3.3 %conv_forward.1 = bf16[4,96,288]{2,1,0:T(8,128)(2,1)S(1)} custom-call(s32[3]{0:T(128)S(1)} %pad_add_fusion.where_ref, bf16[288,1024]{1,0:T(8,128)(2,1)S(1)} %bitcast.23, bf16[5,288,512]{2,1,0:T(8,128)(2,1)S(1)} %bitcast.21, bf16[5,288,512]{2,1,0:T(8,128)(2,1)S(1)} %collective-permute-done.5.second_ref, bf16[32,512]{1,0:T(8,128)(2,1)S(1)} %copy-done.18, ...), custom_call_target="tpu_custom_call" | custom-call | tf_op jit(solution)/shard_map/conv_forward/pallas_call | solution.py:158
  58.6 11.5 %all_to_all.30.y_ref = bf16[4,96,288]{2,1,0:T(8,128)(2,1)S(1)} all-to-all(bf16[4,96,288]{2,1,0:T(8,128)(2,1)S(1)} %conv_forward.1), channel_id=1, replica_groups=mesh['zh'=4,'x'=4,'core'=2,'zl'=4,'y'=4] {'zl'}, dimensions={0} | all-to-all | bytes 442368 | tf_op jit(solution)/shard_map/all_to_all | solution.py:370
  74.3 5.9 %all-to-all-start.2 = ((bf16[16,96,128]{2,1,0:T(8,128)(2,1)}), bf16[16,96,128]{2,1,0:T(8,128)(2,1)}, u32[]{:S(2)}, u32[]{:S(2)}) async-start(bf16[16,96,128]{2,1,0:T(8,128)(2,1)} %copy-done.12), calls=%async_computation.2 | async-start | bytes 786432 | tf_op jit(solution)/shard_map/all_to_all | solution.py:372
  80.2 3.8 %collective-permute-start.6 = (bf16[288,1024]{1,0:T(8,128)(2,1)S(1)}, bf16[288,1024]{1,0:T(8,128)(2,1)S(1)}, u32[]{:S(2)}, u32[]{:S(2)}) collective-permute-start(bf16[288,1024]{1,0:T(8,128)(2,1)S(1)} %bitcast.24), channel_id=1, source_target_pairs={{0,1},{1,2},{2,3},{3,0},{4,5},{5,6},{6,7},{7,4},{8,9},{9,10},{10,1... | collective-permute-start | bytes 1769480 | tf_op jit(solution)/shard_map/ppermute | solution.py:35
  84.0 3.3 %collective-permute-start.7 = (bf16[288,1024]{1,0:T(8,128)(2,1)S(1)}, bf16[288,1024]{1,0:T(8,128)(2,1)S(1)}, u32[]{:S(2)}, u32[]{:S(2)}) collective-permute-start(bf16[288,1024]{1,0:T(8,128)(2,1)S(1)} %bitcast.25), channel_id=1, source_target_pairs={{0,3},{1,0},{2,1},{3,2},{4,7},{5,4},{6,5},{7,6},{8,11},{9,8},{10,9... | collective-permute-start | bytes 1769480 | tf_op jit(solution)/shard_map/ppermute | solution.py:35
  87.3 4.1 %collective-permute-start.8 = (bf16[288,1024]{1,0:T(8,128)(2,1)S(1)}, bf16[288,1024]{1,0:T(8,128)(2,1)S(1)}, u32[]{:S(2)}, u32[]{:S(2)}) collective-permute-start(bf16[288,1024]{1,0:T(8,128)(2,1)S(1)} %bitcast.26), channel_id=1, source_target_pairs={{0,2},{1,3},{2,0},{3,1},{4,6},{5,7},{6,4},{7,5},{8,10},{9,11},{10,... | collective-permute-start | bytes 1769480 | tf_op jit(solution)/shard_map/ppermute | solution.py:35
  91.4 10.2 %collective-permute-done.6.refs_1_ = bf16[288,1024]{1,0:T(8,128)(2,1)S(1)} collective-permute-done((bf16[288,1024]{1,0:T(8,128)(2,1)S(1)}, bf16[288,1024]{1,0:T(8,128)(2,1)S(1)}, u32[]{:S(2)}, u32[]{:S(2)}) %collective-permute-start.6) | collective-permute-done | bytes 589856 | tf_op jit(solution)/shard_map/ppermute | solution.py:35
  102.4 10.1 %collective-permute-done.7.refs_2_ = bf16[288,1024]{1,0:T(8,128)(2,1)S(1)} collective-permute-done((bf16[288,1024]{1,0:T(8,128)(2,1)S(1)}, bf16[288,1024]{1,0:T(8,128)(2,1)S(1)}, u32[]{:S(2)}, u32[]{:S(2)}) %collective-permute-start.7) | collective-permute-done | bytes 589856 | tf_op jit(solution)/shard_map/ppermute | solution.py:35
  117.6 4.6 %shard_map.61 = (f32[16,32,360]{2,1,0:T(8,128)S(1)}, bf16[16,32,360]{2,1,0:T(8,128)(2,1)S(1)}, bf16[512,72]{1,0:T(8,128)(2,1)S(1)}) custom-call(s32[3]{0:T(128)S(1)} %pad_add_fusion.where_ref, bf16[16,96,128]{2,1,0:T(8,128)(2,1)} %all-to-all-done.2.back_ref, bf16[288,1024]{1,0:T(8,128)(2,1)S(1)} %bitcast.27, bf16[288,1024]{1,0:T(8,128)(2,1)S(1)} %copy-done.7, ...), custom_call_target="tpu_custom_call" | custom-call | tf_op jit(solution)/shard_map/pallas_call | solution.py:45
  122.3 2.1 %collective-permute-start.14 = (bf16[16,32,360]{2,1,0:T(8,128)(2,1)S(1)}, bf16[16,32,360]{2,1,0:T(8,128)(2,1)S(1)}, u32[]{:S(2)}, u32[]{:S(2)}) collective-permute-start(bf16[16,32,360]{2,1,0:T(8,128)(2,1)S(1)} %get-tuple-element.32), channel_id=1, source_target_pairs={{0,16},{16,0},{1,17},{17,1},{2,18},{18,2},{3,19},{19,3},{4,20},{20... | collective-permute-start | bytes 1105928 | tf_op jit(solution)/shard_map/ppermute | solution.py:385
  126.9 5.8 %all-to-all-start.4 = ((bf16[4,4,32,360]{3,2,1,0:T(8,128)(2,1)}), bf16[4,4,32,360]{3,2,1,0:T(8,128)(2,1)}, u32[]{:S(2)}, u32[]{:S(2)}) async-start(bf16[4,4,32,360]{3,2,1,0:T(8,128)(2,1)} %bitcast.29), calls=%async_computation.4 | async-start | bytes 786432 | tf_op jit(solution)/shard_map/all_to_all | solution.py:387
  132.7 6.3 %collective-permute-start.10 = (bf16[4,8,288]{2,1,0:T(8,128)(2,1)S(1)}, bf16[4,8,288]{2,1,0:T(8,128)(2,1)S(1)}, u32[]{:S(2)}, u32[]{:S(2)}) collective-permute-start(bf16[4,8,288]{2,1,0:T(8,128)(2,1)S(1)} %copy-done.22), channel_id=1, source_target_pairs={{1,0},{2,1},{3,2},{4,3},{5,4},{6,5},{7,6},{8,7},{9,8},{10,9},{11,1... | collective-permute-start | bytes 55304 | tf_op jit(solution)/shard_map/ppermute | solution.py:30
  138.9 1.9 collective-permute-start.9
  140.9 8.1 %collective-permute-done.9 = bf16[4,8,288]{2,1,0:T(8,128)(2,1)S(1)} collective-permute-done((bf16[4,8,288]{2,1,0:T(8,128)(2,1)S(1)}, bf16[4,8,288]{2,1,0:T(8,128)(2,1)S(1)}, u32[]{:S(2)}, u32[]{:S(2)}) %collective-permute-start.9) | collective-permute-done | bytes 18464 | tf_op jit(solution)/shard_map/ppermute | solution.py:30
  149.7 3.4 %all-to-all-start.3 = ((bf16[4,80,288]{2,1,0:T(8,128)(2,1)}), bf16[4,80,288]{2,1,0:T(8,128)(2,1)S(1)}, u32[]{:S(2)}, u32[]{:S(2)}) async-start(bf16[4,80,288]{2,1,0:T(8,128)(2,1)} %pad_maximum_fusion), calls=%async_computation.3 | async-start | bytes 491520 | tf_op jit(solution)/shard_map/all_to_all | solution.py:375
  153.1 1.7 reduce_sum.21
  154.8 7.3 %all-to-all-done.3 = bf16[4,80,288]{2,1,0:T(8,128)(2,1)S(1)} async-done(((bf16[4,80,288]{2,1,0:T(8,128)(2,1)}), bf16[4,80,288]{2,1,0:T(8,128)(2,1)S(1)}, u32[]{:S(2)}, u32[]{:S(2)}) %all-to-all-start.3) | async-done | bytes 184352 | tf_op jit(solution)/shard_map/all_to_all | solution.py:375
  162.1 13.1 %all-to-all-start.5 = ((bf16[4,32,360]{2,1,0:T(8,128)(2,1)}), bf16[4,32,360]{2,1,0:T(8,128)(2,1)S(1)}, u32[]{:S(2)}, u32[]{:S(2)}) async-start(bf16[4,32,360]{2,1,0:T(8,128)(2,1)} %reduce_sum.21), calls=%async_computation.5 | async-start | bytes 196608 | tf_op jit(solution)/shard_map/all_to_all | solution.py:389
  175.3 3.1 %shard_map.62 = (bf16[64,1024]{1,0:T(8,128)(2,1)S(1)}, bf16[64,1024]{1,0:T(8,128)(2,1)S(1)}, bf16[64,1024]{1,0:T(8,128)(2,1)S(1)}, bf16[64,1024]{1,0:T(8,128)(2,1)S(1)}) custom-call(s32[3]{0:T(128)S(1)} %pad_add_fusion.where_ref, bf16[320,288]{1,0:T(8,128)(2,1)S(1)} %bitcast.28, bf16[5,288,512]{2,1,0:T(8,128)(2,1)S(1)} %bitcast.22, ...), custom_call_target="tpu_custom_call" | custom-call | tf_op jit(solution)/shard_map/pallas_call | solution.py:45
  178.3 1.9 collective-permute-start.11
  180.2 3.9 %collective-permute-start.12 = (bf16[64,1024]{1,0:T(8,128)(2,1)S(1)}, bf16[64,1024]{1,0:T(8,128)(2,1)S(1)}, u32[]{:S(2)}, u32[]{:S(2)}) collective-permute-start(bf16[64,1024]{1,0:T(8,128)(2,1)S(1)} %get-tuple-element.29), channel_id=1, source_target_pairs={{0,4},{4,8},{8,12},{12,0},{1,5},{5,9},{9,13},{13,1},{2,6},{6,10},{... | collective-permute-start | bytes 393224 | tf_op jit(solution)/shard_map/ppermute | solution.py:35
  184.2 3.7 %collective-permute-start.13 = (bf16[64,1024]{1,0:T(8,128)(2,1)S(1)}, bf16[64,1024]{1,0:T(8,128)(2,1)S(1)}, u32[]{:S(2)}, u32[]{:S(2)}) collective-permute-start(bf16[64,1024]{1,0:T(8,128)(2,1)S(1)} %get-tuple-element.30), channel_id=1, source_target_pairs={{0,12},{4,0},{8,4},{12,8},{1,13},{5,1},{9,5},{13,9},{2,14},{6,2},{... | collective-permute-start | bytes 393224 | tf_op jit(solution)/shard_map/ppermute | solution.py:35
  187.9 4.6 %collective-permute-done.11.refs_1_ = bf16[64,1024]{1,0:T(8,128)(2,1)S(1)} collective-permute-done((bf16[64,1024]{1,0:T(8,128)(2,1)S(1)}, bf16[64,1024]{1,0:T(8,128)(2,1)S(1)}, u32[]{:S(2)}, u32[]{:S(2)}) %collective-permute-start.11) | collective-permute-done | bytes 131104 | tf_op jit(solution)/shard_map/ppermute | solution.py:35
  (81 shorter events, 28.8 us)
Async XLA Ops:
  1.7 1.1 copy-start
  2.8 25.2 %copy-start.1 = (bf16[5,72,1024]{2,1,0:T(8,128)(2,1)S(1)}, bf16[5,72,1024]{2,1,0:T(8,128)(2,1)}, u32[]{:S(2)}) copy-start(bf16[5,72,1024]{2,1,0:T(8,128)(2,1)} %weight_ref.1) | copy-start | bytes 2211844
  5.1 26.0 %copy-start.4 = (bf16[128,1024]{1,0:T(8,128)(2,1)S(1)}, bf16[128,1024]{1,0:T(8,128)(2,1)}, u32[]{:S(2)}) copy-start(bf16[128,1024]{1,0:T(8,128)(2,1)} %act_ref.1) | copy-start | bytes 786436
  5.1 33.4 %collective-permute-start.2 = (bf16[392,512]{1,0:T(8,128)(2,1)}, bf16[392,512]{1,0:T(8,128)(2,1)S(1)}, u32[]{:S(2)}, u32[]{:S(2)}) collective-permute-start(bf16[392,512]{1,0:T(8,128)(2,1)} %get-tuple-element.18), channel_id=1, source_target_pairs={{0,1},{1,2},{2,3},{3,0},{4,5},{5,6},{6,7},{7,4},{8,9},{9,10},{10,1... | collective-permute-start | bytes 1204232 | tf_op jit(solution)/shard_map/ppermute | solution.py:35
  8.7 29.9 %collective-permute-start.3 = (bf16[392,512]{1,0:T(8,128)(2,1)}, bf16[392,512]{1,0:T(8,128)(2,1)}, u32[]{:S(2)}, u32[]{:S(2)}) collective-permute-start(bf16[392,512]{1,0:T(8,128)(2,1)} %get-tuple-element.19), channel_id=1, source_target_pairs={{0,2},{1,3},{2,0},{3,1},{4,6},{5,7},{6,4},{7,5},{8,10},{9,11},{10,... | collective-permute-start | bytes 1204232 | tf_op jit(solution)/shard_map/ppermute | solution.py:35
  13.5 26.2 %collective-permute-start.4 = (bf16[392,512]{1,0:T(8,128)(2,1)}, bf16[392,512]{1,0:T(8,128)(2,1)}, u32[]{:S(2)}, u32[]{:S(2)}) collective-permute-start(bf16[392,512]{1,0:T(8,128)(2,1)} %get-tuple-element.20), channel_id=1, source_target_pairs={{0,3},{1,0},{2,1},{3,2},{4,7},{5,4},{6,5},{7,6},{8,11},{9,8},{10,9... | collective-permute-start | bytes 1204232 | tf_op jit(solution)/shard_map/ppermute | solution.py:35
  17.5 10.7 %collective-permute-start = (bf16[8,1024]{1,0:T(8,128)(2,1)S(1)}, bf16[8,1024]{1,0:T(8,128)(2,1)S(1)}, u32[]{:S(2)}, u32[]{:S(2)}) collective-permute-start(bf16[8,1024]{1,0:T(8,128)(2,1)S(1)} %get-tuple-element.43), channel_id=1, source_target_pairs={{0,1},{1,2},{2,3},{3,4},{4,5},{5,6},{6,7},{7,8},{8,9},{9,10},{10,1... | collective-permute-start | bytes 49160 | tf_op jit(solution)/shard_map/ppermute | solution.py:30
  20.1 11.0 %collective-permute-start.1 = (bf16[8,1024]{1,0:T(8,128)(2,1)S(1)}, bf16[8,1024]{1,0:T(8,128)(2,1)S(1)}, u32[]{:S(2)}, u32[]{:S(2)}) collective-permute-start(bf16[8,1024]{1,0:T(8,128)(2,1)S(1)} %get-tuple-element.42), channel_id=1, source_target_pairs={{1,0},{2,1},{3,2},{4,3},{5,4},{6,5},{7,6},{8,7},{9,8},{10,9},{11,1... | collective-permute-start | bytes 49160 | tf_op jit(solution)/shard_map/ppermute | solution.py:30
  32.6 20.8 %all-to-all-start = ((bf16[4,72,1024]{2,1,0:T(8,128)(2,1)}), bf16[4,72,1024]{2,1,0:T(8,128)(2,1)S(1)}, u32[]{:S(2)}, u32[]{:S(2)}) async-start(bf16[4,72,1024]{2,1,0:T(8,128)(2,1)} %broadcast_in_dim.9), calls=%async_computation | async-start | bytes 1179648 | tf_op jit(solution)/shard_map/all_to_all | solution.py:40
  38.5 2.2 %copy-start.2 = (bf16[392,512]{1,0:T(8,128)(2,1)}, bf16[392,512]{1,0:T(8,128)(2,1)S(1)}, u32[]{:S(2)}) copy-start(bf16[392,512]{1,0:T(8,128)(2,1)S(1)} %collective-permute-done.2.refs_1_) | copy-start | bytes 1204228
  40.8 12.6 %collective-permute-start.5 = (bf16[5,288,512]{2,1,0:T(8,128)(2,1)S(1)}, bf16[5,288,512]{2,1,0:T(8,128)(2,1)S(1)}, u32[]{:S(2)}, u32[]{:S(2)}) collective-permute-start(bf16[5,288,512]{2,1,0:T(8,128)(2,1)S(1)} %bitcast.20), channel_id=1, source_target_pairs={{0,16},{16,0},{1,17},{17,1},{2,18},{18,2},{3,19},{19,3},{4,20},{20... | collective-permute-start | bytes 4423688 | tf_op jit(solution)/shard_map/ppermute | solution.py:361
  74.3 40.1 %all-to-all-start.2 = ((bf16[16,96,128]{2,1,0:T(8,128)(2,1)}), bf16[16,96,128]{2,1,0:T(8,128)(2,1)}, u32[]{:S(2)}, u32[]{:S(2)}) async-start(bf16[16,96,128]{2,1,0:T(8,128)(2,1)} %copy-done.12), calls=%async_computation.2 | async-start | bytes 786432 | tf_op jit(solution)/shard_map/all_to_all | solution.py:372
  80.2 21.3 %collective-permute-start.6 = (bf16[288,1024]{1,0:T(8,128)(2,1)S(1)}, bf16[288,1024]{1,0:T(8,128)(2,1)S(1)}, u32[]{:S(2)}, u32[]{:S(2)}) collective-permute-start(bf16[288,1024]{1,0:T(8,128)(2,1)S(1)} %bitcast.24), channel_id=1, source_target_pairs={{0,1},{1,2},{2,3},{3,0},{4,5},{5,6},{6,7},{7,4},{8,9},{9,10},{10,1... | collective-permute-start | bytes 1769480 | tf_op jit(solution)/shard_map/ppermute | solution.py:35
  84.0 28.5 %collective-permute-start.7 = (bf16[288,1024]{1,0:T(8,128)(2,1)S(1)}, bf16[288,1024]{1,0:T(8,128)(2,1)S(1)}, u32[]{:S(2)}, u32[]{:S(2)}) collective-permute-start(bf16[288,1024]{1,0:T(8,128)(2,1)S(1)} %bitcast.25), channel_id=1, source_target_pairs={{0,3},{1,0},{2,1},{3,2},{4,7},{5,4},{6,5},{7,6},{8,11},{9,8},{10,9... | collective-permute-start | bytes 1769480 | tf_op jit(solution)/shard_map/ppermute | solution.py:35
  87.3 26.3 %collective-permute-start.8 = (bf16[288,1024]{1,0:T(8,128)(2,1)S(1)}, bf16[288,1024]{1,0:T(8,128)(2,1)S(1)}, u32[]{:S(2)}, u32[]{:S(2)}) collective-permute-start(bf16[288,1024]{1,0:T(8,128)(2,1)S(1)} %bitcast.26), channel_id=1, source_target_pairs={{0,2},{1,3},{2,0},{3,1},{4,6},{5,7},{6,4},{7,5},{8,10},{9,11},{10,... | collective-permute-start | bytes 1769480 | tf_op jit(solution)/shard_map/ppermute | solution.py:35
  114.4 1.1 copy-start.7
  115.5 1.1 copy-start.9
  122.2 4.7 %copy-start.15 = (bf16[512,72]{1,0:T(8,128)(2,1)}, bf16[512,72]{1,0:T(8,128)(2,1)S(1)}, u32[]{:S(2)}) copy-start(bf16[512,72]{1,0:T(8,128)(2,1)S(1)} %get-tuple-element.39) | copy-start | bytes 221188
  122.2 10.4 %copy-start.22 = (bf16[4,8,288]{2,1,0:T(8,128)(2,1)S(1)}, bf16[4,8,288]{2,1,0:T(8,128)(2,1)}, u32[]{:S(2)}) copy-start(bf16[4,8,288]{2,1,0:T(8,128)(2,1)} %copy-done.21) | copy-start | bytes 55300
  122.3 16.7 %copy-start.20 = (bf16[4,8,288]{2,1,0:T(8,128)(2,1)S(1)}, bf16[4,8,288]{2,1,0:T(8,128)(2,1)}, u32[]{:S(2)}) copy-start(bf16[4,8,288]{2,1,0:T(8,128)(2,1)} %copy-done.19) | copy-start | bytes 55300
  122.3 26.7 %copy-start.14 = (bf16[4,64,288]{2,1,0:T(8,128)(2,1)S(1)}, bf16[4,64,288]{2,1,0:T(8,128)(2,1)}, u32[]{:S(2)}) copy-start(bf16[4,64,288]{2,1,0:T(8,128)(2,1)} %copy-done.13) | copy-start | bytes 442372
  122.3 3.7 %collective-permute-start.14 = (bf16[16,32,360]{2,1,0:T(8,128)(2,1)S(1)}, bf16[16,32,360]{2,1,0:T(8,128)(2,1)S(1)}, u32[]{:S(2)}, u32[]{:S(2)}) collective-permute-start(bf16[16,32,360]{2,1,0:T(8,128)(2,1)S(1)} %get-tuple-element.32), channel_id=1, source_target_pairs={{0,16},{16,0},{1,17},{17,1},{2,18},{18,2},{3,19},{19,3},{4,20},{20... | collective-permute-start | bytes 1105928 | tf_op jit(solution)/shard_map/ppermute | solution.py:385
  126.9 22.8 %all-to-all-start.4 = ((bf16[4,4,32,360]{3,2,1,0:T(8,128)(2,1)}), bf16[4,4,32,360]{3,2,1,0:T(8,128)(2,1)}, u32[]{:S(2)}, u32[]{:S(2)}) async-start(bf16[4,4,32,360]{3,2,1,0:T(8,128)(2,1)} %bitcast.29), calls=%async_computation.4 | async-start | bytes 786432 | tf_op jit(solution)/shard_map/all_to_all | solution.py:387
  132.7 8.2 %collective-permute-start.10 = (bf16[4,8,288]{2,1,0:T(8,128)(2,1)S(1)}, bf16[4,8,288]{2,1,0:T(8,128)(2,1)S(1)}, u32[]{:S(2)}, u32[]{:S(2)}) collective-permute-start(bf16[4,8,288]{2,1,0:T(8,128)(2,1)S(1)} %copy-done.22), channel_id=1, source_target_pairs={{1,0},{2,1},{3,2},{4,3},{5,4},{6,5},{7,6},{8,7},{9,8},{10,9},{11,1... | collective-permute-start | bytes 55304 | tf_op jit(solution)/shard_map/ppermute | solution.py:30
  138.9 10.0 %collective-permute-start.9 = (bf16[4,8,288]{2,1,0:T(8,128)(2,1)S(1)}, bf16[4,8,288]{2,1,0:T(8,128)(2,1)S(1)}, u32[]{:S(2)}, u32[]{:S(2)}) collective-permute-start(bf16[4,8,288]{2,1,0:T(8,128)(2,1)S(1)} %copy-done.20), channel_id=1, source_target_pairs={{0,1},{1,2},{2,3},{3,4},{4,5},{5,6},{6,7},{7,8},{8,9},{9,10},{10,1... | collective-permute-start | bytes 55304 | tf_op jit(solution)/shard_map/ppermute | solution.py:30
  149.7 12.5 %all-to-all-start.3 = ((bf16[4,80,288]{2,1,0:T(8,128)(2,1)}), bf16[4,80,288]{2,1,0:T(8,128)(2,1)S(1)}, u32[]{:S(2)}, u32[]{:S(2)}) async-start(bf16[4,80,288]{2,1,0:T(8,128)(2,1)} %pad_maximum_fusion), calls=%async_computation.3 | async-start | bytes 491520 | tf_op jit(solution)/shard_map/all_to_all | solution.py:375
  162.1 34.1 %all-to-all-start.5 = ((bf16[4,32,360]{2,1,0:T(8,128)(2,1)}), bf16[4,32,360]{2,1,0:T(8,128)(2,1)S(1)}, u32[]{:S(2)}, u32[]{:S(2)}) async-start(bf16[4,32,360]{2,1,0:T(8,128)(2,1)} %reduce_sum.21), calls=%async_computation.5 | async-start | bytes 196608 | tf_op jit(solution)/shard_map/all_to_all | solution.py:389
  175.3 18.8 %copy-start.5 = (bf16[128,1024]{1,0:T(8,128)(2,1)S(1)}, bf16[128,1024]{1,0:T(8,128)(2,1)}, u32[]{:S(2)}) copy-start(bf16[128,1024]{1,0:T(8,128)(2,1)} %act_ref.1) | copy-start | bytes 786436
  175.3 20.2 %copy-start.16 = (bf16[512,72]{1,0:T(8,128)(2,1)S(1)}, bf16[512,72]{1,0:T(8,128)(2,1)}, u32[]{:S(2)}) copy-start(bf16[512,72]{1,0:T(8,128)(2,1)} %copy-done.15) | copy-start | bytes 221188
  178.3 14.2 %collective-permute-start.11 = (bf16[64,1024]{1,0:T(8,128)(2,1)S(1)}, bf16[64,1024]{1,0:T(8,128)(2,1)S(1)}, u32[]{:S(2)}, u32[]{:S(2)}) collective-permute-start(bf16[64,1024]{1,0:T(8,128)(2,1)S(1)} %get-tuple-element.28), channel_id=1, source_target_pairs={{0,8},{4,12},{8,0},{12,4},{1,9},{5,13},{9,1},{13,5},{2,10},{6,14},... | collective-permute-start | bytes 393224 | tf_op jit(solution)/shard_map/ppermute | solution.py:35
  180.2 12.3 %collective-permute-start.12 = (bf16[64,1024]{1,0:T(8,128)(2,1)S(1)}, bf16[64,1024]{1,0:T(8,128)(2,1)S(1)}, u32[]{:S(2)}, u32[]{:S(2)}) collective-permute-start(bf16[64,1024]{1,0:T(8,128)(2,1)S(1)} %get-tuple-element.29), channel_id=1, source_target_pairs={{0,4},{4,8},{8,12},{12,0},{1,5},{5,9},{9,13},{13,1},{2,6},{6,10},{... | collective-permute-start | bytes 393224 | tf_op jit(solution)/shard_map/ppermute | solution.py:35
  184.2 9.8 %collective-permute-start.13 = (bf16[64,1024]{1,0:T(8,128)(2,1)S(1)}, bf16[64,1024]{1,0:T(8,128)(2,1)S(1)}, u32[]{:S(2)}, u32[]{:S(2)}) collective-permute-start(bf16[64,1024]{1,0:T(8,128)(2,1)S(1)} %get-tuple-element.30), channel_id=1, source_target_pairs={{0,12},{4,0},{8,4},{12,8},{1,13},{5,1},{9,5},{13,9},{2,14},{6,2},{... | collective-permute-start | bytes 393224 | tf_op jit(solution)/shard_map/ppermute | solution.py:35
  (11 other events, 8.6 us)

commit v11 on v7

--- a/solution.py
+++ b/solution.py
@@ -263,8 +263,9 @@
         step = mine_ref.shape[1]
         near = pl.ds(pl.multiple_of(c * 2 * step + core * step, step), step)
         far = pl.ds(pl.multiple_of(c * 2 * step + (1 - core) * step, step), step)
-        mine_ref[c] = part_ref[near, : taps * block]
-        other_ref[c] = part_ref[far, : taps * block].astype(bf16)
+        at = c % 4 * 4 + c // 4
+        mine_ref[at] = part_ref[near, : taps * block]
+        other_ref[at] = part_ref[far, : taps * block].astype(bf16)
 
 
 def weight_partial(where, back, ring, taps, block):
@@ -318,7 +319,9 @@
     cot, _ = lax.optimization_barrier((cotangent, block))
     cot = cot.reshape(4, 4, step, out_width)
     cots = [lax.dynamic_index_in_dim(cot, (y + j) % 4, 1, keepdims=False) for j in range(4)]
-    cots = cots[:1] + [turn(cots[j], "y", j) for j in (1, 2, 3)]
+    second_cot = turn(cots[2], "y", 2)
+    first_cot = turn(cots[1], "y", 1)
+    cots = [cots[0], first_cot, second_cot, turn(cots[3], "y", 3)]
 
     conv_out = conv_forward(where, flat, first, second, cots)
     up, down = turn(flat, "y", 1), turn(flat, "y", -1)
@@ -331,8 +334,8 @@
     framed = lax.all_to_all(framed, "zl", 0, 0)
 
     own = conv_backward(where, framed.reshape(-1, group), first, second, rows)
-    parts = [own[0], turn(own[2], "zl", 2)]
-    parts = parts + [turn(own[1], "zl", 1), turn(own[3], "zl", 3)]
+    parts = [own[0], turn(own[2], "zl", 2), turn(own[1], "zl", 1)]
+    parts = parts + [turn(own[3], "zl", 3)]
     input_grad = input_gradient(activations, parts)
 
     mine, other, features = weight_partial(
@@ -340,7 +343,9 @@
     )
     other = lax.ppermute(other, "core", [(0, 1), (1, 0)])
     total = (mine + other.astype(f32)).astype(bf16)
-    total = lax.all_to_all(total, ("zh", "x"), 0, 0)
+    total = lax.all_to_all(total.reshape(4, 4, *total.shape[1:]), "x", 0, 0)
+    total = jnp.sum(total.astype(f32), axis=0).astype(bf16)
+    total = lax.all_to_all(total, "zh", 0, 0)
     weight_grad = jnp.sum(total.astype(f32), axis=0).reshape(-1, tap_count, out_width)
     return (features, input_grad, weight_grad)
 

time: 193 us -> 199 us (1.031)
  the two profiles are of different devices: /device:TPU:34 before, /device:TPU:27 now
where the time goes in v11:
time: 199 us; the launch traced here: 197 us
  starting transfers between devices  93.8 us (47%)
  waiting for transfers between devices  50.5 us (25%)
  local copies, waits for them, and re-layouts  21.6 us (11%)
  Pallas kernels  13.7 us (7%)
  blocking collectives  11 us (6%)
  other arithmetic  5.47 us (3%)
    ppermute x12, starting transfers between devices, turn(): lax.ppermute(block, axis, [(i, (i + step) % count) for i in range(count)])  36.1 us
    ppermute x12, waiting for transfers between devices, turn(): lax.ppermute(block, axis, [(i, (i + step) % count) for i in range(count)])  32.9 us
    unnamed x50, local copies, waits for them, and re-layouts  14.6 us
    pallas_call x6, Pallas kernels, local_call(): pl.pallas_call(kernel, out_shape=shapes, in_specs=[pl.BlockSpec(memory_sp...  13.7 us
    ppermute x4, starting transfers between devices, shift(): return lax.ppermute(block, axis, pairs)  12.7 us
    all_to_all x1, starting transfers between devices, per_device(): total = lax.all_to_all(total, 'zh', 0, 0)  12.5 us
    all_to_all x1, blocking collectives, per_device(): conv_out = lax.all_to_all(conv_out, 'zl', 0, 0)  11 us
    ppermute x4, waiting for transfers between devices, shift(): return lax.ppermute(block, axis, pairs)  10.6 us
  transfers between devices with their start and end apart: 23, of which 10 were waited for; matrix products, arithmetic and copies ran while one was open for 5% of the time, Pallas kernels for 3%

profile of v11, /device:TPU:27, one launch (start us, length us, event | category | flops | bytes accessed | tf_op | source)
XLA Modules:
  0.0 197.3 jit_solution(3684784372656788456)
XLA Ops:
  1.8 2.4 %collective-permute-start.4 = (bf16[5,72,512]{2,1,0:T(8,128)(2,1)S(1)}, bf16[5,72,512]{2,1,0:T(8,128)(2,1)S(1)}, u32[]{:S(2)}, u32[]{:S(2)}) collective-permute-start(bf16[5,72,512]{2,1,0:T(8,128)(2,1)S(1)} %slice_select_fusion), channel_id=1, source_target_pairs={{0,3},{1,0},{2,1},{3,2},{4,7},{5,4},{6,5},{7,6},{8,11},{9,8},{10,9... | collective-permute-start | bytes 1105928 | tf_op jit(solution)/shard_map/ppermute | solution.py:35
  4.2 2.6 %collective-permute-start.3 = (bf16[5,72,512]{2,1,0:T(8,128)(2,1)S(1)}, bf16[5,72,512]{2,1,0:T(8,128)(2,1)}, u32[]{:S(2)}, u32[]{:S(2)}) collective-permute-start(bf16[5,72,512]{2,1,0:T(8,128)(2,1)S(1)} %slice_select_fusion), channel_id=1, source_target_pairs={{0,2},{1,3},{2,0},{3,1},{4,6},{5,7},{6,4},{7,5},{8,10},{9,11},{10,... | collective-permute-start | bytes 1105928 | tf_op jit(solution)/shard_map/ppermute | solution.py:35
  6.8 3.8 %collective-permute-start.2 = (bf16[5,72,512]{2,1,0:T(8,128)(2,1)S(1)}, bf16[5,72,512]{2,1,0:T(8,128)(2,1)}, u32[]{:S(2)}, u32[]{:S(2)}) collective-permute-start(bf16[5,72,512]{2,1,0:T(8,128)(2,1)S(1)} %slice_select_fusion), channel_id=1, source_target_pairs={{0,1},{1,2},{2,3},{3,0},{4,5},{5,6},{6,7},{7,4},{8,9},{9,10},{10,1... | collective-permute-start | bytes 1105928 | tf_op jit(solution)/shard_map/ppermute | solution.py:35
  11.4 2.1 %collective-permute-start.1 = (bf16[8,1024]{1,0:T(8,128)(2,1)S(1)}, bf16[8,1024]{1,0:T(8,128)(2,1)S(1)}, u32[]{:S(2)}, u32[]{:S(2)}) collective-permute-start(bf16[8,1024]{1,0:T(8,128)(2,1)S(1)} %get-tuple-element.36), channel_id=1, source_target_pairs={{1,0},{2,1},{3,2},{4,3},{5,4},{6,5},{7,6},{8,7},{9,8},{10,9},{11,1... | collective-permute-start | bytes 49160 | tf_op jit(solution)/shard_map/ppermute | solution.py:30
  13.5 5.2 %collective-permute-start = (bf16[8,1024]{1,0:T(8,128)(2,1)S(1)}, bf16[8,1024]{1,0:T(8,128)(2,1)S(1)}, u32[]{:S(2)}, u32[]{:S(2)}) collective-permute-start(bf16[8,1024]{1,0:T(8,128)(2,1)S(1)} %get-tuple-element.37), channel_id=1, source_target_pairs={{0,1},{1,2},{2,3},{3,4},{4,5},{5,6},{6,7},{7,8},{8,9},{9,10},{10,1... | collective-permute-start | bytes 49160 | tf_op jit(solution)/shard_map/ppermute | solution.py:30
  19.8 5.3 %collective-permute-done.low_ref = bf16[8,1024]{1,0:T(8,128)(2,1)S(1)} collective-permute-done((bf16[8,1024]{1,0:T(8,128)(2,1)S(1)}, bf16[8,1024]{1,0:T(8,128)(2,1)S(1)}, u32[]{:S(2)}, u32[]{:S(2)}) %collective-permute-start) | collective-permute-done | bytes 16416 | tf_op jit(solution)/shard_map/ppermute | solution.py:30
  26.5 5.6 %all-to-all-start = ((bf16[4,72,1024]{2,1,0:T(8,128)(2,1)}), bf16[4,72,1024]{2,1,0:T(8,128)(2,1)S(1)}, u32[]{:S(2)}, u32[]{:S(2)}) async-start(bf16[4,72,1024]{2,1,0:T(8,128)(2,1)} %broadcast_in_dim.18), calls=%async_computation | async-start | bytes 1179648 | tf_op jit(solution)/shard_map/all_to_all | solution.py:40
  34.3 3.9 %collective-permute-start.5 = (bf16[5,288,512]{2,1,0:T(8,128)(2,1)S(1)}, bf16[5,288,512]{2,1,0:T(8,128)(2,1)S(1)}, u32[]{:S(2)}, u32[]{:S(2)}) collective-permute-start(bf16[5,288,512]{2,1,0:T(8,128)(2,1)S(1)} %bitcast.32), channel_id=1, source_target_pairs={{0,16},{16,0},{1,17},{17,1},{2,18},{18,2},{3,19},{19,3},{4,20},{20... | collective-permute-start | bytes 4423688 | tf_op jit(solution)/shard_map/ppermute | solution.py:312
  41.3 2.2 %collective-permute-start.8 = (bf16[4,32,72]{2,1,0:T(8,128)(2,1)S(1)}, bf16[4,32,72]{2,1,0:T(8,128)(2,1)S(1)}, u32[]{:S(2)}, u32[]{:S(2)}) collective-permute-start(bf16[4,32,72]{2,1,0:T(8,128)(2,1)S(1)} %get-tuple-element.38), channel_id=1, source_target_pairs={{0,3},{1,0},{2,1},{3,2},{4,7},{5,4},{6,5},{7,6},{8,11},{9,8},{10,9... | collective-permute-start | bytes 55304 | tf_op jit(solution)/shard_map/ppermute | solution.py:35
  43.5 4.0 %collective-permute-start.7 = (bf16[4,32,72]{2,1,0:T(8,128)(2,1)S(1)}, bf16[4,32,72]{2,1,0:T(8,128)(2,1)S(1)}, u32[]{:S(2)}, u32[]{:S(2)}) collective-permute-start(bf16[4,32,72]{2,1,0:T(8,128)(2,1)S(1)} %get-tuple-element.39), channel_id=1, source_target_pairs={{0,2},{1,3},{2,0},{3,1},{4,6},{5,7},{6,4},{7,5},{8,10},{9,11},{10,... | collective-permute-start | bytes 55304 | tf_op jit(solution)/shard_map/ppermute | solution.py:35
  47.5 2.5 %collective-permute-start.6 = (bf16[4,32,72]{2,1,0:T(8,128)(2,1)S(1)}, bf16[4,32,72]{2,1,0:T(8,128)(2,1)S(1)}, u32[]{:S(2)}, u32[]{:S(2)}) collective-permute-start(bf16[4,32,72]{2,1,0:T(8,128)(2,1)S(1)} %get-tuple-element.40), channel_id=1, source_target_pairs={{0,1},{1,2},{2,3},{3,0},{4,5},{5,6},{6,7},{7,4},{8,9},{9,10},{10,1... | collective-permute-start | bytes 55304 | tf_op jit(solution)/shard_map/ppermute | solution.py:35
  55.9 2.5 %shard_map.59 = bf16[4,96,288]{2,1,0:T(8,128)(2,1)S(1)} custom-call(s32[3]{0:T(128)S(1)} %pad_add_fusion.where_ref, bf16[288,1024]{1,0:T(8,128)(2,1)S(1)} %bitcast.35, bf16[5,288,512]{2,1,0:T(8,128)(2,1)S(1)} %bitcast.33, bf16[5,288,512]{2,1,0:T(8,128)(2,1)S(1)} %collective-permute-done.5.second_ref, bf16[4,32,72]{2,1,0:T(8,128)(2,1)S(1)} %copy-done.11, ...), custom_call_target="tpu_custom_call" | custom-call | tf_op jit(solution)/shard_map/pallas_call | solution.py:45
  58.4 11.0 %all_to_all.30.y_ref = bf16[4,96,288]{2,1,0:T(8,128)(2,1)S(1)} all-to-all(bf16[4,96,288]{2,1,0:T(8,128)(2,1)S(1)} %shard_map.59), channel_id=1, replica_groups=mesh['zh'=4,'x'=4,'core'=2,'zl'=4,'y'=4] {'zl'}, dimensions={0} | all-to-all | bytes 442368 | tf_op jit(solution)/shard_map/all_to_all | solution.py:329
  73.6 8.2 %all-to-all-start.2 = ((bf16[16,96,128]{2,1,0:T(8,128)(2,1)}), bf16[16,96,128]{2,1,0:T(8,128)(2,1)}, u32[]{:S(2)}, u32[]{:S(2)}) async-start(bf16[16,96,128]{2,1,0:T(8,128)(2,1)} %copy-done.8), calls=%async_computation.2 | async-start | bytes 786432 | tf_op jit(solution)/shard_map/all_to_all | solution.py:331
  81.8 3.1 %collective-permute-start.11 = (bf16[288,1024]{1,0:T(8,128)(2,1)S(1)}, bf16[288,1024]{1,0:T(8,128)(2,1)S(1)}, u32[]{:S(2)}, u32[]{:S(2)}) collective-permute-start(bf16[288,1024]{1,0:T(8,128)(2,1)S(1)} %bitcast.36), channel_id=1, source_target_pairs={{0,2},{1,3},{2,0},{3,1},{4,6},{5,7},{6,4},{7,5},{8,10},{9,11},{10,... | collective-permute-start | bytes 1769480 | tf_op jit(solution)/shard_map/ppermute | solution.py:35
  86.8 4.6 %collective-permute-start.9 = (bf16[288,1024]{1,0:T(8,128)(2,1)S(1)}, bf16[288,1024]{1,0:T(8,128)(2,1)S(1)}, u32[]{:S(2)}, u32[]{:S(2)}) collective-permute-start(bf16[288,1024]{1,0:T(8,128)(2,1)S(1)} %bitcast.38), channel_id=1, source_target_pairs={{0,1},{1,2},{2,3},{3,0},{4,5},{5,6},{6,7},{7,4},{8,9},{9,10},{10,1... | collective-permute-start | bytes 1769480 | tf_op jit(solution)/shard_map/ppermute | solution.py:35
  91.4 10.2 %collective-permute-done.11.refs_3_ = bf16[288,1024]{1,0:T(8,128)(2,1)S(1)} collective-permute-done((bf16[288,1024]{1,0:T(8,128)(2,1)S(1)}, bf16[288,1024]{1,0:T(8,128)(2,1)S(1)}, u32[]{:S(2)}, u32[]{:S(2)}) %collective-permute-start.11) | collective-permute-done | bytes 589856 | tf_op jit(solution)/shard_map/ppermute | solution.py:35
  102.5 13.0 %collective-permute-done.10.refs_2_ = bf16[288,1024]{1,0:T(8,128)(2,1)S(1)} collective-permute-done((bf16[288,1024]{1,0:T(8,128)(2,1)S(1)}, bf16[288,1024]{1,0:T(8,128)(2,1)S(1)}, u32[]{:S(2)}, u32[]{:S(2)}) %collective-permute-start.10) | collective-permute-done | bytes 589856 | tf_op jit(solution)/shard_map/ppermute | solution.py:35
  120.4 4.6 %shard_map.61 = (f32[16,32,360]{2,1,0:T(8,128)S(1)}, bf16[16,32,360]{2,1,0:T(8,128)(2,1)S(1)}, bf16[512,72]{1,0:T(8,128)(2,1)S(1)}) custom-call(s32[3]{0:T(128)S(1)} %pad_add_fusion.where_ref, bf16[16,96,128]{2,1,0:T(8,128)(2,1)} %all-to-all-done.2.back_ref, bf16[288,1024]{1,0:T(8,128)(2,1)S(1)} %bitcast.39, bf16[288,1024]{1,0:T(8,128)(2,1)S(1)} %copy-done.7, ...), custom_call_target="tpu_custom_call" | custom-call | tf_op jit(solution)/shard_map/pallas_call | solution.py:45
  125.0 2.4 %collective-permute-start.17 = (bf16[16,32,360]{2,1,0:T(8,128)(2,1)S(1)}, bf16[16,32,360]{2,1,0:T(8,128)(2,1)S(1)}, u32[]{:S(2)}, u32[]{:S(2)}) collective-permute-start(bf16[16,32,360]{2,1,0:T(8,128)(2,1)S(1)} %get-tuple-element.26), channel_id=1, source_target_pairs={{0,16},{16,0},{1,17},{17,1},{2,18},{18,2},{3,19},{19,3},{4,20},{20... | collective-permute-start | bytes 1105928 | tf_op jit(solution)/shard_map/ppermute | solution.py:344
  129.7 4.3 %all-to-all-start.4 = ((bf16[4,4,32,360]{3,2,1,0:T(8,128)(2,1)}), bf16[4,4,32,360]{3,2,1,0:T(8,128)(2,1)}, u32[]{:S(2)}, u32[]{:S(2)}) async-start(bf16[4,4,32,360]{3,2,1,0:T(8,128)(2,1)} %bitcast.41), calls=%async_computation.4 | async-start | bytes 786432 | tf_op jit(solution)/shard_map/all_to_all | solution.py:346
  134.0 3.2 %collective-permute-start.12 = (bf16[4,8,288]{2,1,0:T(8,128)(2,1)S(1)}, bf16[4,8,288]{2,1,0:T(8,128)(2,1)S(1)}, u32[]{:S(2)}, u32[]{:S(2)}) collective-permute-start(bf16[4,8,288]{2,1,0:T(8,128)(2,1)S(1)} %copy-done.23), channel_id=1, source_target_pairs={{0,1},{1,2},{2,3},{3,4},{4,5},{5,6},{6,7},{7,8},{8,9},{9,10},{10,1... | collective-permute-start | bytes 55304 | tf_op jit(solution)/shard_map/ppermute | solution.py:30
  137.2 2.1 %collective-permute-start.13 = (bf16[4,8,288]{2,1,0:T(8,128)(2,1)S(1)}, bf16[4,8,288]{2,1,0:T(8,128)(2,1)S(1)}, u32[]{:S(2)}, u32[]{:S(2)}) collective-permute-start(bf16[4,8,288]{2,1,0:T(8,128)(2,1)S(1)} %copy-done.21), channel_id=1, source_target_pairs={{1,0},{2,1},{3,2},{4,3},{5,4},{6,5},{7,6},{8,7},{9,8},{10,9},{11,1... | collective-permute-start | bytes 55304 | tf_op jit(solution)/shard_map/ppermute | solution.py:30
  139.3 4.6 %collective-permute-done.13 = bf16[4,8,288]{2,1,0:T(8,128)(2,1)S(1)} collective-permute-done((bf16[4,8,288]{2,1,0:T(8,128)(2,1)S(1)}, bf16[4,8,288]{2,1,0:T(8,128)(2,1)S(1)}, u32[]{:S(2)}, u32[]{:S(2)}) %collective-permute-start.13) | collective-permute-done | bytes 18464 | tf_op jit(solution)/shard_map/ppermute | solution.py:30
  144.6 8.2 %all-to-all-start.3 = ((bf16[4,80,288]{2,1,0:T(8,128)(2,1)}), bf16[4,80,288]{2,1,0:T(8,128)(2,1)S(1)}, u32[]{:S(2)}, u32[]{:S(2)}) async-start(bf16[4,80,288]{2,1,0:T(8,128)(2,1)} %pad_maximum_fusion), calls=%async_computation.3 | async-start | bytes 491520 | tf_op jit(solution)/shard_map/all_to_all | solution.py:334
  154.5 5.7 %all-to-all-done.3 = bf16[4,80,288]{2,1,0:T(8,128)(2,1)S(1)} async-done(((bf16[4,80,288]{2,1,0:T(8,128)(2,1)}), bf16[4,80,288]{2,1,0:T(8,128)(2,1)S(1)}, u32[]{:S(2)}, u32[]{:S(2)}) %all-to-all-start.3) | async-done | bytes 184352 | tf_op jit(solution)/shard_map/all_to_all | solution.py:334
  160.2 12.5 %all-to-all-start.5 = ((bf16[4,32,360]{2,1,0:T(8,128)(2,1)}), bf16[4,32,360]{2,1,0:T(8,128)(2,1)}, u32[]{:S(2)}, u32[]{:S(2)}) async-start(bf16[4,32,360]{2,1,0:T(8,128)(2,1)} %reduce_sum.21), calls=%async_computation.5 | async-start | bytes 196608 | tf_op jit(solution)/shard_map/all_to_all | solution.py:348
  172.6 3.0 %shard_map.62 = (bf16[64,1024]{1,0:T(8,128)(2,1)S(1)}, bf16[64,1024]{1,0:T(8,128)(2,1)S(1)}, bf16[64,1024]{1,0:T(8,128)(2,1)S(1)}, bf16[64,1024]{1,0:T(8,128)(2,1)S(1)}) custom-call(s32[3]{0:T(128)S(1)} %pad_add_fusion.where_ref, bf16[320,288]{1,0:T(8,128)(2,1)S(1)} %bitcast.40, bf16[5,288,512]{2,1,0:T(8,128)(2,1)S(1)} %bitcast.34, ...), custom_call_target="tpu_custom_call" | custom-call | tf_op jit(solution)/shard_map/pallas_call | solution.py:45
  177.6 3.4 %collective-permute-start.15 = (bf16[64,1024]{1,0:T(8,128)(2,1)S(1)}, bf16[64,1024]{1,0:T(8,128)(2,1)S(1)}, u32[]{:S(2)}, u32[]{:S(2)}) collective-permute-start(bf16[64,1024]{1,0:T(8,128)(2,1)S(1)} %get-tuple-element.23), channel_id=1, source_target_pairs={{0,4},{4,8},{8,12},{12,0},{1,5},{5,9},{9,13},{13,1},{2,6},{6,10},{... | collective-permute-start | bytes 393224 | tf_op jit(solution)/shard_map/ppermute | solution.py:35
  180.9 3.7 %collective-permute-start.16 = (bf16[64,1024]{1,0:T(8,128)(2,1)S(1)}, bf16[64,1024]{1,0:T(8,128)(2,1)S(1)}, u32[]{:S(2)}, u32[]{:S(2)}) collective-permute-start(bf16[64,1024]{1,0:T(8,128)(2,1)S(1)} %get-tuple-element.24), channel_id=1, source_target_pairs={{0,12},{4,0},{8,4},{12,8},{1,13},{5,1},{9,5},{13,9},{2,14},{6,2},{... | collective-permute-start | bytes 393224 | tf_op jit(solution)/shard_map/ppermute | solution.py:35
  184.7 6.1 %collective-permute-done.14.refs_1_ = bf16[64,1024]{1,0:T(8,128)(2,1)S(1)} collective-permute-done((bf16[64,1024]{1,0:T(8,128)(2,1)S(1)}, bf16[64,1024]{1,0:T(8,128)(2,1)S(1)}, u32[]{:S(2)}, u32[]{:S(2)}) %collective-permute-start.14) | collective-permute-done | bytes 131104 | tf_op jit(solution)/shard_map/ppermute | solution.py:35
  190.8 2.7 %collective-permute-done.16.refs_3_ = bf16[64,1024]{1,0:T(8,128)(2,1)S(1)} collective-permute-done((bf16[64,1024]{1,0:T(8,128)(2,1)S(1)}, bf16[64,1024]{1,0:T(8,128)(2,1)S(1)}, u32[]{:S(2)}, u32[]{:S(2)}) %collective-permute-start.16) | collective-permute-done | bytes 131104 | tf_op jit(solution)/shard_map/ppermute | solution.py:35
  (87 shorter events, 37.5 us)
Async XLA Ops:
  0.6 24.4 %copy-start = (bf16[128,1024]{1,0:T(8,128)(2,1)S(1)}, bf16[128,1024]{1,0:T(8,128)(2,1)}, u32[]{:S(2)}) copy-start(bf16[128,1024]{1,0:T(8,128)(2,1)} %act_ref.1) | copy-start | bytes 786436
  1.8 32.4 %collective-permute-start.4 = (bf16[5,72,512]{2,1,0:T(8,128)(2,1)S(1)}, bf16[5,72,512]{2,1,0:T(8,128)(2,1)S(1)}, u32[]{:S(2)}, u32[]{:S(2)}) collective-permute-start(bf16[5,72,512]{2,1,0:T(8,128)(2,1)S(1)} %slice_select_fusion), channel_id=1, source_target_pairs={{0,3},{1,0},{2,1},{3,2},{4,7},{5,4},{6,5},{7,6},{8,11},{9,8},{10,9... | collective-permute-start | bytes 1105928 | tf_op jit(solution)/shard_map/ppermute | solution.py:35
  4.2 29.0 %collective-permute-start.3 = (bf16[5,72,512]{2,1,0:T(8,128)(2,1)S(1)}, bf16[5,72,512]{2,1,0:T(8,128)(2,1)}, u32[]{:S(2)}, u32[]{:S(2)}) collective-permute-start(bf16[5,72,512]{2,1,0:T(8,128)(2,1)S(1)} %slice_select_fusion), channel_id=1, source_target_pairs={{0,2},{1,3},{2,0},{3,1},{4,6},{5,7},{6,4},{7,5},{8,10},{9,11},{10,... | collective-permute-start | bytes 1105928 | tf_op jit(solution)/shard_map/ppermute | solution.py:35
  6.8 25.4 %collective-permute-start.2 = (bf16[5,72,512]{2,1,0:T(8,128)(2,1)S(1)}, bf16[5,72,512]{2,1,0:T(8,128)(2,1)}, u32[]{:S(2)}, u32[]{:S(2)}) collective-permute-start(bf16[5,72,512]{2,1,0:T(8,128)(2,1)S(1)} %slice_select_fusion), channel_id=1, source_target_pairs={{0,1},{1,2},{2,3},{3,0},{4,5},{5,6},{6,7},{7,4},{8,9},{9,10},{10,1... | collective-permute-start | bytes 1105928 | tf_op jit(solution)/shard_map/ppermute | solution.py:35
  11.4 8.4 %collective-permute-start.1 = (bf16[8,1024]{1,0:T(8,128)(2,1)S(1)}, bf16[8,1024]{1,0:T(8,128)(2,1)S(1)}, u32[]{:S(2)}, u32[]{:S(2)}) collective-permute-start(bf16[8,1024]{1,0:T(8,128)(2,1)S(1)} %get-tuple-element.36), channel_id=1, source_target_pairs={{1,0},{2,1},{3,2},{4,3},{5,4},{6,5},{7,6},{8,7},{9,8},{10,9},{11,1... | collective-permute-start | bytes 49160 | tf_op jit(solution)/shard_map/ppermute | solution.py:30
  13.5 11.5 %collective-permute-start = (bf16[8,1024]{1,0:T(8,128)(2,1)S(1)}, bf16[8,1024]{1,0:T(8,128)(2,1)S(1)}, u32[]{:S(2)}, u32[]{:S(2)}) collective-permute-start(bf16[8,1024]{1,0:T(8,128)(2,1)S(1)} %get-tuple-element.37), channel_id=1, source_target_pairs={{0,1},{1,2},{2,3},{3,4},{4,5},{5,6},{6,7},{7,8},{8,9},{9,10},{10,1... | collective-permute-start | bytes 49160 | tf_op jit(solution)/shard_map/ppermute | solution.py:30
  26.5 26.3 %all-to-all-start = ((bf16[4,72,1024]{2,1,0:T(8,128)(2,1)}), bf16[4,72,1024]{2,1,0:T(8,128)(2,1)S(1)}, u32[]{:S(2)}, u32[]{:S(2)}) async-start(bf16[4,72,1024]{2,1,0:T(8,128)(2,1)} %broadcast_in_dim.18), calls=%async_computation | async-start | bytes 1179648 | tf_op jit(solution)/shard_map/all_to_all | solution.py:40
  34.3 18.6 %collective-permute-start.5 = (bf16[5,288,512]{2,1,0:T(8,128)(2,1)S(1)}, bf16[5,288,512]{2,1,0:T(8,128)(2,1)S(1)}, u32[]{:S(2)}, u32[]{:S(2)}) collective-permute-start(bf16[5,288,512]{2,1,0:T(8,128)(2,1)S(1)} %bitcast.32), channel_id=1, source_target_pairs={{0,16},{16,0},{1,17},{17,1},{2,18},{18,2},{3,19},{19,3},{4,20},{20... | collective-permute-start | bytes 4423688 | tf_op jit(solution)/shard_map/ppermute | solution.py:312
  41.3 8.8 %collective-permute-start.8 = (bf16[4,32,72]{2,1,0:T(8,128)(2,1)S(1)}, bf16[4,32,72]{2,1,0:T(8,128)(2,1)S(1)}, u32[]{:S(2)}, u32[]{:S(2)}) collective-permute-start(bf16[4,32,72]{2,1,0:T(8,128)(2,1)S(1)} %get-tuple-element.38), channel_id=1, source_target_pairs={{0,3},{1,0},{2,1},{3,2},{4,7},{5,4},{6,5},{7,6},{8,11},{9,8},{10,9... | collective-permute-start | bytes 55304 | tf_op jit(solution)/shard_map/ppermute | solution.py:35
  43.5 7.2 %collective-permute-start.7 = (bf16[4,32,72]{2,1,0:T(8,128)(2,1)S(1)}, bf16[4,32,72]{2,1,0:T(8,128)(2,1)S(1)}, u32[]{:S(2)}, u32[]{:S(2)}) collective-permute-start(bf16[4,32,72]{2,1,0:T(8,128)(2,1)S(1)} %get-tuple-element.39), channel_id=1, source_target_pairs={{0,2},{1,3},{2,0},{3,1},{4,6},{5,7},{6,4},{7,5},{8,10},{9,11},{10,... | collective-permute-start | bytes 55304 | tf_op jit(solution)/shard_map/ppermute | solution.py:35
  47.5 4.7 %collective-permute-start.6 = (bf16[4,32,72]{2,1,0:T(8,128)(2,1)S(1)}, bf16[4,32,72]{2,1,0:T(8,128)(2,1)S(1)}, u32[]{:S(2)}, u32[]{:S(2)}) collective-permute-start(bf16[4,32,72]{2,1,0:T(8,128)(2,1)S(1)} %get-tuple-element.40), channel_id=1, source_target_pairs={{0,1},{1,2},{2,3},{3,0},{4,5},{5,6},{6,7},{7,4},{8,9},{9,10},{10,1... | collective-permute-start | bytes 55304 | tf_op jit(solution)/shard_map/ppermute | solution.py:35
  73.6 43.6 %all-to-all-start.2 = ((bf16[16,96,128]{2,1,0:T(8,128)(2,1)}), bf16[16,96,128]{2,1,0:T(8,128)(2,1)}, u32[]{:S(2)}, u32[]{:S(2)}) async-start(bf16[16,96,128]{2,1,0:T(8,128)(2,1)} %copy-done.8), calls=%async_computation.2 | async-start | bytes 786432 | tf_op jit(solution)/shard_map/all_to_all | solution.py:331
  81.8 19.8 %collective-permute-start.11 = (bf16[288,1024]{1,0:T(8,128)(2,1)S(1)}, bf16[288,1024]{1,0:T(8,128)(2,1)S(1)}, u32[]{:S(2)}, u32[]{:S(2)}) collective-permute-start(bf16[288,1024]{1,0:T(8,128)(2,1)S(1)} %bitcast.36), channel_id=1, source_target_pairs={{0,2},{1,3},{2,0},{3,1},{4,6},{5,7},{6,4},{7,5},{8,10},{9,11},{10,... | collective-permute-start | bytes 1769480 | tf_op jit(solution)/shard_map/ppermute | solution.py:35
  84.9 30.6 %collective-permute-start.10 = (bf16[288,1024]{1,0:T(8,128)(2,1)S(1)}, bf16[288,1024]{1,0:T(8,128)(2,1)S(1)}, u32[]{:S(2)}, u32[]{:S(2)}) collective-permute-start(bf16[288,1024]{1,0:T(8,128)(2,1)S(1)} %bitcast.37), channel_id=1, source_target_pairs={{0,3},{1,0},{2,1},{3,2},{4,7},{5,4},{6,5},{7,6},{8,11},{9,8},{10,9... | collective-permute-start | bytes 1769480 | tf_op jit(solution)/shard_map/ppermute | solution.py:35
  86.8 29.5 %collective-permute-start.9 = (bf16[288,1024]{1,0:T(8,128)(2,1)S(1)}, bf16[288,1024]{1,0:T(8,128)(2,1)S(1)}, u32[]{:S(2)}, u32[]{:S(2)}) collective-permute-start(bf16[288,1024]{1,0:T(8,128)(2,1)S(1)} %bitcast.38), channel_id=1, source_target_pairs={{0,1},{1,2},{2,3},{3,0},{4,5},{5,6},{6,7},{7,4},{8,9},{9,10},{10,1... | collective-permute-start | bytes 1769480 | tf_op jit(solution)/shard_map/ppermute | solution.py:35
  117.2 1.1 copy-start.3
  118.3 1.1 copy-start.5
  125.0 4.7 %copy-start.12 = (bf16[512,72]{1,0:T(8,128)(2,1)}, bf16[512,72]{1,0:T(8,128)(2,1)S(1)}, u32[]{:S(2)}) copy-start(bf16[512,72]{1,0:T(8,128)(2,1)S(1)} %get-tuple-element.33) | copy-start | bytes 221188
  125.0 9.0 %copy-start.23 = (bf16[4,8,288]{2,1,0:T(8,128)(2,1)S(1)}, bf16[4,8,288]{2,1,0:T(8,128)(2,1)}, u32[]{:S(2)}) copy-start(bf16[4,8,288]{2,1,0:T(8,128)(2,1)} %copy-done.22) | copy-start | bytes 55300
  125.0 12.1 %copy-start.21 = (bf16[4,8,288]{2,1,0:T(8,128)(2,1)S(1)}, bf16[4,8,288]{2,1,0:T(8,128)(2,1)}, u32[]{:S(2)}) copy-start(bf16[4,8,288]{2,1,0:T(8,128)(2,1)} %copy-done.20) | copy-start | bytes 55300
  125.0 18.8 %copy-start.10 = (bf16[4,64,288]{2,1,0:T(8,128)(2,1)S(1)}, bf16[4,64,288]{2,1,0:T(8,128)(2,1)}, u32[]{:S(2)}) copy-start(bf16[4,64,288]{2,1,0:T(8,128)(2,1)} %copy-done.9) | copy-start | bytes 442372
  125.0 3.8 %collective-permute-start.17 = (bf16[16,32,360]{2,1,0:T(8,128)(2,1)S(1)}, bf16[16,32,360]{2,1,0:T(8,128)(2,1)S(1)}, u32[]{:S(2)}, u32[]{:S(2)}) collective-permute-start(bf16[16,32,360]{2,1,0:T(8,128)(2,1)S(1)} %get-tuple-element.26), channel_id=1, source_target_pairs={{0,16},{16,0},{1,17},{17,1},{2,18},{18,2},{3,19},{19,3},{4,20},{20... | collective-permute-start | bytes 1105928 | tf_op jit(solution)/shard_map/ppermute | solution.py:344
  129.7 14.9 %all-to-all-start.4 = ((bf16[4,4,32,360]{3,2,1,0:T(8,128)(2,1)}), bf16[4,4,32,360]{3,2,1,0:T(8,128)(2,1)}, u32[]{:S(2)}, u32[]{:S(2)}) async-start(bf16[4,4,32,360]{3,2,1,0:T(8,128)(2,1)} %bitcast.41), calls=%async_computation.4 | async-start | bytes 786432 | tf_op jit(solution)/shard_map/all_to_all | solution.py:346
  134.0 5.3 %collective-permute-start.12 = (bf16[4,8,288]{2,1,0:T(8,128)(2,1)S(1)}, bf16[4,8,288]{2,1,0:T(8,128)(2,1)S(1)}, u32[]{:S(2)}, u32[]{:S(2)}) collective-permute-start(bf16[4,8,288]{2,1,0:T(8,128)(2,1)S(1)} %copy-done.23), channel_id=1, source_target_pairs={{0,1},{1,2},{2,3},{3,4},{4,5},{5,6},{6,7},{7,8},{8,9},{9,10},{10,1... | collective-permute-start | bytes 55304 | tf_op jit(solution)/shard_map/ppermute | solution.py:30
  137.2 6.7 %collective-permute-start.13 = (bf16[4,8,288]{2,1,0:T(8,128)(2,1)S(1)}, bf16[4,8,288]{2,1,0:T(8,128)(2,1)S(1)}, u32[]{:S(2)}, u32[]{:S(2)}) collective-permute-start(bf16[4,8,288]{2,1,0:T(8,128)(2,1)S(1)} %copy-done.21), channel_id=1, source_target_pairs={{1,0},{2,1},{3,2},{4,3},{5,4},{6,5},{7,6},{8,7},{9,8},{10,9},{11,1... | collective-permute-start | bytes 55304 | tf_op jit(solution)/shard_map/ppermute | solution.py:30
  144.6 15.6 %all-to-all-start.3 = ((bf16[4,80,288]{2,1,0:T(8,128)(2,1)}), bf16[4,80,288]{2,1,0:T(8,128)(2,1)S(1)}, u32[]{:S(2)}, u32[]{:S(2)}) async-start(bf16[4,80,288]{2,1,0:T(8,128)(2,1)} %pad_maximum_fusion), calls=%async_computation.3 | async-start | bytes 491520 | tf_op jit(solution)/shard_map/all_to_all | solution.py:334
  160.2 35.5 %all-to-all-start.5 = ((bf16[4,32,360]{2,1,0:T(8,128)(2,1)}), bf16[4,32,360]{2,1,0:T(8,128)(2,1)}, u32[]{:S(2)}, u32[]{:S(2)}) async-start(bf16[4,32,360]{2,1,0:T(8,128)(2,1)} %reduce_sum.21), calls=%async_computation.5 | async-start | bytes 196608 | tf_op jit(solution)/shard_map/all_to_all | solution.py:348
  172.6 20.8 %copy-start.1 = (bf16[128,1024]{1,0:T(8,128)(2,1)S(1)}, bf16[128,1024]{1,0:T(8,128)(2,1)}, u32[]{:S(2)}) copy-start(bf16[128,1024]{1,0:T(8,128)(2,1)} %act_ref.1) | copy-start | bytes 786436
  172.6 22.3 %copy-start.13 = (bf16[512,72]{1,0:T(8,128)(2,1)S(1)}, bf16[512,72]{1,0:T(8,128)(2,1)}, u32[]{:S(2)}) copy-start(bf16[512,72]{1,0:T(8,128)(2,1)} %copy-done.12) | copy-start | bytes 221188
  175.6 15.1 %collective-permute-start.14 = (bf16[64,1024]{1,0:T(8,128)(2,1)S(1)}, bf16[64,1024]{1,0:T(8,128)(2,1)S(1)}, u32[]{:S(2)}, u32[]{:S(2)}) collective-permute-start(bf16[64,1024]{1,0:T(8,128)(2,1)S(1)} %get-tuple-element.22), channel_id=1, source_target_pairs={{0,8},{4,12},{8,0},{12,4},{1,9},{5,13},{9,1},{13,5},{2,10},{6,14},... | collective-permute-start | bytes 393224 | tf_op jit(solution)/shard_map/ppermute | solution.py:35
  177.6 13.2 %collective-permute-start.15 = (bf16[64,1024]{1,0:T(8,128)(2,1)S(1)}, bf16[64,1024]{1,0:T(8,128)(2,1)S(1)}, u32[]{:S(2)}, u32[]{:S(2)}) collective-permute-start(bf16[64,1024]{1,0:T(8,128)(2,1)S(1)} %get-tuple-element.23), channel_id=1, source_target_pairs={{0,4},{4,8},{8,12},{12,0},{1,5},{5,9},{9,13},{13,1},{2,6},{6,10},{... | collective-permute-start | bytes 393224 | tf_op jit(solution)/shard_map/ppermute | solution.py:35
  180.9 12.5 %collective-permute-start.16 = (bf16[64,1024]{1,0:T(8,128)(2,1)S(1)}, bf16[64,1024]{1,0:T(8,128)(2,1)S(1)}, u32[]{:S(2)}, u32[]{:S(2)}) collective-permute-start(bf16[64,1024]{1,0:T(8,128)(2,1)S(1)} %get-tuple-element.24), channel_id=1, source_target_pairs={{0,12},{4,0},{8,4},{12,8},{1,13},{5,1},{9,5},{13,9},{2,14},{6,2},{... | collective-permute-start | bytes 393224 | tf_op jit(solution)/shard_map/ppermute | solution.py:35
  (15 other events, 11.1 us)
